TPU v7x, 32 devices: a whole 2x2x4 slice. The times are simulated.
32 devices in a mesh: groups: 2 (over x), expert: 16 (over z, y, core).
Axes of the slice: x: 2, y: 2, z: 4, core: 2. Of those that a mesh axis runs over, the one named last changes fastest.
Arguments:
- h_rows: bfloat16 [4096, 8, 768], P(('groups', 'expert')), parts along dimension 0, may hold values from -6 to 6
- gates: float32 [4096, 8], P(('groups', 'expert')), parts along dimension 0, may hold values from 0.05 to 0.5
- expert_ids: int32 [4096, 8], P(('groups', 'expert')), parts along dimension 0, may hold values from 0 to 15, all different within a row; in each aligned block of 128 rows (0 to 127, 128 to 255, ...) at most 96 rows name the same one
- cotangent: bfloat16 [4096, 2048], P(('groups', 'expert')), parts along dimension 0, may hold values from -1.1953125 to 1.1953125
- down_weight: bfloat16 [16, 768, 2048], P('expert'), may hold values from -0.21875 to 0.21875
- swapped: int32 [8], replicated, may hold values 0 or 1
Outputs:
- mixed: bfloat16 [4096, 2048], P(('groups', 'expert')), parts along dimension 0
- gate_grad: float32 [4096, 8], P(('groups', 'expert')), parts along dimension 0
- h_grad: bfloat16 [4096, 8, 768], P(('groups', 'expert')), parts along dimension 0
- weight_grad: bfloat16 [32, 768, 2048], P(('groups', 'expert')), parts along dimension 0
There are 2 independent parts, one for each index of `groups`. A program takes and returns all parts, laid end to end along the dimension named above; an argument that names none is the same for every part. Nothing has to cross between parts.
Inputs may be any that keep to these rules, and one draw needn't show every extreme that they name: `expert_ids`: among the rows of one device, no expert is named by more than 96 of the (token, choice) pairs, and in every draw some expert is named by exactly 96 of them on some device; each token names 8 different experts.
All inputs are finite; a program needn't handle non-finite values.
Results may differ from a plain program's by a relative error of at most 0.008.
Values may be sent and summed in bfloat16 or wider, within the bound.
No kernel may reach another device: no remote copies, remote signals or barrier semaphores. Data moves between devices by JAX's collectives and lax.ppermute only.
A program may use at most 128 MiB of HBM per device.

v0:
```python
import jax
import jax.numpy as jnp
from jax import lax
from jax.sharding import PartitionSpec as P


def passed_along(value, axis, steps):
    count = lax.axis_size(axis)
    pairs = [(source, (source + steps) % count) for source in range(count)]
    return lax.ppermute(value, axis, pairs)


def place_rows(values, target, ranks, devices, capacity):
    buffer = jnp.zeros((devices, capacity, values.shape[-1]), values.dtype)
    return buffer.at[target, ranks].set(values)


def shards(h_rows, gates, expert_ids, cotangent, down_weight, swapped):
    devices = lax.axis_size("expert")
    half_way = devices // 2
    here = lax.axis_index("expert")
    tokens_here, top_count, hidden = h_rows.shape
    width = cotangent.shape[1]
    capacity = min(tokens_here, 3 * tokens_here * top_count // (2 * devices))
    experts = jnp.arange(devices, dtype=jnp.int32)
    flat_ids = expert_ids.reshape(-1)
    own_weight = down_weight[0]
    flag = swapped[here % half_way]
    partner_weight = passed_along(down_weight, "expert", half_way)[0]
    weight = jnp.where(flag > 0, partner_weight, own_weight)
    onehot = (flat_ids[:, None] == experts[None, :]).astype(jnp.int32)
    ranks = jnp.sum((jnp.cumsum(onehot, axis=0) - onehot) * onehot, axis=1)
    send_h = place_rows(h_rows.reshape(-1, hidden), flat_ids, ranks, devices, capacity)
    received = lax.all_to_all(send_h, "expert", split_axis=0, concat_axis=0, tiled=True)
    result = jnp.einsum("sch,hd->scd", received, weight, preferred_element_type=jnp.float32)
    results = result.astype(jnp.bfloat16)
    returned = lax.all_to_all(results, "expert", split_axis=0, concat_axis=0, tiled=True)
    out_rows = returned[flat_ids, ranks].reshape(tokens_here, top_count, width)
    mixed = jnp.einsum("tk,tkd->td", gates, out_rows.astype(jnp.float32)).astype(jnp.bfloat16)
    gate_grad = jnp.einsum("td,tkd->tk", cotangent, out_rows, preferred_element_type=jnp.float32)
    scaled = (gates[:, :, None] * cotangent[:, None, :].astype(jnp.float32)).astype(jnp.bfloat16)
    send_z = place_rows(scaled.reshape(-1, width), flat_ids, ranks, devices, capacity)
    recv_z = lax.all_to_all(send_z, "expert", split_axis=0, concat_axis=0, tiled=True)
    flat_z = recv_z.reshape(-1, width)
    flat_h = received.reshape(-1, hidden)
    grad_sum = lax.dot_general(
        flat_h, flat_z, (((0,), (0,)), ((), ())), preferred_element_type=jnp.float32
    )
    back = lax.dot_general(
        flat_z, weight, (((1,), (1,)), ((), ())), preferred_element_type=jnp.float32
    ).astype(jnp.bfloat16)
    back_rows = lax.all_to_all(
        back.reshape(devices, capacity, hidden), "expert", split_axis=0, concat_axis=0, tiled=True
    )
    h_grad = back_rows[flat_ids, ranks].reshape(tokens_here, top_count, hidden)
    own_grad = grad_sum.astype(jnp.bfloat16)[None]
    partner_grad = passed_along(own_grad, "expert", half_way)
    weight_grad = jnp.where(flag > 0, partner_grad, own_grad)
    return (mixed, gate_grad, h_grad, weight_grad)


def solution(mesh):
    in_specs = (
        P(("groups", "expert"), None, None),
        P(("groups", "expert"), None),
        P(("groups", "expert"), None),
        P(("groups", "expert"), None),
        P("expert", None, None),
        P(),
    )
    out_specs = (
        P(("groups", "expert"), None),
        P(("groups", "expert"), None),
        P(("groups", "expert"), None, None),
        P(("groups", "expert"), None, None),
    )
    return jax.shard_map(shards, mesh=mesh, in_specs=in_specs, out_specs=out_specs, check_vma=False)
```

profile of v0, /device:TPU:0, one launch (start us, length us, event | category | flops | bytes accessed | tf_op | source)
XLA Modules:
  0.0 725.4 jit_solution(1131208353273639457)
XLA Ops:
  0.6 0.0 copy-start
  0.6 0.9 copy.12
  1.6 0.1 eq.31
  1.6 0.1 eq.27
  1.7 0.1 reshape.97
  1.8 4.5 reduce-window.6
  6.4 0.1 slice.12
  6.4 0.1 copy.15
  6.6 0.1 copy.16
  6.7 0.1 broadcast_add_fusion
  6.8 0.8 and_reduce_fusion
  7.6 0.7 multiply_reduce_fusion
  8.3 0.0 copy-done
  8.4 6.9 scatter_custom_fusion
  15.2 0.0 copy-start.3
  15.2 0.0 copy-start.2
  15.2 7.6 %all-to-all-start = ((bf16[16,96,768]{2,1,0:T(8,128)(2,1)}), bf16[16,96,768]{2,1,0:T(8,128)(2,1)}, u32[]{:S(2)}, u32[]{:S(2)}) async-start(bf16[16,96,768]{2,1,0:T(8,128)(2,1)} %bitcast.67), calls=%async_computation | async-start | bytes 4718592 | tf_op jit(solution)/shard_map/all_to_all | solution.py:34
  22.8 0.0 copy-done.3
  22.8 0.1 copy.17
  22.9 0.1 mul.22
  23.0 0.0 copy-done.2
  23.0 0.1 convert_element_type.32
  23.1 10.6 %scatter_custom_fusion.1 = bf16[1536,2048]{1,0:T(8,128)(2,1)} fusion(s32[1024]{0:T(1024)S(1)} %broadcast_select_fusion.4, f32[128,2048]{1,0:T(8,128)S(1)} %convert_element_type.32, f32[1024]{0:T(1024)S(1)} %mul.22, bf16[]{:T(256)} %constant.24.clone.1), kind=kCustom, calls=%fused_computation.8 | custom fusion | flops 4194304 | bytes 7344130
  33.7 34.8 %all-to-all-done = bf16[16,96,768]{2,1,0:T(8,128)(2,1)} async-done(((bf16[16,96,768]{2,1,0:T(8,128)(2,1)}), bf16[16,96,768]{2,1,0:T(8,128)(2,1)}, u32[]{:S(2)}, u32[]{:S(2)}) %all-to-all-start) | async-done | bytes 2359328 | tf_op jit(solution)/shard_map/all_to_all | solution.py:34
  68.5 0.0 copy-start.5
  68.6 12.5 %all-to-all-start.2 = ((bf16[16,96,2048]{2,1,0:T(8,128)(2,1)}), bf16[16,96,2048]{2,1,0:T(8,128)(2,1)}, u32[]{:S(2)}, u32[]{:S(2)}) async-start(bf16[16,96,2048]{2,1,0:T(8,128)(2,1)} %bitcast.66), calls=%async_computation.2 | async-start | bytes 12582912 | tf_op jit(solution)/shard_map/all_to_all | solution.py:43
  81.0 2.9 collective-permute-start
  83.9 0.0 copy-done.5
  83.9 0.6 dynamic_slice.3
  85.1 269.8 %collective-permute-done = bf16[1,768,2048]{2,1,0:T(8,128)(2,1)} collective-permute-done((bf16[1,768,2048]{2,1,0:T(8,128)(2,1)}, bf16[1,768,2048]{2,1,0:T(8,128)(2,1)}, u32[]{:S(2)}, u32[]{:S(2)}) %collective-permute-start) | collective-permute-done | bytes 3145760 | tf_op jit(solution)/shard_map/ppermute | solution.py:10
  354.9 9.1 %convolution_convert_fusion = bf16[16,96,2048]{2,1,0:T(8,128)(2,1)} fusion(bf16[16,96,768]{2,1,0:T(8,128)(2,1)} %all-to-all-done, bf16[1,768,2048]{2,1,0:T(8,128)(2,1)} %collective-permute-done, bf16[1,768,2048]{2,1,0:T(8,128)(2,1)} %param.10, pred[]{:T(512)} %bitcast.5), kind=kOutput, calls=%fused_computation.7 | convolution fusion | flops 4836556800 | bytes 14942209 | tf_op jit(solution)/shard_map/sch,hd->scd/dot_general | solution.py:35
  364.0 0.0 all-to-all-done.2
  364.0 4.6 all-to-all-start.1
  368.7 0.0 copy-start.4
  368.7 9.2 %fusion.12 = bf16[1,768,2048]{2,1,0:T(8,128)(2,1)} fusion(bf16[16,96,768]{2,1,0:T(8,128)(2,1)} %all-to-all-done, bf16[16,96,2048]{2,1,0:T(8,128)(2,1)} %all-to-all-done.2), kind=kOutput, calls=%fused_computation.21 | convolution fusion | flops 4833411072 | bytes 11796480 | tf_op jit(solution)/shard_map/dot_general | solution.py:46
  377.9 2.7 collective-permute-start.1
  380.6 0.0 copy-done.4
  380.6 8.2 %convolution_convert_fusion.1 = bf16[1536,768]{1,0:T(8,128)(2,1)} fusion(bf16[1536,2048]{1,0:T(8,128)(2,1)} %bitcast.16, bf16[1,768,2048]{2,1,0:T(8,128)(2,1)} %collective-permute-done, bf16[1,768,2048]{2,1,0:T(8,128)(2,1)S(1)} %copy-done.4, pred[]{:T(512)} %bitcast.5), kind=kOutput, calls=%fused_computation.15 | convolution fusion | flops 4834590720 | bytes 14942209 | tf_op jit(solution)/shard_map/dot_general | solution.py:49
  388.8 161.4 %all-to-all-done.1 = bf16[16,96,2048]{2,1,0:T(8,128)(2,1)} async-done(((bf16[16,96,2048]{2,1,0:T(8,128)(2,1)}), bf16[16,96,2048]{2,1,0:T(8,128)(2,1)}, u32[]{:S(2)}, u32[]{:S(2)}) %all-to-all-start.1) | async-done | bytes 6291488 | tf_op jit(solution)/shard_map/all_to_all | solution.py:37
  550.2 28.5 %all-to-all-start.3 = ((bf16[16,96,768]{2,1,0:T(8,128)(2,1)}), bf16[16,96,768]{2,1,0:T(8,128)(2,1)}, u32[]{:S(2)}, u32[]{:S(2)}) async-start(bf16[16,96,768]{2,1,0:T(8,128)(2,1)} %bitcast.68), calls=%async_computation.3 | async-start | bytes 4718592 | tf_op jit(solution)/shard_map/all_to_all | solution.py:52
  578.7 0.1 copy.18
  578.8 89.5 %collective-permute-done.1 = bf16[1,768,2048]{2,1,0:T(8,128)(2,1)} collective-permute-done((bf16[1,768,2048]{2,1,0:T(8,128)(2,1)}, bf16[1,768,2048]{2,1,0:T(8,128)(2,1)}, u32[]{:S(2)}, u32[]{:S(2)}) %collective-permute-start.1) | collective-permute-done | bytes 3145760 | tf_op jit(solution)/shard_map/ppermute | solution.py:10
  668.3 3.9 broadcast_select_fusion
  672.2 25.5 %gather_fusion = bf16[1024,2048]{1,0:T(8,128)(2,1)} fusion(bf16[16,96,2048]{2,1,0:T(8,128)(2,1)} %all-to-all-done.1, s32[1024]{0:T(1024)S(1)} %bitcast.64), kind=kCustom, calls=%fused_computation | custom fusion | bytes 8396800 | tf_op jit(solution)/shard_map/gather | solution.py:38
  697.8 0.0 copy-start.1
  697.8 3.6 fusion.5
  701.3 1.1 copy.27
  702.4 0.0 copy-done.1
  702.4 2.7 fusion.3
  705.1 0.7 copy.21
  705.8 0.0 all-to-all-done.3
  705.8 19.6 %gather_fusion.1 = bf16[1024,768]{1,0:T(8,128)(2,1)} fusion(bf16[16,96,768]{2,1,0:T(8,128)(2,1)} %all-to-all-done.3, s32[1024]{0:T(1024)S(1)} %bitcast.65), kind=kCustom, calls=%fused_computation.1 | custom fusion | bytes 3153920 | tf_op jit(solution)/shard_map/gather | solution.py:55
  (6 shorter events, 0.1 us)
Async XLA Ops:
  0.6 7.7 %copy-start = (bf16[128,8,768]{2,1,0:T(8,128)(2,1)S(1)}, bf16[128,8,768]{2,1,0:T(8,128)(2,1)}, u32[]{:S(2)}) copy-start(bf16[128,8,768]{2,1,0:T(8,128)(2,1)} %param.6) | copy-start | bytes 4718596
  15.2 7.6 %copy-start.3 = (f32[128,8]{0,1:T(8,128)S(1)}, f32[128,8]{0,1:T(8,128)}, u32[]{:S(2)}) copy-start(f32[128,8]{0,1:T(8,128)} %param.7) | copy-start | bytes 12292
  15.2 7.8 %copy-start.2 = (bf16[128,2048]{1,0:T(8,128)(2,1)S(1)}, bf16[128,2048]{1,0:T(8,128)(2,1)}, u32[]{:S(2)}) copy-start(bf16[128,2048]{1,0:T(8,128)(2,1)} %param.9) | copy-start | bytes 1572868
  15.2 53.3 %all-to-all-start = ((bf16[16,96,768]{2,1,0:T(8,128)(2,1)}), bf16[16,96,768]{2,1,0:T(8,128)(2,1)}, u32[]{:S(2)}, u32[]{:S(2)}) async-start(bf16[16,96,768]{2,1,0:T(8,128)(2,1)} %bitcast.67), calls=%async_computation | async-start | bytes 4718592 | tf_op jit(solution)/shard_map/all_to_all | solution.py:34
  68.5 15.3 %copy-start.5 = (s32[8]{0:T(128)S(1)}, s32[8]{0:T(128)}, u32[]{:S(2)}) copy-start(s32[8]{0:T(128)} %param.11) | copy-start | bytes 100
  68.6 295.5 %all-to-all-start.2 = ((bf16[16,96,2048]{2,1,0:T(8,128)(2,1)}), bf16[16,96,2048]{2,1,0:T(8,128)(2,1)}, u32[]{:S(2)}, u32[]{:S(2)}) async-start(bf16[16,96,2048]{2,1,0:T(8,128)(2,1)} %bitcast.66), calls=%async_computation.2 | async-start | bytes 12582912 | tf_op jit(solution)/shard_map/all_to_all | solution.py:43
  81.0 273.9 %collective-permute-start = (bf16[1,768,2048]{2,1,0:T(8,128)(2,1)}, bf16[1,768,2048]{2,1,0:T(8,128)(2,1)}, u32[]{:S(2)}, u32[]{:S(2)}) collective-permute-start(bf16[1,768,2048]{2,1,0:T(8,128)(2,1)} %param.10), channel_id=1, source_target_pairs={{0,8},{1,9},{2,10},{3,11},{4,12},{5,13},{6,14},{7,15},{8,0},{9,1},... | collective-permute-start | bytes 9437192 | tf_op jit(solution)/shard_map/ppermute | solution.py:10
  364.0 186.2 %all-to-all-start.1 = ((bf16[16,96,2048]{2,1,0:T(8,128)(2,1)}), bf16[16,96,2048]{2,1,0:T(8,128)(2,1)}, u32[]{:S(2)}, u32[]{:S(2)}) async-start(bf16[16,96,2048]{2,1,0:T(8,128)(2,1)} %convolution_convert_fusion), calls=%async_computation.1 | async-start | bytes 12582912 | tf_op jit(solution)/shard_map/all_to_all | solution.py:37
  368.7 11.9 %copy-start.4 = (bf16[1,768,2048]{2,1,0:T(8,128)(2,1)S(1)}, bf16[1,768,2048]{2,1,0:T(8,128)(2,1)}, u32[]{:S(2)}) copy-start(bf16[1,768,2048]{2,1,0:T(8,128)(2,1)} %param.10) | copy-start | bytes 9437188
  377.9 290.4 %collective-permute-start.1 = (bf16[1,768,2048]{2,1,0:T(8,128)(2,1)}, bf16[1,768,2048]{2,1,0:T(8,128)(2,1)}, u32[]{:S(2)}, u32[]{:S(2)}) collective-permute-start(bf16[1,768,2048]{2,1,0:T(8,128)(2,1)} %fusion.12), channel_id=1, source_target_pairs={{0,8},{1,9},{2,10},{3,11},{4,12},{5,13},{6,14},{7,15},{8,0},{9,1},... | collective-permute-start | bytes 9437192 | tf_op jit(solution)/shard_map/ppermute | solution.py:10
  550.2 155.6 %all-to-all-start.3 = ((bf16[16,96,768]{2,1,0:T(8,128)(2,1)}), bf16[16,96,768]{2,1,0:T(8,128)(2,1)}, u32[]{:S(2)}, u32[]{:S(2)}) async-start(bf16[16,96,768]{2,1,0:T(8,128)(2,1)} %bitcast.68), calls=%async_computation.3 | async-start | bytes 4718592 | tf_op jit(solution)/shard_map/all_to_all | solution.py:52
  697.8 4.7 copy-start.1
where the time goes:
time: 726 us; the launch traced here: 725 us
  waiting for transfers between devices  555 us (76%)
  starting transfers between devices  58.7 us (8%)
  local copies, waits for them, and re-layouts  56.2 us (8%)
  matrix products  32.9 us (5%)
  other arithmetic  20.8 us (3%)
    ppermute x2, waiting for transfers between devices, passed_along(): return lax.ppermute(value, axis, pairs)  359 us
    all_to_all x1, waiting for transfers between devices, shards(): lax.all_to_all(results, 'expert', split_axis=0, concat_axis=0, tiled=True)  161 us
    all_to_all x1, waiting for transfers between devices, shards(): lax.all_to_all(send_h, 'expert', split_axis=0, concat_axis=0, tiled=True)  34.8 us
    all_to_all x1, starting transfers between devices, shards(): lax.all_to_all(back.reshape(devices, capacity, hidden), 'expert', split_a...  28.5 us
    gather x1, local copies, waits for them, and re-layouts, shards(): out_rows = returned[flat_ids, ranks].reshape(tokens_here, top_count, width)  25.5 us
    gather x1, local copies, waits for them, and re-layouts, shards(): h_grad = back_rows[flat_ids, ranks].reshape(tokens_here, top_count, hidden)  19.6 us
  transfers between devices with their start and end apart: 6, of which 4 were waited for; matrix products, arithmetic and copies ran while one was open for 10% of the time, Pallas kernels for 0%

commit v1 on v0

--- a/solution.py
+++ b/solution.py
@@ -2,12 +2,6 @@
 import jax.numpy as jnp
 from jax import lax
 from jax.sharding import PartitionSpec as P
-
-
-def passed_along(value, axis, steps):
-    count = lax.axis_size(axis)
-    pairs = [(source, (source + steps) % count) for source in range(count)]
-    return lax.ppermute(value, axis, pairs)
 
 
 def place_rows(values, target, ranks, devices, capacity):
@@ -18,16 +12,14 @@
 def shards(h_rows, gates, expert_ids, cotangent, down_weight, swapped):
     devices = lax.axis_size("expert")
     half_way = devices // 2
-    here = lax.axis_index("expert")
     tokens_here, top_count, hidden = h_rows.shape
     width = cotangent.shape[1]
     capacity = min(tokens_here, 3 * tokens_here * top_count // (2 * devices))
     experts = jnp.arange(devices, dtype=jnp.int32)
-    flat_ids = expert_ids.reshape(-1)
-    own_weight = down_weight[0]
-    flag = swapped[here % half_way]
-    partner_weight = passed_along(down_weight, "expert", half_way)[0]
-    weight = jnp.where(flag > 0, partner_weight, own_weight)
+    named = expert_ids.reshape(-1)
+    weight = down_weight[0]
+    table = (experts + half_way * swapped[experts % half_way]) % devices
+    flat_ids = jnp.sum(jnp.where(named[:, None] == experts[None, :], table[None, :], 0), axis=1)
     onehot = (flat_ids[:, None] == experts[None, :]).astype(jnp.int32)
     ranks = jnp.sum((jnp.cumsum(onehot, axis=0) - onehot) * onehot, axis=1)
     send_h = place_rows(h_rows.reshape(-1, hidden), flat_ids, ranks, devices, capacity)
@@ -53,9 +45,7 @@
         back.reshape(devices, capacity, hidden), "expert", split_axis=0, concat_axis=0, tiled=True
     )
     h_grad = back_rows[flat_ids, ranks].reshape(tokens_here, top_count, hidden)
-    own_grad = grad_sum.astype(jnp.bfloat16)[None]
-    partner_grad = passed_along(own_grad, "expert", half_way)
-    weight_grad = jnp.where(flag > 0, partner_grad, own_grad)
+    weight_grad = grad_sum.astype(jnp.bfloat16)[None]
     return (mixed, gate_grad, h_grad, weight_grad)
 
 

time: 726 us -> 440 us (0.61)
  waiting for transfers between devices: 555 us -> 246 us
  starting transfers between devices: 58.7 us -> 76 us
    ppermute x2 -> x0, waiting for transfers between devices: 359 us -> none  [passed_along(): return lax.ppermute(value, axis, pairs)]
    all_to_all x1, waiting for transfers between devices: 0.01 us -> 106 us  [shards(): lax.all_to_all(send_z, 'expert', split_axis=0, concat_axis=0, tiled=True)]
    all_to_all x1, waiting for transfers between devices: 161 us -> 105 us  [shards(): lax.all_to_all(results, 'expert', split_axis=0, concat_axis=0, tiled=True)]
    all_to_all x1, starting transfers between devices: 4.63 us -> 28.1 us  [shards(): lax.all_to_all(results, 'expert', split_axis=0, concat_axis=0, tiled=True)]
  transfers between devices with their start and end apart: 6 -> 4, of which waited for: 4 -> 4; matrix products, arithmetic and copies ran while one was open for 10% -> 17% of each run, Pallas kernels for 0% -> 0%
where the time goes in v1:
time: 440 us; the launch traced here: 432 us
  waiting for transfers between devices  246 us (56%)
  starting transfers between devices  76 us (17%)
  local copies, waits for them, and re-layouts  57.2 us (13%)
  matrix products  33.4 us (8%)
  other arithmetic  19.4 us (4%)
    all_to_all x1, waiting for transfers between devices, shards(): lax.all_to_all(send_z, 'expert', split_axis=0, concat_axis=0, tiled=True)  106 us
    all_to_all x1, waiting for transfers between devices, shards(): lax.all_to_all(results, 'expert', split_axis=0, concat_axis=0, tiled=True)  105 us
    all_to_all x1, waiting for transfers between devices, shards(): lax.all_to_all(send_h, 'expert', split_axis=0, concat_axis=0, tiled=True)  32.4 us
    all_to_all x1, starting transfers between devices, shards(): lax.all_to_all(results, 'expert', split_axis=0, concat_axis=0, tiled=True)  28.1 us
    all_to_all x1, starting transfers between devices, shards(): lax.all_to_all(back.reshape(devices, capacity, hidden), 'expert', split_a...  28.1 us
    gather x1, local copies, waits for them, and re-layouts, shards(): out_rows = returned[flat_ids, ranks].reshape(tokens_here, top_count, width)  25.5 us
    gather x1, local copies, waits for them, and re-layouts, shards(): h_grad = back_rows[flat_ids, ranks].reshape(tokens_here, top_count, hidden)  19.5 us
    unnamed x4, other arithmetic  12.5 us
  transfers between devices with their start and end apart: 4, of which 4 were waited for; matrix products, arithmetic and copies ran while one was open for 17% of the time, Pallas kernels for 0%

profile of v1, /device:TPU:0, one launch (start us, length us, event | category | flops | bytes accessed | tf_op | source)
XLA Modules:
  0.0 432.5 jit_solution(9573581135624002253)
XLA Ops:
  0.6 0.0 copy-start
  0.7 1.5 gather_fusion
  2.2 0.8 copy.12
  2.9 0.1 eq.41
  3.0 0.1 select_reduce_fusion
  3.1 4.5 %reduce-window.6 = s32[16,8,128]{2,1,0:T(8,128)S(1)} reduce-window(s32[16,8,128]{2,1,0:T(8,128)S(1)} %fusion.20, s32[]{:T(128)} %constant.36.clone.1), window={size=1x1x128 pad=0_0x0_0x127_0}, to_apply=%region_1.2 | reduce-window | flops 2080768 | bytes 131076 | tf_op jit(solution)/shard_map/reduce-window
  7.7 0.1 slice.14
  7.7 0.1 copy.13
  7.9 0.1 copy.14
  8.0 0.1 broadcast_add_fusion
  8.1 0.8 and_reduce_fusion
  8.9 0.7 multiply_reduce_fusion
  9.6 0.0 copy-start.3
  9.7 7.5 %scatter_custom_fusion = bf16[1536,768]{1,0:T(8,128)(2,1)} fusion(s32[1024]{0:T(1024)S(1)} %broadcast_select_fusion, bf16[128,8,768]{2,1,0:T(8,128)(2,1)} %param.6, bf16[]{:T(256)} %constant.34.clone.1), kind=kCustom, calls=%fused_computation.21 | custom fusion | bytes 3932162
  17.1 7.4 %all-to-all-start = ((bf16[16,96,768]{2,1,0:T(8,128)(2,1)}), bf16[16,96,768]{2,1,0:T(8,128)(2,1)}, u32[]{:S(2)}, u32[]{:S(2)}) async-start(bf16[16,96,768]{2,1,0:T(8,128)(2,1)} %bitcast.68), calls=%async_computation | async-start | bytes 4718592 | tf_op jit(solution)/shard_map/all_to_all | solution.py:26
  24.6 2.1 convert_element_type.32
  26.7 0.0 copy-done.3
  26.7 0.1 copy.15
  26.8 0.1 mul.30
  26.9 11.0 %scatter_custom_fusion.1 = bf16[1536,2048]{1,0:T(8,128)(2,1)} fusion(s32[1024]{0:T(1024)S(1)} %broadcast_select_fusion, f32[128,2048]{1,0:T(8,128)} %convert_element_type.32, f32[1024]{0:T(1024)S(1)} %mul.30, bf16[]{:T(256)} %constant.34.clone.1), kind=kCustom, calls=%fused_computation.9 | custom fusion | flops 4194304 | bytes 7344130
  37.9 32.4 %all-to-all-done = bf16[16,96,768]{2,1,0:T(8,128)(2,1)} async-done(((bf16[16,96,768]{2,1,0:T(8,128)(2,1)}), bf16[16,96,768]{2,1,0:T(8,128)(2,1)}, u32[]{:S(2)}, u32[]{:S(2)}) %all-to-all-start) | async-done | bytes 2359328 | tf_op jit(solution)/shard_map/all_to_all | solution.py:26
  70.3 12.3 %all-to-all-start.2 = ((bf16[16,96,2048]{2,1,0:T(8,128)(2,1)}), bf16[16,96,2048]{2,1,0:T(8,128)(2,1)}, u32[]{:S(2)}, u32[]{:S(2)}) async-start(bf16[16,96,2048]{2,1,0:T(8,128)(2,1)} %bitcast.67), calls=%async_computation.2 | async-start | bytes 12582912 | tf_op jit(solution)/shard_map/all_to_all | solution.py:35
  82.6 0.0 copy-done
  82.6 8.7 %convolution_convert_fusion = bf16[16,96,2048]{2,1,0:T(8,128)(2,1)} fusion(bf16[16,96,768]{2,1,0:T(8,128)(2,1)} %all-to-all-done, bf16[1,768,2048]{2,1,0:T(8,128)(2,1)S(1)} %copy-done), kind=kOutput, calls=%fused_computation.8 | convolution fusion | flops 4834983936 | bytes 11796480 | tf_op jit(solution)/shard_map/sch,hd->scd/dot_general | solution.py:27
  91.3 105.5 %all-to-all-done.2 = bf16[16,96,2048]{2,1,0:T(8,128)(2,1)} async-done(((bf16[16,96,2048]{2,1,0:T(8,128)(2,1)}), bf16[16,96,2048]{2,1,0:T(8,128)(2,1)}, u32[]{:S(2)}, u32[]{:S(2)}) %all-to-all-start.2) | async-done | bytes 6291488 | tf_op jit(solution)/shard_map/all_to_all | solution.py:35
  196.8 28.1 %all-to-all-start.1 = ((bf16[16,96,2048]{2,1,0:T(8,128)(2,1)}), bf16[16,96,2048]{2,1,0:T(8,128)(2,1)}, u32[]{:S(2)}, u32[]{:S(2)}) async-start(bf16[16,96,2048]{2,1,0:T(8,128)(2,1)} %convolution_convert_fusion), calls=%async_computation.1 | async-start | bytes 12582912 | tf_op jit(solution)/shard_map/all_to_all | solution.py:29
  224.9 9.3 %convolution_convert_fusion.1 = bf16[1536,768]{1,0:T(8,128)(2,1)} fusion(bf16[1536,2048]{1,0:T(8,128)(2,1)} %bitcast.18, bf16[1,768,2048]{2,1,0:T(8,128)(2,1)S(1)} %copy-done), kind=kOutput, calls=%fused_computation.16 | convolution fusion | flops 4833017856 | bytes 11796480 | tf_op jit(solution)/shard_map/dot_general | solution.py:41
  234.3 104.8 %all-to-all-done.1 = bf16[16,96,2048]{2,1,0:T(8,128)(2,1)} async-done(((bf16[16,96,2048]{2,1,0:T(8,128)(2,1)}), bf16[16,96,2048]{2,1,0:T(8,128)(2,1)}, u32[]{:S(2)}, u32[]{:S(2)}) %all-to-all-start.1) | async-done | bytes 6291488 | tf_op jit(solution)/shard_map/all_to_all | solution.py:29
  339.1 28.1 %all-to-all-start.3 = ((bf16[16,96,768]{2,1,0:T(8,128)(2,1)}), bf16[16,96,768]{2,1,0:T(8,128)(2,1)}, u32[]{:S(2)}, u32[]{:S(2)}) async-start(bf16[16,96,768]{2,1,0:T(8,128)(2,1)} %bitcast.69), calls=%async_computation.3 | async-start | bytes 4718592 | tf_op jit(solution)/shard_map/all_to_all | solution.py:44
  367.2 0.1 copy.16
  367.4 9.1 %fusion.12 = bf16[1,768,2048]{2,1,0:T(8,128)(2,1)} fusion(bf16[16,96,768]{2,1,0:T(8,128)(2,1)} %all-to-all-done, bf16[16,96,2048]{2,1,0:T(8,128)(2,1)} %all-to-all-done.2), kind=kOutput, calls=%fused_computation.20 | convolution fusion | flops 4833411072 | bytes 11796480 | tf_op jit(solution)/shard_map/dot_general | solution.py:38
  376.5 25.5 %gather_fusion.1 = bf16[1024,2048]{1,0:T(8,128)(2,1)} fusion(bf16[16,96,2048]{2,1,0:T(8,128)(2,1)} %all-to-all-done.1, s32[1024]{0:T(1024)S(1)} %bitcast.65), kind=kCustom, calls=%fused_computation.1 | custom fusion | bytes 8396800 | tf_op jit(solution)/shard_map/gather | solution.py:30
  402.0 0.0 copy-start.1
  402.0 0.0 copy-start.2
  402.0 3.6 fusion.5
  405.5 1.1 copy.25
  406.6 0.0 copy-done.1
  406.6 0.0 copy-done.2
  406.6 2.7 fusion.3
  409.3 0.7 copy.19
  410.0 3.0 all-to-all-done.3
  413.0 19.5 %gather_fusion.2 = bf16[1024,768]{1,0:T(8,128)(2,1)} fusion(bf16[16,96,768]{2,1,0:T(8,128)(2,1)} %all-to-all-done.3, s32[1024]{0:T(1024)S(1)} %bitcast.66), kind=kCustom, calls=%fused_computation.2 | custom fusion | bytes 3153920 | tf_op jit(solution)/shard_map/gather | solution.py:47
  (9 shorter events, 0.1 us)
Async XLA Ops:
  0.6 82.0 %copy-start = (bf16[1,768,2048]{2,1,0:T(8,128)(2,1)S(1)}, bf16[1,768,2048]{2,1,0:T(8,128)(2,1)}, u32[]{:S(2)}) copy-start(bf16[1,768,2048]{2,1,0:T(8,128)(2,1)} %param.10) | copy-start | bytes 9437188
  9.6 17.0 %copy-start.3 = (f32[128,8]{0,1:T(8,128)S(1)}, f32[128,8]{0,1:T(8,128)}, u32[]{:S(2)}) copy-start(f32[128,8]{0,1:T(8,128)} %param.7) | copy-start | bytes 12292
  17.1 53.2 %all-to-all-start = ((bf16[16,96,768]{2,1,0:T(8,128)(2,1)}), bf16[16,96,768]{2,1,0:T(8,128)(2,1)}, u32[]{:S(2)}, u32[]{:S(2)}) async-start(bf16[16,96,768]{2,1,0:T(8,128)(2,1)} %bitcast.68), calls=%async_computation | async-start | bytes 4718592 | tf_op jit(solution)/shard_map/all_to_all | solution.py:26
  70.3 126.5 %all-to-all-start.2 = ((bf16[16,96,2048]{2,1,0:T(8,128)(2,1)}), bf16[16,96,2048]{2,1,0:T(8,128)(2,1)}, u32[]{:S(2)}, u32[]{:S(2)}) async-start(bf16[16,96,2048]{2,1,0:T(8,128)(2,1)} %bitcast.67), calls=%async_computation.2 | async-start | bytes 12582912 | tf_op jit(solution)/shard_map/all_to_all | solution.py:35
  196.8 142.3 %all-to-all-start.1 = ((bf16[16,96,2048]{2,1,0:T(8,128)(2,1)}), bf16[16,96,2048]{2,1,0:T(8,128)(2,1)}, u32[]{:S(2)}, u32[]{:S(2)}) async-start(bf16[16,96,2048]{2,1,0:T(8,128)(2,1)} %convolution_convert_fusion), calls=%async_computation.1 | async-start | bytes 12582912 | tf_op jit(solution)/shard_map/all_to_all | solution.py:29
  339.1 73.9 %all-to-all-start.3 = ((bf16[16,96,768]{2,1,0:T(8,128)(2,1)}), bf16[16,96,768]{2,1,0:T(8,128)(2,1)}, u32[]{:S(2)}, u32[]{:S(2)}) async-start(bf16[16,96,768]{2,1,0:T(8,128)(2,1)} %bitcast.69), calls=%async_computation.3 | async-start | bytes 4718592 | tf_op jit(solution)/shard_map/all_to_all | solution.py:44
  402.0 4.7 %copy-start.1 = (bf16[1024,2048]{1,0:T(8,128)(2,1)S(1)}, bf16[1024,2048]{1,0:T(8,128)(2,1)}, u32[]{:S(2)}) copy-start(bf16[1024,2048]{1,0:T(8,128)(2,1)} %gather_fusion.1) | copy-start | bytes 12582916
  402.0 4.7 %copy-start.2 = (bf16[128,2048]{1,0:T(8,128)(2,1)S(1)}, bf16[128,2048]{1,0:T(8,128)(2,1)}, u32[]{:S(2)}) copy-start(bf16[128,2048]{1,0:T(8,128)(2,1)} %param.9) | copy-start | bytes 1572868

commit v2 on v1

v2 whole, which is shorter than its diff:
```python
import functools

import jax
import jax.numpy as jnp
from jax import lax
from jax.experimental import pallas as pl
from jax.experimental.pallas import tpu as pltpu
from jax.sharding import PartitionSpec as P

F32 = jnp.float32
BF16 = jnp.bfloat16
MIB = 1 << 20


def slots_of(ids, swapped, devices):
    half_way = devices // 2
    table = jnp.arange(devices, dtype=jnp.int32)
    table = (table + half_way * swapped[table % half_way]) % devices
    return jnp.sum(jnp.where(ids[..., None] == jnp.arange(devices, dtype=jnp.int32), table, 0), axis=-1)


def place_rows(values, target, ranks, devices, capacity):
    buffer = jnp.zeros((devices, capacity, values.shape[-1]), values.dtype)
    return buffer.at[target, ranks].set(values)


def sparse_shards(h_rows, gates, expert_ids, cotangent, down_weight, swapped):
    devices = lax.axis_size("expert")
    tokens_here, top_count, hidden = h_rows.shape
    width = cotangent.shape[1]
    capacity = min(tokens_here, 3 * tokens_here * top_count // (2 * devices))
    experts = jnp.arange(devices, dtype=jnp.int32)
    weight = down_weight[0]
    flat_ids = slots_of(expert_ids.reshape(-1), swapped, devices)
    onehot = (flat_ids[:, None] == experts[None, :]).astype(jnp.int32)
    ranks = jnp.sum((jnp.cumsum(onehot, axis=0) - onehot) * onehot, axis=1)
    send_h = place_rows(h_rows.reshape(-1, hidden), flat_ids, ranks, devices, capacity)
    received = lax.all_to_all(send_h, "expert", split_axis=0, concat_axis=0, tiled=True)
    result = jnp.einsum("sch,hd->scd", received, weight, preferred_element_type=F32)
    results = result.astype(BF16)
    returned = lax.all_to_all(results, "expert", split_axis=0, concat_axis=0, tiled=True)
    out_rows = returned[flat_ids, ranks].reshape(tokens_here, top_count, width)
    mixed = jnp.einsum("tk,tkd->td", gates, out_rows.astype(F32)).astype(BF16)
    gate_grad = jnp.einsum("td,tkd->tk", cotangent, out_rows, preferred_element_type=F32)
    scaled = (gates[:, :, None] * cotangent[:, None, :].astype(F32)).astype(BF16)
    send_z = place_rows(scaled.reshape(-1, width), flat_ids, ranks, devices, capacity)
    recv_z = lax.all_to_all(send_z, "expert", split_axis=0, concat_axis=0, tiled=True)
    flat_z = recv_z.reshape(-1, width)
    flat_h = received.reshape(-1, hidden)
    grad_sum = lax.dot_general(flat_h, flat_z, (((0,), (0,)), ((), ())), preferred_element_type=F32)
    back = lax.dot_general(flat_z, weight, (((1,), (1,)), ((), ())), preferred_element_type=F32).astype(BF16)
    back_rows = lax.all_to_all(
        back.reshape(devices, capacity, hidden), "expert", split_axis=0, concat_axis=0, tiled=True
    )
    h_grad = back_rows[flat_ids, ranks].reshape(tokens_here, top_count, hidden)
    return (mixed, gate_grad, h_grad, grad_sum.astype(BF16)[None])


def upper(size):
    rows = lax.broadcasted_iota(jnp.int32, (size, size), 0)
    columns = lax.broadcasted_iota(jnp.int32, (size, size), 1)
    return (rows < columns).astype(F32).astype(BF16)


def pack_kernel(devices, capacity, ids_ref, h_ref, place_ref, sent_ref, place_scratch):
    pairs = ids_ref.shape[1]
    rows = sent_ref.shape[0]

    @pl.when(pl.program_id(0) == 0)
    def _():
        before = jnp.zeros((devices, 1), F32)
        for tile in range(pairs // 128):
            ids = ids_ref[:, tile * 128:(tile + 1) * 128]
            named = lax.broadcasted_iota(jnp.int32, (devices, 128), 0) == ids
            ones = jnp.where(named, 1.0, 0.0)
            rank = jnp.dot(ones.astype(BF16), upper(128), preferred_element_type=F32) + before
            before = before + jnp.sum(ones, axis=1, keepdims=True)
            rank = jnp.sum(jnp.where(named, rank, 0.0), axis=0, keepdims=True)
            place_scratch[:, tile * 128:(tile + 1) * 128] = ids * capacity + rank.astype(jnp.int32)
        place_ref[...] = place_scratch[...]

    first = pl.program_id(0) * rows
    wanted = lax.broadcasted_iota(jnp.int32, (rows, pairs), 0) + first
    chosen = jnp.where(wanted == place_scratch[...], 1.0, 0.0).astype(BF16)
    sent_ref[...] = jnp.dot(chosen, h_ref[...], preferred_element_type=F32).astype(BF16)


def pack(ids, h_flat, devices, capacity, steps=4):
    pairs, hidden = h_flat.shape
    rows = devices * capacity // steps
    return pl.pallas_call(
        functools.partial(pack_kernel, devices, capacity),
        grid=(steps,),
        in_specs=[
            pl.BlockSpec((1, pairs), lambda i: (0, 0)),
            pl.BlockSpec((pairs, hidden), lambda i: (0, 0)),
        ],
        out_specs=[
            pl.BlockSpec((1, pairs), lambda i: (0, 0)),
            pl.BlockSpec((rows, hidden), lambda i: (i, 0)),
        ],
        out_shape=[
            jax.ShapeDtypeStruct((1, pairs), jnp.int32),
            jax.ShapeDtypeStruct((devices * capacity, hidden), BF16),
        ],
        scratch_shapes=[pltpu.VMEM((1, pairs), jnp.int32)],
        compiler_params=pltpu.CompilerParams(vmem_limit_bytes=48 * MIB),
        cost_estimate=pl.CostEstimate(
            flops=2 * devices * capacity * pairs * hidden, transcendentals=0,
            bytes_accessed=2 * hidden * (pairs + devices * capacity),
        ),
        name="pack",
    )(ids, h_flat)


def unpack_kernel(slots, place_ref, gate_ref, h_ref, back_ref, grad_ref, gate_grad_ref):
    rows = place_ref.shape[0]
    chosen = lax.broadcasted_iota(jnp.int32, (rows, slots), 1) == place_ref[...]
    grad = jnp.dot(jnp.where(chosen, 1.0, 0.0).astype(BF16), back_ref[...], preferred_element_type=F32)
    grad_ref[...] = grad.astype(BF16)
    gate_grad_ref[...] = jnp.sum(grad * h_ref[...].astype(F32), axis=1, keepdims=True) / gate_ref[...]


def unpack(place, gates, h_flat, back_rows, steps=4):
    pairs, hidden = h_flat.shape
    slots = back_rows.shape[0]
    rows = pairs // steps
    return pl.pallas_call(
        functools.partial(unpack_kernel, slots),
        grid=(steps,),
        in_specs=[
            pl.BlockSpec((rows, 1), lambda i: (i, 0)),
            pl.BlockSpec((rows, 1), lambda i: (i, 0)),
            pl.BlockSpec((rows, hidden), lambda i: (i, 0)),
            pl.BlockSpec((slots, hidden), lambda i: (0, 0)),
        ],
        out_specs=[
            pl.BlockSpec((rows, hidden), lambda i: (i, 0)),
            pl.BlockSpec((rows, 1), lambda i: (i, 0)),
        ],
        out_shape=[
            jax.ShapeDtypeStruct((pairs, hidden), BF16),
            jax.ShapeDtypeStruct((pairs, 1), F32),
        ],
        compiler_params=pltpu.CompilerParams(vmem_limit_bytes=48 * MIB),
        cost_estimate=pl.CostEstimate(
            flops=2 * slots * pairs * hidden, transcendentals=0,
            bytes_accessed=2 * hidden * (2 * pairs + slots),
        ),
        name="unpack",
    )(place, gates, h_flat, back_rows)


def route_kernel(devices, top, here_ref, routing_ref, rank_ref, gate_ref):
    mine = here_ref[0].astype(F32)
    marks, picked = [], []
    for source in range(devices):
        ids = routing_ref[2 * top * source:2 * top * source + top, :]
        gates = routing_ref[2 * top * source + top:2 * top * (source + 1), :]
        named = ids == mine
        marks.append(jnp.sum(jnp.where(named, 1.0, 0.0), axis=0, keepdims=True))
        picked.append(jnp.sum(jnp.where(named, gates, 0.0), axis=0, keepdims=True))
    mark = jnp.concatenate(marks, axis=0)
    rank = jnp.dot(mark.astype(BF16), upper(mark.shape[1]), preferred_element_type=F32)
    rank_ref[...] = jnp.where(mark > 0, rank, -1.0).astype(jnp.int32)
    gate_ref[...] = jnp.concatenate(picked, axis=0)


def route(here, routing, devices, top):
    tokens = routing.shape[1]
    return pl.pallas_call(
        functools.partial(route_kernel, devices, top),
        in_specs=[pl.BlockSpec(memory_space=pltpu.SMEM), pl.BlockSpec(memory_space=pltpu.VMEM)],
        out_specs=[pl.BlockSpec(memory_space=pltpu.VMEM)] * 2,
        out_shape=[
            jax.ShapeDtypeStruct((devices, tokens), jnp.int32),
            jax.ShapeDtypeStruct((devices, tokens), F32),
        ],
        name="route",
    )(here, routing)


def picks(rank_ref, gate_ref, source, capacity):
    rank = rank_ref[pl.ds(source, 1), :]
    chosen = lax.broadcasted_iota(jnp.int32, (capacity, rank.shape[1]), 0) == rank
    gate = jnp.sum(jnp.where(chosen, gate_ref[pl.ds(source, 1), :], 0.0), axis=1, keepdims=True)
    return jnp.where(chosen, 1.0, 0.0).astype(BF16), gate


def back_kernel(capacity, rank_ref, gate_ref, cot_ref, weight_ref, z_ref, back_ref):
    each = cot_ref.shape[0]
    for j in range(each):
        chosen, gate = picks(rank_ref, gate_ref, pl.program_id(0) * each + j, capacity)
        rows = jnp.dot(chosen, cot_ref[j], preferred_element_type=F32)
        z_ref[j * capacity:(j + 1) * capacity, :] = (rows * gate).astype(BF16)
    back_ref[...] = jnp.dot(z_ref[...], weight_ref[...], preferred_element_type=F32).astype(BF16)


def backward_rows(rank, gate, cotangents, weight_t, capacity, each=4):
    devices, tokens, width = cotangents.shape
    hidden = weight_t.shape[1]
    rows = each * capacity
    return pl.pallas_call(
        functools.partial(back_kernel, capacity),
        grid=(devices // each,),
        in_specs=[
            pl.BlockSpec((devices, tokens), lambda i: (0, 0)),
            pl.BlockSpec((devices, tokens), lambda i: (0, 0)),
            pl.BlockSpec((each, tokens, width), lambda i: (i, 0, 0)),
            pl.BlockSpec((width, hidden), lambda i: (0, 0)),
        ],
        out_specs=[
            pl.BlockSpec((rows, width), lambda i: (i, 0)),
            pl.BlockSpec((rows, hidden), lambda i: (i, 0)),
        ],
        out_shape=[
            jax.ShapeDtypeStruct((devices * capacity, width), BF16),
            jax.ShapeDtypeStruct((devices * capacity, hidden), BF16),
        ],
        compiler_params=pltpu.CompilerParams(vmem_limit_bytes=48 * MIB),
        cost_estimate=pl.CostEstimate(
            flops=2 * devices * capacity * width * (hidden + tokens), transcendentals=0,
            bytes_accessed=2 * devices * (tokens * width + capacity * (width + hidden)) + 2 * width * hidden,
        ),
        name="backward_rows",
    )(rank, gate, cotangents, weight_t)


def forward_kernel(capacity, rank_ref, gate_ref, h_ref, weight_ref, part_ref):
    each = part_ref.shape[0]
    out = jnp.dot(h_ref[...], weight_ref[...], preferred_element_type=F32)
    out = out.astype(BF16).astype(F32)
    for j in range(each):
        chosen, gate = picks(rank_ref, gate_ref, pl.program_id(0) * each + j, capacity)
        rows = (out[j * capacity:(j + 1) * capacity, :] * gate).astype(BF16)
        part = lax.dot_general(chosen, rows, (((0,), (0,)), ((), ())), preferred_element_type=F32)
        part_ref[j] = part.astype(BF16)


def forward_parts(rank, gate, rows_h, weight, capacity, each=8, columns=512):
    devices, tokens = rank.shape
    hidden, width = weight.shape
    rows = each * capacity
    return pl.pallas_call(
        functools.partial(forward_kernel, capacity),
        grid=(devices // each, width // columns),
        in_specs=[
            pl.BlockSpec((devices, tokens), lambda i, j: (0, 0)),
            pl.BlockSpec((devices, tokens), lambda i, j: (0, 0)),
            pl.BlockSpec((rows, hidden), lambda i, j: (i, 0)),
            pl.BlockSpec((hidden, columns), lambda i, j: (0, j)),
        ],
        out_specs=pl.BlockSpec((each, tokens, columns), lambda i, j: (i, 0, j)),
        out_shape=jax.ShapeDtypeStruct((devices, tokens, width), BF16),
        compiler_params=pltpu.CompilerParams(vmem_limit_bytes=48 * MIB),
        cost_estimate=pl.CostEstimate(
            flops=2 * devices * capacity * width * (hidden + tokens), transcendentals=0,
            bytes_accessed=2 * devices * (tokens * width + capacity * hidden) + 2 * width * hidden,
        ),
        name="forward_parts",
    )(rank, gate, rows_h, weight)


def dense_shards(h_rows, gates, expert_ids, cotangent, down_weight, swapped):
    devices = lax.axis_size("expert")
    here = lax.axis_index("expert")
    tokens, top, hidden = h_rows.shape
    width = cotangent.shape[1]
    capacity = min(tokens, 3 * tokens * top // (2 * devices))
    weight = down_weight[0]
    slot_ids = slots_of(expert_ids, swapped, devices)
    h_flat = h_rows.reshape(-1, hidden)

    cotangents = lax.all_gather(cotangent, "expert", axis=0, tiled=False)
    routing = jnp.concatenate([slot_ids.T.astype(F32), gates.T], axis=0)
    routing = lax.all_gather(routing, "expert", axis=0, tiled=True)
    place, send_h = pack(slot_ids.reshape(1, -1), h_flat, devices, capacity)
    rows_h = lax.all_to_all(
        send_h.reshape(devices, capacity, hidden), "expert", split_axis=0, concat_axis=0, tiled=True
    ).reshape(-1, hidden)
    rank, gate = route(here.reshape(1), routing, devices, top)

    z_rows, back = backward_rows(rank, gate, cotangents, weight.T, capacity)
    back_rows = lax.all_to_all(
        back.reshape(devices, capacity, hidden), "expert", split_axis=0, concat_axis=0, tiled=True
    ).reshape(-1, hidden)
    parts = forward_parts(rank, gate, rows_h, weight, capacity)
    mixed = lax.psum_scatter(parts.reshape(-1, width), "expert", scatter_dimension=0, tiled=True)
    grad_sum = lax.dot_general(rows_h, z_rows, (((0,), (0,)), ((), ())), preferred_element_type=F32)
    h_grad, gate_grad = unpack(place.reshape(-1, 1), gates.reshape(-1, 1), h_flat, back_rows)
    return (
        mixed,
        gate_grad.reshape(tokens, top),
        h_grad.reshape(tokens, top, hidden),
        grad_sum.astype(BF16)[None],
    )


def shards(h_rows, *rest):
    devices = lax.axis_size("expert")
    dense = devices <= 2 * h_rows.shape[1]
    return (dense_shards if dense else sparse_shards)(h_rows, *rest)


def solution(mesh):
    in_specs = (
        P(("groups", "expert"), None, None),
        P(("groups", "expert"), None),
        P(("groups", "expert"), None),
        P(("groups", "expert"), None),
        P("expert", None, None),
        P(),
    )
    out_specs = (
        P(("groups", "expert"), None),
        P(("groups", "expert"), None),
        P(("groups", "expert"), None, None),
        P(("groups", "expert"), None, None),
    )
    return jax.shard_map(shards, mesh=mesh, in_specs=in_specs, out_specs=out_specs, check_vma=False)
```

time: 440 us -> 303 us (0.69); the launches traced: 432 us -> 302 us
  waiting for transfers between devices: 246 us -> 111 us
  blocking collectives: 0 us -> 81.3 us
  local copies, waits for them, and re-layouts: 57.2 us -> 15.7 us
  starting transfers between devices: 76 us -> 39.6 us
  Pallas kernels: 0 us -> 30.4 us
  matrix products: 33.4 us -> 9.23 us
  other arithmetic: 19.4 us -> 1.01 us
  between operations: 0.78 us -> 14.2 us
    all_to_all x4 -> x2, waiting for transfers between devices: 246 us -> 66.2 us  [the longest x1 66.2 us: dense_shards(): lax.all_to_all(back.reshape(devices, capacity, hidden), 'expert', split_a...]
    all_gather x0 -> x1, blocking collectives: none -> 81.3 us  [dense_shards(): routing = lax.all_gather(routing, 'expert', axis=0, tiled=True)]
    gather x3 -> x1, local copies, waits for them, and re-layouts: 46.4 us -> 0.66 us  [slots_of(): table = (table + half_way * swapped[table % half_way]) % devices]
    reduce_scatter x0 -> x1, waiting for transfers between devices: none -> 39.2 us  [dense_shards(): lax.psum_scatter(parts.reshape(-1, width), 'expert', scatter_dimension=0,...]
    all_to_all x4 -> x2, starting transfers between devices: 76 us -> 39.6 us  [the longest x1 31.9 us: dense_shards(): lax.all_to_all(back.reshape(devices, capacity, hidden), 'expert', split_a...]
    pallas_call x0 -> x5, Pallas kernels: none -> 30.4 us  [the longest x1 11.7 us: forward_parts(): pl.pallas_call(functools.partial(forward_kernel, capacity), grid=(devices...]
    dot_general x5 -> x1, matrix products: 33.4 us -> 9.23 us  [dense_shards(): lax.dot_general(rows_h, z_rows, (((0,), (0,)), ((), ())), preferred_eleme...]
    unnamed x4 -> x0, other arithmetic: 12.5 us -> none
  transfers between devices with their start and end apart: 4 -> 4, of which waited for: 4 -> 3; matrix products, arithmetic and copies ran while one was open for 17% -> 5% of each run, Pallas kernels for 0% -> 10%
where the time goes in v2:
time: 303 us; the launch traced here: 302 us
  waiting for transfers between devices  111 us (37%)
  blocking collectives  81.3 us (27%)
  starting transfers between devices  39.6 us (13%)
  Pallas kernels  30.4 us (10%)
  local copies, waits for them, and re-layouts  15.7 us (5%)
  between operations  14.2 us (5%)
  matrix products  9.23 us (3%)
    all_gather x1, blocking collectives, dense_shards(): routing = lax.all_gather(routing, 'expert', axis=0, tiled=True)  81.3 us
    all_to_all x1, waiting for transfers between devices, dense_shards(): lax.all_to_all(back.reshape(devices, capacity, hidden), 'expert', split_a...  66.2 us
    reduce_scatter x1, waiting for transfers between devices, dense_shards(): lax.psum_scatter(parts.reshape(-1, width), 'expert', scatter_dimension=0,...  39.2 us
    all_to_all x1, starting transfers between devices, dense_shards(): lax.all_to_all(back.reshape(devices, capacity, hidden), 'expert', split_a...  31.9 us
    unnamed x29, local copies, waits for them, and re-layouts  13.6 us
    pallas_call x1, Pallas kernels, forward_parts(): pl.pallas_call(functools.partial(forward_kernel, capacity), grid=(devices...  11.7 us
    dot_general x1, matrix products, dense_shards(): lax.dot_general(rows_h, z_rows, (((0,), (0,)), ((), ())), preferred_eleme...  9.23 us
    pallas_call x1, Pallas kernels, backward_rows(): pl.pallas_call(functools.partial(back_kernel, capacity), grid=(devices //...  8.97 us
  transfers between devices with their start and end apart: 4, of which 3 were waited for; matrix products, arithmetic and copies ran while one was open for 5% of the time, Pallas kernels for 10%

profile of v2, /device:TPU:0, one launch (start us, length us, event | category | flops | bytes accessed | tf_op | source)
XLA Modules:
  0.0 302.4 jit_solution(854329221178304201)
XLA Ops:
  7.2 0.0 copy-start
  7.2 0.0 all-gather.3.cloned.1.call-start
  7.2 0.7 all-gather.3.cloned.1.call-update
  7.9 0.0 copy-done
  7.9 0.7 gather_fusion
  8.6 0.8 select_reduce_fusion
  9.4 0.1 copy.24
  9.5 0.1 reshape.77.ids_ref
  9.6 0.0 copy-start.6
  9.6 1.4 copy-done.6
  11.0 3.4 %pack.1 = (s32[1,1024]{1,0:T(1,128)S(1)}, bf16[1536,768]{1,0:T(8,128)(2,1)S(1)}) custom-call(s32[1,1024]{1,0:T(1,128)S(1)} %reshape.77.ids_ref, bf16[1024,768]{1,0:T(8,128)(2,1)S(1)} %bitcast.29), custom_call_target="tpu_custom_call" | custom-call | flops 2415919104 | bytes 3932160 | tf_op jit(solution)/shard_map/pack/pallas_call | solution.py:91
  14.4 0.0 copy-start.3
  14.4 1.4 copy-done.3
  15.8 0.0 copy-start.12
  15.8 0.0 copy-start.1
  15.8 7.7 %all-to-all-start = ((bf16[16,96,768]{2,1,0:T(8,128)(2,1)}), bf16[16,96,768]{2,1,0:T(8,128)(2,1)}, u32[]{:S(2)}, u32[]{:S(2)}) async-start(bf16[16,96,768]{2,1,0:T(8,128)(2,1)} %bitcast.25), calls=%async_computation | async-start | bytes 4718592 | tf_op jit(solution)/shard_map/all_to_all | solution.py:278
  23.5 0.0 reduce-scatter.2.cloned.1.call-start
  23.6 0.0 copy-done.12
  23.6 81.3 %all_gather.9.routing_ref = f32[256,128]{1,0:T(8,128)} all-gather(f32[16,128]{1,0:T(8,128)S(1)} %pad_maximum_fusion), channel_id=1, replica_groups=mesh['groups'=2,'expert'=16] {'expert'}, dimensions={0}, use_global_device_ids=true | all-gather | bytes 139264 | tf_op jit(solution)/shard_map/all_gather | solution.py:276
  104.9 1.6 route.1
  106.5 0.0 all-to-all-done
  106.5 0.0 copy-done.1
  106.5 0.0 copy-start.8
  106.6 0.7 copy-done.8
  107.3 0.0 copy-start.10
  107.3 0.7 copy-done.10
  107.9 11.7 %forward_parts.1 = bf16[16,128,2048]{2,1,0:T(8,128)(2,1)} custom-call(s32[16,128]{1,0:T(8,128)S(1)} %copy-done.8, f32[16,128]{1,0:T(8,128)S(1)} %copy-done.10, bf16[1536,768]{1,0:T(8,128)(2,1)} %bitcast.6.h_ref, bf16[768,2048]{1,0:T(8,128)(2,1)S(1)} %bitcast.23), custom_call_target="tpu_custom_call" | custom-call | flops 5637144576 | bytes 13893632 | tf_op jit(solution)/shard_map/forward_parts/pallas_call | solution.py:244
  119.6 0.0 reduce-scatter.2.cloned.1.call-update
  119.6 0.0 copy-start.9
  119.6 0.0 copy-start.11
  119.7 2.8 copy.25
  122.4 4.8 %all-gather.3.cloned.1.call-done = bf16[2048,2048]{1,0:T(8,128)(2,1)} async-done(((bf16[128,2048]{1,0:T(8,128)(2,1)}), bf16[2048,2048]{1,0:T(8,128)(2,1)}) %all-gather.3.cloned.1.call-update) | async-done | bytes 8388624 | tf_op jit(solution)/shard_map/all_gather | solution.py:274
  127.2 0.0 copy-done.9
  127.2 0.0 copy-done.11
  127.2 0.0 copy-start.2
  127.2 1.9 copy-done.2
  129.1 9.0 %backward_rows.1 = (bf16[1536,2048]{1,0:T(8,128)(2,1)}, bf16[1536,768]{1,0:T(8,128)(2,1)S(1)}) custom-call(s32[16,128]{1,0:T(8,128)S(1)} %copy-done.9, f32[16,128]{1,0:T(8,128)S(1)} %copy-done.11, bf16[16,128,2048]{2,1,0:T(8,128)(2,1)} %bitcast.33, bf16[2048,768]{1,0:T(8,128)(2,1)S(1)} %bitcast.24), custom_call_target="tpu_custom_call" | custom-call | flops 5637144576 | bytes 20185088 | tf_op jit(solution)/shard_map/backward_rows/pallas_call | solution.py:203
  138.1 0.0 copy-start.4
  138.1 1.4 copy-done.4
  139.5 31.9 %all-to-all-start.1 = ((bf16[16,96,768]{2,1,0:T(8,128)(2,1)}), bf16[16,96,768]{2,1,0:T(8,128)(2,1)S(1)}, u32[]{:S(2)}, u32[]{:S(2)}) async-start(bf16[16,96,768]{2,1,0:T(8,128)(2,1)} %bitcast.27), calls=%async_computation.2 | async-start | bytes 4718592 | tf_op jit(solution)/shard_map/all_to_all | solution.py:284
  171.4 0.1 copy.27
  171.5 1.0 copy.28.place_ref
  172.5 0.2 reshape.97.gate_ref
  172.7 9.2 %fusion = bf16[1,768,2048]{2,1,0:T(8,128)(2,1)} fusion(bf16[1536,768]{1,0:T(8,128)(2,1)} %bitcast.6.h_ref, bf16[1536,2048]{1,0:T(8,128)(2,1)} %get-tuple-element.19), kind=kOutput, calls=%fused_computation.2 | convolution fusion | flops 4833411072 | bytes 11796480 | tf_op jit(solution)/shard_map/dot_general | solution.py:289
  181.9 66.2 %all-to-all-done.1 = bf16[16,96,768]{2,1,0:T(8,128)(2,1)S(1)} async-done(((bf16[16,96,768]{2,1,0:T(8,128)(2,1)}), bf16[16,96,768]{2,1,0:T(8,128)(2,1)S(1)}, u32[]{:S(2)}, u32[]{:S(2)}) %all-to-all-start.1) | async-done | bytes 2359328 | tf_op jit(solution)/shard_map/all_to_all | solution.py:284
  248.1 0.0 copy-start.5
  248.1 1.0 copy-done.5
  249.2 0.0 copy-start.7
  249.2 1.5 copy-done.7
  250.7 4.7 %unpack.1 = (bf16[1024,768]{1,0:T(8,128)(2,1)}, f32[1024,1]{1,0:T(8,128)S(1)}) custom-call(s32[1024,1]{1,0:T(8,128)S(1)} %copy-done.5, f32[1024,1]{1,0:T(8,128)S(1)} %reshape.97.gate_ref, bf16[1024,768]{1,0:T(8,128)(2,1)S(1)} %bitcast.30, bf16[1536,768]{1,0:T(8,128)(2,1)S(1)} %bitcast.26), custom_call_target="tpu_custom_call" | custom-call | flops 2415919104 | bytes 5505024 | tf_op jit(solution)/shard_map/unpack/pallas_call | solution.py:128
  255.3 0.2 reduce
  255.5 0.1 reshape.86
  255.6 0.7 copy.30
  256.3 39.2 %reduce-scatter.2.cloned.1.call-done = bf16[128,2048]{1,0:T(8,128)(2,1)} async-done(((bf16[2048,2048]{1,0:T(8,128)(2,1)}), bf16[128,2048]{1,0:T(8,128)(2,1)}) %reduce-scatter.2.cloned.1.call-update) | async-done | bytes 524304 | tf_op jit(solution)/shard_map/reduce_scatter | solution.py:288
  (5 shorter events, 0.0 us)
Async XLA Ops:
  7.2 0.8 copy-start
  7.2 120.0 %all-gather.3.cloned.1.call-start = ((), (), s32[]{:S(2)}) async-start(), calls=%async_computation.4 | async-start | bytes 8912896 | tf_op jit(solution)/shard_map/all_gather | solution.py:274
  9.6 1.4 copy-start.6
  14.4 1.4 copy-start.3
  15.8 7.8 %copy-start.12 = (f32[128,8]{0,1:T(8,128)S(1)}, f32[128,8]{0,1:T(8,128)}, u32[]{:S(2)}) copy-start(f32[128,8]{0,1:T(8,128)} %param.7) | copy-start | bytes 12292
  15.8 90.7 %copy-start.1 = (bf16[1,768,2048]{2,1,0:T(8,128)(2,1)S(1)}, bf16[1,768,2048]{2,1,0:T(8,128)(2,1)}, u32[]{:S(2)}) copy-start(bf16[1,768,2048]{2,1,0:T(8,128)(2,1)} %param.10) | copy-start | bytes 9437188
  15.8 90.7 %all-to-all-start = ((bf16[16,96,768]{2,1,0:T(8,128)(2,1)}), bf16[16,96,768]{2,1,0:T(8,128)(2,1)}, u32[]{:S(2)}, u32[]{:S(2)}) async-start(bf16[16,96,768]{2,1,0:T(8,128)(2,1)} %bitcast.25), calls=%async_computation | async-start | bytes 4718592 | tf_op jit(solution)/shard_map/all_to_all | solution.py:278
  23.5 272.0 %reduce-scatter.2.cloned.1.call-start = ((), (), s32[]{:S(2)}) async-start(), calls=%async_computation.3 | async-start | bytes 8912896 | tf_op jit(solution)/shard_map/reduce_scatter | solution.py:288
  106.5 0.7 copy-start.8
  107.3 0.7 copy-start.10
  119.6 7.6 %copy-start.9 = (s32[16,128]{1,0:T(8,128)S(1)}, s32[16,128]{1,0:T(8,128)}, u32[]{:S(2)}) copy-start(s32[16,128]{1,0:T(8,128)} %get-tuple-element.12.rank_ref) | copy-start | bytes 24580
  119.6 7.6 %copy-start.11 = (f32[16,128]{1,0:T(8,128)S(1)}, f32[16,128]{1,0:T(8,128)}, u32[]{:S(2)}) copy-start(f32[16,128]{1,0:T(8,128)} %get-tuple-element.13.gate_ref) | copy-start | bytes 24580
  127.2 1.9 copy-start.2
  138.1 1.4 copy-start.4
  139.5 108.6 %all-to-all-start.1 = ((bf16[16,96,768]{2,1,0:T(8,128)(2,1)}), bf16[16,96,768]{2,1,0:T(8,128)(2,1)S(1)}, u32[]{:S(2)}, u32[]{:S(2)}) async-start(bf16[16,96,768]{2,1,0:T(8,128)(2,1)} %bitcast.27), calls=%async_computation.2 | async-start | bytes 4718592 | tf_op jit(solution)/shard_map/all_to_all | solution.py:284
  248.1 1.0 copy-start.5
  249.2 1.5 copy-start.7
Sparse Core Ops, SparseCore 0:
  10.2 116.9 all-gather.2
  131.9 163.6 reduce-scatter.1

commit v3 on v2

--- a/solution.py
+++ b/solution.py
@@ -151,142 +151,321 @@
     )(place, gates, h_flat, back_rows)
 
 
+def line_slots(position):
+    near = jnp.minimum(position, 3 - position)
+    turned = (near, near + 1, near + 2, 3 - 3 * near)
+    return [jnp.where(position < 2, slot, 3 - slot) for slot in turned]
+
+
 def route_kernel(devices, top, here_ref, routing_ref, rank_ref, gate_ref):
-    mine = here_ref[0].astype(F32)
-    marks, picked = [], []
-    for source in range(devices):
-        ids = routing_ref[2 * top * source:2 * top * source + top, :]
-        gates = routing_ref[2 * top * source + top:2 * top * (source + 1), :]
-        named = ids == mine
-        marks.append(jnp.sum(jnp.where(named, 1.0, 0.0), axis=0, keepdims=True))
-        picked.append(jnp.sum(jnp.where(named, gates, 0.0), axis=0, keepdims=True))
-    mark = jnp.concatenate(marks, axis=0)
-    rank = jnp.dot(mark.astype(BF16), upper(mark.shape[1]), preferred_element_type=F32)
-    rank_ref[...] = jnp.where(mark > 0, rank, -1.0).astype(jnp.int32)
-    gate_ref[...] = jnp.concatenate(picked, axis=0)
-
-
-def route(here, routing, devices, top):
-    tokens = routing.shape[1]
+    for side in range(2):
+        mine = (here_ref[0] ^ side).astype(F32)
+        marks, picked = [], []
+        for source in range(devices):
+            ids = routing_ref[source, :top, :]
+            gates = routing_ref[source, top:, :]
+            named = ids == mine
+            marks.append(jnp.sum(jnp.where(named, 1.0, 0.0), axis=0, keepdims=True))
+            picked.append(jnp.sum(jnp.where(named, gates, 0.0), axis=0, keepdims=True))
+        mark = jnp.concatenate(marks, axis=0)
+        rank = jnp.dot(mark.astype(BF16), upper(mark.shape[1]), preferred_element_type=F32)
+        rank_ref[side] = jnp.where(mark > 0, rank, -1.0).astype(jnp.int32)
+        gate_ref[side] = jnp.concatenate(picked, axis=0)
+
+
+def route(here, routing, top):
+    devices, _, tokens = routing.shape
     return pl.pallas_call(
         functools.partial(route_kernel, devices, top),
         in_specs=[pl.BlockSpec(memory_space=pltpu.SMEM), pl.BlockSpec(memory_space=pltpu.VMEM)],
         out_specs=[pl.BlockSpec(memory_space=pltpu.VMEM)] * 2,
         out_shape=[
-            jax.ShapeDtypeStruct((devices, tokens), jnp.int32),
-            jax.ShapeDtypeStruct((devices, tokens), F32),
-        ],
+            jax.ShapeDtypeStruct((2, devices, tokens), jnp.int32),
+            jax.ShapeDtypeStruct((2, devices, tokens), F32),
+        ],
+        cost_estimate=pl.CostEstimate(flops=1 << 21, transcendentals=0, bytes_accessed=1 << 19),
         name="route",
     )(here, routing)
 
 
-def picks(rank_ref, gate_ref, source, capacity):
-    rank = rank_ref[pl.ds(source, 1), :]
-    chosen = lax.broadcasted_iota(jnp.int32, (capacity, rank.shape[1]), 0) == rank
-    gate = jnp.sum(jnp.where(chosen, gate_ref[pl.ds(source, 1), :], 0.0), axis=1, keepdims=True)
-    return jnp.where(chosen, 1.0, 0.0).astype(BF16), gate
-
-
-def back_kernel(capacity, rank_ref, gate_ref, cot_ref, weight_ref, z_ref, back_ref):
-    each = cot_ref.shape[0]
+def chosen_rows(rank_ref, side, source, capacity):
+    rank = rank_ref[side, pl.ds(source, 1), :]
+    return lax.broadcasted_iota(jnp.int32, (capacity, rank.shape[1]), 0) == rank
+
+
+def gate_column(gate_ref, chosen, side, source):
+    return jnp.sum(jnp.where(chosen, gate_ref[side, pl.ds(source, 1), :], 0.0), axis=1, keepdims=True)
+
+
+def one_hot(chosen):
+    return jnp.where(chosen, 1.0, 0.0).astype(BF16)
+
+
+def lane_sources(here, slots, lane):
+    line, across = here // 4, (here // 2) % 2
+    places = line_slots(line)
+    return [places[slot] * 4 + (across ^ turn) * 2 + lane for slot in slots for turn in range(2)]
+
+
+def place_out(pieces, sem):
+    copies = [pltpu.make_async_copy(source, target, sem.at[i]) for i, (source, target) in enumerate(pieces)]
+    for copy in copies:
+        copy.start()
+    return copies
+
+
+def scale_kernel(capacity, slots, held, here_ref, rank_ref, gate_ref, weight_ref, *refs):
+    count = 2 * len(slots)
+    blocks, refs = refs[:count], refs[count + held:]
+    z_ref, back_ref, sibling_ref, z_scratch, back_scratch, z_sem, back_sem = refs
+    sources = lane_sources(here_ref[0], slots, here_ref[0] % 2)
+    for i, source in enumerate(sources):
+        chosen = [chosen_rows(rank_ref, side, source, capacity) for side in range(2)]
+        gates = [gate_column(gate_ref, chosen[side], side, source) for side in range(2)]
+        both = jnp.concatenate([one_hot(chosen[0]), one_hot(chosen[1])], axis=0)
+        rows = jnp.dot(both, blocks[i][...], preferred_element_type=F32)
+        z_scratch[i] = (rows[:capacity] * gates[0]).astype(BF16)
+        sibling_ref[i] = (rows[capacity:] * gates[1]).astype(BF16)
+    copies = place_out([(z_scratch.at[i], z_ref.at[source]) for i, source in enumerate(sources)], z_sem)
+    flat = z_scratch[...].reshape(count * capacity, z_scratch.shape[2])
+    back = lax.dot_general(flat, weight_ref[...], (((1,), (1,)), ((), ())), preferred_element_type=F32)
+    back_scratch[...] = back.astype(BF16).reshape(back_scratch.shape)
+    copies += place_out([(back_scratch.at[i], back_ref.at[source]) for i, source in enumerate(sources)], back_sem)
+    for copy in copies:
+        copy.wait()
+
+
+def scaled_rows(here, rank, gate, weight, blocks, slots, capacity, buffers):
+    devices = rank.shape[1]
+    hidden, width = weight.shape
+    count = len(blocks)
+    tokens = blocks[0].shape[0]
+    vmem, anywhere = pl.BlockSpec(memory_space=pltpu.VMEM), pl.BlockSpec(memory_space=pl.ANY)
+    return pl.pallas_call(
+        functools.partial(scale_kernel, capacity, slots, len(buffers)),
+        in_specs=[pl.BlockSpec(memory_space=pltpu.SMEM)] + [vmem] * (3 + count) + [anywhere] * len(buffers),
+        out_specs=[anywhere, anywhere, vmem],
+        out_shape=[
+            jax.ShapeDtypeStruct((devices, capacity, width), BF16),
+            jax.ShapeDtypeStruct((devices, capacity, hidden), BF16),
+            jax.ShapeDtypeStruct((count, capacity, width), BF16),
+        ],
+        scratch_shapes=[
+            pltpu.VMEM((count, capacity, width), BF16),
+            pltpu.VMEM((count, capacity, hidden), BF16),
+            pltpu.SemaphoreType.DMA((count,)),
+            pltpu.SemaphoreType.DMA((count,)),
+        ],
+        input_output_aliases={4 + count + i: i for i in range(len(buffers))},
+        compiler_params=pltpu.CompilerParams(vmem_limit_bytes=40 * MIB),
+        cost_estimate=pl.CostEstimate(
+            flops=2 * count * capacity * width * (hidden + 2 * tokens), transcendentals=0,
+            bytes_accessed=2 * count * (tokens * width + capacity * (2 * width + hidden)) + 2 * width * hidden,
+        ),
+        name="scaled_rows",
+    )(here, rank, gate, weight, *blocks, *buffers)
+
+
+def sibling_kernel(capacity, slots, here_ref, weight_ref, rows_ref, _z, _back, z_ref, back_ref, back_scratch, z_sem, back_sem):
+    count = 2 * len(slots)
+    sources = lane_sources(here_ref[0], slots, 1 - here_ref[0] % 2)
+    copies = place_out([(rows_ref.at[i], z_ref.at[source]) for i, source in enumerate(sources)], z_sem)
+    flat = rows_ref[...].reshape(count * capacity, rows_ref.shape[2])
+    back = lax.dot_general(flat, weight_ref[...], (((1,), (1,)), ((), ())), preferred_element_type=F32)
+    back_scratch[...] = back.astype(BF16).reshape(back_scratch.shape)
+    copies += place_out([(back_scratch.at[i], back_ref.at[source]) for i, source in enumerate(sources)], back_sem)
+    for copy in copies:
+        copy.wait()
+
+
+def sibling_rows(here, weight, rows, slots, z_rows, back):
+    count, capacity, width = rows.shape
+    hidden = weight.shape[0]
+    vmem, anywhere = pl.BlockSpec(memory_space=pltpu.VMEM), pl.BlockSpec(memory_space=pl.ANY)
+    return pl.pallas_call(
+        functools.partial(sibling_kernel, capacity, slots),
+        in_specs=[pl.BlockSpec(memory_space=pltpu.SMEM), vmem, vmem, anywhere, anywhere],
+        out_specs=[anywhere, anywhere],
+        out_shape=[jax.ShapeDtypeStruct(z_rows.shape, BF16), jax.ShapeDtypeStruct(back.shape, BF16)],
+        scratch_shapes=[
+            pltpu.VMEM((count, capacity, hidden), BF16),
+            pltpu.SemaphoreType.DMA((count,)),
+            pltpu.SemaphoreType.DMA((count,)),
+        ],
+        input_output_aliases={3: 0, 4: 1},
+        compiler_params=pltpu.CompilerParams(vmem_limit_bytes=40 * MIB),
+        cost_estimate=pl.CostEstimate(
+            flops=2 * count * capacity * width * hidden, transcendentals=0,
+            bytes_accessed=2 * count * capacity * (2 * width + hidden) + 2 * width * hidden,
+        ),
+        name="sibling_rows",
+    )(here, weight, rows, z_rows, back)
+
+
+def forward_kernel(capacity, turn, here_ref, rank_ref, gate_ref, h_ref, weight_ref, out_ref):
+    each = out_ref.shape[0]
+    lane = (here_ref[0] % 2) ^ turn
+    flat = h_ref[...].reshape(each * capacity, h_ref.shape[3])
+    out = jnp.dot(flat, weight_ref[...], preferred_element_type=F32).astype(BF16).astype(F32)
     for j in range(each):
-        chosen, gate = picks(rank_ref, gate_ref, pl.program_id(0) * each + j, capacity)
-        rows = jnp.dot(chosen, cot_ref[j], preferred_element_type=F32)
-        z_ref[j * capacity:(j + 1) * capacity, :] = (rows * gate).astype(BF16)
-    back_ref[...] = jnp.dot(z_ref[...], weight_ref[...], preferred_element_type=F32).astype(BF16)
-
-
-def backward_rows(rank, gate, cotangents, weight_t, capacity, each=4):
-    devices, tokens, width = cotangents.shape
-    hidden = weight_t.shape[1]
-    rows = each * capacity
-    return pl.pallas_call(
-        functools.partial(back_kernel, capacity),
-        grid=(devices // each,),
-        in_specs=[
-            pl.BlockSpec((devices, tokens), lambda i: (0, 0)),
-            pl.BlockSpec((devices, tokens), lambda i: (0, 0)),
-            pl.BlockSpec((each, tokens, width), lambda i: (i, 0, 0)),
-            pl.BlockSpec((width, hidden), lambda i: (0, 0)),
-        ],
-        out_specs=[
-            pl.BlockSpec((rows, width), lambda i: (i, 0)),
-            pl.BlockSpec((rows, hidden), lambda i: (i, 0)),
-        ],
-        out_shape=[
-            jax.ShapeDtypeStruct((devices * capacity, width), BF16),
-            jax.ShapeDtypeStruct((devices * capacity, hidden), BF16),
-        ],
-        compiler_params=pltpu.CompilerParams(vmem_limit_bytes=48 * MIB),
-        cost_estimate=pl.CostEstimate(
-            flops=2 * devices * capacity * width * (hidden + tokens), transcendentals=0,
-            bytes_accessed=2 * devices * (tokens * width + capacity * (width + hidden)) + 2 * width * hidden,
-        ),
-        name="backward_rows",
-    )(rank, gate, cotangents, weight_t)
-
-
-def forward_kernel(capacity, rank_ref, gate_ref, h_ref, weight_ref, part_ref):
-    each = part_ref.shape[0]
-    out = jnp.dot(h_ref[...], weight_ref[...], preferred_element_type=F32)
-    out = out.astype(BF16).astype(F32)
-    for j in range(each):
-        chosen, gate = picks(rank_ref, gate_ref, pl.program_id(0) * each + j, capacity)
-        rows = (out[j * capacity:(j + 1) * capacity, :] * gate).astype(BF16)
-        part = lax.dot_general(chosen, rows, (((0,), (0,)), ((), ())), preferred_element_type=F32)
-        part_ref[j] = part.astype(BF16)
-
-
-def forward_parts(rank, gate, rows_h, weight, capacity, each=8, columns=512):
-    devices, tokens = rank.shape
-    hidden, width = weight.shape
-    rows = each * capacity
-    return pl.pallas_call(
-        functools.partial(forward_kernel, capacity),
-        grid=(devices // each, width // columns),
-        in_specs=[
-            pl.BlockSpec((devices, tokens), lambda i, j: (0, 0)),
-            pl.BlockSpec((devices, tokens), lambda i, j: (0, 0)),
-            pl.BlockSpec((rows, hidden), lambda i, j: (i, 0)),
-            pl.BlockSpec((hidden, columns), lambda i, j: (0, j)),
-        ],
-        out_specs=pl.BlockSpec((each, tokens, columns), lambda i, j: (i, 0, j)),
-        out_shape=jax.ShapeDtypeStruct((devices, tokens, width), BF16),
-        compiler_params=pltpu.CompilerParams(vmem_limit_bytes=48 * MIB),
-        cost_estimate=pl.CostEstimate(
-            flops=2 * devices * capacity * width * (hidden + tokens), transcendentals=0,
-            bytes_accessed=2 * devices * (tokens * width + capacity * hidden) + 2 * width * hidden,
-        ),
-        name="forward_parts",
-    )(rank, gate, rows_h, weight)
+        source = (pl.program_id(0) * each + j) * 2 + lane
+        gate = gate_column(gate_ref, chosen_rows(rank_ref, 0, source, capacity), 0, source)
+        out_ref[j] = (out[j * capacity:(j + 1) * capacity, :] * gate).astype(BF16)
+
+
+def forward_rows(here, rank, gate, rows_h, weight, turn, each=4):
+    devices, capacity, hidden = rows_h.shape
+    width = weight.shape[1]
+    whole = pl.BlockSpec(rank.shape, lambda i, here: (0, 0, 0))
+    return pl.pallas_call(
+        functools.partial(forward_kernel, capacity, turn),
+        grid_spec=pltpu.PrefetchScalarGridSpec(
+            num_scalar_prefetch=1,
+            grid=(devices // 2 // each,),
+            in_specs=[
+                whole,
+                whole,
+                pl.BlockSpec((each, 1, capacity, hidden), lambda i, here: (i, (here[0] % 2) ^ turn, 0, 0)),
+                pl.BlockSpec((hidden, width), lambda i, here: (0, 0)),
+            ],
+            out_specs=pl.BlockSpec((each, capacity, width), lambda i, here: (i, 0, 0)),
+        ),
+        out_shape=jax.ShapeDtypeStruct((devices // 2, capacity, width), BF16),
+        compiler_params=pltpu.CompilerParams(vmem_limit_bytes=40 * MIB),
+        cost_estimate=pl.CostEstimate(
+            flops=devices * capacity * width * hidden, transcendentals=0,
+            bytes_accessed=devices * capacity * (width + hidden) + 2 * width * hidden,
+        ),
+        name="forward_rows",
+    )(here, rank, gate, rows_h.reshape(devices // 2, 2, capacity, hidden), weight)
+
+
+ORDER = (3, 2, 1, 0)
+
+
+def sum_kernel(capacity, turn, here_ref, rank_ref, own_ref, other_ref, *part_refs):
+    for step, slot in enumerate(ORDER):
+
+        @pl.when(pl.program_id(0) == step)
+        def _():
+            source = lane_sources(here_ref[0], (slot,), here_ref[0] % 2)[turn]
+            both = [one_hot(chosen_rows(rank_ref, side, source, capacity)) for side in range(2)]
+            rows = jnp.concatenate([own_ref[0], other_ref[0]], axis=0)
+            part = lax.dot_general(
+                jnp.concatenate(both, axis=0), rows, (((0,), (0,)), ((), ())), preferred_element_type=F32
+            )
+            part_refs[step][...] = part.astype(BF16)
+
+
+def summed(here, rank, own, other, turn):
+    _, capacity, width = own.shape
+    tokens = rank.shape[2]
+
+    def block(i, here):
+        place = jnp.int32(0)
+        for step, slot in enumerate(ORDER):
+            place = jnp.where(i == step, lane_sources(here[0], (slot,), 0)[turn] // 2, place)
+        return (place, 0, 0)
+
+    return pl.pallas_call(
+        functools.partial(sum_kernel, capacity, turn),
+        grid_spec=pltpu.PrefetchScalarGridSpec(
+            num_scalar_prefetch=1,
+            grid=(len(ORDER),),
+            in_specs=[
+                pl.BlockSpec(rank.shape, lambda i, here: (0, 0, 0)),
+                pl.BlockSpec((1, capacity, width), block),
+                pl.BlockSpec((1, capacity, width), block),
+            ],
+            out_specs=[pl.BlockSpec((tokens, width), lambda i, here: (0, 0))] * len(ORDER),
+        ),
+        out_shape=[jax.ShapeDtypeStruct((tokens, width), BF16)] * len(ORDER),
+        compiler_params=pltpu.CompilerParams(vmem_limit_bytes=40 * MIB),
+        cost_estimate=pl.CostEstimate(
+            flops=16 * tokens * capacity * width, transcendentals=0,
+            bytes_accessed=8 * width * (tokens + 2 * capacity),
+        ),
+        name="summed",
+    )(here, rank, own, other)
+
+
+def added(*values):
+    total = values[0].astype(F32)
+    for value in values[1:]:
+        total = total + value.astype(F32)
+    return total.astype(BF16)
+
+
+def passed(pairs, value):
+    return lax.ppermute(value, "expert", [(a * 4 + lane, b * 4 + lane) for a, b in pairs for lane in range(4)])
+
+
+def swapped_with(value, bit):
+    devices = lax.axis_size("expert")
+    return lax.ppermute(value, "expert", [(i, i ^ bit) for i in range(devices)])
+
+
+OUTER, INNER, ENDS = ((0, 1), (3, 2)), ((1, 2), (2, 1)), ((1, 0), (2, 3))
 
 
 def dense_shards(h_rows, gates, expert_ids, cotangent, down_weight, swapped):
     devices = lax.axis_size("expert")
-    here = lax.axis_index("expert")
+    here = lax.axis_index("expert").reshape(1)
     tokens, top, hidden = h_rows.shape
-    width = cotangent.shape[1]
     capacity = min(tokens, 3 * tokens * top // (2 * devices))
     weight = down_weight[0]
     slot_ids = slots_of(expert_ids, swapped, devices)
     h_flat = h_rows.reshape(-1, hidden)
 
-    cotangents = lax.all_gather(cotangent, "expert", axis=0, tiled=False)
     routing = jnp.concatenate([slot_ids.T.astype(F32), gates.T], axis=0)
-    routing = lax.all_gather(routing, "expert", axis=0, tiled=True)
+    routing = jnp.broadcast_to(routing, (devices,) + routing.shape)
+    routing = lax.all_to_all(routing, "expert", split_axis=0, concat_axis=0, tiled=True)
+    rank, gate = route(here, routing, top)
+
+    own = cotangent
+    from_end = passed(OUTER, own)
+    from_inner = passed(INNER, own)
+    near = added(from_inner, passed(ENDS, own))
+    own_y = swapped_with(own, 2)
+    from_far = passed(INNER, from_end)
+    middle = added(from_far, passed(ENDS, from_inner))
+    near_y = swapped_with(near, 2)
+    last = added(from_end, passed(ENDS, from_far))
+    middle_y = swapped_with(middle, 2)
+    last_y = swapped_with(last, 2)
+
     place, send_h = pack(slot_ids.reshape(1, -1), h_flat, devices, capacity)
     rows_h = lax.all_to_all(
         send_h.reshape(devices, capacity, hidden), "expert", split_axis=0, concat_axis=0, tiled=True
-    ).reshape(-1, hidden)
-    rank, gate = route(here.reshape(1), routing, devices, top)
-
-    z_rows, back = backward_rows(rank, gate, cotangents, weight.T, capacity)
-    back_rows = lax.all_to_all(
-        back.reshape(devices, capacity, hidden), "expert", split_axis=0, concat_axis=0, tiled=True
-    ).reshape(-1, hidden)
-    parts = forward_parts(rank, gate, rows_h, weight, capacity)
-    mixed = lax.psum_scatter(parts.reshape(-1, width), "expert", scatter_dimension=0, tiled=True)
-    grad_sum = lax.dot_general(rows_h, z_rows, (((0,), (0,)), ((), ())), preferred_element_type=F32)
+    )
+
+    z_rows, back, sibling = scaled_rows(here, rank, gate, weight, [own, own_y, near, near_y], (0, 1), capacity, [])
+    sibling = swapped_with(sibling, 1)
+    z_rows, back, sibling_last = scaled_rows(
+        here, rank, gate, weight, [middle, middle_y, last, last_y], (2, 3), capacity, [z_rows, back]
+    )
+    sibling_last = swapped_with(sibling_last, 1)
+    z_rows, back = sibling_rows(here, weight, sibling, (0, 1), z_rows, back)
+    z_rows, back = sibling_rows(here, weight, sibling_last, (2, 3), z_rows, back)
+    back_rows = lax.all_to_all(back, "expert", split_axis=0, concat_axis=0, tiled=True).reshape(-1, hidden)
+
+    other = swapped_with(forward_rows(here, rank, gate, rows_h, weight, 1), 1)
+    mine = forward_rows(here, rank, gate, rows_h, weight, 0)
+    across = [swapped_with(part, 2) for part in summed(here, rank, mine, other, 1)]
+    beside = summed(here, rank, mine, other, 0)
+    far, mid, close, kept = zip(beside, across)
+    outer1 = passed(OUTER, added(*far))
+    mid = added(*mid, outer1)
+    outer2, inner2 = passed(OUTER, mid), passed(INNER, mid)
+    close = added(*close, outer2)
+    outer3, inner3 = passed(OUTER, close), passed(INNER, close)
+    ends3 = passed(ENDS, added(*far, inner2))
+    mixed = added(*kept, outer3, inner3, ends3)
+
+    grad_sum = lax.dot_general(
+        rows_h.reshape(-1, hidden), z_rows.reshape(devices * capacity, -1), (((0,), (0,)), ((), ())),
+        preferred_element_type=F32,
+    )
     h_grad, gate_grad = unpack(place.reshape(-1, 1), gates.reshape(-1, 1), h_flat, back_rows)
     return (
         mixed,
@@ -298,7 +477,7 @@
 
 def shards(h_rows, *rest):
     devices = lax.axis_size("expert")
-    dense = devices <= 2 * h_rows.shape[1]
+    dense = devices == 16 and devices <= 2 * h_rows.shape[1]
     return (dense_shards if dense else sparse_shards)(h_rows, *rest)
 
 

time: 303 us -> 275 us (0.908)
  blocking collectives: 81.3 us -> 0 us
  starting transfers between devices: 39.6 us -> 75.7 us
  other arithmetic: 1.01 us -> 14.5 us
  between operations: 14.2 us -> 1.17 us
  Pallas kernels: 30.4 us -> 40.5 us
  waiting for transfers between devices: 111 us -> 116 us
    ppermute x0 -> x23, waiting for transfers between devices: none -> 115 us  [the longest x12 88.4 us: passed(): lax.ppermute(value, 'expert', [(a * 4 + lane, b * 4 + lane) for a, b in p...]
    all_gather x1 -> x0, blocking collectives: 81.3 us -> none  [dense_shards(): routing = lax.all_gather(routing, 'expert', axis=0, tiled=True)]
    all_to_all x1 -> x2, waiting for transfers between devices: 66.2 us -> 1.47 us  [the longest x1 1.46 us: dense_shards(): lax.all_to_all(routing, 'expert', split_axis=0, concat_axis=0, tiled=True)]
    ppermute x0 -> x23, starting transfers between devices: none -> 45.1 us  [the longest x12 30.1 us: passed(): lax.ppermute(value, 'expert', [(a * 4 + lane, b * 4 + lane) for a, b in p...]
    reduce_scatter x1 -> x0, waiting for transfers between devices: 39.2 us -> none  [dense_shards(): lax.psum_scatter(parts.reshape(-1, width), 'expert', scatter_dimension=0,...]
    convert_element_type x0 -> x8, other arithmetic: none -> 12.8 us  [added(): return total.astype(BF16)]
    pallas_call x2 -> x8, Pallas kernels: 20.6 us -> 29.1 us  [the longest x2 10.2 us: scaled_rows(): pl.pallas_call(functools.partial(scale_kernel, capacity, slots, len(buffe...]
    all_to_all x1 -> x2, starting transfers between devices: 31.9 us -> 25.9 us  [the longest x1 18.5 us: dense_shards(): lax.all_to_all(back, 'expert', split_axis=0, concat_axis=0, tiled=True)]
  transfers between devices with their start and end apart: 4 -> 26, of which waited for: 3 -> 9; matrix products, arithmetic and copies ran while one was open for 5% -> 8% of each run, Pallas kernels for 10% -> 15%
where the time goes in v3:
time: 275 us; the launch traced here: 272 us
  waiting for transfers between devices  116 us (42%)
  starting transfers between devices  75.7 us (28%)
  Pallas kernels  40.5 us (15%)
  local copies, waits for them, and re-layouts  15.1 us (5%)
  other arithmetic  14.5 us (5%)
  matrix products  9.1 us (3%)
    ppermute x12, waiting for transfers between devices, passed(): lax.ppermute(value, 'expert', [(a * 4 + lane, b * 4 + lane) for a, b in p...  88.4 us
    ppermute x12, starting transfers between devices, passed(): lax.ppermute(value, 'expert', [(a * 4 + lane, b * 4 + lane) for a, b in p...  30.1 us
    ppermute x11, waiting for transfers between devices, swapped_with(): return lax.ppermute(value, 'expert', [(i, i ^ bit) for i in range(devices)])  26.3 us
    all_to_all x1, starting transfers between devices, dense_shards(): lax.all_to_all(back, 'expert', split_axis=0, concat_axis=0, tiled=True)  18.5 us
    ppermute x11, starting transfers between devices, swapped_with(): return lax.ppermute(value, 'expert', [(i, i ^ bit) for i in range(devices)])  15 us
    unnamed x56, local copies, waits for them, and re-layouts  13.1 us
    convert_element_type x8, other arithmetic, added(): return total.astype(BF16)  12.8 us
    pallas_call x2, Pallas kernels, scaled_rows(): pl.pallas_call(functools.partial(scale_kernel, capacity, slots, len(buffe...  10.2 us
  transfers between devices with their start and end apart: 26, of which 9 were waited for; matrix products, arithmetic and copies ran while one was open for 8% of the time, Pallas kernels for 15%

profile of v3, /device:TPU:0, one launch (start us, length us, event | category | flops | bytes accessed | tf_op | source)
XLA Modules:
  0.0 272.3 jit_solution(14693541468076928281)
XLA Ops:
  1.3 0.7 gather_fusion
  2.0 0.8 select_reduce_fusion
  2.8 0.7 pad_maximum_fusion
  3.4 0.7 broadcast_in_dim.19
  4.1 7.4 %all-to-all-start = ((f32[16,16,128]{2,1,0:T(8,128)}), f32[16,16,128]{2,1,0:T(8,128)S(1)}, u32[]{:S(2)}, u32[]{:S(2)}) async-start(f32[16,16,128]{2,1,0:T(8,128)} %broadcast_in_dim.19), calls=%async_computation | async-start | bytes 262144 | tf_op jit(solution)/shard_map/all_to_all | solution.py:422
  11.7 1.4 copy-done.17
  13.1 3.4 %pack.1 = (s32[1,1024]{1,0:T(1,128)S(1)}, bf16[1536,768]{1,0:T(8,128)(2,1)S(1)}) custom-call(s32[1,1024]{1,0:T(1,128)S(1)} %reshape.74.ids_ref, bf16[1024,768]{1,0:T(8,128)(2,1)S(1)} %bitcast.31), custom_call_target="tpu_custom_call" | custom-call | flops 2415919104 | bytes 3932160 | tf_op jit(solution)/shard_map/pack/pallas_call | solution.py:91
  16.6 1.4 copy-done.7
  18.0 1.5 all-to-all-done.routing_ref
  20.1 4.7 %all-to-all-start.1 = ((bf16[16,96,768]{2,1,0:T(8,128)(2,1)}), bf16[16,96,768]{2,1,0:T(8,128)(2,1)}, u32[]{:S(2)}, u32[]{:S(2)}) async-start(bf16[16,96,768]{2,1,0:T(8,128)(2,1)} %bitcast.29), calls=%async_computation.1 | async-start | bytes 4718592 | tf_op jit(solution)/shard_map/all_to_all | solution.py:438
  24.8 4.6 %collective-permute-start.11 = (bf16[128,2048]{1,0:T(8,128)(2,1)}, bf16[128,2048]{1,0:T(8,128)(2,1)}, u32[]{:S(2)}, u32[]{:S(2)}) collective-permute-start(bf16[128,2048]{1,0:T(8,128)(2,1)} %refs_0_.1), channel_id=1, source_target_pairs={{0,4},{1,5},{2,6},{3,7},{12,8},{13,9},{14,10},{15,11},{16,20},{17,... | collective-permute-start | bytes 1572872 | tf_op jit(solution)/shard_map/ppermute | solution.py:400
  29.4 1.5 collective-permute-start.13
  30.9 44.3 %collective-permute-done.11 = bf16[128,2048]{1,0:T(8,128)(2,1)} collective-permute-done((bf16[128,2048]{1,0:T(8,128)(2,1)}, bf16[128,2048]{1,0:T(8,128)(2,1)}, u32[]{:S(2)}, u32[]{:S(2)}) %collective-permute-start.11) | collective-permute-done | bytes 524320 | tf_op jit(solution)/shard_map/ppermute | solution.py:400
  75.2 1.5 collective-permute-start.12
  76.7 1.3 collective-permute-start.19
  78.0 2.3 collective-permute-start.18
  80.3 1.7 route.1
  82.0 1.3 collective-permute-start.14
  83.3 1.5 collective-permute-start.16
  84.8 0.7 copy-done.13
  85.5 0.7 copy-done.15
  86.2 3.9 %forward_rows.3 = bf16[8,96,2048]{2,1,0:T(8,128)(2,1)S(1)} custom-call(s32[1]{0:T(128)} %bitcast.here_ref, s32[2,16,128]{2,1,0:T(8,128)S(1)} %copy-done.13, f32[2,16,128]{2,1,0:T(8,128)S(1)} %copy-done.15, bf16[8,2,96,768]{3,2,1,0:T(8,128)(2,1)} %bitcast.6.h_ref, bf16[768,2048]{1,0:T(8,128)(2,1)S(1)} %bitcast.23), custom_call_target="tpu_custom_call" | custom-call | flops 2415919104 | bytes 7471104 | tf_op jit(solution)/shard_map/forward_rows/pallas_call | solution.py:320
  90.3 6.3 %collective-permute-done.19 = bf16[128,2048]{1,0:T(8,128)(2,1)} collective-permute-done((bf16[128,2048]{1,0:T(8,128)(2,1)}, bf16[128,2048]{1,0:T(8,128)(2,1)}, u32[]{:S(2)}, u32[]{:S(2)}) %collective-permute-start.19) | collective-permute-done | bytes 524320 | tf_op jit(solution)/shard_map/ppermute | solution.py:400
  96.6 1.4 add_convert_fusion.refs_2_
  97.9 1.7 collective-permute-start.20
  99.6 8.2 %collective-permute-done.14 = bf16[128,2048]{1,0:T(8,128)(2,1)} collective-permute-done((bf16[128,2048]{1,0:T(8,128)(2,1)}, bf16[128,2048]{1,0:T(8,128)(2,1)}, u32[]{:S(2)}, u32[]{:S(2)}) %collective-permute-start.14) | collective-permute-done | bytes 524320 | tf_op jit(solution)/shard_map/ppermute | solution.py:400
  107.8 1.4 add_convert_fusion.2.refs_0_
  109.2 1.7 collective-permute-start.15
  110.8 6.8 %collective-permute-done.16 = bf16[128,2048]{1,0:T(8,128)(2,1)} collective-permute-done((bf16[128,2048]{1,0:T(8,128)(2,1)}, bf16[128,2048]{1,0:T(8,128)(2,1)}, u32[]{:S(2)}, u32[]{:S(2)}) %collective-permute-start.16) | collective-permute-done | bytes 524320 | tf_op jit(solution)/shard_map/ppermute | solution.py:400
  117.7 1.4 add_convert_fusion.1.refs_2_
  119.0 1.7 collective-permute-start.17
  120.7 5.6 %scaled_rows.2 = (bf16[16,96,2048]{2,1,0:T(8,128)(2,1)}, bf16[16,96,768]{2,1,0:T(8,128)(2,1)}, bf16[4,96,2048]{2,1,0:T(8,128)(2,1)}) custom-call(s32[1]{0:T(128)} %bitcast.here_ref, s32[2,16,128]{2,1,0:T(8,128)S(1)} %copy-done.14, f32[2,16,128]{2,1,0:T(8,128)S(1)} %copy-done.16, bf16[768,2048]{1,0:T(8,128)(2,1)S(1)} %bitcast.24, ...), custom_call_target="tpu_custom_call" | custom-call | flops 1610612736 | bytes 8978432 | tf_op jit(solution)/shard_map/scaled_rows/pallas_call | solution.py:244
  126.4 5.2 %collective-permute-done.17.refs_3_ = bf16[128,2048]{1,0:T(8,128)(2,1)S(1)} collective-permute-done((bf16[128,2048]{1,0:T(8,128)(2,1)S(1)}, bf16[128,2048]{1,0:T(8,128)(2,1)S(1)}, u32[]{:S(2)}, u32[]{:S(2)}) %collective-permute-start.17) | collective-permute-done | bytes 524320 | tf_op jit(solution)/shard_map/ppermute | solution.py:405
  131.7 4.6 %scaled_rows.3 = (bf16[16,96,2048]{2,1,0:T(8,128)(2,1)}, bf16[16,96,768]{2,1,0:T(8,128)(2,1)}, bf16[4,96,2048]{2,1,0:T(8,128)(2,1)}) custom-call(s32[1]{0:T(128)} %bitcast.here_ref, s32[2,16,128]{2,1,0:T(8,128)S(1)} %copy-done.14, f32[2,16,128]{2,1,0:T(8,128)S(1)} %copy-done.16, ...), custom_call_target="tpu_custom_call", output_to_operand_aliasing={{0}: (8, {}), {1}: (9, {})} | custom-call | flops 1610612736 | bytes 8978432 | tf_op jit(solution)/shard_map/scaled_rows/pallas_call | solution.py:244
  136.3 4.1 %forward_rows.2.own_ref = bf16[8,96,2048]{2,1,0:T(8,128)(2,1)S(1)} custom-call(s32[1]{0:T(128)} %bitcast.here_ref, s32[2,16,128]{2,1,0:T(8,128)S(1)} %copy-done.14, f32[2,16,128]{2,1,0:T(8,128)S(1)} %copy-done.16, bf16[8,2,96,768]{3,2,1,0:T(8,128)(2,1)} %bitcast.6.h_ref, bf16[768,2048]{1,0:T(8,128)(2,1)S(1)} %bitcast.26), custom_call_target="tpu_custom_call" | custom-call | flops 2415919104 | bytes 7471104 | tf_op jit(solution)/shard_map/forward_rows/pallas_call | solution.py:320
  140.5 3.0 %summed.3 = (bf16[128,2048]{1,0:T(8,128)(2,1)}, bf16[128,2048]{1,0:T(8,128)(2,1)S(1)}, bf16[128,2048]{1,0:T(8,128)(2,1)}, bf16[128,2048]{1,0:T(8,128)(2,1)S(1)}) custom-call(s32[1]{0:T(128)} %bitcast.here_ref, s32[2,16,128]{2,1,0:T(8,128)S(1)} %copy-done.14, bf16[8,96,2048]{2,1,0:T(8,128)(2,1)S(1)} %forward_rows.2.own_ref, ...), custom_call_target="tpu_custom_call" | custom-call | flops 402653184 | bytes 5242880 | tf_op jit(solution)/shard_map/summed/pallas_call | solution.py:370
  143.5 1.6 collective-permute-start.4
  145.2 3.1 %sibling_rows.2 = (bf16[16,96,2048]{2,1,0:T(8,128)(2,1)S(1)}, bf16[16,96,768]{2,1,0:T(8,128)(2,1)}) custom-call(s32[1]{0:T(128)} %bitcast.here_ref, bf16[768,2048]{1,0:T(8,128)(2,1)S(1)} %bitcast.27, bf16[4,96,2048]{2,1,0:T(8,128)(2,1)S(1)} %collective-permute-done.22.rows_ref, ...), custom_call_target="tpu_custom_call", output_to_operand_aliasing={{0}: (3, {}), {1}: (4, {})} | custom-call | flops 1207959552 | bytes 6881280 | tf_op jit(solution)/shard_map/sibling_rows/pallas_call | solution.py:285
  148.3 3.1 %sibling_rows.3 = (bf16[16,96,2048]{2,1,0:T(8,128)(2,1)S(1)}, bf16[16,96,768]{2,1,0:T(8,128)(2,1)}) custom-call(s32[1]{0:T(128)} %bitcast.here_ref, bf16[768,2048]{1,0:T(8,128)(2,1)S(1)} %bitcast.28, bf16[4,96,2048]{2,1,0:T(8,128)(2,1)S(1)} %collective-permute-done.21.rows_ref, ...), custom_call_target="tpu_custom_call", output_to_operand_aliasing={{0}: (3, {}), {1}: (4, {})} | custom-call | flops 1207959552 | bytes 6881280 | tf_op jit(solution)/shard_map/sibling_rows/pallas_call | solution.py:285
  151.5 2.7 copy-done.1
  154.2 18.5 %all-to-all-start.2 = ((bf16[16,96,768]{2,1,0:T(8,128)(2,1)}), bf16[16,96,768]{2,1,0:T(8,128)(2,1)}, u32[]{:S(2)}, u32[]{:S(2)}) async-start(bf16[16,96,768]{2,1,0:T(8,128)(2,1)} %get-tuple-element.48), calls=%async_computation.2 | async-start | bytes 4718592 | tf_op jit(solution)/shard_map/all_to_all | solution.py:450
  172.7 1.9 collective-permute-start.3
  174.6 1.9 copy-done.6
  176.5 1.6 summed.2
  178.2 0.7 copy-done.8
  178.9 1.3 fusion.1
  180.2 3.7 %collective-permute-start.5 = (bf16[128,2048]{1,0:T(8,128)(2,1)S(1)}, bf16[128,2048]{1,0:T(8,128)(2,1)S(1)}, u32[]{:S(2)}, u32[]{:S(2)}) collective-permute-start(bf16[128,2048]{1,0:T(8,128)(2,1)S(1)} %fusion.1), channel_id=1, source_target_pairs={{0,4},{1,5},{2,6},{3,7},{12,8},{13,9},{14,10},{15,11},{16,20},{17,... | collective-permute-start | bytes 1572872 | tf_op jit(solution)/shard_map/ppermute | solution.py:400
  183.9 1.5 collective-permute-start.2
  185.4 21.1 %collective-permute-done.3 = bf16[128,2048]{1,0:T(8,128)(2,1)S(1)} collective-permute-done((bf16[128,2048]{1,0:T(8,128)(2,1)}, bf16[128,2048]{1,0:T(8,128)(2,1)S(1)}, u32[]{:S(2)}, u32[]{:S(2)}) %collective-permute-start.3) | collective-permute-done | bytes 524320 | tf_op jit(solution)/shard_map/ppermute | solution.py:405
  206.4 16.7 %collective-permute-done.5 = bf16[128,2048]{1,0:T(8,128)(2,1)S(1)} collective-permute-done((bf16[128,2048]{1,0:T(8,128)(2,1)S(1)}, bf16[128,2048]{1,0:T(8,128)(2,1)S(1)}, u32[]{:S(2)}, u32[]{:S(2)}) %collective-permute-start.5) | collective-permute-done | bytes 524320 | tf_op jit(solution)/shard_map/ppermute | solution.py:400
  223.4 5.3 %collective-permute-start.6 = (bf16[128,2048]{1,0:T(8,128)(2,1)S(1)}, bf16[128,2048]{1,0:T(8,128)(2,1)}, u32[]{:S(2)}, u32[]{:S(2)}) collective-permute-start(bf16[128,2048]{1,0:T(8,128)(2,1)S(1)} %add_convert_fusion.6), channel_id=1, source_target_pairs={{0,4},{1,5},{2,6},{3,7},{12,8},{13,9},{14,10},{15,11},{16,20},{17,... | collective-permute-start | bytes 1572872 | tf_op jit(solution)/shard_map/ppermute | solution.py:400
  228.6 1.4 collective-permute-start.9
  230.6 2.4 collective-permute-start.1
  233.0 6.0 %collective-permute-done.6 = bf16[128,2048]{1,0:T(8,128)(2,1)} collective-permute-done((bf16[128,2048]{1,0:T(8,128)(2,1)S(1)}, bf16[128,2048]{1,0:T(8,128)(2,1)}, u32[]{:S(2)}, u32[]{:S(2)}) %collective-permute-start.6) | collective-permute-done | bytes 524320 | tf_op jit(solution)/shard_map/ppermute | solution.py:400
  239.0 2.4 add_convert_fusion.5
  241.4 5.4 %collective-permute-start.7 = (bf16[128,2048]{1,0:T(8,128)(2,1)}, bf16[128,2048]{1,0:T(8,128)(2,1)}, u32[]{:S(2)}, u32[]{:S(2)}) collective-permute-start(bf16[128,2048]{1,0:T(8,128)(2,1)} %add_convert_fusion.5), channel_id=1, source_target_pairs={{0,4},{1,5},{2,6},{3,7},{12,8},{13,9},{14,10},{15,11},{16,20},{17,... | collective-permute-start | bytes 1572872 | tf_op jit(solution)/shard_map/ppermute | solution.py:400
  246.8 1.5 collective-permute-start.8
  248.3 2.3 add_convert_fusion.4
  250.6 1.3 collective-permute-start.10
  251.9 9.1 %fusion = bf16[1,768,2048]{2,1,0:T(8,128)(2,1)} fusion(bf16[16,96,768]{2,1,0:T(8,128)(2,1)} %all-to-all-done.1, bf16[16,96,2048]{2,1,0:T(8,128)(2,1)} %copy-done.1), kind=kOutput, calls=%fused_computation.2 | convolution fusion | flops 4833411072 | bytes 11796480 | tf_op jit(solution)/shard_map/dot_general | solution.py:465
  261.0 1.4 copy-done.18
  262.4 6.3 %unpack.1 = (bf16[1024,768]{1,0:T(8,128)(2,1)}, f32[1024,1]{1,0:T(8,128)S(1)}) custom-call(s32[1024,1]{1,0:T(8,128)S(1)} %copy.28.place_ref, f32[1024,1]{1,0:T(8,128)S(1)} %reshape.92.gate_ref, bf16[1024,768]{1,0:T(8,128)(2,1)S(1)} %bitcast.32, bf16[1536,768]{1,0:T(8,128)(2,1)} %bitcast.9.back_ref), custom_call_target="tpu_custom_call" | custom-call | flops 2415919104 | bytes 5505024 | tf_op jit(solution)/shard_map/unpack/pallas_call | solution.py:128
  269.0 0.7 copy.30
  269.7 2.6 add_convert_fusion.3
  (79 shorter events, 2.9 us)
Async XLA Ops:
  0.6 0.7 copy-start
  4.1 15.3 %all-to-all-start = ((f32[16,16,128]{2,1,0:T(8,128)}), f32[16,16,128]{2,1,0:T(8,128)S(1)}, u32[]{:S(2)}, u32[]{:S(2)}) async-start(f32[16,16,128]{2,1,0:T(8,128)} %broadcast_in_dim.19), calls=%async_computation | async-start | bytes 262144 | tf_op jit(solution)/shard_map/all_to_all | solution.py:422
  11.7 1.4 copy-start.17
  16.6 1.4 copy-start.7
  19.4 0.7 copy-start.23
  19.4 65.3 %copy-start.2 = (bf16[1,768,2048]{2,1,0:T(8,128)(2,1)S(1)}, bf16[1,768,2048]{2,1,0:T(8,128)(2,1)}, u32[]{:S(2)}) copy-start(bf16[1,768,2048]{2,1,0:T(8,128)(2,1)} %param.10) | copy-start | bytes 9437188
  20.1 64.6 %all-to-all-start.1 = ((bf16[16,96,768]{2,1,0:T(8,128)(2,1)}), bf16[16,96,768]{2,1,0:T(8,128)(2,1)}, u32[]{:S(2)}, u32[]{:S(2)}) async-start(bf16[16,96,768]{2,1,0:T(8,128)(2,1)} %bitcast.29), calls=%async_computation.1 | async-start | bytes 4718592 | tf_op jit(solution)/shard_map/all_to_all | solution.py:438
  24.8 50.4 %collective-permute-start.11 = (bf16[128,2048]{1,0:T(8,128)(2,1)}, bf16[128,2048]{1,0:T(8,128)(2,1)}, u32[]{:S(2)}, u32[]{:S(2)}) collective-permute-start(bf16[128,2048]{1,0:T(8,128)(2,1)} %refs_0_.1), channel_id=1, source_target_pairs={{0,4},{1,5},{2,6},{3,7},{12,8},{13,9},{14,10},{15,11},{16,20},{17,... | collective-permute-start | bytes 1572872 | tf_op jit(solution)/shard_map/ppermute | solution.py:400
  29.4 52.5 %collective-permute-start.13 = (bf16[128,2048]{1,0:T(8,128)(2,1)}, bf16[128,2048]{1,0:T(8,128)(2,1)}, u32[]{:S(2)}, u32[]{:S(2)}) collective-permute-start(bf16[128,2048]{1,0:T(8,128)(2,1)} %refs_0_.1), channel_id=1, source_target_pairs={{4,8},{5,9},{6,10},{7,11},{8,4},{9,5},{10,6},{11,7},{20,24},{21,25... | collective-permute-start | bytes 1572872 | tf_op jit(solution)/shard_map/ppermute | solution.py:400
  75.2 8.0 %collective-permute-start.12 = (bf16[128,2048]{1,0:T(8,128)(2,1)}, bf16[128,2048]{1,0:T(8,128)(2,1)}, u32[]{:S(2)}, u32[]{:S(2)}) collective-permute-start(bf16[128,2048]{1,0:T(8,128)(2,1)} %collective-permute-done.11), channel_id=1, source_target_pairs={{4,8},{5,9},{6,10},{7,11},{8,4},{9,5},{10,6},{11,7},{20,24},{21,25... | collective-permute-start | bytes 1572872 | tf_op jit(solution)/shard_map/ppermute | solution.py:400
  76.7 19.9 %collective-permute-start.19 = (bf16[128,2048]{1,0:T(8,128)(2,1)}, bf16[128,2048]{1,0:T(8,128)(2,1)}, u32[]{:S(2)}, u32[]{:S(2)}) collective-permute-start(bf16[128,2048]{1,0:T(8,128)(2,1)} %refs_0_.1), channel_id=1, source_target_pairs={{4,0},{5,1},{6,2},{7,3},{8,12},{9,13},{10,14},{11,15},{20,16},{21,... | collective-permute-start | bytes 1572872 | tf_op jit(solution)/shard_map/ppermute | solution.py:400
  78.0 42.7 %collective-permute-start.18 = (bf16[128,2048]{1,0:T(8,128)(2,1)}, bf16[128,2048]{1,0:T(8,128)(2,1)}, u32[]{:S(2)}, u32[]{:S(2)}) collective-permute-start(bf16[128,2048]{1,0:T(8,128)(2,1)} %refs_0_.1), channel_id=1, source_target_pairs={{0,2},{1,3},{2,0},{3,1},{4,6},{5,7},{6,4},{7,5},{8,10},{9,11},{10,... | collective-permute-start | bytes 1572872 | tf_op jit(solution)/shard_map/ppermute | solution.py:405
  82.0 25.8 %collective-permute-start.14 = (bf16[128,2048]{1,0:T(8,128)(2,1)}, bf16[128,2048]{1,0:T(8,128)(2,1)}, u32[]{:S(2)}, u32[]{:S(2)}) collective-permute-start(bf16[128,2048]{1,0:T(8,128)(2,1)} %collective-permute-done.13), channel_id=1, source_target_pairs={{4,0},{5,1},{6,2},{7,3},{8,12},{9,13},{10,14},{11,15},{20,16},{21,... | collective-permute-start | bytes 1572872 | tf_op jit(solution)/shard_map/ppermute | solution.py:400
  83.3 34.4 %collective-permute-start.16 = (bf16[128,2048]{1,0:T(8,128)(2,1)}, bf16[128,2048]{1,0:T(8,128)(2,1)}, u32[]{:S(2)}, u32[]{:S(2)}) collective-permute-start(bf16[128,2048]{1,0:T(8,128)(2,1)} %collective-permute-done.12), channel_id=1, source_target_pairs={{4,0},{5,1},{6,2},{7,3},{8,12},{9,13},{10,14},{11,15},{20,16},{21,... | collective-permute-start | bytes 1572872 | tf_op jit(solution)/shard_map/ppermute | solution.py:400
  84.8 0.7 copy-start.13
  85.5 0.7 copy-start.15
  90.1 30.6 %copy-start.14 = (s32[2,16,128]{2,1,0:T(8,128)S(1)}, s32[2,16,128]{2,1,0:T(8,128)}, u32[]{:S(2)}) copy-start(s32[2,16,128]{2,1,0:T(8,128)} %get-tuple-element.28.rank_ref) | copy-start | bytes 49156
  90.2 30.6 %copy-start.16 = (f32[2,16,128]{2,1,0:T(8,128)S(1)}, f32[2,16,128]{2,1,0:T(8,128)}, u32[]{:S(2)}) copy-start(f32[2,16,128]{2,1,0:T(8,128)} %get-tuple-element.29.gate_ref) | copy-start | bytes 49156
  90.2 30.6 %copy-start.19 = (bf16[128,2048]{1,0:T(8,128)(2,1)S(1)}, bf16[128,2048]{1,0:T(8,128)(2,1)}, u32[]{:S(2)}) copy-start(bf16[128,2048]{1,0:T(8,128)(2,1)} %refs_0_.1) | copy-start | bytes 1572868
  90.2 50.3 %collective-permute-start = (bf16[8,96,2048]{2,1,0:T(8,128)(2,1)S(1)}, bf16[8,96,2048]{2,1,0:T(8,128)(2,1)S(1)}, u32[]{:S(2)}, u32[]{:S(2)}) collective-permute-start(bf16[8,96,2048]{2,1,0:T(8,128)(2,1)S(1)} %forward_rows.3), channel_id=1, source_target_pairs={{0,1},{1,0},{2,3},{3,2},{4,5},{5,4},{6,7},{7,6},{8,9},{9,8},{10,11... | collective-permute-start | bytes 9437192 | tf_op jit(solution)/shard_map/ppermute | solution.py:405
  97.9 22.8 %collective-permute-start.20 = (bf16[128,2048]{1,0:T(8,128)(2,1)S(1)}, bf16[128,2048]{1,0:T(8,128)(2,1)S(1)}, u32[]{:S(2)}, u32[]{:S(2)}) collective-permute-start(bf16[128,2048]{1,0:T(8,128)(2,1)S(1)} %add_convert_fusion.refs_2_), channel_id=1, source_target_pairs={{0,2},{1,3},{2,0},{3,1},{4,6},{5,7},{6,4},{7,5},{8,10},{9,11},{10,... | collective-permute-start | bytes 1572872 | tf_op jit(solution)/shard_map/ppermute | solution.py:405
  109.2 17.3 %collective-permute-start.15 = (bf16[128,2048]{1,0:T(8,128)(2,1)S(1)}, bf16[128,2048]{1,0:T(8,128)(2,1)S(1)}, u32[]{:S(2)}, u32[]{:S(2)}) collective-permute-start(bf16[128,2048]{1,0:T(8,128)(2,1)S(1)} %add_convert_fusion.2.refs_0_), channel_id=1, source_target_pairs={{0,2},{1,3},{2,0},{3,1},{4,6},{5,7},{6,4},{7,5},{8,10},{9,11},{10,... | collective-permute-start | bytes 1572872 | tf_op jit(solution)/shard_map/ppermute | solution.py:405
  119.0 12.6 %collective-permute-start.17 = (bf16[128,2048]{1,0:T(8,128)(2,1)S(1)}, bf16[128,2048]{1,0:T(8,128)(2,1)S(1)}, u32[]{:S(2)}, u32[]{:S(2)}) collective-permute-start(bf16[128,2048]{1,0:T(8,128)(2,1)S(1)} %add_convert_fusion.1.refs_2_), channel_id=1, source_target_pairs={{0,2},{1,3},{2,0},{3,1},{4,6},{5,7},{6,4},{7,5},{8,10},{9,11},{10,... | collective-permute-start | bytes 1572872 | tf_op jit(solution)/shard_map/ppermute | solution.py:405
  126.3 18.8 %collective-permute-start.22 = (bf16[4,96,2048]{2,1,0:T(8,128)(2,1)}, bf16[4,96,2048]{2,1,0:T(8,128)(2,1)S(1)}, u32[]{:S(2)}, u32[]{:S(2)}) collective-permute-start(bf16[4,96,2048]{2,1,0:T(8,128)(2,1)} %get-tuple-element.43), channel_id=1, source_target_pairs={{0,1},{1,0},{2,3},{3,2},{4,5},{5,4},{6,7},{7,6},{8,9},{9,8},{10,11... | collective-permute-start | bytes 4718600 | tf_op jit(solution)/shard_map/ppermute | solution.py:405
  136.2 8.9 %slice-start = ((s8[6291456]{0:T(1024)(128)(4,1)}), s8[4194304]{0:T(1024)(128)(4,1)S(1)}, s32[]{:S(2)}) async-start(s8[6291456]{0:T(1024)(128)(4,1)} %bitcast.21), calls=%async_computation.3 | async-start | bytes 8388608
  136.2 8.9 %slice-start.1 = ((s8[6291456]{0:T(1024)(128)(4,1)}), s8[2097152]{0:T(1024)(128)(4,1)S(1)}, s32[]{:S(2)}) async-start(s8[6291456]{0:T(1024)(128)(4,1)} %bitcast.21), calls=%async_computation.4 | async-start | bytes 4194304
  136.3 12.1 %collective-permute-start.21 = (bf16[4,96,2048]{2,1,0:T(8,128)(2,1)}, bf16[4,96,2048]{2,1,0:T(8,128)(2,1)S(1)}, u32[]{:S(2)}, u32[]{:S(2)}) collective-permute-start(bf16[4,96,2048]{2,1,0:T(8,128)(2,1)} %get-tuple-element.42), channel_id=1, source_target_pairs={{0,1},{1,0},{2,3},{3,2},{4,5},{5,4},{6,7},{7,6},{8,9},{9,8},{10,11... | collective-permute-start | bytes 4718600 | tf_op jit(solution)/shard_map/ppermute | solution.py:405
  140.4 3.1 %copy-start.5 = (bf16[8,96,2048]{2,1,0:T(8,128)(2,1)}, bf16[8,96,2048]{2,1,0:T(8,128)(2,1)S(1)}, u32[]{:S(2)}) copy-start(bf16[8,96,2048]{2,1,0:T(8,128)(2,1)S(1)} %forward_rows.2.own_ref) | copy-start | bytes 9437188
  140.5 3.0 %copy-start.3 = (bf16[8,96,2048]{2,1,0:T(8,128)(2,1)}, bf16[8,96,2048]{2,1,0:T(8,128)(2,1)S(1)}, u32[]{:S(2)}) copy-start(bf16[8,96,2048]{2,1,0:T(8,128)(2,1)S(1)} %collective-permute-done.other_ref) | copy-start | bytes 9437188
  143.5 4.8 %copy-start.20 = (bf16[128,2048]{1,0:T(8,128)(2,1)}, bf16[128,2048]{1,0:T(8,128)(2,1)S(1)}, u32[]{:S(2)}) copy-start(bf16[128,2048]{1,0:T(8,128)(2,1)S(1)} %get-tuple-element.32) | copy-start | bytes 1572868
  143.5 8.0 %copy-start.22 = (bf16[128,2048]{1,0:T(8,128)(2,1)}, bf16[128,2048]{1,0:T(8,128)(2,1)S(1)}, u32[]{:S(2)}) copy-start(bf16[128,2048]{1,0:T(8,128)(2,1)S(1)} %get-tuple-element.36) | copy-start | bytes 1572868
  143.5 34.6 %collective-permute-start.4 = (bf16[128,2048]{1,0:T(8,128)(2,1)}, bf16[128,2048]{1,0:T(8,128)(2,1)}, u32[]{:S(2)}, u32[]{:S(2)}) collective-permute-start(bf16[128,2048]{1,0:T(8,128)(2,1)} %get-tuple-element.38), channel_id=1, source_target_pairs={{0,2},{1,3},{2,0},{3,1},{4,6},{5,7},{6,4},{7,5},{8,10},{9,11},{10,... | collective-permute-start | bytes 1572872 | tf_op jit(solution)/shard_map/ppermute | solution.py:405
  151.5 2.7 copy-start.1
  154.2 20.5 %copy-start.4 = (bf16[8,96,2048]{2,1,0:T(8,128)(2,1)S(1)}, bf16[8,96,2048]{2,1,0:T(8,128)(2,1)}, u32[]{:S(2)}) copy-start(bf16[8,96,2048]{2,1,0:T(8,128)(2,1)} %copy-done.3) | copy-start | bytes 9437188
  154.2 106.8 %all-to-all-start.2 = ((bf16[16,96,768]{2,1,0:T(8,128)(2,1)}), bf16[16,96,768]{2,1,0:T(8,128)(2,1)}, u32[]{:S(2)}, u32[]{:S(2)}) async-start(bf16[16,96,768]{2,1,0:T(8,128)(2,1)} %get-tuple-element.48), calls=%async_computation.2 | async-start | bytes 4718592 | tf_op jit(solution)/shard_map/all_to_all | solution.py:450
  172.7 33.7 %collective-permute-start.3 = (bf16[128,2048]{1,0:T(8,128)(2,1)}, bf16[128,2048]{1,0:T(8,128)(2,1)S(1)}, u32[]{:S(2)}, u32[]{:S(2)}) collective-permute-start(bf16[128,2048]{1,0:T(8,128)(2,1)} %copy-done.22), channel_id=1, source_target_pairs={{0,2},{1,3},{2,0},{3,1},{4,6},{5,7},{6,4},{7,5},{8,10},{9,11},{10,... | collective-permute-start | bytes 1572872 | tf_op jit(solution)/shard_map/ppermute | solution.py:405
  174.6 1.9 copy-start.6
  178.1 0.8 copy-start.8
  178.1 45.0 %copy-start.10 = (bf16[128,2048]{1,0:T(8,128)(2,1)}, bf16[128,2048]{1,0:T(8,128)(2,1)S(1)}, u32[]{:S(2)}) copy-start(bf16[128,2048]{1,0:T(8,128)(2,1)S(1)} %get-tuple-element.31) | copy-start | bytes 1572868
  178.1 45.0 %copy-start.12 = (bf16[128,2048]{1,0:T(8,128)(2,1)}, bf16[128,2048]{1,0:T(8,128)(2,1)S(1)}, u32[]{:S(2)}) copy-start(bf16[128,2048]{1,0:T(8,128)(2,1)S(1)} %get-tuple-element.33) | copy-start | bytes 1572868
  178.1 52.0 %copy-start.24 = (f32[128,8]{0,1:T(8,128)S(1)}, f32[128,8]{0,1:T(8,128)}, u32[]{:S(2)}) copy-start(f32[128,8]{0,1:T(8,128)} %param.7) | copy-start | bytes 12292
  178.9 51.7 %copy-start.21 = (bf16[128,2048]{1,0:T(8,128)(2,1)S(1)}, bf16[128,2048]{1,0:T(8,128)(2,1)}, u32[]{:S(2)}) copy-start(bf16[128,2048]{1,0:T(8,128)(2,1)} %copy-done.20) | copy-start | bytes 1572868
  180.2 42.9 %collective-permute-start.5 = (bf16[128,2048]{1,0:T(8,128)(2,1)S(1)}, bf16[128,2048]{1,0:T(8,128)(2,1)S(1)}, u32[]{:S(2)}, u32[]{:S(2)}) collective-permute-start(bf16[128,2048]{1,0:T(8,128)(2,1)S(1)} %fusion.1), channel_id=1, source_target_pairs={{0,4},{1,5},{2,6},{3,7},{12,8},{13,9},{14,10},{15,11},{16,20},{17,... | collective-permute-start | bytes 1572872 | tf_op jit(solution)/shard_map/ppermute | solution.py:400
  183.9 49.2 %collective-permute-start.2 = (bf16[128,2048]{1,0:T(8,128)(2,1)}, bf16[128,2048]{1,0:T(8,128)(2,1)}, u32[]{:S(2)}, u32[]{:S(2)}) collective-permute-start(bf16[128,2048]{1,0:T(8,128)(2,1)} %get-tuple-element.34), channel_id=1, source_target_pairs={{0,2},{1,3},{2,0},{3,1},{4,6},{5,7},{6,4},{7,5},{8,10},{9,11},{10,... | collective-permute-start | bytes 1572872 | tf_op jit(solution)/shard_map/ppermute | solution.py:405
  223.1 25.2 %copy-start.9 = (bf16[128,2048]{1,0:T(8,128)(2,1)S(1)}, bf16[128,2048]{1,0:T(8,128)(2,1)}, u32[]{:S(2)}) copy-start(bf16[128,2048]{1,0:T(8,128)(2,1)} %copy-done.8) | copy-start | bytes 1572868
  223.4 15.6 %collective-permute-start.6 = (bf16[128,2048]{1,0:T(8,128)(2,1)S(1)}, bf16[128,2048]{1,0:T(8,128)(2,1)}, u32[]{:S(2)}, u32[]{:S(2)}) collective-permute-start(bf16[128,2048]{1,0:T(8,128)(2,1)S(1)} %add_convert_fusion.6), channel_id=1, source_target_pairs={{0,4},{1,5},{2,6},{3,7},{12,8},{13,9},{14,10},{15,11},{16,20},{17,... | collective-permute-start | bytes 1572872 | tf_op jit(solution)/shard_map/ppermute | solution.py:400
  228.6 19.7 %collective-permute-start.9 = (bf16[128,2048]{1,0:T(8,128)(2,1)S(1)}, bf16[128,2048]{1,0:T(8,128)(2,1)}, u32[]{:S(2)}, u32[]{:S(2)}) collective-permute-start(bf16[128,2048]{1,0:T(8,128)(2,1)S(1)} %add_convert_fusion.6), channel_id=1, source_target_pairs={{4,8},{5,9},{6,10},{7,11},{8,4},{9,5},{10,6},{11,7},{20,24},{21,25... | collective-permute-start | bytes 1572872 | tf_op jit(solution)/shard_map/ppermute | solution.py:400
  230.6 39.0 %collective-permute-start.1 = (bf16[128,2048]{1,0:T(8,128)(2,1)S(1)}, bf16[128,2048]{1,0:T(8,128)(2,1)S(1)}, u32[]{:S(2)}, u32[]{:S(2)}) collective-permute-start(bf16[128,2048]{1,0:T(8,128)(2,1)S(1)} %copy-done.21), channel_id=1, source_target_pairs={{0,2},{1,3},{2,0},{3,1},{4,6},{5,7},{6,4},{7,5},{8,10},{9,11},{10,... | collective-permute-start | bytes 1572872 | tf_op jit(solution)/shard_map/ppermute | solution.py:405
  241.4 28.2 %collective-permute-start.7 = (bf16[128,2048]{1,0:T(8,128)(2,1)}, bf16[128,2048]{1,0:T(8,128)(2,1)}, u32[]{:S(2)}, u32[]{:S(2)}) collective-permute-start(bf16[128,2048]{1,0:T(8,128)(2,1)} %add_convert_fusion.5), channel_id=1, source_target_pairs={{0,4},{1,5},{2,6},{3,7},{12,8},{13,9},{14,10},{15,11},{16,20},{17,... | collective-permute-start | bytes 1572872 | tf_op jit(solution)/shard_map/ppermute | solution.py:400
  246.8 22.9 %collective-permute-start.8 = (bf16[128,2048]{1,0:T(8,128)(2,1)}, bf16[128,2048]{1,0:T(8,128)(2,1)}, u32[]{:S(2)}, u32[]{:S(2)}) collective-permute-start(bf16[128,2048]{1,0:T(8,128)(2,1)} %add_convert_fusion.5), channel_id=1, source_target_pairs={{4,8},{5,9},{6,10},{7,11},{8,4},{9,5},{10,6},{11,7},{20,24},{21,25... | collective-permute-start | bytes 1572872 | tf_op jit(solution)/shard_map/ppermute | solution.py:400
  250.6 19.1 %collective-permute-start.10 = (bf16[128,2048]{1,0:T(8,128)(2,1)}, bf16[128,2048]{1,0:T(8,128)(2,1)}, u32[]{:S(2)}, u32[]{:S(2)}) collective-permute-start(bf16[128,2048]{1,0:T(8,128)(2,1)} %add_convert_fusion.4), channel_id=1, source_target_pairs={{4,0},{5,1},{6,2},{7,3},{8,12},{9,13},{10,14},{11,15},{20,16},{21,... | collective-permute-start | bytes 1572872 | tf_op jit(solution)/shard_map/ppermute | solution.py:400
  261.0 1.4 copy-start.18
  262.4 7.3 %copy-start.11 = (bf16[128,2048]{1,0:T(8,128)(2,1)S(1)}, bf16[128,2048]{1,0:T(8,128)(2,1)}, u32[]{:S(2)}) copy-start(bf16[128,2048]{1,0:T(8,128)(2,1)} %copy-done.10) | copy-start | bytes 1572868

commit v4 on v3

--- a/solution.py
+++ b/solution.py
@@ -207,99 +207,46 @@
     return [places[slot] * 4 + (across ^ turn) * 2 + lane for slot in slots for turn in range(2)]
 
 
-def place_out(pieces, sem):
-    copies = [pltpu.make_async_copy(source, target, sem.at[i]) for i, (source, target) in enumerate(pieces)]
-    for copy in copies:
-        copy.start()
-    return copies
-
-
-def scale_kernel(capacity, slots, held, here_ref, rank_ref, gate_ref, weight_ref, *refs):
-    count = 2 * len(slots)
-    blocks, refs = refs[:count], refs[count + held:]
-    z_ref, back_ref, sibling_ref, z_scratch, back_scratch, z_sem, back_sem = refs
-    sources = lane_sources(here_ref[0], slots, here_ref[0] % 2)
-    for i, source in enumerate(sources):
-        chosen = [chosen_rows(rank_ref, side, source, capacity) for side in range(2)]
-        gates = [gate_column(gate_ref, chosen[side], side, source) for side in range(2)]
-        both = jnp.concatenate([one_hot(chosen[0]), one_hot(chosen[1])], axis=0)
-        rows = jnp.dot(both, blocks[i][...], preferred_element_type=F32)
-        z_scratch[i] = (rows[:capacity] * gates[0]).astype(BF16)
-        sibling_ref[i] = (rows[capacity:] * gates[1]).astype(BF16)
-    copies = place_out([(z_scratch.at[i], z_ref.at[source]) for i, source in enumerate(sources)], z_sem)
-    flat = z_scratch[...].reshape(count * capacity, z_scratch.shape[2])
-    back = lax.dot_general(flat, weight_ref[...], (((1,), (1,)), ((), ())), preferred_element_type=F32)
-    back_scratch[...] = back.astype(BF16).reshape(back_scratch.shape)
-    copies += place_out([(back_scratch.at[i], back_ref.at[source]) for i, source in enumerate(sources)], back_sem)
-    for copy in copies:
-        copy.wait()
-
-
-def scaled_rows(here, rank, gate, weight, blocks, slots, capacity, buffers):
-    devices = rank.shape[1]
-    hidden, width = weight.shape
-    count = len(blocks)
-    tokens = blocks[0].shape[0]
-    vmem, anywhere = pl.BlockSpec(memory_space=pltpu.VMEM), pl.BlockSpec(memory_space=pl.ANY)
-    return pl.pallas_call(
-        functools.partial(scale_kernel, capacity, slots, len(buffers)),
-        in_specs=[pl.BlockSpec(memory_space=pltpu.SMEM)] + [vmem] * (3 + count) + [anywhere] * len(buffers),
-        out_specs=[anywhere, anywhere, vmem],
+def back_kernel(capacity, rank_ref, gate_ref, cot_ref, weight_ref, z_ref, back_ref):
+    each = cot_ref.shape[0]
+    for j in range(each):
+        source = pl.program_id(0) * each + j
+        chosen = chosen_rows(rank_ref, 0, source, capacity)
+        gate = gate_column(gate_ref, chosen, 0, source)
+        rows = jnp.dot(one_hot(chosen), cot_ref[j], preferred_element_type=F32)
+        z_ref[j * capacity:(j + 1) * capacity, :] = (rows * gate).astype(BF16)
+    back = lax.dot_general(z_ref[...], weight_ref[...], (((1,), (1,)), ((), ())), preferred_element_type=F32)
+    back_ref[...] = back.astype(BF16)
+
+
+def backward_rows(rank, gate, cotangents, weight, capacity, each=4):
+    devices, tokens, width = cotangents.shape
+    hidden = weight.shape[0]
+    rows = each * capacity
+    return pl.pallas_call(
+        functools.partial(back_kernel, capacity),
+        grid=(devices // each,),
+        in_specs=[
+            pl.BlockSpec(rank.shape, lambda i: (0, 0, 0)),
+            pl.BlockSpec(rank.shape, lambda i: (0, 0, 0)),
+            pl.BlockSpec((each, tokens, width), lambda i: (i, 0, 0)),
+            pl.BlockSpec((hidden, width), lambda i: (0, 0)),
+        ],
+        out_specs=[
+            pl.BlockSpec((rows, width), lambda i: (i, 0)),
+            pl.BlockSpec((rows, hidden), lambda i: (i, 0)),
+        ],
         out_shape=[
-            jax.ShapeDtypeStruct((devices, capacity, width), BF16),
-            jax.ShapeDtypeStruct((devices, capacity, hidden), BF16),
-            jax.ShapeDtypeStruct((count, capacity, width), BF16),
-        ],
-        scratch_shapes=[
-            pltpu.VMEM((count, capacity, width), BF16),
-            pltpu.VMEM((count, capacity, hidden), BF16),
-            pltpu.SemaphoreType.DMA((count,)),
-            pltpu.SemaphoreType.DMA((count,)),
-        ],
-        input_output_aliases={4 + count + i: i for i in range(len(buffers))},
-        compiler_params=pltpu.CompilerParams(vmem_limit_bytes=40 * MIB),
-        cost_estimate=pl.CostEstimate(
-            flops=2 * count * capacity * width * (hidden + 2 * tokens), transcendentals=0,
-            bytes_accessed=2 * count * (tokens * width + capacity * (2 * width + hidden)) + 2 * width * hidden,
-        ),
-        name="scaled_rows",
-    )(here, rank, gate, weight, *blocks, *buffers)
-
-
-def sibling_kernel(capacity, slots, here_ref, weight_ref, rows_ref, _z, _back, z_ref, back_ref, back_scratch, z_sem, back_sem):
-    count = 2 * len(slots)
-    sources = lane_sources(here_ref[0], slots, 1 - here_ref[0] % 2)
-    copies = place_out([(rows_ref.at[i], z_ref.at[source]) for i, source in enumerate(sources)], z_sem)
-    flat = rows_ref[...].reshape(count * capacity, rows_ref.shape[2])
-    back = lax.dot_general(flat, weight_ref[...], (((1,), (1,)), ((), ())), preferred_element_type=F32)
-    back_scratch[...] = back.astype(BF16).reshape(back_scratch.shape)
-    copies += place_out([(back_scratch.at[i], back_ref.at[source]) for i, source in enumerate(sources)], back_sem)
-    for copy in copies:
-        copy.wait()
-
-
-def sibling_rows(here, weight, rows, slots, z_rows, back):
-    count, capacity, width = rows.shape
-    hidden = weight.shape[0]
-    vmem, anywhere = pl.BlockSpec(memory_space=pltpu.VMEM), pl.BlockSpec(memory_space=pl.ANY)
-    return pl.pallas_call(
-        functools.partial(sibling_kernel, capacity, slots),
-        in_specs=[pl.BlockSpec(memory_space=pltpu.SMEM), vmem, vmem, anywhere, anywhere],
-        out_specs=[anywhere, anywhere],
-        out_shape=[jax.ShapeDtypeStruct(z_rows.shape, BF16), jax.ShapeDtypeStruct(back.shape, BF16)],
-        scratch_shapes=[
-            pltpu.VMEM((count, capacity, hidden), BF16),
-            pltpu.SemaphoreType.DMA((count,)),
-            pltpu.SemaphoreType.DMA((count,)),
-        ],
-        input_output_aliases={3: 0, 4: 1},
-        compiler_params=pltpu.CompilerParams(vmem_limit_bytes=40 * MIB),
-        cost_estimate=pl.CostEstimate(
-            flops=2 * count * capacity * width * hidden, transcendentals=0,
-            bytes_accessed=2 * count * capacity * (2 * width + hidden) + 2 * width * hidden,
-        ),
-        name="sibling_rows",
-    )(here, weight, rows, z_rows, back)
+            jax.ShapeDtypeStruct((devices * capacity, width), BF16),
+            jax.ShapeDtypeStruct((devices * capacity, hidden), BF16),
+        ],
+        compiler_params=pltpu.CompilerParams(vmem_limit_bytes=48 * MIB),
+        cost_estimate=pl.CostEstimate(
+            flops=2 * devices * capacity * width * (hidden + tokens), transcendentals=0,
+            bytes_accessed=2 * devices * (tokens * width + capacity * (width + hidden)) + 2 * width * hidden,
+        ),
+        name="backward_rows",
+    )(rank, gate, cotangents, weight)
 
 
 def forward_kernel(capacity, turn, here_ref, rank_ref, gate_ref, h_ref, weight_ref, out_ref):
@@ -405,7 +352,8 @@
     return lax.ppermute(value, "expert", [(i, i ^ bit) for i in range(devices)])
 
 
-OUTER, INNER, ENDS = ((0, 1), (3, 2)), ((1, 2), (2, 1)), ((1, 0), (2, 3))
+OUTER, INNER = ((0, 1), (3, 2)), ((1, 2), (2, 1))
+ENDS, ENDS_SWAP = ((1, 0), (2, 3)), ((0, 3), (3, 0))
 
 
 def dense_shards(h_rows, gates, expert_ids, cotangent, down_weight, swapped):
@@ -422,31 +370,360 @@
     routing = lax.all_to_all(routing, "expert", split_axis=0, concat_axis=0, tiled=True)
     rank, gate = route(here, routing, top)
 
-    own = cotangent
-    from_end = passed(OUTER, own)
-    from_inner = passed(INNER, own)
-    near = added(from_inner, passed(ENDS, own))
-    own_y = swapped_with(own, 2)
-    from_far = passed(INNER, from_end)
-    middle = added(from_far, passed(ENDS, from_inner))
-    near_y = swapped_with(near, 2)
-    last = added(from_end, passed(ENDS, from_far))
-    middle_y = swapped_with(middle, 2)
-    last_y = swapped_with(last, 2)
-
+    cotangents = lax.all_gather(cotangent, "expert", axis=0, tiled=False)
     place, send_h = pack(slot_ids.reshape(1, -1), h_flat, devices, capacity)
     rows_h = lax.all_to_all(
         send_h.reshape(devices, capacity, hidden), "expert", split_axis=0, concat_axis=0, tiled=True
     )
 
-    z_rows, back, sibling = scaled_rows(here, rank, gate, weight, [own, own_y, near, near_y], (0, 1), capacity, [])
-    sibling = swapped_with(sibling, 1)
-    z_rows, back, sibling_last = scaled_rows(
-        here, rank, gate, weight, [middle, middle_y, last, last_y], (2, 3), capacity, [z_rows, back]
+    z_rows, back = backward_rows(rank, gate, cotangents, weight, capacity)
+    back = back.reshape(devices, capacity, hidden)
+    back_rows = lax.all_to_all(back, "expert", split_axis=0, concat_axis=0, tiled=True).reshape(-1, hidden)
+
+    other = swapped_with(forward_rows(here, rank, gate, rows_h, weight, 1), 1)
+    mine = forward_rows(here, rank, gate, rows_h, weight, 0)
+    across = [swapped_with(part, 2) for part in summed(here, rank, mine, other, 1)]
+    beside = summed(here, rank, mine, other, 0)
+    far, mid, close, kept = zip(beside, across)
+    far, mid, close = added(*far), added(*mid), added(*close)
+    ends = passed(ENDS_SWAP, far)
+    mid_outer, mid_inner = passed(OUTER, mid), passed(INNER, mid)
+    close_outer = passed(OUTER, close)
+    close_inner = passed(INNER, added(close, mid_outer))
+    far_ends = passed(ENDS, added(far, mid_inner))
+    mixed = added(*kept, ends, close_outer, close_inner, far_ends)
+
+    grad_sum = lax.dot_general(flat_h, flat_z, (((0,), (0,)), ((), ())), preferred_element_type=F32)
+    back = lax.dot_general(flat_z, weight, (((1,), (1,)), ((), ())), preferred_element_type=F32).astype(BF16)
+    back_rows = lax.all_to_all(
+        back.reshape(devices, capacity, hidden), "expert", split_axis=0, concat_axis=0, tiled=True
     )
-    sibling_last = swapped_with(sibling_last, 1)
-    z_rows, back = sibling_rows(here, weight, sibling, (0, 1), z_rows, back)
-    z_rows, back = sibling_rows(here, weight, sibling_last, (2, 3), z_rows, back)
+    h_grad = back_rows[flat_ids, ranks].reshape(tokens_here, top_count, hidden)
+    return (mixed, gate_grad, h_grad, grad_sum.astype(BF16)[None])
+
+
+def upper(size):
+    rows = lax.broadcasted_iota(jnp.int32, (size, size), 0)
+    columns = lax.broadcasted_iota(jnp.int32, (size, size), 1)
+    return (rows < columns).astype(F32).astype(BF16)
+
+
+def pack_kernel(devices, capacity, ids_ref, h_ref, place_ref, sent_ref, place_scratch):
+    pairs = ids_ref.shape[1]
+    rows = sent_ref.shape[0]
+
+    @pl.when(pl.program_id(0) == 0)
+    def _():
+        before = jnp.zeros((devices, 1), F32)
+        for tile in range(pairs // 128):
+            ids = ids_ref[:, tile * 128:(tile + 1) * 128]
+            named = lax.broadcasted_iota(jnp.int32, (devices, 128), 0) == ids
+            ones = jnp.where(named, 1.0, 0.0)
+            rank = jnp.dot(ones.astype(BF16), upper(128), preferred_element_type=F32) + before
+            before = before + jnp.sum(ones, axis=1, keepdims=True)
+            rank = jnp.sum(jnp.where(named, rank, 0.0), axis=0, keepdims=True)
+            place_scratch[:, tile * 128:(tile + 1) * 128] = ids * capacity + rank.astype(jnp.int32)
+        place_ref[...] = place_scratch[...]
+
+    first = pl.program_id(0) * rows
+    wanted = lax.broadcasted_iota(jnp.int32, (rows, pairs), 0) + first
+    chosen = jnp.where(wanted == place_scratch[...], 1.0, 0.0).astype(BF16)
+    sent_ref[...] = jnp.dot(chosen, h_ref[...], preferred_element_type=F32).astype(BF16)
+
+
+def pack(ids, h_flat, devices, capacity, steps=4):
+    pairs, hidden = h_flat.shape
+    rows = devices * capacity // steps
+    return pl.pallas_call(
+        functools.partial(pack_kernel, devices, capacity),
+        grid=(steps,),
+        in_specs=[
+            pl.BlockSpec((1, pairs), lambda i: (0, 0)),
+            pl.BlockSpec((pairs, hidden), lambda i: (0, 0)),
+        ],
+        out_specs=[
+            pl.BlockSpec((1, pairs), lambda i: (0, 0)),
+            pl.BlockSpec((rows, hidden), lambda i: (i, 0)),
+        ],
+        out_shape=[
+            jax.ShapeDtypeStruct((1, pairs), jnp.int32),
+            jax.ShapeDtypeStruct((devices * capacity, hidden), BF16),
+        ],
+        scratch_shapes=[pltpu.VMEM((1, pairs), jnp.int32)],
+        compiler_params=pltpu.CompilerParams(vmem_limit_bytes=48 * MIB),
+        cost_estimate=pl.CostEstimate(
+            flops=2 * devices * capacity * pairs * hidden, transcendentals=0,
+            bytes_accessed=2 * hidden * (pairs + devices * capacity),
+        ),
+        name="pack",
+    )(ids, h_flat)
+
+
+def unpack_kernel(slots, place_ref, gate_ref, h_ref, back_ref, grad_ref, gate_grad_ref):
+    rows = place_ref.shape[0]
+    chosen = lax.broadcasted_iota(jnp.int32, (rows, slots), 1) == place_ref[...]
+    grad = jnp.dot(jnp.where(chosen, 1.0, 0.0).astype(BF16), back_ref[...], preferred_element_type=F32)
+    grad_ref[...] = grad.astype(BF16)
+    gate_grad_ref[...] = jnp.sum(grad * h_ref[...].astype(F32), axis=1, keepdims=True) / gate_ref[...]
+
+
+def unpack(place, gates, h_flat, back_rows, steps=4):
+    pairs, hidden = h_flat.shape
+    slots = back_rows.shape[0]
+    rows = pairs // steps
+    return pl.pallas_call(
+        functools.partial(unpack_kernel, slots),
+        grid=(steps,),
+        in_specs=[
+            pl.BlockSpec((rows, 1), lambda i: (i, 0)),
+            pl.BlockSpec((rows, 1), lambda i: (i, 0)),
+            pl.BlockSpec((rows, hidden), lambda i: (i, 0)),
+            pl.BlockSpec((slots, hidden), lambda i: (0, 0)),
+        ],
+        out_specs=[
+            pl.BlockSpec((rows, hidden), lambda i: (i, 0)),
+            pl.BlockSpec((rows, 1), lambda i: (i, 0)),
+        ],
+        out_shape=[
+            jax.ShapeDtypeStruct((pairs, hidden), BF16),
+            jax.ShapeDtypeStruct((pairs, 1), F32),
+        ],
+        compiler_params=pltpu.CompilerParams(vmem_limit_bytes=48 * MIB),
+        cost_estimate=pl.CostEstimate(
+            flops=2 * slots * pairs * hidden, transcendentals=0,
+            bytes_accessed=2 * hidden * (2 * pairs + slots),
+        ),
+        name="unpack",
+    )(place, gates, h_flat, back_rows)
+
+
+def line_slots(position):
+    near = jnp.minimum(position, 3 - position)
+    turned = (near, near + 1, near + 2, 3 - 3 * near)
+    return [jnp.where(position < 2, slot, 3 - slot) for slot in turned]
+
+
+def route_kernel(devices, top, here_ref, routing_ref, rank_ref, gate_ref):
+    for side in range(2):
+        mine = (here_ref[0] ^ side).astype(F32)
+        marks, picked = [], []
+        for source in range(devices):
+            ids = routing_ref[source, :top, :]
+            gates = routing_ref[source, top:, :]
+            named = ids == mine
+            marks.append(jnp.sum(jnp.where(named, 1.0, 0.0), axis=0, keepdims=True))
+            picked.append(jnp.sum(jnp.where(named, gates, 0.0), axis=0, keepdims=True))
+        mark = jnp.concatenate(marks, axis=0)
+        rank = jnp.dot(mark.astype(BF16), upper(mark.shape[1]), preferred_element_type=F32)
+        rank_ref[side] = jnp.where(mark > 0, rank, -1.0).astype(jnp.int32)
+        gate_ref[side] = jnp.concatenate(picked, axis=0)
+
+
+def route(here, routing, top):
+    devices, _, tokens = routing.shape
+    return pl.pallas_call(
+        functools.partial(route_kernel, devices, top),
+        in_specs=[pl.BlockSpec(memory_space=pltpu.SMEM), pl.BlockSpec(memory_space=pltpu.VMEM)],
+        out_specs=[pl.BlockSpec(memory_space=pltpu.VMEM)] * 2,
+        out_shape=[
+            jax.ShapeDtypeStruct((2, devices, tokens), jnp.int32),
+            jax.ShapeDtypeStruct((2, devices, tokens), F32),
+        ],
+        cost_estimate=pl.CostEstimate(flops=1 << 21, transcendentals=0, bytes_accessed=1 << 19),
+        name="route",
+    )(here, routing)
+
+
+def chosen_rows(rank_ref, side, source, capacity):
+    rank = rank_ref[side, pl.ds(source, 1), :]
+    return lax.broadcasted_iota(jnp.int32, (capacity, rank.shape[1]), 0) == rank
+
+
+def gate_column(gate_ref, chosen, side, source):
+    return jnp.sum(jnp.where(chosen, gate_ref[side, pl.ds(source, 1), :], 0.0), axis=1, keepdims=True)
+
+
+def one_hot(chosen):
+    return jnp.where(chosen, 1.0, 0.0).astype(BF16)
+
+
+def lane_sources(here, slots, lane):
+    line, across = here // 4, (here // 2) % 2
+    places = line_slots(line)
+    return [places[slot] * 4 + (across ^ turn) * 2 + lane for slot in slots for turn in range(2)]
+
+
+def back_kernel(capacity, rank_ref, gate_ref, cot_ref, weight_ref, z_ref, back_ref):
+    each = cot_ref.shape[0]
+    for j in range(each):
+        source = pl.program_id(0) * each + j
+        chosen = chosen_rows(rank_ref, 0, source, capacity)
+        gate = gate_column(gate_ref, chosen, 0, source)
+        rows = jnp.dot(one_hot(chosen), cot_ref[j], preferred_element_type=F32)
+        z_ref[j * capacity:(j + 1) * capacity, :] = (rows * gate).astype(BF16)
+    back = lax.dot_general(z_ref[...], weight_ref[...], (((1,), (1,)), ((), ())), preferred_element_type=F32)
+    back_ref[...] = back.astype(BF16)
+
+
+def backward_rows(rank, gate, cotangents, weight, capacity, each=4):
+    devices, tokens, width = cotangents.shape
+    hidden = weight.shape[0]
+    rows = each * capacity
+    return pl.pallas_call(
+        functools.partial(back_kernel, capacity),
+        grid=(devices // each,),
+        in_specs=[
+            pl.BlockSpec(rank.shape, lambda i: (0, 0, 0)),
+            pl.BlockSpec(rank.shape, lambda i: (0, 0, 0)),
+            pl.BlockSpec((each, tokens, width), lambda i: (i, 0, 0)),
+            pl.BlockSpec((hidden, width), lambda i: (0, 0)),
+        ],
+        out_specs=[
+            pl.BlockSpec((rows, width), lambda i: (i, 0)),
+            pl.BlockSpec((rows, hidden), lambda i: (i, 0)),
+        ],
+        out_shape=[
+            jax.ShapeDtypeStruct((devices * capacity, width), BF16),
+            jax.ShapeDtypeStruct((devices * capacity, hidden), BF16),
+        ],
+        compiler_params=pltpu.CompilerParams(vmem_limit_bytes=48 * MIB),
+        cost_estimate=pl.CostEstimate(
+            flops=2 * devices * capacity * width * (hidden + tokens), transcendentals=0,
+            bytes_accessed=2 * devices * (tokens * width + capacity * (width + hidden)) + 2 * width * hidden,
+        ),
+        name="backward_rows",
+    )(rank, gate, cotangents, weight)
+
+
+def forward_kernel(capacity, turn, here_ref, rank_ref, gate_ref, h_ref, weight_ref, out_ref):
+    each = out_ref.shape[0]
+    lane = (here_ref[0] % 2) ^ turn
+    flat = h_ref[...].reshape(each * capacity, h_ref.shape[3])
+    out = jnp.dot(flat, weight_ref[...], preferred_element_type=F32).astype(BF16).astype(F32)
+    for j in range(each):
+        source = (pl.program_id(0) * each + j) * 2 + lane
+        gate = gate_column(gate_ref, chosen_rows(rank_ref, 0, source, capacity), 0, source)
+        out_ref[j] = (out[j * capacity:(j + 1) * capacity, :] * gate).astype(BF16)
+
+
+def forward_rows(here, rank, gate, rows_h, weight, turn, each=4):
+    devices, capacity, hidden = rows_h.shape
+    width = weight.shape[1]
+    whole = pl.BlockSpec(rank.shape, lambda i, here: (0, 0, 0))
+    return pl.pallas_call(
+        functools.partial(forward_kernel, capacity, turn),
+        grid_spec=pltpu.PrefetchScalarGridSpec(
+            num_scalar_prefetch=1,
+            grid=(devices // 2 // each,),
+            in_specs=[
+                whole,
+                whole,
+                pl.BlockSpec((each, 1, capacity, hidden), lambda i, here: (i, (here[0] % 2) ^ turn, 0, 0)),
+                pl.BlockSpec((hidden, width), lambda i, here: (0, 0)),
+            ],
+            out_specs=pl.BlockSpec((each, capacity, width), lambda i, here: (i, 0, 0)),
+        ),
+        out_shape=jax.ShapeDtypeStruct((devices // 2, capacity, width), BF16),
+        compiler_params=pltpu.CompilerParams(vmem_limit_bytes=40 * MIB),
+        cost_estimate=pl.CostEstimate(
+            flops=devices * capacity * width * hidden, transcendentals=0,
+            bytes_accessed=devices * capacity * (width + hidden) + 2 * width * hidden,
+        ),
+        name="forward_rows",
+    )(here, rank, gate, rows_h.reshape(devices // 2, 2, capacity, hidden), weight)
+
+
+ORDER = (3, 2, 1, 0)
+
+
+def sum_kernel(capacity, turn, here_ref, rank_ref, own_ref, other_ref, *part_refs):
+    for step, slot in enumerate(ORDER):
+
+        @pl.when(pl.program_id(0) == step)
+        def _():
+            source = lane_sources(here_ref[0], (slot,), here_ref[0] % 2)[turn]
+            both = [one_hot(chosen_rows(rank_ref, side, source, capacity)) for side in range(2)]
+            rows = jnp.concatenate([own_ref[0], other_ref[0]], axis=0)
+            part = lax.dot_general(
+                jnp.concatenate(both, axis=0), rows, (((0,), (0,)), ((), ())), preferred_element_type=F32
+            )
+            part_refs[step][...] = part.astype(BF16)
+
+
+def summed(here, rank, own, other, turn):
+    _, capacity, width = own.shape
+    tokens = rank.shape[2]
+
+    def block(i, here):
+        place = jnp.int32(0)
+        for step, slot in enumerate(ORDER):
+            place = jnp.where(i == step, lane_sources(here[0], (slot,), 0)[turn] // 2, place)
+        return (place, 0, 0)
+
+    return pl.pallas_call(
+        functools.partial(sum_kernel, capacity, turn),
+        grid_spec=pltpu.PrefetchScalarGridSpec(
+            num_scalar_prefetch=1,
+            grid=(len(ORDER),),
+            in_specs=[
+                pl.BlockSpec(rank.shape, lambda i, here: (0, 0, 0)),
+                pl.BlockSpec((1, capacity, width), block),
+                pl.BlockSpec((1, capacity, width), block),
+            ],
+            out_specs=[pl.BlockSpec((tokens, width), lambda i, here: (0, 0))] * len(ORDER),
+        ),
+        out_shape=[jax.ShapeDtypeStruct((tokens, width), BF16)] * len(ORDER),
+        compiler_params=pltpu.CompilerParams(vmem_limit_bytes=40 * MIB),
+        cost_estimate=pl.CostEstimate(
+            flops=16 * tokens * capacity * width, transcendentals=0,
+            bytes_accessed=8 * width * (tokens + 2 * capacity),
+        ),
+        name="summed",
+    )(here, rank, own, other)
+
+
+def added(*values):
+    total = values[0].astype(F32)
+    for value in values[1:]:
+        total = total + value.astype(F32)
+    return total.astype(BF16)
+
+
+def passed(pairs, value):
+    return lax.ppermute(value, "expert", [(a * 4 + lane, b * 4 + lane) for a, b in pairs for lane in range(4)])
+
+
+def swapped_with(value, bit):
+    devices = lax.axis_size("expert")
+    return lax.ppermute(value, "expert", [(i, i ^ bit) for i in range(devices)])
+
+
+OUTER, INNER = ((0, 1), (3, 2)), ((1, 2), (2, 1))
+ENDS, ENDS_SWAP = ((1, 0), (2, 3)), ((0, 3), (3, 0))
+
+
+def dense_shards(h_rows, gates, expert_ids, cotangent, down_weight, swapped):
+    devices = lax.axis_size("expert")
+    here = lax.axis_index("expert").reshape(1)
+    tokens, top, hidden = h_rows.shape
+    capacity = min(tokens, 3 * tokens * top // (2 * devices))
+    weight = down_weight[0]
+    slot_ids = slots_of(expert_ids, swapped, devices)
+    h_flat = h_rows.reshape(-1, hidden)
+
+    routing = jnp.concatenate([slot_ids.T.astype(F32), gates.T], axis=0)
+    routing = jnp.broadcast_to(routing, (devices,) + routing.shape)
+    routing = lax.all_to_all(routing, "expert", split_axis=0, concat_axis=0, tiled=True)
+    rank, gate = route(here, routing, top)
+
+    cotangents = lax.all_gather(cotangent, "expert", axis=0, tiled=False)
+    place, send_h = pack(slot_ids.reshape(1, -1), h_flat, devices, capacity)
+    rows_h = lax.all_to_all(
+        send_h.reshape(devices, capacity, hidden), "expert", split_axis=0, concat_axis=0, tiled=True
+    )
+
+    z_rows, back = backward_rows(rank, gate, cotangents, weight, capacity)
+    back = back.reshape(devices, capacity, hidden)
     back_rows = lax.all_to_all(back, "expert", split_axis=0, concat_axis=0, tiled=True).reshape(-1, hidden)
 
     other = swapped_with(forward_rows(here, rank, gate, rows_h, weight, 1), 1)
@@ -463,7 +740,7 @@
     mixed = added(*kept, outer3, inner3, ends3)
 
     grad_sum = lax.dot_general(
-        rows_h.reshape(-1, hidden), z_rows.reshape(devices * capacity, -1), (((0,), (0,)), ((), ())),
+        rows_h.reshape(-1, hidden), z_rows, (((0,), (0,)), ((), ())),
         preferred_element_type=F32,
     )
     h_grad, gate_grad = unpack(place.reshape(-1, 1), gates.reshape(-1, 1), h_flat, back_rows)

time: 275 us -> 293 us (1.065)
  waiting for transfers between devices: 116 us -> 131 us
  between operations: 1.17 us -> 14.3 us
  Pallas kernels: 40.5 us -> 30.4 us
  other arithmetic: 14.5 us -> 10.2 us
  starting transfers between devices: 75.7 us -> 79.9 us
    all_to_all x1, waiting for transfers between devices: 0.01 us -> 71.5 us  [dense_shards(): lax.all_to_all(send_h.reshape(devices, capacity, hidden), 'expert', split...]
    ppermute x12 -> x6, waiting for transfers between devices: 88.4 us -> 25.4 us  [passed(): lax.ppermute(value, 'expert', [(a * 4 + lane, b * 4 + lane) for a, b in p...]
    ppermute x12 -> x6, starting transfers between devices: 30.1 us -> 50.4 us  [passed(): lax.ppermute(value, 'expert', [(a * 4 + lane, b * 4 + lane) for a, b in p...]
    all_to_all x1, starting transfers between devices: 18.5 us -> 4.44 us  [dense_shards(): lax.all_to_all(back, 'expert', split_axis=0, concat_axis=0, tiled=True)]
    pallas_call x4 -> x1, Pallas kernels: 16.5 us -> 9.12 us  [backward_rows(): pl.pallas_call(functools.partial(back_kernel, capacity), grid=(devices //...]
    ppermute x11 -> x5, waiting for transfers between devices: 26.3 us -> 32.4 us  [swapped_with(): return lax.ppermute(value, 'expert', [(i, i ^ bit) for i in range(devices)])]
    convert_element_type x8 -> x5, other arithmetic: 12.8 us -> 8.55 us  [added(): return total.astype(BF16)]
    ppermute x11 -> x5, starting transfers between devices: 15 us -> 13 us  [swapped_with(): return lax.ppermute(value, 'expert', [(i, i ^ bit) for i in range(devices)])]
  transfers between devices with their start and end apart: 26 -> 15, of which waited for: 9 -> 8; matrix products, arithmetic and copies ran while one was open for 8% -> 7% of each run, Pallas kernels for 15% -> 8%
where the time goes in v4:
time: 293 us; the launch traced here: 292 us
  waiting for transfers between devices  131 us (45%)
  starting transfers between devices  79.9 us (27%)
  Pallas kernels  30.4 us (10%)
  local copies, waits for them, and re-layouts  16.8 us (6%)
  between operations  14.3 us (5%)
  other arithmetic  10.2 us (3%)
  matrix products  9.3 us (3%)
    all_to_all x1, waiting for transfers between devices, dense_shards(): lax.all_to_all(send_h.reshape(devices, capacity, hidden), 'expert', split...  71.5 us
    ppermute x6, starting transfers between devices, passed(): lax.ppermute(value, 'expert', [(a * 4 + lane, b * 4 + lane) for a, b in p...  50.4 us
    ppermute x5, waiting for transfers between devices, swapped_with(): return lax.ppermute(value, 'expert', [(i, i ^ bit) for i in range(devices)])  32.4 us
    ppermute x6, waiting for transfers between devices, passed(): lax.ppermute(value, 'expert', [(a * 4 + lane, b * 4 + lane) for a, b in p...  25.4 us
    unnamed x40, local copies, waits for them, and re-layouts  14.8 us
    ppermute x5, starting transfers between devices, swapped_with(): return lax.ppermute(value, 'expert', [(i, i ^ bit) for i in range(devices)])  13 us
    dot_general x1, matrix products, dense_shards(): lax.dot_general(rows_h.reshape(-1, hidden), z_rows, (((0,), (0,)), ((), (...  9.3 us
    pallas_call x1, Pallas kernels, backward_rows(): pl.pallas_call(functools.partial(back_kernel, capacity), grid=(devices //...  9.12 us
  transfers between devices with their start and end apart: 15, of which 8 were waited for; matrix products, arithmetic and copies ran while one was open for 7% of the time, Pallas kernels for 8%

profile of v4, /device:TPU:0, one launch (start us, length us, event | category | flops | bytes accessed | tf_op | source)
XLA Modules:
  0.0 292.4 jit_solution(16601895723149973308)
XLA Ops:
  7.2 0.0 copy-start
  7.2 0.0 all-gather.3.cloned.1.call-start
  7.2 0.7 all-gather.3.cloned.1.call-update
  8.0 0.7 gather_fusion
  8.6 0.8 select_reduce_fusion
  9.4 0.7 pad_maximum_fusion
  10.1 0.7 broadcast_in_dim.19
  10.8 7.4 %all-to-all-start = ((f32[16,16,128]{2,1,0:T(8,128)}), f32[16,16,128]{2,1,0:T(8,128)S(1)}, u32[]{:S(2)}, u32[]{:S(2)}) async-start(f32[16,16,128]{2,1,0:T(8,128)} %broadcast_in_dim.19), calls=%async_computation | async-start | bytes 262144 | tf_op jit(solution)/shard_map/all_to_all | solution.py:716
  18.2 0.1 copy.20
  18.3 0.1 reshape.78.ids_ref
  18.4 1.4 copy-done.10
  19.8 3.4 %pack.1 = (s32[1,1024]{1,0:T(1,128)S(1)}, bf16[1536,768]{1,0:T(8,128)(2,1)S(1)}) custom-call(s32[1,1024]{1,0:T(1,128)S(1)} %reshape.78.ids_ref, bf16[1024,768]{1,0:T(8,128)(2,1)S(1)} %bitcast.29), custom_call_target="tpu_custom_call" | custom-call | flops 2415919104 | bytes 3932160 | tf_op jit(solution)/shard_map/pack/pallas_call | solution.py:437
  23.2 1.4 copy-done.2
  24.6 1.5 all-to-all-done.routing_ref
  26.1 4.5 %all-to-all-start.1 = ((bf16[16,96,768]{2,1,0:T(8,128)(2,1)}), bf16[16,96,768]{2,1,0:T(8,128)(2,1)S(1)}, u32[]{:S(2)}, u32[]{:S(2)}) async-start(bf16[16,96,768]{2,1,0:T(8,128)(2,1)} %bitcast.24), calls=%async_computation.1 | async-start | bytes 4718592 | tf_op jit(solution)/shard_map/all_to_all | solution.py:721
  30.7 1.7 route.1
  32.4 71.5 %all-to-all-done.1 = bf16[16,96,768]{2,1,0:T(8,128)(2,1)S(1)} async-done(((bf16[16,96,768]{2,1,0:T(8,128)(2,1)}), bf16[16,96,768]{2,1,0:T(8,128)(2,1)S(1)}, u32[]{:S(2)}, u32[]{:S(2)}) %all-to-all-start.1) | async-done | bytes 2359328 | tf_op jit(solution)/shard_map/all_to_all | solution.py:721
  103.9 0.7 copy-done.5
  104.6 1.9 copy-done.7
  106.5 0.7 copy-done.14
  107.2 3.0 %forward_rows.3 = bf16[8,96,2048]{2,1,0:T(8,128)(2,1)S(1)} custom-call(s32[1]{0:T(128)} %bitcast.here_ref, s32[2,16,128]{2,1,0:T(8,128)S(1)} %copy-done.5, f32[2,16,128]{2,1,0:T(8,128)S(1)} %copy-done.14, bf16[8,2,96,768]{3,2,1,0:T(8,128)(2,1)S(1)} %bitcast.20, bf16[768,2048]{1,0:T(8,128)(2,1)S(1)} %bitcast.26), custom_call_target="tpu_custom_call" | custom-call | flops 2415919104 | bytes 7471104 | tf_op jit(solution)/shard_map/forward_rows/pallas_call | solution.py:613
  110.2 0.2 collective-permute-start
  110.4 3.0 %forward_rows.2.own_ref = bf16[8,96,2048]{2,1,0:T(8,128)(2,1)S(1)} custom-call(s32[1]{0:T(128)} %bitcast.here_ref, s32[2,16,128]{2,1,0:T(8,128)S(1)} %copy-done.6, f32[2,16,128]{2,1,0:T(8,128)S(1)} %copy-done.14, bf16[8,2,96,768]{3,2,1,0:T(8,128)(2,1)S(1)} %bitcast.21, bf16[768,2048]{1,0:T(8,128)(2,1)S(1)} %bitcast.27), custom_call_target="tpu_custom_call" | custom-call | flops 2415919104 | bytes 7471104 | tf_op jit(solution)/shard_map/forward_rows/pallas_call | solution.py:613
  113.4 2.5 collective-permute-done.other_ref
  115.9 2.4 summed.3
  118.3 0.8 copy-done.13
  119.1 10.2 %collective-permute-start.4 = (bf16[128,2048]{1,0:T(8,128)(2,1)S(1)}, bf16[128,2048]{1,0:T(8,128)(2,1)S(1)}, u32[]{:S(2)}, u32[]{:S(2)}) collective-permute-start(bf16[128,2048]{1,0:T(8,128)(2,1)S(1)} %get-tuple-element.30), channel_id=1, source_target_pairs={{0,2},{1,3},{2,0},{3,1},{4,6},{5,7},{6,4},{7,5},{8,10},{9,11},{10,... | collective-permute-start | bytes 1572872 | tf_op jit(solution)/shard_map/ppermute | solution.py:698
  129.2 0.0 collective-permute-start.3
  129.3 1.6 summed.2
  130.8 0.8 copy-done.3
  131.6 0.8 copy-done.4
  132.4 9.6 %collective-permute-done.4 = bf16[128,2048]{1,0:T(8,128)(2,1)S(1)} collective-permute-done((bf16[128,2048]{1,0:T(8,128)(2,1)S(1)}, bf16[128,2048]{1,0:T(8,128)(2,1)S(1)}, u32[]{:S(2)}, u32[]{:S(2)}) %collective-permute-start.4) | collective-permute-done | bytes 524320 | tf_op jit(solution)/shard_map/ppermute | solution.py:698
  142.0 0.8 copy-done.16
  142.8 0.9 fusion.1
  143.7 17.1 %collective-permute-start.5 = (bf16[128,2048]{1,0:T(8,128)(2,1)}, bf16[128,2048]{1,0:T(8,128)(2,1)}, u32[]{:S(2)}, u32[]{:S(2)}) collective-permute-start(bf16[128,2048]{1,0:T(8,128)(2,1)} %fusion.1), channel_id=1, source_target_pairs={{0,4},{1,5},{2,6},{3,7},{12,8},{13,9},{14,10},{15,11},{16,20},{17,... | collective-permute-start | bytes 1572872 | tf_op jit(solution)/shard_map/ppermute | solution.py:693
  160.8 1.9 copy-done.9
  162.7 9.1 %backward_rows.1 = (bf16[1536,2048]{1,0:T(8,128)(2,1)}, bf16[1536,768]{1,0:T(8,128)(2,1)S(1)}) custom-call(s32[2,16,128]{2,1,0:T(8,128)S(1)} %copy-done.6, f32[2,16,128]{2,1,0:T(8,128)S(1)} %copy-done.15, bf16[16,128,2048]{2,1,0:T(8,128)(2,1)} %bitcast.32, bf16[768,2048]{1,0:T(8,128)(2,1)S(1)} %bitcast.28), custom_call_target="tpu_custom_call" | custom-call | flops 5637144576 | bytes 20185088 | tf_op jit(solution)/shard_map/backward_rows/pallas_call | solution.py:572
  171.8 1.4 copy-done.1
  173.2 4.4 %all-to-all-start.2 = ((bf16[16,96,768]{2,1,0:T(8,128)(2,1)}), bf16[16,96,768]{2,1,0:T(8,128)(2,1)}, u32[]{:S(2)}, u32[]{:S(2)}) async-start(bf16[16,96,768]{2,1,0:T(8,128)(2,1)} %bitcast.23), calls=%async_computation.2 | async-start | bytes 4718592 | tf_op jit(solution)/shard_map/all_to_all | solution.py:727
  177.7 0.0 copy-start.18
  177.7 1.6 add_convert_fusion.3
  179.3 0.7 collective-permute-start.9
  180.0 2.0 collective-permute-start.2
  182.1 5.9 %collective-permute-start.6 = (bf16[128,2048]{1,0:T(8,128)(2,1)S(1)}, bf16[128,2048]{1,0:T(8,128)(2,1)S(1)}, u32[]{:S(2)}, u32[]{:S(2)}) collective-permute-start(bf16[128,2048]{1,0:T(8,128)(2,1)S(1)} %add_convert_fusion.3), channel_id=1, source_target_pairs={{0,4},{1,5},{2,6},{3,7},{12,8},{13,9},{14,10},{15,11},{16,20},{17,... | collective-permute-start | bytes 1572872 | tf_op jit(solution)/shard_map/ppermute | solution.py:693
  188.0 0.6 collective-permute-start.1
  188.6 2.1 add_convert_fusion.1
  190.7 1.3 collective-permute-start.10
  192.0 20.3 %collective-permute-done.2 = bf16[128,2048]{1,0:T(8,128)(2,1)S(1)} collective-permute-done((bf16[128,2048]{1,0:T(8,128)(2,1)}, bf16[128,2048]{1,0:T(8,128)(2,1)S(1)}, u32[]{:S(2)}, u32[]{:S(2)}) %collective-permute-start.2) | collective-permute-done | bytes 524320 | tf_op jit(solution)/shard_map/ppermute | solution.py:698
  212.3 15.7 %collective-permute-done.6 = bf16[128,2048]{1,0:T(8,128)(2,1)S(1)} collective-permute-done((bf16[128,2048]{1,0:T(8,128)(2,1)S(1)}, bf16[128,2048]{1,0:T(8,128)(2,1)S(1)}, u32[]{:S(2)}, u32[]{:S(2)}) %collective-permute-start.6) | collective-permute-done | bytes 524320 | tf_op jit(solution)/shard_map/ppermute | solution.py:693
  228.0 1.0 add_convert_fusion.2
  229.0 1.5 collective-permute-start.8
  230.5 24.0 %collective-permute-start.7 = (bf16[128,2048]{1,0:T(8,128)(2,1)}, bf16[128,2048]{1,0:T(8,128)(2,1)}, u32[]{:S(2)}, u32[]{:S(2)}) collective-permute-start(bf16[128,2048]{1,0:T(8,128)(2,1)} %add_convert_fusion.2), channel_id=1, source_target_pairs={{0,4},{1,5},{2,6},{3,7},{12,8},{13,9},{14,10},{15,11},{16,20},{17,... | collective-permute-start | bytes 1572872 | tf_op jit(solution)/shard_map/ppermute | solution.py:693
  254.5 0.1 copy.21
  254.6 0.2 reshape.98.gate_ref
  254.8 0.2 copy.22.place_ref
  255.1 4.5 %collective-permute-done.10 = bf16[128,2048]{1,0:T(8,128)(2,1)} collective-permute-done((bf16[128,2048]{1,0:T(8,128)(2,1)}, bf16[128,2048]{1,0:T(8,128)(2,1)}, u32[]{:S(2)}, u32[]{:S(2)}) %collective-permute-start.10) | collective-permute-done | bytes 524320 | tf_op jit(solution)/shard_map/ppermute | solution.py:693
  259.6 5.2 %collective-permute-done.7 = bf16[128,2048]{1,0:T(8,128)(2,1)} collective-permute-done((bf16[128,2048]{1,0:T(8,128)(2,1)}, bf16[128,2048]{1,0:T(8,128)(2,1)}, u32[]{:S(2)}, u32[]{:S(2)}) %collective-permute-start.7) | collective-permute-done | bytes 524320 | tf_op jit(solution)/shard_map/ppermute | solution.py:693
  264.7 2.9 add_convert_fusion
  267.6 9.3 %fusion = bf16[1,768,2048]{2,1,0:T(8,128)(2,1)} fusion(bf16[1536,768]{1,0:T(8,128)(2,1)S(1)} %bitcast.22, bf16[1536,2048]{1,0:T(8,128)(2,1)} %get-tuple-element.35), kind=kOutput, calls=%fused_computation.2 | convolution fusion | flops 4833411072 | bytes 11796480 | tf_op jit(solution)/shard_map/dot_general | solution.py:742
  276.9 1.4 copy-done.11
  278.3 6.2 %unpack.1 = (bf16[1024,768]{1,0:T(8,128)(2,1)}, f32[1024,1]{1,0:T(8,128)S(1)}) custom-call(s32[1024,1]{1,0:T(8,128)S(1)} %copy.22.place_ref, f32[1024,1]{1,0:T(8,128)S(1)} %reshape.98.gate_ref, bf16[1024,768]{1,0:T(8,128)(2,1)S(1)} %bitcast.30, bf16[1536,768]{1,0:T(8,128)(2,1)} %bitcast.11.back_ref), custom_call_target="tpu_custom_call" | custom-call | flops 2415919104 | bytes 5505024 | tf_op jit(solution)/shard_map/unpack/pallas_call | solution.py:474
  284.6 0.2 reduce
  284.8 0.1 reshape.86
  284.9 0.7 copy.24
  (35 shorter events, 0.1 us)
Async XLA Ops:
  7.2 0.8 copy-start
  7.2 153.6 %all-gather.3.cloned.1.call-start = ((), (), s32[]{:S(2)}) async-start(), calls=%async_computation.3 | async-start | bytes 8912896 | tf_op jit(solution)/shard_map/all_gather | solution.py:719
  10.8 15.4 %all-to-all-start = ((f32[16,16,128]{2,1,0:T(8,128)}), f32[16,16,128]{2,1,0:T(8,128)S(1)}, u32[]{:S(2)}, u32[]{:S(2)}) async-start(f32[16,16,128]{2,1,0:T(8,128)} %broadcast_in_dim.19), calls=%async_computation | async-start | bytes 262144 | tf_op jit(solution)/shard_map/all_to_all | solution.py:716
  18.4 1.4 copy-start.10
  23.2 1.4 copy-start.2
  26.1 4.5 %copy-start.17 = (f32[16,16,128]{2,1,0:T(8,128)}, f32[16,16,128]{2,1,0:T(8,128)S(1)}, u32[]{:S(2)}) copy-start(f32[16,16,128]{2,1,0:T(8,128)S(1)} %all-to-all-done.routing_ref) | copy-start | bytes 393220
  26.1 77.7 %all-to-all-start.1 = ((bf16[16,96,768]{2,1,0:T(8,128)(2,1)}), bf16[16,96,768]{2,1,0:T(8,128)(2,1)S(1)}, u32[]{:S(2)}, u32[]{:S(2)}) async-start(bf16[16,96,768]{2,1,0:T(8,128)(2,1)} %bitcast.24), calls=%async_computation.1 | async-start | bytes 4718592 | tf_op jit(solution)/shard_map/all_to_all | solution.py:721
  103.9 0.7 copy-start.5
  104.6 1.9 copy-start.7
  106.5 0.7 copy-start.14
  107.2 3.2 %copy-start.6 = (s32[2,16,128]{2,1,0:T(8,128)S(1)}, s32[2,16,128]{2,1,0:T(8,128)}, u32[]{:S(2)}) copy-start(s32[2,16,128]{2,1,0:T(8,128)} %get-tuple-element.20.rank_ref) | copy-start | bytes 49156
  107.2 3.2 %copy-start.8 = (bf16[1,768,2048]{2,1,0:T(8,128)(2,1)S(1)}, bf16[1,768,2048]{2,1,0:T(8,128)(2,1)}, u32[]{:S(2)}) copy-start(bf16[1,768,2048]{2,1,0:T(8,128)(2,1)} %param.10) | copy-start | bytes 9437188
  110.2 5.7 %collective-permute-start = (bf16[8,96,2048]{2,1,0:T(8,128)(2,1)S(1)}, bf16[8,96,2048]{2,1,0:T(8,128)(2,1)S(1)}, u32[]{:S(2)}, u32[]{:S(2)}) collective-permute-start(bf16[8,96,2048]{2,1,0:T(8,128)(2,1)S(1)} %forward_rows.3), channel_id=1, source_target_pairs={{0,1},{1,0},{2,3},{3,2},{4,5},{5,4},{6,7},{7,6},{8,9},{9,8},{10,11... | collective-permute-start | bytes 9437192 | tf_op jit(solution)/shard_map/ppermute | solution.py:698
  118.3 0.8 copy-start.13
  119.1 11.8 %copy-start.12 = (bf16[128,2048]{1,0:T(8,128)(2,1)}, bf16[128,2048]{1,0:T(8,128)(2,1)S(1)}, u32[]{:S(2)}) copy-start(bf16[128,2048]{1,0:T(8,128)(2,1)S(1)} %get-tuple-element.24) | copy-start | bytes 1572868
  119.1 22.9 %collective-permute-start.4 = (bf16[128,2048]{1,0:T(8,128)(2,1)S(1)}, bf16[128,2048]{1,0:T(8,128)(2,1)S(1)}, u32[]{:S(2)}, u32[]{:S(2)}) collective-permute-start(bf16[128,2048]{1,0:T(8,128)(2,1)S(1)} %get-tuple-element.30), channel_id=1, source_target_pairs={{0,2},{1,3},{2,0},{3,1},{4,6},{5,7},{6,4},{7,5},{8,10},{9,11},{10,... | collective-permute-start | bytes 1572872 | tf_op jit(solution)/shard_map/ppermute | solution.py:698
  129.2 31.6 %copy-start.15 = (f32[2,16,128]{2,1,0:T(8,128)S(1)}, f32[2,16,128]{2,1,0:T(8,128)}, u32[]{:S(2)}) copy-start(f32[2,16,128]{2,1,0:T(8,128)} %get-tuple-element.21.gate_ref) | copy-start | bytes 49156
  129.2 48.5 %collective-permute-start.3 = (bf16[128,2048]{1,0:T(8,128)(2,1)}, bf16[128,2048]{1,0:T(8,128)(2,1)}, u32[]{:S(2)}, u32[]{:S(2)}) collective-permute-start(bf16[128,2048]{1,0:T(8,128)(2,1)} %get-tuple-element.28), channel_id=1, source_target_pairs={{0,2},{1,3},{2,0},{3,1},{4,6},{5,7},{6,4},{7,5},{8,10},{9,11},{10,... | collective-permute-start | bytes 1572872 | tf_op jit(solution)/shard_map/ppermute | solution.py:698
  130.8 0.8 copy-start.3
  131.6 0.8 copy-start.4
  142.0 0.8 copy-start.16
  143.7 34.0 %collective-permute-start.5 = (bf16[128,2048]{1,0:T(8,128)(2,1)}, bf16[128,2048]{1,0:T(8,128)(2,1)}, u32[]{:S(2)}, u32[]{:S(2)}) collective-permute-start(bf16[128,2048]{1,0:T(8,128)(2,1)} %fusion.1), channel_id=1, source_target_pairs={{0,4},{1,5},{2,6},{3,7},{12,8},{13,9},{14,10},{15,11},{16,20},{17,... | collective-permute-start | bytes 1572872 | tf_op jit(solution)/shard_map/ppermute | solution.py:693
  160.8 1.9 copy-start.9
  171.8 1.4 copy-start.1
  173.2 103.7 %all-to-all-start.2 = ((bf16[16,96,768]{2,1,0:T(8,128)(2,1)}), bf16[16,96,768]{2,1,0:T(8,128)(2,1)}, u32[]{:S(2)}, u32[]{:S(2)}) async-start(bf16[16,96,768]{2,1,0:T(8,128)(2,1)} %bitcast.23), calls=%async_computation.2 | async-start | bytes 4718592 | tf_op jit(solution)/shard_map/all_to_all | solution.py:727
  177.7 76.8 %copy-start.18 = (f32[128,8]{0,1:T(8,128)S(1)}, f32[128,8]{0,1:T(8,128)}, u32[]{:S(2)}) copy-start(f32[128,8]{0,1:T(8,128)} %param.7) | copy-start | bytes 12292
  179.3 9.3 %collective-permute-start.9 = (bf16[128,2048]{1,0:T(8,128)(2,1)S(1)}, bf16[128,2048]{1,0:T(8,128)(2,1)S(1)}, u32[]{:S(2)}, u32[]{:S(2)}) collective-permute-start(bf16[128,2048]{1,0:T(8,128)(2,1)S(1)} %add_convert_fusion.3), channel_id=1, source_target_pairs={{4,8},{5,9},{6,10},{7,11},{8,4},{9,5},{10,6},{11,7},{20,24},{21,25... | collective-permute-start | bytes 1572872 | tf_op jit(solution)/shard_map/ppermute | solution.py:693
  180.0 32.2 %collective-permute-start.2 = (bf16[128,2048]{1,0:T(8,128)(2,1)}, bf16[128,2048]{1,0:T(8,128)(2,1)S(1)}, u32[]{:S(2)}, u32[]{:S(2)}) collective-permute-start(bf16[128,2048]{1,0:T(8,128)(2,1)} %copy-done.13), channel_id=1, source_target_pairs={{0,2},{1,3},{2,0},{3,1},{4,6},{5,7},{6,4},{7,5},{8,10},{9,11},{10,... | collective-permute-start | bytes 1572872 | tf_op jit(solution)/shard_map/ppermute | solution.py:698
  182.1 45.9 %collective-permute-start.6 = (bf16[128,2048]{1,0:T(8,128)(2,1)S(1)}, bf16[128,2048]{1,0:T(8,128)(2,1)S(1)}, u32[]{:S(2)}, u32[]{:S(2)}) collective-permute-start(bf16[128,2048]{1,0:T(8,128)(2,1)S(1)} %add_convert_fusion.3), channel_id=1, source_target_pairs={{0,4},{1,5},{2,6},{3,7},{12,8},{13,9},{14,10},{15,11},{16,20},{17,... | collective-permute-start | bytes 1572872 | tf_op jit(solution)/shard_map/ppermute | solution.py:693
  188.0 67.1 %collective-permute-start.1 = (bf16[128,2048]{1,0:T(8,128)(2,1)}, bf16[128,2048]{1,0:T(8,128)(2,1)}, u32[]{:S(2)}, u32[]{:S(2)}) collective-permute-start(bf16[128,2048]{1,0:T(8,128)(2,1)} %copy-done.12), channel_id=1, source_target_pairs={{0,2},{1,3},{2,0},{3,1},{4,6},{5,7},{6,4},{7,5},{8,10},{9,11},{10,... | collective-permute-start | bytes 1572872 | tf_op jit(solution)/shard_map/ppermute | solution.py:698
  190.7 68.9 %collective-permute-start.10 = (bf16[128,2048]{1,0:T(8,128)(2,1)}, bf16[128,2048]{1,0:T(8,128)(2,1)}, u32[]{:S(2)}, u32[]{:S(2)}) collective-permute-start(bf16[128,2048]{1,0:T(8,128)(2,1)} %add_convert_fusion.1), channel_id=1, source_target_pairs={{4,0},{5,1},{6,2},{7,3},{8,12},{9,13},{10,14},{11,15},{20,16},{21,... | collective-permute-start | bytes 1572872 | tf_op jit(solution)/shard_map/ppermute | solution.py:693
  229.0 30.5 %collective-permute-start.8 = (bf16[128,2048]{1,0:T(8,128)(2,1)}, bf16[128,2048]{1,0:T(8,128)(2,1)}, u32[]{:S(2)}, u32[]{:S(2)}) collective-permute-start(bf16[128,2048]{1,0:T(8,128)(2,1)} %add_convert_fusion.2), channel_id=1, source_target_pairs={{4,8},{5,9},{6,10},{7,11},{8,4},{9,5},{10,6},{11,7},{20,24},{21,25... | collective-permute-start | bytes 1572872 | tf_op jit(solution)/shard_map/ppermute | solution.py:693
  230.5 34.2 %collective-permute-start.7 = (bf16[128,2048]{1,0:T(8,128)(2,1)}, bf16[128,2048]{1,0:T(8,128)(2,1)}, u32[]{:S(2)}, u32[]{:S(2)}) collective-permute-start(bf16[128,2048]{1,0:T(8,128)(2,1)} %add_convert_fusion.2), channel_id=1, source_target_pairs={{0,4},{1,5},{2,6},{3,7},{12,8},{13,9},{14,10},{15,11},{16,20},{17,... | collective-permute-start | bytes 1572872 | tf_op jit(solution)/shard_map/ppermute | solution.py:693
  276.9 1.4 copy-start.11
Sparse Core Ops, SparseCore 0:
  10.2 116.8 all-gather.2

commit v5 on v4

--- a/solution.py
+++ b/solution.py
@@ -207,46 +207,99 @@
     return [places[slot] * 4 + (across ^ turn) * 2 + lane for slot in slots for turn in range(2)]
 
 
-def back_kernel(capacity, rank_ref, gate_ref, cot_ref, weight_ref, z_ref, back_ref):
-    each = cot_ref.shape[0]
-    for j in range(each):
-        source = pl.program_id(0) * each + j
-        chosen = chosen_rows(rank_ref, 0, source, capacity)
-        gate = gate_column(gate_ref, chosen, 0, source)
-        rows = jnp.dot(one_hot(chosen), cot_ref[j], preferred_element_type=F32)
-        z_ref[j * capacity:(j + 1) * capacity, :] = (rows * gate).astype(BF16)
-    back = lax.dot_general(z_ref[...], weight_ref[...], (((1,), (1,)), ((), ())), preferred_element_type=F32)
-    back_ref[...] = back.astype(BF16)
-
-
-def backward_rows(rank, gate, cotangents, weight, capacity, each=4):
-    devices, tokens, width = cotangents.shape
+def place_out(pieces, sem):
+    copies = [pltpu.make_async_copy(source, target, sem.at[i]) for i, (source, target) in enumerate(pieces)]
+    for copy in copies:
+        copy.start()
+    return copies
+
+
+def scale_kernel(capacity, slots, held, here_ref, rank_ref, gate_ref, weight_ref, *refs):
+    count = 2 * len(slots)
+    blocks, refs = refs[:count], refs[count + held:]
+    z_ref, back_ref, sibling_ref, z_scratch, back_scratch, z_sem, back_sem = refs
+    sources = lane_sources(here_ref[0], slots, here_ref[0] % 2)
+    for i, source in enumerate(sources):
+        chosen = [chosen_rows(rank_ref, side, source, capacity) for side in range(2)]
+        gates = [gate_column(gate_ref, chosen[side], side, source) for side in range(2)]
+        both = jnp.concatenate([one_hot(chosen[0]), one_hot(chosen[1])], axis=0)
+        rows = jnp.dot(both, blocks[i][...], preferred_element_type=F32)
+        z_scratch[i] = (rows[:capacity] * gates[0]).astype(BF16)
+        sibling_ref[i] = (rows[capacity:] * gates[1]).astype(BF16)
+    copies = place_out([(z_scratch.at[i], z_ref.at[source]) for i, source in enumerate(sources)], z_sem)
+    flat = z_scratch[...].reshape(count * capacity, z_scratch.shape[2])
+    back = lax.dot_general(flat, weight_ref[...], (((1,), (1,)), ((), ())), preferred_element_type=F32)
+    back_scratch[...] = back.astype(BF16).reshape(back_scratch.shape)
+    copies += place_out([(back_scratch.at[i], back_ref.at[source]) for i, source in enumerate(sources)], back_sem)
+    for copy in copies:
+        copy.wait()
+
+
+def scaled_rows(here, rank, gate, weight, blocks, slots, capacity, buffers):
+    devices = rank.shape[1]
+    hidden, width = weight.shape
+    count = len(blocks)
+    tokens = blocks[0].shape[0]
+    vmem, anywhere = pl.BlockSpec(memory_space=pltpu.VMEM), pl.BlockSpec(memory_space=pl.ANY)
+    return pl.pallas_call(
+        functools.partial(scale_kernel, capacity, slots, len(buffers)),
+        in_specs=[pl.BlockSpec(memory_space=pltpu.SMEM)] + [vmem] * (3 + count) + [anywhere] * len(buffers),
+        out_specs=[anywhere, anywhere, vmem],
+        out_shape=[
+            jax.ShapeDtypeStruct((devices, capacity, width), BF16),
+            jax.ShapeDtypeStruct((devices, capacity, hidden), BF16),
+            jax.ShapeDtypeStruct((count, capacity, width), BF16),
+        ],
+        scratch_shapes=[
+            pltpu.VMEM((count, capacity, width), BF16),
+            pltpu.VMEM((count, capacity, hidden), BF16),
+            pltpu.SemaphoreType.DMA((count,)),
+            pltpu.SemaphoreType.DMA((count,)),
+        ],
+        input_output_aliases={4 + count + i: i for i in range(len(buffers))},
+        compiler_params=pltpu.CompilerParams(vmem_limit_bytes=40 * MIB),
+        cost_estimate=pl.CostEstimate(
+            flops=2 * count * capacity * width * (hidden + 2 * tokens), transcendentals=0,
+            bytes_accessed=2 * count * (tokens * width + capacity * (2 * width + hidden)) + 2 * width * hidden,
+        ),
+        name="scaled_rows",
+    )(here, rank, gate, weight, *blocks, *buffers)
+
+
+def sibling_kernel(capacity, slots, here_ref, weight_ref, rows_ref, _z, _back, z_ref, back_ref, back_scratch, z_sem, back_sem):
+    count = 2 * len(slots)
+    sources = lane_sources(here_ref[0], slots, 1 - here_ref[0] % 2)
+    copies = place_out([(rows_ref.at[i], z_ref.at[source]) for i, source in enumerate(sources)], z_sem)
+    flat = rows_ref[...].reshape(count * capacity, rows_ref.shape[2])
+    back = lax.dot_general(flat, weight_ref[...], (((1,), (1,)), ((), ())), preferred_element_type=F32)
+    back_scratch[...] = back.astype(BF16).reshape(back_scratch.shape)
+    copies += place_out([(back_scratch.at[i], back_ref.at[source]) for i, source in enumerate(sources)], back_sem)
+    for copy in copies:
+        copy.wait()
+
+
+def sibling_rows(here, weight, rows, slots, z_rows, back):
+    count, capacity, width = rows.shape
     hidden = weight.shape[0]
-    rows = each * capacity
-    return pl.pallas_call(
-        functools.partial(back_kernel, capacity),
-        grid=(devices // each,),
-        in_specs=[
-            pl.BlockSpec(rank.shape, lambda i: (0, 0, 0)),
-            pl.BlockSpec(rank.shape, lambda i: (0, 0, 0)),
-            pl.BlockSpec((each, tokens, width), lambda i: (i, 0, 0)),
-            pl.BlockSpec((hidden, width), lambda i: (0, 0)),
-        ],
-        out_specs=[
-            pl.BlockSpec((rows, width), lambda i: (i, 0)),
-            pl.BlockSpec((rows, hidden), lambda i: (i, 0)),
-        ],
-        out_shape=[
-            jax.ShapeDtypeStruct((devices * capacity, width), BF16),
-            jax.ShapeDtypeStruct((devices * capacity, hidden), BF16),
-        ],
-        compiler_params=pltpu.CompilerParams(vmem_limit_bytes=48 * MIB),
-        cost_estimate=pl.CostEstimate(
-            flops=2 * devices * capacity * width * (hidden + tokens), transcendentals=0,
-            bytes_accessed=2 * devices * (tokens * width + capacity * (width + hidden)) + 2 * width * hidden,
-        ),
-        name="backward_rows",
-    )(rank, gate, cotangents, weight)
+    vmem, anywhere = pl.BlockSpec(memory_space=pltpu.VMEM), pl.BlockSpec(memory_space=pl.ANY)
+    return pl.pallas_call(
+        functools.partial(sibling_kernel, capacity, slots),
+        in_specs=[pl.BlockSpec(memory_space=pltpu.SMEM), vmem, vmem, anywhere, anywhere],
+        out_specs=[anywhere, anywhere],
+        out_shape=[jax.ShapeDtypeStruct(z_rows.shape, BF16), jax.ShapeDtypeStruct(back.shape, BF16)],
+        scratch_shapes=[
+            pltpu.VMEM((count, capacity, hidden), BF16),
+            pltpu.SemaphoreType.DMA((count,)),
+            pltpu.SemaphoreType.DMA((count,)),
+        ],
+        input_output_aliases={3: 0, 4: 1},
+        compiler_params=pltpu.CompilerParams(vmem_limit_bytes=40 * MIB),
+        cost_estimate=pl.CostEstimate(
+            flops=2 * count * capacity * width * hidden, transcendentals=0,
+            bytes_accessed=2 * count * capacity * (2 * width + hidden) + 2 * width * hidden,
+        ),
+        name="sibling_rows",
+    )(here, weight, rows, z_rows, back)
 
 
 def forward_kernel(capacity, turn, here_ref, rank_ref, gate_ref, h_ref, weight_ref, out_ref):
@@ -370,16 +423,36 @@
     routing = lax.all_to_all(routing, "expert", split_axis=0, concat_axis=0, tiled=True)
     rank, gate = route(here, routing, top)
 
-    cotangents = lax.all_gather(cotangent, "expert", axis=0, tiled=False)
+    own = cotangent
+    from_end, from_inner, from_near_end = passed(OUTER, own), passed(INNER, own), passed(ENDS, own)
+    from_far_end = passed(ENDS_SWAP, own)
+    own_y = swapped_with(own, 2)
+    from_end, from_inner, from_near_end, from_far_end, own_y = lax.optimization_barrier(
+        (from_end, from_inner, from_near_end, from_far_end, own_y)
+    )
+    near, last = added(from_inner, from_near_end), added(from_end, from_far_end)
+    middle_inner, middle_end = passed(INNER, from_end), passed(ENDS, from_inner)
+    near_y, last_y = swapped_with(near, 2), swapped_with(last, 2)
+    middle = added(middle_inner, middle_end)
+    middle_y = swapped_with(middle, 2)
+
     place, send_h = pack(slot_ids.reshape(1, -1), h_flat, devices, capacity)
+    send_h, middle = lax.optimization_barrier((send_h, middle))
     rows_h = lax.all_to_all(
         send_h.reshape(devices, capacity, hidden), "expert", split_axis=0, concat_axis=0, tiled=True
     )
 
-    z_rows, back = backward_rows(rank, gate, cotangents, weight, capacity)
-    back = back.reshape(devices, capacity, hidden)
+    z_rows, back, sibling = scaled_rows(here, rank, gate, weight, [own, own_y, near, near_y], (0, 1), capacity, [])
+    sibling = swapped_with(sibling, 1)
+    z_rows, back, sibling_last = scaled_rows(
+        here, rank, gate, weight, [middle, middle_y, last, last_y], (2, 3), capacity, [z_rows, back]
+    )
+    sibling_last = swapped_with(sibling_last, 1)
+    z_rows, back = sibling_rows(here, weight, sibling, (0, 1), z_rows, back)
+    z_rows, back = sibling_rows(here, weight, sibling_last, (2, 3), z_rows, back)
     back_rows = lax.all_to_all(back, "expert", split_axis=0, concat_axis=0, tiled=True).reshape(-1, hidden)
 
+    rows_h, _ = lax.optimization_barrier((rows_h, back))
     other = swapped_with(forward_rows(here, rank, gate, rows_h, weight, 1), 1)
     mine = forward_rows(here, rank, gate, rows_h, weight, 0)
     across = [swapped_with(part, 2) for part in summed(here, rank, mine, other, 1)]
@@ -553,46 +626,99 @@
     return [places[slot] * 4 + (across ^ turn) * 2 + lane for slot in slots for turn in range(2)]
 
 
-def back_kernel(capacity, rank_ref, gate_ref, cot_ref, weight_ref, z_ref, back_ref):
-    each = cot_ref.shape[0]
-    for j in range(each):
-        source = pl.program_id(0) * each + j
-        chosen = chosen_rows(rank_ref, 0, source, capacity)
-        gate = gate_column(gate_ref, chosen, 0, source)
-        rows = jnp.dot(one_hot(chosen), cot_ref[j], preferred_element_type=F32)
-        z_ref[j * capacity:(j + 1) * capacity, :] = (rows * gate).astype(BF16)
-    back = lax.dot_general(z_ref[...], weight_ref[...], (((1,), (1,)), ((), ())), preferred_element_type=F32)
-    back_ref[...] = back.astype(BF16)
-
-
-def backward_rows(rank, gate, cotangents, weight, capacity, each=4):
-    devices, tokens, width = cotangents.shape
+def place_out(pieces, sem):
+    copies = [pltpu.make_async_copy(source, target, sem.at[i]) for i, (source, target) in enumerate(pieces)]
+    for copy in copies:
+        copy.start()
+    return copies
+
+
+def scale_kernel(capacity, slots, held, here_ref, rank_ref, gate_ref, weight_ref, *refs):
+    count = 2 * len(slots)
+    blocks, refs = refs[:count], refs[count + held:]
+    z_ref, back_ref, sibling_ref, z_scratch, back_scratch, z_sem, back_sem = refs
+    sources = lane_sources(here_ref[0], slots, here_ref[0] % 2)
+    for i, source in enumerate(sources):
+        chosen = [chosen_rows(rank_ref, side, source, capacity) for side in range(2)]
+        gates = [gate_column(gate_ref, chosen[side], side, source) for side in range(2)]
+        both = jnp.concatenate([one_hot(chosen[0]), one_hot(chosen[1])], axis=0)
+        rows = jnp.dot(both, blocks[i][...], preferred_element_type=F32)
+        z_scratch[i] = (rows[:capacity] * gates[0]).astype(BF16)
+        sibling_ref[i] = (rows[capacity:] * gates[1]).astype(BF16)
+    copies = place_out([(z_scratch.at[i], z_ref.at[source]) for i, source in enumerate(sources)], z_sem)
+    flat = z_scratch[...].reshape(count * capacity, z_scratch.shape[2])
+    back = lax.dot_general(flat, weight_ref[...], (((1,), (1,)), ((), ())), preferred_element_type=F32)
+    back_scratch[...] = back.astype(BF16).reshape(back_scratch.shape)
+    copies += place_out([(back_scratch.at[i], back_ref.at[source]) for i, source in enumerate(sources)], back_sem)
+    for copy in copies:
+        copy.wait()
+
+
+def scaled_rows(here, rank, gate, weight, blocks, slots, capacity, buffers):
+    devices = rank.shape[1]
+    hidden, width = weight.shape
+    count = len(blocks)
+    tokens = blocks[0].shape[0]
+    vmem, anywhere = pl.BlockSpec(memory_space=pltpu.VMEM), pl.BlockSpec(memory_space=pl.ANY)
+    return pl.pallas_call(
+        functools.partial(scale_kernel, capacity, slots, len(buffers)),
+        in_specs=[pl.BlockSpec(memory_space=pltpu.SMEM)] + [vmem] * (3 + count) + [anywhere] * len(buffers),
+        out_specs=[anywhere, anywhere, vmem],
+        out_shape=[
+            jax.ShapeDtypeStruct((devices, capacity, width), BF16),
+            jax.ShapeDtypeStruct((devices, capacity, hidden), BF16),
+            jax.ShapeDtypeStruct((count, capacity, width), BF16),
+        ],
+        scratch_shapes=[
+            pltpu.VMEM((count, capacity, width), BF16),
+            pltpu.VMEM((count, capacity, hidden), BF16),
+            pltpu.SemaphoreType.DMA((count,)),
+            pltpu.SemaphoreType.DMA((count,)),
+        ],
+        input_output_aliases={4 + count + i: i for i in range(len(buffers))},
+        compiler_params=pltpu.CompilerParams(vmem_limit_bytes=40 * MIB),
+        cost_estimate=pl.CostEstimate(
+            flops=2 * count * capacity * width * (hidden + 2 * tokens), transcendentals=0,
+            bytes_accessed=2 * count * (tokens * width + capacity * (2 * width + hidden)) + 2 * width * hidden,
+        ),
+        name="scaled_rows",
+    )(here, rank, gate, weight, *blocks, *buffers)
+
+
+def sibling_kernel(capacity, slots, here_ref, weight_ref, rows_ref, _z, _back, z_ref, back_ref, back_scratch, z_sem, back_sem):
+    count = 2 * len(slots)
+    sources = lane_sources(here_ref[0], slots, 1 - here_ref[0] % 2)
+    copies = place_out([(rows_ref.at[i], z_ref.at[source]) for i, source in enumerate(sources)], z_sem)
+    flat = rows_ref[...].reshape(count * capacity, rows_ref.shape[2])
+    back = lax.dot_general(flat, weight_ref[...], (((1,), (1,)), ((), ())), preferred_element_type=F32)
+    back_scratch[...] = back.astype(BF16).reshape(back_scratch.shape)
+    copies += place_out([(back_scratch.at[i], back_ref.at[source]) for i, source in enumerate(sources)], back_sem)
+    for copy in copies:
+        copy.wait()
+
+
+def sibling_rows(here, weight, rows, slots, z_rows, back):
+    count, capacity, width = rows.shape
     hidden = weight.shape[0]
-    rows = each * capacity
-    return pl.pallas_call(
-        functools.partial(back_kernel, capacity),
-        grid=(devices // each,),
-        in_specs=[
-            pl.BlockSpec(rank.shape, lambda i: (0, 0, 0)),
-            pl.BlockSpec(rank.shape, lambda i: (0, 0, 0)),
-            pl.BlockSpec((each, tokens, width), lambda i: (i, 0, 0)),
-            pl.BlockSpec((hidden, width), lambda i: (0, 0)),
-        ],
-        out_specs=[
-            pl.BlockSpec((rows, width), lambda i: (i, 0)),
-            pl.BlockSpec((rows, hidden), lambda i: (i, 0)),
-        ],
-        out_shape=[
-            jax.ShapeDtypeStruct((devices * capacity, width), BF16),
-            jax.ShapeDtypeStruct((devices * capacity, hidden), BF16),
-        ],
-        compiler_params=pltpu.CompilerParams(vmem_limit_bytes=48 * MIB),
-        cost_estimate=pl.CostEstimate(
-            flops=2 * devices * capacity * width * (hidden + tokens), transcendentals=0,
-            bytes_accessed=2 * devices * (tokens * width + capacity * (width + hidden)) + 2 * width * hidden,
-        ),
-        name="backward_rows",
-    )(rank, gate, cotangents, weight)
+    vmem, anywhere = pl.BlockSpec(memory_space=pltpu.VMEM), pl.BlockSpec(memory_space=pl.ANY)
+    return pl.pallas_call(
+        functools.partial(sibling_kernel, capacity, slots),
+        in_specs=[pl.BlockSpec(memory_space=pltpu.SMEM), vmem, vmem, anywhere, anywhere],
+        out_specs=[anywhere, anywhere],
+        out_shape=[jax.ShapeDtypeStruct(z_rows.shape, BF16), jax.ShapeDtypeStruct(back.shape, BF16)],
+        scratch_shapes=[
+            pltpu.VMEM((count, capacity, hidden), BF16),
+            pltpu.SemaphoreType.DMA((count,)),
+            pltpu.SemaphoreType.DMA((count,)),
+        ],
+        input_output_aliases={3: 0, 4: 1},
+        compiler_params=pltpu.CompilerParams(vmem_limit_bytes=40 * MIB),
+        cost_estimate=pl.CostEstimate(
+            flops=2 * count * capacity * width * hidden, transcendentals=0,
+            bytes_accessed=2 * count * capacity * (2 * width + hidden) + 2 * width * hidden,
+        ),
+        name="sibling_rows",
+    )(here, weight, rows, z_rows, back)
 
 
 def forward_kernel(capacity, turn, here_ref, rank_ref, gate_ref, h_ref, weight_ref, out_ref):
@@ -716,16 +842,36 @@
     routing = lax.all_to_all(routing, "expert", split_axis=0, concat_axis=0, tiled=True)
     rank, gate = route(here, routing, top)
 
-    cotangents = lax.all_gather(cotangent, "expert", axis=0, tiled=False)
+    own = cotangent
+    from_end, from_inner, from_near_end = passed(OUTER, own), passed(INNER, own), passed(ENDS, own)
+    from_far_end = passed(ENDS_SWAP, own)
+    own_y = swapped_with(own, 2)
+    from_end, from_inner, from_near_end, from_far_end, own_y = lax.optimization_barrier(
+        (from_end, from_inner, from_near_end, from_far_end, own_y)
+    )
+    near, last = added(from_inner, from_near_end), added(from_end, from_far_end)
+    middle_inner, middle_end = passed(INNER, from_end), passed(ENDS, from_inner)
+    near_y, last_y = swapped_with(near, 2), swapped_with(last, 2)
+    middle = added(middle_inner, middle_end)
+    middle_y = swapped_with(middle, 2)
+
     place, send_h = pack(slot_ids.reshape(1, -1), h_flat, devices, capacity)
+    send_h, middle = lax.optimization_barrier((send_h, middle))
     rows_h = lax.all_to_all(
         send_h.reshape(devices, capacity, hidden), "expert", split_axis=0, concat_axis=0, tiled=True
     )
 
-    z_rows, back = backward_rows(rank, gate, cotangents, weight, capacity)
-    back = back.reshape(devices, capacity, hidden)
+    z_rows, back, sibling = scaled_rows(here, rank, gate, weight, [own, own_y, near, near_y], (0, 1), capacity, [])
+    sibling = swapped_with(sibling, 1)
+    z_rows, back, sibling_last = scaled_rows(
+        here, rank, gate, weight, [middle, middle_y, last, last_y], (2, 3), capacity, [z_rows, back]
+    )
+    sibling_last = swapped_with(sibling_last, 1)
+    z_rows, back = sibling_rows(here, weight, sibling, (0, 1), z_rows, back)
+    z_rows, back = sibling_rows(here, weight, sibling_last, (2, 3), z_rows, back)
     back_rows = lax.all_to_all(back, "expert", split_axis=0, concat_axis=0, tiled=True).reshape(-1, hidden)
 
+    rows_h, _ = lax.optimization_barrier((rows_h, back))
     other = swapped_with(forward_rows(here, rank, gate, rows_h, weight, 1), 1)
     mine = forward_rows(here, rank, gate, rows_h, weight, 0)
     across = [swapped_with(part, 2) for part in summed(here, rank, mine, other, 1)]
@@ -740,7 +886,7 @@
     mixed = added(*kept, outer3, inner3, ends3)
 
     grad_sum = lax.dot_general(
-        rows_h.reshape(-1, hidden), z_rows, (((0,), (0,)), ((), ())),
+        rows_h.reshape(-1, hidden), z_rows.reshape(devices * capacity, -1), (((0,), (0,)), ((), ())),
         preferred_element_type=F32,
     )
     h_grad, gate_grad = unpack(place.reshape(-1, 1), gates.reshape(-1, 1), h_flat, back_rows)

time: 293 us -> 264 us (0.901)
  waiting for transfers between devices: 131 us -> 113 us
  starting transfers between devices: 79.9 us -> 63.9 us
  between operations: 14.3 us -> 1.05 us
  Pallas kernels: 30.4 us -> 39.9 us
  other arithmetic: 10.2 us -> 15.8 us
    all_to_all x1, waiting for transfers between devices: 71.5 us -> 0.01 us  [dense_shards(): lax.all_to_all(send_h.reshape(devices, capacity, hidden), 'expert', split...]
    ppermute x5 -> x11, waiting for transfers between devices: 32.4 us -> 75.3 us  [swapped_with(): return lax.ppermute(value, 'expert', [(i, i ^ bit) for i in range(devices)])]
    ppermute x6 -> x12, starting transfers between devices: 50.4 us -> 34.3 us  [passed(): lax.ppermute(value, 'expert', [(a * 4 + lane, b * 4 + lane) for a, b in p...]
    ppermute x6 -> x12, waiting for transfers between devices: 25.4 us -> 34.6 us  [passed(): lax.ppermute(value, 'expert', [(a * 4 + lane, b * 4 + lane) for a, b in p...]
    pallas_call x1 -> x4, Pallas kernels: 9.12 us -> 15.7 us  [the longest x2 9.4 us: scaled_rows(): pl.pallas_call(functools.partial(scale_kernel, capacity, slots, len(buffe...]
    convert_element_type x5 -> x8, other arithmetic: 8.55 us -> 14.1 us  [added(): return total.astype(BF16)]
    unnamed x40 -> x64, local copies, waits for them, and re-layouts: 14.8 us -> 17.6 us
    ppermute x5 -> x11, starting transfers between devices: 13 us -> 11.2 us  [swapped_with(): return lax.ppermute(value, 'expert', [(i, i ^ bit) for i in range(devices)])]
  transfers between devices with their start and end apart: 15 -> 26, of which waited for: 8 -> 11; matrix products, arithmetic and copies ran while one was open for 7% -> 10% of each run, Pallas kernels for 8% -> 13%
where the time goes in v5:
time: 264 us; the launch traced here: 262 us
  waiting for transfers between devices  113 us (43%)
  starting transfers between devices  63.9 us (24%)
  Pallas kernels  39.9 us (15%)
  local copies, waits for them, and re-layouts  19.6 us (7%)
  other arithmetic  15.8 us (6%)
  matrix products  9.1 us (3%)
    ppermute x11, waiting for transfers between devices, swapped_with(): return lax.ppermute(value, 'expert', [(i, i ^ bit) for i in range(devices)])  75.3 us
    ppermute x12, waiting for transfers between devices, passed(): lax.ppermute(value, 'expert', [(a * 4 + lane, b * 4 + lane) for a, b in p...  34.6 us
    ppermute x12, starting transfers between devices, passed(): lax.ppermute(value, 'expert', [(a * 4 + lane, b * 4 + lane) for a, b in p...  34.3 us
    unnamed x64, local copies, waits for them, and re-layouts  17.6 us
    convert_element_type x8, other arithmetic, added(): return total.astype(BF16)  14.1 us
    ppermute x11, starting transfers between devices, swapped_with(): return lax.ppermute(value, 'expert', [(i, i ^ bit) for i in range(devices)])  11.2 us
    pallas_call x2, Pallas kernels, scaled_rows(): pl.pallas_call(functools.partial(scale_kernel, capacity, slots, len(buffe...  9.4 us
    dot_general x1, matrix products, dense_shards(): lax.dot_general(rows_h.reshape(-1, hidden), z_rows.reshape(devices * capa...  9.1 us
  transfers between devices with their start and end apart: 26, of which 11 were waited for; matrix products, arithmetic and copies ran while one was open for 10% of the time, Pallas kernels for 13%

profile of v5, /device:TPU:0, one launch (start us, length us, event | category | flops | bytes accessed | tf_op | source)
XLA Modules:
  0.0 262.1 jit_solution(12242824140370722271)
XLA Ops:
  0.6 5.8 %collective-permute-start = (bf16[128,2048]{1,0:T(8,128)(2,1)}, bf16[128,2048]{1,0:T(8,128)(2,1)}, u32[]{:S(2)}, u32[]{:S(2)}) collective-permute-start(bf16[128,2048]{1,0:T(8,128)(2,1)} %refs_0_.1), channel_id=1, source_target_pairs={{0,4},{1,5},{2,6},{3,7},{12,8},{13,9},{14,10},{15,11},{16,20},{17,... | collective-permute-start | bytes 1572872 | tf_op jit(solution)/shard_map/ppermute | solution.py:819
  7.1 1.3 collective-permute-start.2
  8.4 4.4 %collective-permute-start.3 = (bf16[128,2048]{1,0:T(8,128)(2,1)}, bf16[128,2048]{1,0:T(8,128)(2,1)S(1)}, u32[]{:S(2)}, u32[]{:S(2)}) collective-permute-start(bf16[128,2048]{1,0:T(8,128)(2,1)} %refs_0_.1), channel_id=1, source_target_pairs={{0,12},{1,13},{2,14},{3,15},{12,0},{13,1},{14,2},{15,3},{16,28},{1... | collective-permute-start | bytes 1572872 | tf_op jit(solution)/shard_map/ppermute | solution.py:819
  12.8 1.6 collective-permute-start.4
  15.1 0.8 select_reduce_fusion
  15.8 2.4 collective-permute-done
  18.2 15.6 %collective-permute-done.2 = bf16[128,2048]{1,0:T(8,128)(2,1)S(1)} collective-permute-done((bf16[128,2048]{1,0:T(8,128)(2,1)}, bf16[128,2048]{1,0:T(8,128)(2,1)S(1)}, u32[]{:S(2)}, u32[]{:S(2)}) %collective-permute-start.2) | collective-permute-done | bytes 524320 | tf_op jit(solution)/shard_map/ppermute | solution.py:819
  33.8 0.8 copy-done.23
  34.7 1.3 collective-permute-start.6
  36.0 0.7 collective-permute-start.5
  36.7 0.7 pad_maximum_fusion
  38.0 7.8 %all-to-all-start = ((f32[16,16,128]{2,1,0:T(8,128)}), f32[16,16,128]{2,1,0:T(8,128)S(1)}, u32[]{:S(2)}, u32[]{:S(2)}) async-start(f32[16,16,128]{2,1,0:T(8,128)} %broadcast_in_dim.19), calls=%async_computation | async-start | bytes 262144 | tf_op jit(solution)/shard_map/all_to_all | solution.py:842
  46.1 1.4 copy-done.18
  47.5 4.3 %pack.1 = (s32[1,1024]{1,0:T(1,128)S(1)}, bf16[1536,768]{1,0:T(8,128)(2,1)}) custom-call(s32[1,1024]{1,0:T(1,128)S(1)} %reshape.74.ids_ref, bf16[1024,768]{1,0:T(8,128)(2,1)S(1)} %bitcast.28), custom_call_target="tpu_custom_call" | custom-call | flops 2415919104 | bytes 3932160 | tf_op jit(solution)/shard_map/pack/pallas_call | solution.py:510
  51.7 0.9 add_convert_fusion.6.refs_0_
  52.6 2.9 %all-to-all-done.routing_ref = f32[16,16,128]{2,1,0:T(8,128)S(1)} async-done(((f32[16,16,128]{2,1,0:T(8,128)}), f32[16,16,128]{2,1,0:T(8,128)S(1)}, u32[]{:S(2)}, u32[]{:S(2)}) %all-to-all-start) | async-done | bytes 131104 | tf_op jit(solution)/shard_map/all_to_all | solution.py:842
  56.2 4.6 %all-to-all-start.1 = ((bf16[16,96,768]{2,1,0:T(8,128)(2,1)}), bf16[16,96,768]{2,1,0:T(8,128)(2,1)}, u32[]{:S(2)}, u32[]{:S(2)}) async-start(bf16[16,96,768]{2,1,0:T(8,128)(2,1)} %bitcast.5), calls=%async_computation.1 | async-start | bytes 4718592 | tf_op jit(solution)/shard_map/all_to_all | solution.py:860
  60.8 2.3 add_convert_fusion.4.refs_2_
  63.1 1.6 collective-permute-start.9
  64.7 2.1 add_convert_fusion.5.refs_2_
  67.3 1.6 collective-permute-start.7
  68.8 1.7 route.1
  70.5 24.9 %collective-permute-done.9.refs_3_ = bf16[128,2048]{1,0:T(8,128)(2,1)} collective-permute-done((bf16[128,2048]{1,0:T(8,128)(2,1)}, bf16[128,2048]{1,0:T(8,128)(2,1)}, u32[]{:S(2)}, u32[]{:S(2)}) %collective-permute-start.9) | collective-permute-done | bytes 524320 | tf_op jit(solution)/shard_map/ppermute | solution.py:824
  95.4 0.7 copy-done.14
  96.1 0.7 copy-done.16
  96.8 1.0 copy-done.20
  97.9 1.0 copy-done.24
  98.9 4.7 %scaled_rows.2 = (bf16[16,96,2048]{2,1,0:T(8,128)(2,1)}, bf16[16,96,768]{2,1,0:T(8,128)(2,1)}, bf16[4,96,2048]{2,1,0:T(8,128)(2,1)S(1)}) custom-call(s32[1]{0:T(128)} %bitcast.here_ref, s32[2,16,128]{2,1,0:T(8,128)S(1)} %copy-done.14, f32[2,16,128]{2,1,0:T(8,128)S(1)} %copy-done.16, bf16[768,2048]{1,0:T(8,128)(2,1)S(1)} %bitcast.21, ...), custom_call_target="tpu_custom_call" | custom-call | flops 1610612736 | bytes 8978432 | tf_op jit(solution)/shard_map/scaled_rows/pallas_call | solution.py:663
  103.7 8.2 %collective-permute-done.8.refs_3_ = bf16[128,2048]{1,0:T(8,128)(2,1)} collective-permute-done((bf16[128,2048]{1,0:T(8,128)(2,1)}, bf16[128,2048]{1,0:T(8,128)(2,1)}, u32[]{:S(2)}, u32[]{:S(2)}) %collective-permute-start.8) | collective-permute-done | bytes 524320 | tf_op jit(solution)/shard_map/ppermute | solution.py:824
  111.9 10.8 %collective-permute-done.7.refs_1_ = bf16[128,2048]{1,0:T(8,128)(2,1)} collective-permute-done((bf16[128,2048]{1,0:T(8,128)(2,1)}, bf16[128,2048]{1,0:T(8,128)(2,1)}, u32[]{:S(2)}, u32[]{:S(2)}) %collective-permute-start.7) | collective-permute-done | bytes 524320 | tf_op jit(solution)/shard_map/ppermute | solution.py:824
  122.7 4.7 %scaled_rows.3 = (bf16[16,96,2048]{2,1,0:T(8,128)(2,1)}, bf16[16,96,768]{2,1,0:T(8,128)(2,1)}, bf16[4,96,2048]{2,1,0:T(8,128)(2,1)S(1)}) custom-call(s32[1]{0:T(128)} %bitcast.here_ref, s32[2,16,128]{2,1,0:T(8,128)S(1)} %copy-done.14, f32[2,16,128]{2,1,0:T(8,128)S(1)} %copy-done.16, ...), custom_call_target="tpu_custom_call", output_to_operand_aliasing={{0}: (8, {}), {1}: (9, {})} | custom-call | flops 1610612736 | bytes 8978432 | tf_op jit(solution)/shard_map/scaled_rows/pallas_call | solution.py:663
  127.5 2.8 %copy-done.1 = bf16[16,96,2048]{2,1,0:T(8,128)(2,1)S(1)} copy-done((bf16[16,96,2048]{2,1,0:T(8,128)(2,1)S(1)}, bf16[16,96,2048]{2,1,0:T(8,128)(2,1)}, u32[]{:S(2)}) %copy-start.1) | copy-done | bytes 6291480
  130.3 3.1 %sibling_rows.2 = (bf16[16,96,2048]{2,1,0:T(8,128)(2,1)S(1)}, bf16[16,96,768]{2,1,0:T(8,128)(2,1)}) custom-call(s32[1]{0:T(128)} %bitcast.here_ref, bf16[768,2048]{1,0:T(8,128)(2,1)S(1)} %bitcast.23, bf16[4,96,2048]{2,1,0:T(8,128)(2,1)S(1)} %collective-permute-done.11.rows_ref, ...), custom_call_target="tpu_custom_call", output_to_operand_aliasing={{0}: (3, {}), {1}: (4, {})} | custom-call | flops 1207959552 | bytes 6881280 | tf_op jit(solution)/shard_map/sibling_rows/pallas_call | solution.py:704
  133.4 3.1 %sibling_rows.3 = (bf16[16,96,2048]{2,1,0:T(8,128)(2,1)S(1)}, bf16[16,96,768]{2,1,0:T(8,128)(2,1)}) custom-call(s32[1]{0:T(128)} %bitcast.here_ref, bf16[768,2048]{1,0:T(8,128)(2,1)S(1)} %bitcast.24, bf16[4,96,2048]{2,1,0:T(8,128)(2,1)S(1)} %collective-permute-done.10.rows_ref, ...), custom_call_target="tpu_custom_call", output_to_operand_aliasing={{0}: (3, {}), {1}: (4, {})} | custom-call | flops 1207959552 | bytes 6881280 | tf_op jit(solution)/shard_map/sibling_rows/pallas_call | solution.py:704
  136.6 2.6 %copy-done.2 = bf16[16,96,2048]{2,1,0:T(8,128)(2,1)} copy-done((bf16[16,96,2048]{2,1,0:T(8,128)(2,1)}, bf16[16,96,2048]{2,1,0:T(8,128)(2,1)S(1)}, u32[]{:S(2)}) %copy-start.2) | copy-done | bytes 6291480
  139.3 4.0 %forward_rows.3 = bf16[8,96,2048]{2,1,0:T(8,128)(2,1)S(1)} custom-call(s32[1]{0:T(128)} %bitcast.here_ref, s32[2,16,128]{2,1,0:T(8,128)S(1)} %copy-done.15, f32[2,16,128]{2,1,0:T(8,128)S(1)} %copy-done.17, bf16[8,2,96,768]{3,2,1,0:T(8,128)(2,1)} %bitcast.7.h_ref, bf16[768,2048]{1,0:T(8,128)(2,1)S(1)} %bitcast.25), custom_call_target="tpu_custom_call" | custom-call | flops 2415919104 | bytes 7471104 | tf_op jit(solution)/shard_map/forward_rows/pallas_call | solution.py:739
  143.8 3.9 %forward_rows.2.own_ref = bf16[8,96,2048]{2,1,0:T(8,128)(2,1)S(1)} custom-call(s32[1]{0:T(128)} %bitcast.here_ref, s32[2,16,128]{2,1,0:T(8,128)S(1)} %copy-done.15, f32[2,16,128]{2,1,0:T(8,128)S(1)} %copy-done.17, bf16[8,2,96,768]{3,2,1,0:T(8,128)(2,1)} %bitcast.7.h_ref, bf16[768,2048]{1,0:T(8,128)(2,1)S(1)} %bitcast.26), custom_call_target="tpu_custom_call" | custom-call | flops 2415919104 | bytes 7471104 | tf_op jit(solution)/shard_map/forward_rows/pallas_call | solution.py:739
  147.7 1.3 collective-permute-done.12.other_ref
  149.1 2.6 summed.3
  151.6 0.8 copy-done.21
  152.5 0.8 copy-done.25
  153.7 5.9 %all-to-all-start.2 = ((bf16[16,96,768]{2,1,0:T(8,128)(2,1)}), bf16[16,96,768]{2,1,0:T(8,128)(2,1)}, u32[]{:S(2)}, u32[]{:S(2)}) async-start(bf16[16,96,768]{2,1,0:T(8,128)(2,1)} %get-tuple-element.54), calls=%async_computation.2 | async-start | bytes 4718592 | tf_op jit(solution)/shard_map/all_to_all | solution.py:872
  159.6 1.9 collective-permute-start.15
  161.5 1.9 copy-done.7
  163.4 1.6 summed.2
  165.0 7.6 %collective-permute-done.16 = bf16[128,2048]{1,0:T(8,128)(2,1)} collective-permute-done((bf16[128,2048]{1,0:T(8,128)(2,1)}, bf16[128,2048]{1,0:T(8,128)(2,1)}, u32[]{:S(2)}, u32[]{:S(2)}) %collective-permute-start.16) | collective-permute-done | bytes 524320 | tf_op jit(solution)/shard_map/ppermute | solution.py:824
  172.6 1.3 fusion.1
  173.9 2.6 collective-permute-start.17
  176.5 0.7 collective-permute-start.14
  177.2 22.4 %collective-permute-done.15 = bf16[128,2048]{1,0:T(8,128)(2,1)S(1)} collective-permute-done((bf16[128,2048]{1,0:T(8,128)(2,1)}, bf16[128,2048]{1,0:T(8,128)(2,1)S(1)}, u32[]{:S(2)}, u32[]{:S(2)}) %collective-permute-start.15) | collective-permute-done | bytes 524320 | tf_op jit(solution)/shard_map/ppermute | solution.py:824
  199.6 10.4 %collective-permute-done.17 = bf16[128,2048]{1,0:T(8,128)(2,1)S(1)} collective-permute-done((bf16[128,2048]{1,0:T(8,128)(2,1)S(1)}, bf16[128,2048]{1,0:T(8,128)(2,1)S(1)}, u32[]{:S(2)}, u32[]{:S(2)}) %collective-permute-start.17) | collective-permute-done | bytes 524320 | tf_op jit(solution)/shard_map/ppermute | solution.py:819
  210.3 5.3 %collective-permute-start.18 = (bf16[128,2048]{1,0:T(8,128)(2,1)S(1)}, bf16[128,2048]{1,0:T(8,128)(2,1)}, u32[]{:S(2)}, u32[]{:S(2)}) collective-permute-start(bf16[128,2048]{1,0:T(8,128)(2,1)S(1)} %add_convert_fusion.3), channel_id=1, source_target_pairs={{0,4},{1,5},{2,6},{3,7},{12,8},{13,9},{14,10},{15,11},{16,20},{17,... | collective-permute-start | bytes 1572872 | tf_op jit(solution)/shard_map/ppermute | solution.py:819
  215.6 1.5 collective-permute-start.21
  217.5 2.3 collective-permute-start.13
  219.9 6.2 %collective-permute-done.18 = bf16[128,2048]{1,0:T(8,128)(2,1)} collective-permute-done((bf16[128,2048]{1,0:T(8,128)(2,1)S(1)}, bf16[128,2048]{1,0:T(8,128)(2,1)}, u32[]{:S(2)}, u32[]{:S(2)}) %collective-permute-start.18) | collective-permute-done | bytes 524320 | tf_op jit(solution)/shard_map/ppermute | solution.py:819
  226.0 2.4 add_convert_fusion.2
  228.5 1.5 collective-permute-start.20
  230.0 8.2 %collective-permute-start.19 = (bf16[128,2048]{1,0:T(8,128)(2,1)}, bf16[128,2048]{1,0:T(8,128)(2,1)}, u32[]{:S(2)}, u32[]{:S(2)}) collective-permute-start(bf16[128,2048]{1,0:T(8,128)(2,1)} %add_convert_fusion.2), channel_id=1, source_target_pairs={{0,4},{1,5},{2,6},{3,7},{12,8},{13,9},{14,10},{15,11},{16,20},{17,... | collective-permute-start | bytes 1572872 | tf_op jit(solution)/shard_map/ppermute | solution.py:819
  238.1 2.3 add_convert_fusion.1
  240.4 1.3 collective-permute-start.22
  241.7 9.1 %fusion = bf16[1,768,2048]{2,1,0:T(8,128)(2,1)} fusion(bf16[16,96,768]{2,1,0:T(8,128)(2,1)} %all-to-all-done.1, bf16[16,96,2048]{2,1,0:T(8,128)(2,1)} %copy-done.2), kind=kOutput, calls=%fused_computation.2 | convolution fusion | flops 4833411072 | bytes 11796480 | tf_op jit(solution)/shard_map/dot_general | solution.py:888
  250.8 1.4 copy-done.19
  252.2 6.3 %unpack.1 = (bf16[1024,768]{1,0:T(8,128)(2,1)}, f32[1024,1]{1,0:T(8,128)S(1)}) custom-call(s32[1024,1]{1,0:T(8,128)S(1)} %copy.28.place_ref, f32[1024,1]{1,0:T(8,128)S(1)} %reshape.92.gate_ref, bf16[1024,768]{1,0:T(8,128)(2,1)S(1)} %bitcast.29, bf16[1536,768]{1,0:T(8,128)(2,1)} %bitcast.9.back_ref), custom_call_target="tpu_custom_call" | custom-call | flops 2415919104 | bytes 5505024 | tf_op jit(solution)/shard_map/unpack/pallas_call | solution.py:547
  259.5 2.6 add_convert_fusion
  (86 shorter events, 6.3 us)
Async XLA Ops:
  0.6 13.8 %copy-start = (s32[8]{0:T(128)S(1)}, s32[8]{0:T(128)}, u32[]{:S(2)}) copy-start(s32[8]{0:T(128)} %param.11) | copy-start | bytes 100
  0.6 17.6 %collective-permute-start = (bf16[128,2048]{1,0:T(8,128)(2,1)}, bf16[128,2048]{1,0:T(8,128)(2,1)}, u32[]{:S(2)}, u32[]{:S(2)}) collective-permute-start(bf16[128,2048]{1,0:T(8,128)(2,1)} %refs_0_.1), channel_id=1, source_target_pairs={{0,4},{1,5},{2,6},{3,7},{12,8},{13,9},{14,10},{15,11},{16,20},{17,... | collective-permute-start | bytes 1572872 | tf_op jit(solution)/shard_map/ppermute | solution.py:819
  6.4 11.8 %collective-permute-start.1 = (bf16[128,2048]{1,0:T(8,128)(2,1)}, bf16[128,2048]{1,0:T(8,128)(2,1)S(1)}, u32[]{:S(2)}, u32[]{:S(2)}) collective-permute-start(bf16[128,2048]{1,0:T(8,128)(2,1)} %refs_0_.1), channel_id=1, source_target_pairs={{4,8},{5,9},{6,10},{7,11},{8,4},{9,5},{10,6},{11,7},{20,24},{21,25... | collective-permute-start | bytes 1572872 | tf_op jit(solution)/shard_map/ppermute | solution.py:819
  7.1 26.7 %collective-permute-start.2 = (bf16[128,2048]{1,0:T(8,128)(2,1)}, bf16[128,2048]{1,0:T(8,128)(2,1)S(1)}, u32[]{:S(2)}, u32[]{:S(2)}) collective-permute-start(bf16[128,2048]{1,0:T(8,128)(2,1)} %refs_0_.1), channel_id=1, source_target_pairs={{4,0},{5,1},{6,2},{7,3},{8,12},{9,13},{10,14},{11,15},{20,16},{21,... | collective-permute-start | bytes 1572872 | tf_op jit(solution)/shard_map/ppermute | solution.py:819
  8.4 25.4 %collective-permute-start.3 = (bf16[128,2048]{1,0:T(8,128)(2,1)}, bf16[128,2048]{1,0:T(8,128)(2,1)S(1)}, u32[]{:S(2)}, u32[]{:S(2)}) collective-permute-start(bf16[128,2048]{1,0:T(8,128)(2,1)} %refs_0_.1), channel_id=1, source_target_pairs={{0,12},{1,13},{2,14},{3,15},{12,0},{13,1},{14,2},{15,3},{16,28},{1... | collective-permute-start | bytes 1572872 | tf_op jit(solution)/shard_map/ppermute | solution.py:819
  12.8 21.0 %collective-permute-start.4 = (bf16[128,2048]{1,0:T(8,128)(2,1)}, bf16[128,2048]{1,0:T(8,128)(2,1)S(1)}, u32[]{:S(2)}, u32[]{:S(2)}) collective-permute-start(bf16[128,2048]{1,0:T(8,128)(2,1)} %refs_0_.1), channel_id=1, source_target_pairs={{0,2},{1,3},{2,0},{3,1},{4,6},{5,7},{6,4},{7,5},{8,10},{9,11},{10,... | collective-permute-start | bytes 1572872 | tf_op jit(solution)/shard_map/ppermute | solution.py:824
  18.2 37.3 %copy-start.26 = (bf16[128,2048]{1,0:T(8,128)(2,1)}, bf16[128,2048]{1,0:T(8,128)(2,1)S(1)}, u32[]{:S(2)}) copy-start(bf16[128,2048]{1,0:T(8,128)(2,1)S(1)} %collective-permute-done.1) | copy-start | bytes 1572868
  33.8 12.2 %copy-start.28 = (bf16[128,2048]{1,0:T(8,128)(2,1)}, bf16[128,2048]{1,0:T(8,128)(2,1)S(1)}, u32[]{:S(2)}) copy-start(bf16[128,2048]{1,0:T(8,128)(2,1)S(1)} %collective-permute-done.2) | copy-start | bytes 1572868
  33.8 12.2 %copy-start.27 = (bf16[128,2048]{1,0:T(8,128)(2,1)}, bf16[128,2048]{1,0:T(8,128)(2,1)S(1)}, u32[]{:S(2)}) copy-start(bf16[128,2048]{1,0:T(8,128)(2,1)S(1)} %collective-permute-done.3) | copy-start | bytes 1572868
  33.8 0.8 copy-start.23
  34.7 17.0 %collective-permute-start.6 = (bf16[128,2048]{1,0:T(8,128)(2,1)S(1)}, bf16[128,2048]{1,0:T(8,128)(2,1)S(1)}, u32[]{:S(2)}, u32[]{:S(2)}) collective-permute-start(bf16[128,2048]{1,0:T(8,128)(2,1)S(1)} %collective-permute-done.1), channel_id=1, source_target_pairs={{4,0},{5,1},{6,2},{7,3},{8,12},{9,13},{10,14},{11,15},{20,16},{21,... | collective-permute-start | bytes 1572872 | tf_op jit(solution)/shard_map/ppermute | solution.py:819
  36.0 15.8 %collective-permute-start.5 = (bf16[128,2048]{1,0:T(8,128)(2,1)}, bf16[128,2048]{1,0:T(8,128)(2,1)S(1)}, u32[]{:S(2)}, u32[]{:S(2)}) collective-permute-start(bf16[128,2048]{1,0:T(8,128)(2,1)} %collective-permute-done), channel_id=1, source_target_pairs={{4,8},{5,9},{6,10},{7,11},{8,4},{9,5},{10,6},{11,7},{20,24},{21,25... | collective-permute-start | bytes 1572872 | tf_op jit(solution)/shard_map/ppermute | solution.py:819
  38.0 17.5 %all-to-all-start = ((f32[16,16,128]{2,1,0:T(8,128)}), f32[16,16,128]{2,1,0:T(8,128)S(1)}, u32[]{:S(2)}, u32[]{:S(2)}) async-start(f32[16,16,128]{2,1,0:T(8,128)} %broadcast_in_dim.19), calls=%async_computation | async-start | bytes 262144 | tf_op jit(solution)/shard_map/all_to_all | solution.py:842
  46.0 1.4 copy-start.18
  55.5 0.6 copy-start.29
  56.2 83.1 %all-to-all-start.1 = ((bf16[16,96,768]{2,1,0:T(8,128)(2,1)}), bf16[16,96,768]{2,1,0:T(8,128)(2,1)}, u32[]{:S(2)}, u32[]{:S(2)}) async-start(bf16[16,96,768]{2,1,0:T(8,128)(2,1)} %bitcast.5), calls=%async_computation.1 | async-start | bytes 4718592 | tf_op jit(solution)/shard_map/all_to_all | solution.py:860
  60.8 34.6 %copy-start.3 = (bf16[1,768,2048]{2,1,0:T(8,128)(2,1)S(1)}, bf16[1,768,2048]{2,1,0:T(8,128)(2,1)}, u32[]{:S(2)}) copy-start(bf16[1,768,2048]{2,1,0:T(8,128)(2,1)} %param.10) | copy-start | bytes 9437188
  63.1 32.3 %collective-permute-start.9 = (bf16[128,2048]{1,0:T(8,128)(2,1)}, bf16[128,2048]{1,0:T(8,128)(2,1)}, u32[]{:S(2)}, u32[]{:S(2)}) collective-permute-start(bf16[128,2048]{1,0:T(8,128)(2,1)} %add_convert_fusion.4.refs_2_), channel_id=1, source_target_pairs={{0,2},{1,3},{2,0},{3,1},{4,6},{5,7},{6,4},{7,5},{8,10},{9,11},{10,... | collective-permute-start | bytes 1572872 | tf_op jit(solution)/shard_map/ppermute | solution.py:824
  66.8 45.1 %collective-permute-start.8 = (bf16[128,2048]{1,0:T(8,128)(2,1)}, bf16[128,2048]{1,0:T(8,128)(2,1)}, u32[]{:S(2)}, u32[]{:S(2)}) collective-permute-start(bf16[128,2048]{1,0:T(8,128)(2,1)} %add_convert_fusion.5.refs_2_), channel_id=1, source_target_pairs={{0,2},{1,3},{2,0},{3,1},{4,6},{5,7},{6,4},{7,5},{8,10},{9,11},{10,... | collective-permute-start | bytes 1572872 | tf_op jit(solution)/shard_map/ppermute | solution.py:824
  67.3 55.4 %collective-permute-start.7 = (bf16[128,2048]{1,0:T(8,128)(2,1)}, bf16[128,2048]{1,0:T(8,128)(2,1)}, u32[]{:S(2)}, u32[]{:S(2)}) collective-permute-start(bf16[128,2048]{1,0:T(8,128)(2,1)} %add_convert_fusion.6.refs_0_), channel_id=1, source_target_pairs={{0,2},{1,3},{2,0},{3,1},{4,6},{5,7},{6,4},{7,5},{8,10},{9,11},{10,... | collective-permute-start | bytes 1572872 | tf_op jit(solution)/shard_map/ppermute | solution.py:824
  95.4 0.7 copy-start.14
  96.1 0.7 copy-start.16
  96.8 1.0 copy-start.20
  97.9 1.0 copy-start.24
  98.9 23.8 %copy-start.8 = (bf16[128,2048]{1,0:T(8,128)(2,1)S(1)}, bf16[128,2048]{1,0:T(8,128)(2,1)}, u32[]{:S(2)}) copy-start(bf16[128,2048]{1,0:T(8,128)(2,1)} %add_convert_fusion.6.refs_0_) | copy-start | bytes 1572868
  103.6 23.9 %collective-permute-start.11 = (bf16[4,96,2048]{2,1,0:T(8,128)(2,1)S(1)}, bf16[4,96,2048]{2,1,0:T(8,128)(2,1)S(1)}, u32[]{:S(2)}, u32[]{:S(2)}) collective-permute-start(bf16[4,96,2048]{2,1,0:T(8,128)(2,1)S(1)} %get-tuple-element.49), channel_id=1, source_target_pairs={{0,1},{1,0},{2,3},{3,2},{4,5},{5,4},{6,7},{7,6},{8,9},{9,8},{10,11... | collective-permute-start | bytes 4718600 | tf_op jit(solution)/shard_map/ppermute | solution.py:824
  127.4 6.0 %collective-permute-start.10 = (bf16[4,96,2048]{2,1,0:T(8,128)(2,1)S(1)}, bf16[4,96,2048]{2,1,0:T(8,128)(2,1)S(1)}, u32[]{:S(2)}, u32[]{:S(2)}) collective-permute-start(bf16[4,96,2048]{2,1,0:T(8,128)(2,1)S(1)} %get-tuple-element.48), channel_id=1, source_target_pairs={{0,1},{1,0},{2,3},{3,2},{4,5},{5,4},{6,7},{7,6},{8,9},{9,8},{10,11... | collective-permute-start | bytes 4718600 | tf_op jit(solution)/shard_map/ppermute | solution.py:824
  127.5 2.8 %copy-start.1 = (bf16[16,96,2048]{2,1,0:T(8,128)(2,1)S(1)}, bf16[16,96,2048]{2,1,0:T(8,128)(2,1)}, u32[]{:S(2)}) copy-start(bf16[16,96,2048]{2,1,0:T(8,128)(2,1)} %get-tuple-element.50._z) | copy-start | bytes 18874372
  133.4 5.8 %copy-start.15 = (s32[2,16,128]{2,1,0:T(8,128)S(1)}, s32[2,16,128]{2,1,0:T(8,128)}, u32[]{:S(2)}) copy-start(s32[2,16,128]{2,1,0:T(8,128)} %get-tuple-element.36.rank_ref) | copy-start | bytes 49156
  133.4 5.8 %copy-start.17 = (f32[2,16,128]{2,1,0:T(8,128)S(1)}, f32[2,16,128]{2,1,0:T(8,128)}, u32[]{:S(2)}) copy-start(f32[2,16,128]{2,1,0:T(8,128)} %get-tuple-element.37.gate_ref) | copy-start | bytes 49156
  136.6 2.7 %copy-start.2 = (bf16[16,96,2048]{2,1,0:T(8,128)(2,1)}, bf16[16,96,2048]{2,1,0:T(8,128)(2,1)S(1)}, u32[]{:S(2)}) copy-start(bf16[16,96,2048]{2,1,0:T(8,128)(2,1)S(1)} %get-tuple-element.67) | copy-start | bytes 18874372
  143.2 5.9 %collective-permute-start.12 = (bf16[8,96,2048]{2,1,0:T(8,128)(2,1)S(1)}, bf16[8,96,2048]{2,1,0:T(8,128)(2,1)S(1)}, u32[]{:S(2)}, u32[]{:S(2)}) collective-permute-start(bf16[8,96,2048]{2,1,0:T(8,128)(2,1)S(1)} %forward_rows.3), channel_id=1, source_target_pairs={{0,1},{1,0},{2,3},{3,2},{4,5},{5,4},{6,7},{7,6},{8,9},{9,8},{10,11... | collective-permute-start | bytes 9437192 | tf_op jit(solution)/shard_map/ppermute | solution.py:824
  147.7 3.9 %copy-start.6 = (bf16[8,96,2048]{2,1,0:T(8,128)(2,1)}, bf16[8,96,2048]{2,1,0:T(8,128)(2,1)S(1)}, u32[]{:S(2)}) copy-start(bf16[8,96,2048]{2,1,0:T(8,128)(2,1)S(1)} %forward_rows.2.own_ref) | copy-start | bytes 9437188
  149.1 2.6 copy-start.4
  151.6 0.8 copy-start.21
  152.5 0.8 copy-start.25
  153.3 8.2 %copy-start.5 = (bf16[8,96,2048]{2,1,0:T(8,128)(2,1)S(1)}, bf16[8,96,2048]{2,1,0:T(8,128)(2,1)}, u32[]{:S(2)}) copy-start(bf16[8,96,2048]{2,1,0:T(8,128)(2,1)} %copy-done.4) | copy-start | bytes 9437188
  153.3 19.3 %collective-permute-start.16 = (bf16[128,2048]{1,0:T(8,128)(2,1)}, bf16[128,2048]{1,0:T(8,128)(2,1)}, u32[]{:S(2)}, u32[]{:S(2)}) collective-permute-start(bf16[128,2048]{1,0:T(8,128)(2,1)} %get-tuple-element.63), channel_id=1, source_target_pairs={{0,2},{1,3},{2,0},{3,1},{4,6},{5,7},{6,4},{7,5},{8,10},{9,11},{10,... | collective-permute-start | bytes 1572872 | tf_op jit(solution)/shard_map/ppermute | solution.py:824
  153.7 97.1 %all-to-all-start.2 = ((bf16[16,96,768]{2,1,0:T(8,128)(2,1)}), bf16[16,96,768]{2,1,0:T(8,128)(2,1)}, u32[]{:S(2)}, u32[]{:S(2)}) async-start(bf16[16,96,768]{2,1,0:T(8,128)(2,1)} %get-tuple-element.54), calls=%async_computation.2 | async-start | bytes 4718592 | tf_op jit(solution)/shard_map/all_to_all | solution.py:872
  159.6 40.0 %collective-permute-start.15 = (bf16[128,2048]{1,0:T(8,128)(2,1)}, bf16[128,2048]{1,0:T(8,128)(2,1)S(1)}, u32[]{:S(2)}, u32[]{:S(2)}) collective-permute-start(bf16[128,2048]{1,0:T(8,128)(2,1)} %copy-done.25), channel_id=1, source_target_pairs={{0,2},{1,3},{2,0},{3,1},{4,6},{5,7},{6,4},{7,5},{8,10},{9,11},{10,... | collective-permute-start | bytes 1572872 | tf_op jit(solution)/shard_map/ppermute | solution.py:824
  161.5 1.9 copy-start.7
  164.9 7.6 %copy-start.9 = (bf16[128,2048]{1,0:T(8,128)(2,1)}, bf16[128,2048]{1,0:T(8,128)(2,1)S(1)}, u32[]{:S(2)}) copy-start(bf16[128,2048]{1,0:T(8,128)(2,1)S(1)} %get-tuple-element.62) | copy-start | bytes 1572868
  165.0 45.1 %copy-start.11 = (bf16[128,2048]{1,0:T(8,128)(2,1)}, bf16[128,2048]{1,0:T(8,128)(2,1)S(1)}, u32[]{:S(2)}) copy-start(bf16[128,2048]{1,0:T(8,128)(2,1)S(1)} %get-tuple-element.56) | copy-start | bytes 1572868
  165.0 45.1 %copy-start.13 = (bf16[128,2048]{1,0:T(8,128)(2,1)}, bf16[128,2048]{1,0:T(8,128)(2,1)S(1)}, u32[]{:S(2)}) copy-start(bf16[128,2048]{1,0:T(8,128)(2,1)S(1)} %get-tuple-element.58) | copy-start | bytes 1572868
  165.0 52.0 %copy-start.30 = (f32[128,8]{0,1:T(8,128)S(1)}, f32[128,8]{0,1:T(8,128)}, u32[]{:S(2)}) copy-start(f32[128,8]{0,1:T(8,128)} %param.7) | copy-start | bytes 12292
  172.6 45.0 %copy-start.22 = (bf16[128,2048]{1,0:T(8,128)(2,1)S(1)}, bf16[128,2048]{1,0:T(8,128)(2,1)}, u32[]{:S(2)}) copy-start(bf16[128,2048]{1,0:T(8,128)(2,1)} %copy-done.21) | copy-start | bytes 1572868
  173.9 36.2 %collective-permute-start.17 = (bf16[128,2048]{1,0:T(8,128)(2,1)S(1)}, bf16[128,2048]{1,0:T(8,128)(2,1)S(1)}, u32[]{:S(2)}, u32[]{:S(2)}) collective-permute-start(bf16[128,2048]{1,0:T(8,128)(2,1)S(1)} %fusion.1), channel_id=1, source_target_pairs={{0,4},{1,5},{2,6},{3,7},{12,8},{13,9},{14,10},{15,11},{16,20},{17,... | collective-permute-start | bytes 1572872 | tf_op jit(solution)/shard_map/ppermute | solution.py:819
  176.5 43.4 %collective-permute-start.14 = (bf16[128,2048]{1,0:T(8,128)(2,1)}, bf16[128,2048]{1,0:T(8,128)(2,1)}, u32[]{:S(2)}, u32[]{:S(2)}) collective-permute-start(bf16[128,2048]{1,0:T(8,128)(2,1)} %get-tuple-element.59), channel_id=1, source_target_pairs={{0,2},{1,3},{2,0},{3,1},{4,6},{5,7},{6,4},{7,5},{8,10},{9,11},{10,... | collective-permute-start | bytes 1572872 | tf_op jit(solution)/shard_map/ppermute | solution.py:824
  210.0 28.1 %copy-start.10 = (bf16[128,2048]{1,0:T(8,128)(2,1)S(1)}, bf16[128,2048]{1,0:T(8,128)(2,1)}, u32[]{:S(2)}) copy-start(bf16[128,2048]{1,0:T(8,128)(2,1)} %copy-done.9) | copy-start | bytes 1572868
  210.3 15.8 %collective-permute-start.18 = (bf16[128,2048]{1,0:T(8,128)(2,1)S(1)}, bf16[128,2048]{1,0:T(8,128)(2,1)}, u32[]{:S(2)}, u32[]{:S(2)}) collective-permute-start(bf16[128,2048]{1,0:T(8,128)(2,1)S(1)} %add_convert_fusion.3), channel_id=1, source_target_pairs={{0,4},{1,5},{2,6},{3,7},{12,8},{13,9},{14,10},{15,11},{16,20},{17,... | collective-permute-start | bytes 1572872 | tf_op jit(solution)/shard_map/ppermute | solution.py:819
  215.6 22.6 %collective-permute-start.21 = (bf16[128,2048]{1,0:T(8,128)(2,1)S(1)}, bf16[128,2048]{1,0:T(8,128)(2,1)}, u32[]{:S(2)}, u32[]{:S(2)}) collective-permute-start(bf16[128,2048]{1,0:T(8,128)(2,1)S(1)} %add_convert_fusion.3), channel_id=1, source_target_pairs={{4,8},{5,9},{6,10},{7,11},{8,4},{9,5},{10,6},{11,7},{20,24},{21,25... | collective-permute-start | bytes 1572872 | tf_op jit(solution)/shard_map/ppermute | solution.py:819
  217.5 41.9 %collective-permute-start.13 = (bf16[128,2048]{1,0:T(8,128)(2,1)S(1)}, bf16[128,2048]{1,0:T(8,128)(2,1)S(1)}, u32[]{:S(2)}, u32[]{:S(2)}) collective-permute-start(bf16[128,2048]{1,0:T(8,128)(2,1)S(1)} %copy-done.22), channel_id=1, source_target_pairs={{0,2},{1,3},{2,0},{3,1},{4,6},{5,7},{6,4},{7,5},{8,10},{9,11},{10,... | collective-permute-start | bytes 1572872 | tf_op jit(solution)/shard_map/ppermute | solution.py:824
  228.5 31.0 %collective-permute-start.20 = (bf16[128,2048]{1,0:T(8,128)(2,1)}, bf16[128,2048]{1,0:T(8,128)(2,1)}, u32[]{:S(2)}, u32[]{:S(2)}) collective-permute-start(bf16[128,2048]{1,0:T(8,128)(2,1)} %add_convert_fusion.2), channel_id=1, source_target_pairs={{4,8},{5,9},{6,10},{7,11},{8,4},{9,5},{10,6},{11,7},{20,24},{21,25... | collective-permute-start | bytes 1572872 | tf_op jit(solution)/shard_map/ppermute | solution.py:819
  230.0 29.5 %collective-permute-start.19 = (bf16[128,2048]{1,0:T(8,128)(2,1)}, bf16[128,2048]{1,0:T(8,128)(2,1)}, u32[]{:S(2)}, u32[]{:S(2)}) collective-permute-start(bf16[128,2048]{1,0:T(8,128)(2,1)} %add_convert_fusion.2), channel_id=1, source_target_pairs={{0,4},{1,5},{2,6},{3,7},{12,8},{13,9},{14,10},{15,11},{16,20},{17,... | collective-permute-start | bytes 1572872 | tf_op jit(solution)/shard_map/ppermute | solution.py:819
  240.4 19.1 %collective-permute-start.22 = (bf16[128,2048]{1,0:T(8,128)(2,1)}, bf16[128,2048]{1,0:T(8,128)(2,1)}, u32[]{:S(2)}, u32[]{:S(2)}) collective-permute-start(bf16[128,2048]{1,0:T(8,128)(2,1)} %add_convert_fusion.1), channel_id=1, source_target_pairs={{4,0},{5,1},{6,2},{7,3},{8,12},{9,13},{10,14},{11,15},{20,16},{21,... | collective-permute-start | bytes 1572872 | tf_op jit(solution)/shard_map/ppermute | solution.py:819
  250.8 1.4 copy-start.19
  252.2 7.3 %copy-start.12 = (bf16[128,2048]{1,0:T(8,128)(2,1)S(1)}, bf16[128,2048]{1,0:T(8,128)(2,1)}, u32[]{:S(2)}) copy-start(bf16[128,2048]{1,0:T(8,128)(2,1)} %copy-done.11) | copy-start | bytes 1572868

commit v6 on v3

--- a/solution.py
+++ b/solution.py
@@ -405,7 +405,26 @@
     return lax.ppermute(value, "expert", [(i, i ^ bit) for i in range(devices)])
 
 
-OUTER, INNER, ENDS = ((0, 1), (3, 2)), ((1, 2), (2, 1)), ((1, 0), (2, 3))
+OUTER, INNER = ((0, 1), (3, 2)), ((1, 2), (2, 1))
+ENDS, ENDS_SWAP = ((1, 0), (2, 3)), ((0, 3), (3, 0))
+
+
+def gate_kernel(*refs):
+    pass
+
+
+def after(values, *waited):
+    count = len(values)
+    anywhere = pl.BlockSpec(memory_space=pl.ANY)
+    return pl.pallas_call(
+        gate_kernel,
+        in_specs=[anywhere] * (count + len(waited)),
+        out_specs=[anywhere] * count,
+        out_shape=[jax.ShapeDtypeStruct(value.shape, value.dtype) for value in values],
+        input_output_aliases={i: i for i in range(count)},
+        cost_estimate=pl.CostEstimate(flops=0, transcendentals=0, bytes_accessed=0),
+        name="after",
+    )(*values, *waited)
 
 
 def dense_shards(h_rows, gates, expert_ids, cotangent, down_weight, swapped):
@@ -417,27 +436,26 @@
     slot_ids = slots_of(expert_ids, swapped, devices)
     h_flat = h_rows.reshape(-1, hidden)
 
+    own = cotangent
+    from_end, from_inner, from_near_end = passed(OUTER, own), passed(INNER, own), passed(ENDS, own)
+    from_far_end = passed(ENDS_SWAP, own)
+    own_y = swapped_with(own, 2)
     routing = jnp.concatenate([slot_ids.T.astype(F32), gates.T], axis=0)
     routing = jnp.broadcast_to(routing, (devices,) + routing.shape)
     routing = lax.all_to_all(routing, "expert", split_axis=0, concat_axis=0, tiled=True)
+    place, send_h = pack(slot_ids.reshape(1, -1), h_flat, devices, capacity)
     rank, gate = route(here, routing, top)
-
-    own = cotangent
-    from_end = passed(OUTER, own)
-    from_inner = passed(INNER, own)
-    near = added(from_inner, passed(ENDS, own))
-    own_y = swapped_with(own, 2)
-    from_far = passed(INNER, from_end)
-    middle = added(from_far, passed(ENDS, from_inner))
+    near, last = added(from_inner, from_near_end), added(from_end, from_far_end)
+    from_end, from_inner = after((from_end, from_inner), send_h, rank, own_y)
+    middle_inner, middle_end = passed(INNER, from_end), passed(ENDS, from_inner)
     near_y = swapped_with(near, 2)
-    last = added(from_end, passed(ENDS, from_far))
-    middle_y = swapped_with(middle, 2)
-    last_y = swapped_with(last, 2)
-
-    place, send_h = pack(slot_ids.reshape(1, -1), h_flat, devices, capacity)
+    middle = added(middle_inner, middle_end)
+    send_h, = after((send_h,), middle, near_y)
     rows_h = lax.all_to_all(
         send_h.reshape(devices, capacity, hidden), "expert", split_axis=0, concat_axis=0, tiled=True
     )
+    last_y = swapped_with(last, 2)
+    middle_y = swapped_with(middle, 2)
 
     z_rows, back, sibling = scaled_rows(here, rank, gate, weight, [own, own_y, near, near_y], (0, 1), capacity, [])
     sibling = swapped_with(sibling, 1)
@@ -449,18 +467,19 @@
     z_rows, back = sibling_rows(here, weight, sibling_last, (2, 3), z_rows, back)
     back_rows = lax.all_to_all(back, "expert", split_axis=0, concat_axis=0, tiled=True).reshape(-1, hidden)
 
+    rows_h, = after((rows_h,), last_y, middle_y, sibling)
     other = swapped_with(forward_rows(here, rank, gate, rows_h, weight, 1), 1)
     mine = forward_rows(here, rank, gate, rows_h, weight, 0)
     across = [swapped_with(part, 2) for part in summed(here, rank, mine, other, 1)]
     beside = summed(here, rank, mine, other, 0)
     far, mid, close, kept = zip(beside, across)
-    outer1 = passed(OUTER, added(*far))
-    mid = added(*mid, outer1)
-    outer2, inner2 = passed(OUTER, mid), passed(INNER, mid)
-    close = added(*close, outer2)
-    outer3, inner3 = passed(OUTER, close), passed(INNER, close)
-    ends3 = passed(ENDS, added(*far, inner2))
-    mixed = added(*kept, outer3, inner3, ends3)
+    far, mid, close = added(*far), added(*mid), added(*close)
+    ends = passed(ENDS_SWAP, far)
+    mid_outer, mid_inner = passed(OUTER, mid), passed(INNER, mid)
+    close_outer = passed(OUTER, close)
+    close_inner = passed(INNER, added(close, mid_outer))
+    far_ends = passed(ENDS, added(far, mid_inner))
+    mixed = added(*kept, ends, close_outer, close_inner, far_ends)
 
     grad_sum = lax.dot_general(
         rows_h.reshape(-1, hidden), z_rows.reshape(devices * capacity, -1), (((0,), (0,)), ((), ())),

time: 275 us -> 249 us (0.905)
  starting transfers between devices: 75.7 us -> 54.8 us
  waiting for transfers between devices: 116 us -> 105 us
  local copies, waits for them, and re-layouts: 15.1 us -> 20.5 us
    ppermute x12, waiting for transfers between devices: 88.4 us -> 23.6 us  [passed(): lax.ppermute(value, 'expert', [(a * 4 + lane, b * 4 + lane) for a, b in p...]
    ppermute x11, waiting for transfers between devices: 26.3 us -> 74.4 us  [swapped_with(): return lax.ppermute(value, 'expert', [(i, i ^ bit) for i in range(devices)])]
    all_to_all x1, starting transfers between devices: 18.5 us -> 6.44 us  [dense_shards(): lax.all_to_all(back, 'expert', split_axis=0, concat_axis=0, tiled=True)]
    all_to_all x1, waiting for transfers between devices: 1.46 us -> 7.22 us  [dense_shards(): lax.all_to_all(routing, 'expert', split_axis=0, concat_axis=0, tiled=True)]
    unnamed x56 -> x58, local copies, waits for them, and re-layouts: 13.1 us -> 18.5 us
    ppermute x11, starting transfers between devices: 15 us -> 11.2 us  [swapped_with(): return lax.ppermute(value, 'expert', [(i, i ^ bit) for i in range(devices)])]
    all_to_all x1, starting transfers between devices: 7.39 us -> 3.69 us  [dense_shards(): lax.all_to_all(routing, 'expert', split_axis=0, concat_axis=0, tiled=True)]
    pallas_call x2, Pallas kernels: 10.2 us -> 6.8 us  [scaled_rows(): pl.pallas_call(functools.partial(scale_kernel, capacity, slots, len(buffe...]
  transfers between devices with their start and end apart: 26 -> 26, of which waited for: 9 -> 9; matrix products, arithmetic and copies ran while one was open for 8% -> 10% of each run, Pallas kernels for 15% -> 15%
where the time goes in v6:
time: 249 us; the launch traced here: 248 us
  waiting for transfers between devices  105 us (42%)
  starting transfers between devices  54.8 us (22%)
  Pallas kernels  42.7 us (17%)
  local copies, waits for them, and re-layouts  20.5 us (8%)
  other arithmetic  14.7 us (6%)
  matrix products  9.1 us (4%)
    ppermute x11, waiting for transfers between devices, swapped_with(): return lax.ppermute(value, 'expert', [(i, i ^ bit) for i in range(devices)])  74.4 us
    ppermute x12, starting transfers between devices, passed(): lax.ppermute(value, 'expert', [(a * 4 + lane, b * 4 + lane) for a, b in p...  28.4 us
    ppermute x12, waiting for transfers between devices, passed(): lax.ppermute(value, 'expert', [(a * 4 + lane, b * 4 + lane) for a, b in p...  23.6 us
    unnamed x58, local copies, waits for them, and re-layouts  18.5 us
    convert_element_type x7, other arithmetic, added(): return total.astype(BF16)  13 us
    ppermute x11, starting transfers between devices, swapped_with(): return lax.ppermute(value, 'expert', [(i, i ^ bit) for i in range(devices)])  11.2 us
    pallas_call x2, Pallas kernels, forward_rows(): pl.pallas_call(functools.partial(forward_kernel, capacity, turn), grid_sp...  9.18 us
    dot_general x1, matrix products, dense_shards(): lax.dot_general(rows_h.reshape(-1, hidden), z_rows.reshape(devices * capa...  9.1 us
  transfers between devices with their start and end apart: 26, of which 9 were waited for; matrix products, arithmetic and copies ran while one was open for 10% of the time, Pallas kernels for 15%

profile of v6, /device:TPU:0, one launch (start us, length us, event | category | flops | bytes accessed | tf_op | source)
XLA Modules:
  0.0 248.2 jit_solution(10132553670160750003)
XLA Ops:
  0.6 5.0 %collective-permute-start = (bf16[128,2048]{1,0:T(8,128)(2,1)}, bf16[128,2048]{1,0:T(8,128)(2,1)S(1)}, u32[]{:S(2)}, u32[]{:S(2)}) collective-permute-start(bf16[128,2048]{1,0:T(8,128)(2,1)} %refs_0_.1), channel_id=1, source_target_pairs={{0,4},{1,5},{2,6},{3,7},{12,8},{13,9},{14,10},{15,11},{16,20},{17,... | collective-permute-start | bytes 1572872 | tf_op jit(solution)/shard_map/ppermute | solution.py:400
  5.6 4.4 %collective-permute-start.7 = (bf16[128,2048]{1,0:T(8,128)(2,1)}, bf16[128,2048]{1,0:T(8,128)(2,1)}, u32[]{:S(2)}, u32[]{:S(2)}) collective-permute-start(bf16[128,2048]{1,0:T(8,128)(2,1)} %refs_0_.1), channel_id=1, source_target_pairs={{0,12},{1,13},{2,14},{3,15},{12,0},{13,1},{14,2},{15,3},{16,28},{1... | collective-permute-start | bytes 1572872 | tf_op jit(solution)/shard_map/ppermute | solution.py:400
  10.7 0.8 select_reduce_fusion
  11.5 0.7 pad_maximum_fusion
  12.9 3.7 %all-to-all-start = ((f32[16,16,128]{2,1,0:T(8,128)}), f32[16,16,128]{2,1,0:T(8,128)S(1)}, u32[]{:S(2)}, u32[]{:S(2)}) async-start(f32[16,16,128]{2,1,0:T(8,128)} %broadcast_in_dim.19), calls=%async_computation | async-start | bytes 262144 | tf_op jit(solution)/shard_map/all_to_all | solution.py:445
  16.6 0.7 collective-permute-start.1
  17.3 1.3 collective-permute-start.5
  18.6 2.0 collective-permute-start.2
  20.8 1.4 copy-done.21
  22.2 3.4 %pack.1 = (s32[1,1024]{1,0:T(1,128)S(1)}, bf16[1536,768]{1,0:T(8,128)(2,1)S(1)}) custom-call(s32[1,1024]{1,0:T(1,128)S(1)} %reshape.74.ids_ref, bf16[1024,768]{1,0:T(8,128)(2,1)S(1)} %bitcast.29), custom_call_target="tpu_custom_call" | custom-call | flops 2415919104 | bytes 3932160 | tf_op jit(solution)/shard_map/pack/pallas_call | solution.py:91
  25.6 1.4 copy-done.4
  27.0 7.2 %all-to-all-done.routing_ref = f32[16,16,128]{2,1,0:T(8,128)S(1)} async-done(((f32[16,16,128]{2,1,0:T(8,128)}), f32[16,16,128]{2,1,0:T(8,128)S(1)}, u32[]{:S(2)}, u32[]{:S(2)}) %all-to-all-start) | async-done | bytes 131104 | tf_op jit(solution)/shard_map/all_to_all | solution.py:445
  34.9 1.7 route.1
  36.6 2.2 add_convert_fusion.6.refs_2_
  38.7 5.2 %collective-permute-done.5 = bf16[128,2048]{1,0:T(8,128)(2,1)} collective-permute-done((bf16[128,2048]{1,0:T(8,128)(2,1)}, bf16[128,2048]{1,0:T(8,128)(2,1)}, u32[]{:S(2)}, u32[]{:S(2)}) %collective-permute-start.5) | collective-permute-done | bytes 524320 | tf_op jit(solution)/shard_map/ppermute | solution.py:400
  43.9 1.2 add_convert_fusion.7.refs_2_
  45.1 0.8 copy-done.13
  45.9 0.7 collective-permute-start.3
  46.6 1.3 collective-permute-start.4
  47.9 1.6 collective-permute-start.6
  49.5 0.8 copy-done.15
  50.3 13.0 %collective-permute-done.4 = bf16[128,2048]{1,0:T(8,128)(2,1)S(1)} collective-permute-done((bf16[128,2048]{1,0:T(8,128)(2,1)}, bf16[128,2048]{1,0:T(8,128)(2,1)S(1)}, u32[]{:S(2)}, u32[]{:S(2)}) %collective-permute-start.4) | collective-permute-done | bytes 524320 | tf_op jit(solution)/shard_map/ppermute | solution.py:400
  63.3 0.9 add_convert_fusion.8.refs_1_.refs_0_
  64.2 0.8 copy-done.17
  65.0 5.0 %all-to-all-start.1 = ((bf16[16,96,768]{2,1,0:T(8,128)(2,1)}), bf16[16,96,768]{2,1,0:T(8,128)(2,1)}, u32[]{:S(2)}, u32[]{:S(2)}) async-start(bf16[16,96,768]{2,1,0:T(8,128)(2,1)} %bitcast.27), calls=%async_computation.1 | async-start | bytes 4718592 | tf_op jit(solution)/shard_map/all_to_all | solution.py:454
  70.1 1.0 copy-done.14
  71.1 1.0 copy-done.16
  72.1 1.0 copy-done.18
  73.2 1.0 copy-done.23
  74.2 3.4 %scaled_rows.2 = (bf16[16,96,2048]{2,1,0:T(8,128)(2,1)}, bf16[16,96,768]{2,1,0:T(8,128)(2,1)}, bf16[4,96,2048]{2,1,0:T(8,128)(2,1)S(1)}) custom-call(s32[1]{0:T(128)} %bitcast.here_ref, s32[2,16,128]{2,1,0:T(8,128)S(1)} %copy-done.19, f32[2,16,128]{2,1,0:T(8,128)S(1)} %copy-done.20, bf16[768,2048]{1,0:T(8,128)(2,1)S(1)} %bitcast.21, ...), custom_call_target="tpu_custom_call" | custom-call | flops 1610612736 | bytes 8978432 | tf_op jit(solution)/shard_map/scaled_rows/pallas_call | solution.py:244
  78.0 1.7 collective-permute-start.8
  80.1 24.6 %collective-permute-done.8.refs_1_.refs_3_ = bf16[128,2048]{1,0:T(8,128)(2,1)S(1)} collective-permute-done((bf16[128,2048]{1,0:T(8,128)(2,1)S(1)}, bf16[128,2048]{1,0:T(8,128)(2,1)S(1)}, u32[]{:S(2)}, u32[]{:S(2)}) %collective-permute-start.8) | collective-permute-done | bytes 524320 | tf_op jit(solution)/shard_map/ppermute | solution.py:405
  104.7 16.2 %collective-permute-done.9.refs_2_.refs_1_ = bf16[128,2048]{1,0:T(8,128)(2,1)S(1)} collective-permute-done((bf16[128,2048]{1,0:T(8,128)(2,1)S(1)}, bf16[128,2048]{1,0:T(8,128)(2,1)S(1)}, u32[]{:S(2)}, u32[]{:S(2)}) %collective-permute-start.9) | collective-permute-done | bytes 524320 | tf_op jit(solution)/shard_map/ppermute | solution.py:405
  120.9 0.8 copy-done.9
  121.7 5.2 %forward_rows.3 = bf16[8,96,2048]{2,1,0:T(8,128)(2,1)} custom-call(s32[1]{0:T(128)} %bitcast.here_ref, s32[2,16,128]{2,1,0:T(8,128)S(1)} %copy-done.19, f32[2,16,128]{2,1,0:T(8,128)S(1)} %copy-done.20, bf16[8,2,96,768]{3,2,1,0:T(8,128)(2,1)} %bitcast.7.h_ref, bf16[768,2048]{1,0:T(8,128)(2,1)S(1)} %bitcast.22), custom_call_target="tpu_custom_call" | custom-call | flops 2415919104 | bytes 7471104 | tf_op jit(solution)/shard_map/forward_rows/pallas_call | solution.py:320
  127.0 3.4 %scaled_rows.3 = (bf16[16,96,2048]{2,1,0:T(8,128)(2,1)}, bf16[16,96,768]{2,1,0:T(8,128)(2,1)}, bf16[4,96,2048]{2,1,0:T(8,128)(2,1)S(1)}) custom-call(s32[1]{0:T(128)} %bitcast.here_ref, s32[2,16,128]{2,1,0:T(8,128)S(1)} %copy-done.19, f32[2,16,128]{2,1,0:T(8,128)S(1)} %copy-done.20, ...), custom_call_target="tpu_custom_call", output_to_operand_aliasing={{0}: (8, {}), {1}: (9, {})} | custom-call | flops 1610612736 | bytes 8978432 | tf_op jit(solution)/shard_map/scaled_rows/pallas_call | solution.py:244
  130.3 0.7 collective-permute-start.22
  131.0 2.8 %copy-done.1 = bf16[16,96,2048]{2,1,0:T(8,128)(2,1)S(1)} copy-done((bf16[16,96,2048]{2,1,0:T(8,128)(2,1)S(1)}, bf16[16,96,2048]{2,1,0:T(8,128)(2,1)}, u32[]{:S(2)}) %copy-start.1) | copy-done | bytes 6291480
  133.8 4.5 %sibling_rows.2 = (bf16[16,96,2048]{2,1,0:T(8,128)(2,1)S(1)}, bf16[16,96,768]{2,1,0:T(8,128)(2,1)}) custom-call(s32[1]{0:T(128)} %bitcast.here_ref, bf16[768,2048]{1,0:T(8,128)(2,1)S(1)} %bitcast.24, bf16[4,96,2048]{2,1,0:T(8,128)(2,1)} %collective-permute-done.10.refs_3_.rows_ref, ...), custom_call_target="tpu_custom_call", output_to_operand_aliasing={{0}: (3, {}), {1}: (4, {})} | custom-call | flops 1207959552 | bytes 6881280 | tf_op jit(solution)/shard_map/sibling_rows/pallas_call | solution.py:285
  138.3 3.2 %sibling_rows.3 = (bf16[16,96,2048]{2,1,0:T(8,128)(2,1)S(1)}, bf16[16,96,768]{2,1,0:T(8,128)(2,1)}) custom-call(s32[1]{0:T(128)} %bitcast.here_ref, bf16[768,2048]{1,0:T(8,128)(2,1)S(1)} %bitcast.25, bf16[4,96,2048]{2,1,0:T(8,128)(2,1)S(1)} %collective-permute-done.22.rows_ref, ...), custom_call_target="tpu_custom_call", output_to_operand_aliasing={{0}: (3, {}), {1}: (4, {})} | custom-call | flops 1207959552 | bytes 6881280 | tf_op jit(solution)/shard_map/sibling_rows/pallas_call | solution.py:285
  141.5 2.6 %copy-done.2 = bf16[16,96,2048]{2,1,0:T(8,128)(2,1)} copy-done((bf16[16,96,2048]{2,1,0:T(8,128)(2,1)}, bf16[16,96,2048]{2,1,0:T(8,128)(2,1)S(1)}, u32[]{:S(2)}) %copy-start.2) | copy-done | bytes 6291480
  144.1 6.4 %all-to-all-start.2 = ((bf16[16,96,768]{2,1,0:T(8,128)(2,1)}), bf16[16,96,768]{2,1,0:T(8,128)(2,1)}, u32[]{:S(2)}, u32[]{:S(2)}) async-start(bf16[16,96,768]{2,1,0:T(8,128)(2,1)} %get-tuple-element.52), calls=%async_computation.2 | async-start | bytes 4718592 | tf_op jit(solution)/shard_map/all_to_all | solution.py:468
  150.6 4.0 %forward_rows.2.own_ref = bf16[8,96,2048]{2,1,0:T(8,128)(2,1)S(1)} custom-call(s32[1]{0:T(128)} %bitcast.here_ref, s32[2,16,128]{2,1,0:T(8,128)S(1)} %copy-done.19, f32[2,16,128]{2,1,0:T(8,128)S(1)} %copy-done.20, bf16[8,2,96,768]{3,2,1,0:T(8,128)(2,1)} %bitcast.7.h_ref, bf16[768,2048]{1,0:T(8,128)(2,1)S(1)} %bitcast.26), custom_call_target="tpu_custom_call" | custom-call | flops 2415919104 | bytes 7471104 | tf_op jit(solution)/shard_map/forward_rows/pallas_call | solution.py:320
  154.5 4.4 %summed.3 = (bf16[128,2048]{1,0:T(8,128)(2,1)}, bf16[128,2048]{1,0:T(8,128)(2,1)S(1)}, bf16[128,2048]{1,0:T(8,128)(2,1)}, bf16[128,2048]{1,0:T(8,128)(2,1)S(1)}) custom-call(s32[1]{0:T(128)} %bitcast.here_ref, s32[2,16,128]{2,1,0:T(8,128)S(1)} %copy-done.19, bf16[8,96,2048]{2,1,0:T(8,128)(2,1)S(1)} %forward_rows.2.own_ref, ...), custom_call_target="tpu_custom_call" | custom-call | flops 402653184 | bytes 5242880 | tf_op jit(solution)/shard_map/summed/pallas_call | solution.py:370
  158.9 1.9 collective-permute-start.17
  161.0 3.4 %summed.2 = (bf16[128,2048]{1,0:T(8,128)(2,1)S(1)}, bf16[128,2048]{1,0:T(8,128)(2,1)S(1)}, bf16[128,2048]{1,0:T(8,128)(2,1)S(1)}, bf16[128,2048]{1,0:T(8,128)(2,1)S(1)}) custom-call(s32[1]{0:T(128)} %bitcast.here_ref, s32[2,16,128]{2,1,0:T(8,128)S(1)} %copy-done.19, bf16[8,96,2048]{2,1,0:T(8,128)(2,1)S(1)} %forward_rows.2.own_ref, ...), custom_call_target="tpu_custom_call" | custom-call | flops 402653184 | bytes 5242880 | tf_op jit(solution)/shard_map/summed/pallas_call | solution.py:370
  164.4 21.4 %collective-permute-done.17 = bf16[128,2048]{1,0:T(8,128)(2,1)S(1)} collective-permute-done((bf16[128,2048]{1,0:T(8,128)(2,1)S(1)}, bf16[128,2048]{1,0:T(8,128)(2,1)S(1)}, u32[]{:S(2)}, u32[]{:S(2)}) %collective-permute-start.17) | collective-permute-done | bytes 524320 | tf_op jit(solution)/shard_map/ppermute | solution.py:405
  185.7 0.9 add_convert_fusion.3
  186.7 2.2 collective-permute-start.18
  188.8 2.5 collective-permute-start.13
  191.3 1.4 collective-permute-start.20
  193.4 8.6 %collective-permute-done.15 = bf16[128,2048]{1,0:T(8,128)(2,1)} collective-permute-done((bf16[128,2048]{1,0:T(8,128)(2,1)}, bf16[128,2048]{1,0:T(8,128)(2,1)}, u32[]{:S(2)}, u32[]{:S(2)}) %collective-permute-start.15) | collective-permute-done | bytes 524320 | tf_op jit(solution)/shard_map/ppermute | solution.py:405
  202.0 2.6 %add_convert_fusion.2 = (bf16[128,2048]{1,0:T(8,128)(2,1)}, bf16[128,2048]{1,0:T(8,128)(2,1)}) fusion(bf16[128,2048]{1,0:T(8,128)(2,1)} %collective-permute-done.18, bf16[128,2048]{1,0:T(8,128)(2,1)} %collective-permute-done.15, bf16[128,2048]{1,0:T(8,128)(2,1)S(1)} %get-tuple-element.40), kind=kLoop, calls=%fused_computation.5 | loop fusion | flops 2097152 | bytes 2621440 | tf_op jit(solution)/shard_map/convert_element_type | solution.py:396
  204.5 3.5 %collective-permute-start.16 = (bf16[128,2048]{1,0:T(8,128)(2,1)}, bf16[128,2048]{1,0:T(8,128)(2,1)S(1)}, u32[]{:S(2)}, u32[]{:S(2)}) collective-permute-start(bf16[128,2048]{1,0:T(8,128)(2,1)} %get-tuple-element.69), channel_id=1, source_target_pairs={{0,4},{1,5},{2,6},{3,7},{12,8},{13,9},{14,10},{15,11},{16,20},{17,... | collective-permute-start | bytes 1572872 | tf_op jit(solution)/shard_map/ppermute | solution.py:400
  208.1 1.5 collective-permute-start.19
  209.6 3.6 %collective-permute-done.13 = bf16[128,2048]{1,0:T(8,128)(2,1)} collective-permute-done((bf16[128,2048]{1,0:T(8,128)(2,1)}, bf16[128,2048]{1,0:T(8,128)(2,1)}, u32[]{:S(2)}, u32[]{:S(2)}) %collective-permute-start.13) | collective-permute-done | bytes 524320 | tf_op jit(solution)/shard_map/ppermute | solution.py:405
  213.2 2.5 add_convert_fusion.1
  215.7 5.2 %collective-permute-start.14 = (bf16[128,2048]{1,0:T(8,128)(2,1)}, bf16[128,2048]{1,0:T(8,128)(2,1)}, u32[]{:S(2)}, u32[]{:S(2)}) collective-permute-start(bf16[128,2048]{1,0:T(8,128)(2,1)} %get-tuple-element.71), channel_id=1, source_target_pairs={{0,12},{1,13},{2,14},{3,15},{12,0},{13,1},{14,2},{15,3},{16,28},{1... | collective-permute-start | bytes 1572872 | tf_op jit(solution)/shard_map/ppermute | solution.py:400
  220.8 1.3 collective-permute-start.21
  222.1 9.1 %fusion = bf16[1,768,2048]{2,1,0:T(8,128)(2,1)} fusion(bf16[16,96,768]{2,1,0:T(8,128)(2,1)} %after.5, bf16[16,96,2048]{2,1,0:T(8,128)(2,1)} %copy-done.2), kind=kOutput, calls=%fused_computation.2 | convolution fusion | flops 4833411072 | bytes 11796480 | tf_op jit(solution)/shard_map/dot_general | solution.py:484
  231.2 1.4 copy-done.22
  232.7 6.2 %unpack.1 = (bf16[1024,768]{1,0:T(8,128)(2,1)}, f32[1024,1]{1,0:T(8,128)S(1)}) custom-call(s32[1024,1]{1,0:T(8,128)S(1)} %copy.32.place_ref, f32[1024,1]{1,0:T(8,128)S(1)} %reshape.92.gate_ref, bf16[1024,768]{1,0:T(8,128)(2,1)S(1)} %bitcast.30, bf16[1536,768]{1,0:T(8,128)(2,1)} %bitcast.9.back_ref), custom_call_target="tpu_custom_call" | custom-call | flops 2415919104 | bytes 5505024 | tf_op jit(solution)/shard_map/unpack/pallas_call | solution.py:128
  239.9 5.5 %collective-permute-done.21 = bf16[128,2048]{1,0:T(8,128)(2,1)} collective-permute-done((bf16[128,2048]{1,0:T(8,128)(2,1)}, bf16[128,2048]{1,0:T(8,128)(2,1)}, u32[]{:S(2)}, u32[]{:S(2)}) %collective-permute-start.21) | collective-permute-done | bytes 524320 | tf_op jit(solution)/shard_map/ppermute | solution.py:400
  245.3 2.8 %add_convert_fusion = bf16[128,2048]{1,0:T(8,128)(2,1)} fusion(bf16[128,2048]{1,0:T(8,128)(2,1)} %collective-permute-done.21, bf16[128,2048]{1,0:T(8,128)(2,1)} %collective-permute-done.19, bf16[128,2048]{1,0:T(8,128)(2,1)S(1)} %collective-permute-done.16, bf16[128,2048]{1,0:T(8,128)(2,1)} %collective-permute-done.14, ...), kind=kLoop, calls=%fused_computation.3 | loop fusion | flops 3145728 | bytes 3670016 | tf_op jit(solution)/shard_map/convert_element_type | solution.py:396
  (82 shorter events, 4.8 us)
Async XLA Ops:
  0.6 9.4 %copy-start = (s32[8]{0:T(128)S(1)}, s32[8]{0:T(128)}, u32[]{:S(2)}) copy-start(s32[8]{0:T(128)} %param.11) | copy-start | bytes 100
  0.6 35.9 %collective-permute-start = (bf16[128,2048]{1,0:T(8,128)(2,1)}, bf16[128,2048]{1,0:T(8,128)(2,1)S(1)}, u32[]{:S(2)}, u32[]{:S(2)}) collective-permute-start(bf16[128,2048]{1,0:T(8,128)(2,1)} %refs_0_.1), channel_id=1, source_target_pairs={{0,4},{1,5},{2,6},{3,7},{12,8},{13,9},{14,10},{15,11},{16,20},{17,... | collective-permute-start | bytes 1572872 | tf_op jit(solution)/shard_map/ppermute | solution.py:400
  5.6 31.0 %collective-permute-start.7 = (bf16[128,2048]{1,0:T(8,128)(2,1)}, bf16[128,2048]{1,0:T(8,128)(2,1)}, u32[]{:S(2)}, u32[]{:S(2)}) collective-permute-start(bf16[128,2048]{1,0:T(8,128)(2,1)} %refs_0_.1), channel_id=1, source_target_pairs={{0,12},{1,13},{2,14},{3,15},{12,0},{13,1},{14,2},{15,3},{16,28},{1... | collective-permute-start | bytes 1572872 | tf_op jit(solution)/shard_map/ppermute | solution.py:400
  12.9 21.4 %all-to-all-start = ((f32[16,16,128]{2,1,0:T(8,128)}), f32[16,16,128]{2,1,0:T(8,128)S(1)}, u32[]{:S(2)}, u32[]{:S(2)}) async-start(f32[16,16,128]{2,1,0:T(8,128)} %broadcast_in_dim.19), calls=%async_computation | async-start | bytes 262144 | tf_op jit(solution)/shard_map/all_to_all | solution.py:445
  16.6 22.2 %collective-permute-start.1 = (bf16[128,2048]{1,0:T(8,128)(2,1)}, bf16[128,2048]{1,0:T(8,128)(2,1)S(1)}, u32[]{:S(2)}, u32[]{:S(2)}) collective-permute-start(bf16[128,2048]{1,0:T(8,128)(2,1)} %refs_0_.1), channel_id=1, source_target_pairs={{4,8},{5,9},{6,10},{7,11},{8,4},{9,5},{10,6},{11,7},{20,24},{21,25... | collective-permute-start | bytes 1572872 | tf_op jit(solution)/shard_map/ppermute | solution.py:400
  17.3 26.6 %collective-permute-start.5 = (bf16[128,2048]{1,0:T(8,128)(2,1)}, bf16[128,2048]{1,0:T(8,128)(2,1)}, u32[]{:S(2)}, u32[]{:S(2)}) collective-permute-start(bf16[128,2048]{1,0:T(8,128)(2,1)} %refs_0_.1), channel_id=1, source_target_pairs={{4,0},{5,1},{6,2},{7,3},{8,12},{9,13},{10,14},{11,15},{20,16},{21,... | collective-permute-start | bytes 1572872 | tf_op jit(solution)/shard_map/ppermute | solution.py:400
  18.6 26.5 %collective-permute-start.2 = (bf16[128,2048]{1,0:T(8,128)(2,1)}, bf16[128,2048]{1,0:T(8,128)(2,1)S(1)}, u32[]{:S(2)}, u32[]{:S(2)}) collective-permute-start(bf16[128,2048]{1,0:T(8,128)(2,1)} %refs_0_.1), channel_id=1, source_target_pairs={{0,2},{1,3},{2,0},{3,1},{4,6},{5,7},{6,4},{7,5},{8,10},{9,11},{10,... | collective-permute-start | bytes 1572872 | tf_op jit(solution)/shard_map/ppermute | solution.py:405
  20.7 1.4 copy-start.21
  25.6 1.4 copy-start.4
  34.2 0.7 copy-start.26
  36.6 8.5 %copy-start.24 = (bf16[128,2048]{1,0:T(8,128)(2,1)}, bf16[128,2048]{1,0:T(8,128)(2,1)S(1)}, u32[]{:S(2)}) copy-start(bf16[128,2048]{1,0:T(8,128)(2,1)S(1)} %collective-permute-done.refs_0_) | copy-start | bytes 1572868
  38.7 6.4 %copy-start.25 = (bf16[128,2048]{1,0:T(8,128)(2,1)}, bf16[128,2048]{1,0:T(8,128)(2,1)S(1)}, u32[]{:S(2)}) copy-start(bf16[128,2048]{1,0:T(8,128)(2,1)S(1)} %collective-permute-done.1.refs_1_) | copy-start | bytes 1572868
  45.1 0.8 copy-start.13
  45.9 4.4 %collective-permute-start.3 = (bf16[128,2048]{1,0:T(8,128)(2,1)}, bf16[128,2048]{1,0:T(8,128)(2,1)S(1)}, u32[]{:S(2)}, u32[]{:S(2)}) collective-permute-start(bf16[128,2048]{1,0:T(8,128)(2,1)} %get-tuple-element.33), channel_id=1, source_target_pairs={{4,8},{5,9},{6,10},{7,11},{8,4},{9,5},{10,6},{11,7},{20,24},{21,25... | collective-permute-start | bytes 1572872 | tf_op jit(solution)/shard_map/ppermute | solution.py:400
  46.6 16.7 %collective-permute-start.4 = (bf16[128,2048]{1,0:T(8,128)(2,1)}, bf16[128,2048]{1,0:T(8,128)(2,1)S(1)}, u32[]{:S(2)}, u32[]{:S(2)}) collective-permute-start(bf16[128,2048]{1,0:T(8,128)(2,1)} %get-tuple-element.34), channel_id=1, source_target_pairs={{4,0},{5,1},{6,2},{7,3},{8,12},{9,13},{10,14},{11,15},{20,16},{21,... | collective-permute-start | bytes 1572872 | tf_op jit(solution)/shard_map/ppermute | solution.py:400
  47.9 16.3 %collective-permute-start.6 = (bf16[128,2048]{1,0:T(8,128)(2,1)S(1)}, bf16[128,2048]{1,0:T(8,128)(2,1)S(1)}, u32[]{:S(2)}, u32[]{:S(2)}) collective-permute-start(bf16[128,2048]{1,0:T(8,128)(2,1)S(1)} %add_convert_fusion.7.refs_2_), channel_id=1, source_target_pairs={{0,2},{1,3},{2,0},{3,1},{4,6},{5,7},{6,4},{7,5},{8,10},{9,11},{10,... | collective-permute-start | bytes 1572872 | tf_op jit(solution)/shard_map/ppermute | solution.py:405
  49.5 0.8 copy-start.15
  64.2 0.8 copy-start.17
  65.0 5.0 %copy-start.3 = (bf16[1,768,2048]{2,1,0:T(8,128)(2,1)S(1)}, bf16[1,768,2048]{2,1,0:T(8,128)(2,1)}, u32[]{:S(2)}) copy-start(bf16[1,768,2048]{2,1,0:T(8,128)(2,1)} %param.10) | copy-start | bytes 9437188
  65.0 5.0 %copy-start.19 = (s32[2,16,128]{2,1,0:T(8,128)S(1)}, s32[2,16,128]{2,1,0:T(8,128)}, u32[]{:S(2)}) copy-start(s32[2,16,128]{2,1,0:T(8,128)} %get-tuple-element.30.refs_3_.rank_ref) | copy-start | bytes 49156
  65.0 5.0 %copy-start.20 = (f32[2,16,128]{2,1,0:T(8,128)S(1)}, f32[2,16,128]{2,1,0:T(8,128)}, u32[]{:S(2)}) copy-start(f32[2,16,128]{2,1,0:T(8,128)} %get-tuple-element.31.gate_ref) | copy-start | bytes 49156
  65.0 56.6 %all-to-all-start.1 = ((bf16[16,96,768]{2,1,0:T(8,128)(2,1)}), bf16[16,96,768]{2,1,0:T(8,128)(2,1)}, u32[]{:S(2)}, u32[]{:S(2)}) async-start(bf16[16,96,768]{2,1,0:T(8,128)(2,1)} %bitcast.27), calls=%async_computation.1 | async-start | bytes 4718592 | tf_op jit(solution)/shard_map/all_to_all | solution.py:454
  70.0 1.0 copy-start.14
  71.1 1.0 copy-start.16
  72.1 1.0 copy-start.18
  73.2 1.0 copy-start.23
  74.2 3.8 %copy-start.11 = (bf16[128,2048]{1,0:T(8,128)(2,1)S(1)}, bf16[128,2048]{1,0:T(8,128)(2,1)}, u32[]{:S(2)}) copy-start(bf16[128,2048]{1,0:T(8,128)(2,1)} %add_convert_fusion.6.refs_2_) | copy-start | bytes 1572868
  74.2 5.5 %copy-start.5 = (bf16[128,2048]{1,0:T(8,128)(2,1)S(1)}, bf16[128,2048]{1,0:T(8,128)(2,1)}, u32[]{:S(2)}) copy-start(bf16[128,2048]{1,0:T(8,128)(2,1)} %add_convert_fusion.8.refs_1_.refs_0_) | copy-start | bytes 1572868
  77.7 44.0 %collective-permute-start.10 = (bf16[4,96,2048]{2,1,0:T(8,128)(2,1)S(1)}, bf16[4,96,2048]{2,1,0:T(8,128)(2,1)}, u32[]{:S(2)}, u32[]{:S(2)}) collective-permute-start(bf16[4,96,2048]{2,1,0:T(8,128)(2,1)S(1)} %get-tuple-element.35), channel_id=1, source_target_pairs={{0,1},{1,0},{2,3},{3,2},{4,5},{5,4},{6,7},{7,6},{8,9},{9,8},{10,11... | collective-permute-start | bytes 4718600 | tf_op jit(solution)/shard_map/ppermute | solution.py:405
  78.0 26.6 %collective-permute-start.8 = (bf16[128,2048]{1,0:T(8,128)(2,1)S(1)}, bf16[128,2048]{1,0:T(8,128)(2,1)S(1)}, u32[]{:S(2)}, u32[]{:S(2)}) collective-permute-start(bf16[128,2048]{1,0:T(8,128)(2,1)S(1)} %copy-done.11), channel_id=1, source_target_pairs={{0,2},{1,3},{2,0},{3,1},{4,6},{5,7},{6,4},{7,5},{8,10},{9,11},{10,... | collective-permute-start | bytes 1572872 | tf_op jit(solution)/shard_map/ppermute | solution.py:405
  79.7 41.1 %collective-permute-start.9 = (bf16[128,2048]{1,0:T(8,128)(2,1)S(1)}, bf16[128,2048]{1,0:T(8,128)(2,1)S(1)}, u32[]{:S(2)}, u32[]{:S(2)}) collective-permute-start(bf16[128,2048]{1,0:T(8,128)(2,1)S(1)} %copy-done.5), channel_id=1, source_target_pairs={{0,2},{1,3},{2,0},{3,1},{4,6},{5,7},{6,4},{7,5},{8,10},{9,11},{10,... | collective-permute-start | bytes 1572872 | tf_op jit(solution)/shard_map/ppermute | solution.py:405
  104.7 16.2 %copy-start.7 = (bf16[128,2048]{1,0:T(8,128)(2,1)}, bf16[128,2048]{1,0:T(8,128)(2,1)S(1)}, u32[]{:S(2)}) copy-start(bf16[128,2048]{1,0:T(8,128)(2,1)S(1)} %collective-permute-done.8.refs_1_.refs_3_) | copy-start | bytes 1572868
  120.9 0.8 copy-start.9
  121.7 5.3 %copy-start.6 = (bf16[128,2048]{1,0:T(8,128)(2,1)S(1)}, bf16[128,2048]{1,0:T(8,128)(2,1)}, u32[]{:S(2)}) copy-start(bf16[128,2048]{1,0:T(8,128)(2,1)} %add_convert_fusion.8.refs_1_.refs_0_) | copy-start | bytes 1572868
  121.7 5.3 %copy-start.8 = (bf16[128,2048]{1,0:T(8,128)(2,1)S(1)}, bf16[128,2048]{1,0:T(8,128)(2,1)}, u32[]{:S(2)}) copy-start(bf16[128,2048]{1,0:T(8,128)(2,1)} %copy-done.7) | copy-start | bytes 1572868
  121.7 5.3 %copy-start.10 = (bf16[128,2048]{1,0:T(8,128)(2,1)S(1)}, bf16[128,2048]{1,0:T(8,128)(2,1)}, u32[]{:S(2)}) copy-start(bf16[128,2048]{1,0:T(8,128)(2,1)} %copy-done.9) | copy-start | bytes 1572868
  121.7 5.3 %copy-start.12 = (bf16[128,2048]{1,0:T(8,128)(2,1)S(1)}, bf16[128,2048]{1,0:T(8,128)(2,1)}, u32[]{:S(2)}) copy-start(bf16[128,2048]{1,0:T(8,128)(2,1)} %add_convert_fusion.6.refs_2_) | copy-start | bytes 1572868
  126.9 27.6 %collective-permute-start.11 = (bf16[8,96,2048]{2,1,0:T(8,128)(2,1)}, bf16[8,96,2048]{2,1,0:T(8,128)(2,1)}, u32[]{:S(2)}, u32[]{:S(2)}) collective-permute-start(bf16[8,96,2048]{2,1,0:T(8,128)(2,1)} %forward_rows.3), channel_id=1, source_target_pairs={{0,1},{1,0},{2,3},{3,2},{4,5},{5,4},{6,7},{7,6},{8,9},{9,8},{10,11... | collective-permute-start | bytes 9437192 | tf_op jit(solution)/shard_map/ppermute | solution.py:405
  130.3 8.0 %collective-permute-start.22 = (bf16[4,96,2048]{2,1,0:T(8,128)(2,1)S(1)}, bf16[4,96,2048]{2,1,0:T(8,128)(2,1)S(1)}, u32[]{:S(2)}, u32[]{:S(2)}) collective-permute-start(bf16[4,96,2048]{2,1,0:T(8,128)(2,1)S(1)} %get-tuple-element.47), channel_id=1, source_target_pairs={{0,1},{1,0},{2,3},{3,2},{4,5},{5,4},{6,7},{7,6},{8,9},{9,8},{10,11... | collective-permute-start | bytes 4718600 | tf_op jit(solution)/shard_map/ppermute | solution.py:405
  131.0 2.8 %copy-start.1 = (bf16[16,96,2048]{2,1,0:T(8,128)(2,1)S(1)}, bf16[16,96,2048]{2,1,0:T(8,128)(2,1)}, u32[]{:S(2)}) copy-start(bf16[16,96,2048]{2,1,0:T(8,128)(2,1)} %get-tuple-element.48._z) | copy-start | bytes 18874372
  141.5 2.7 %copy-start.2 = (bf16[16,96,2048]{2,1,0:T(8,128)(2,1)}, bf16[16,96,2048]{2,1,0:T(8,128)(2,1)S(1)}, u32[]{:S(2)}) copy-start(bf16[16,96,2048]{2,1,0:T(8,128)(2,1)S(1)} %get-tuple-element.55) | copy-start | bytes 18874372
  144.1 87.1 %all-to-all-start.2 = ((bf16[16,96,768]{2,1,0:T(8,128)(2,1)}), bf16[16,96,768]{2,1,0:T(8,128)(2,1)}, u32[]{:S(2)}, u32[]{:S(2)}) async-start(bf16[16,96,768]{2,1,0:T(8,128)(2,1)} %get-tuple-element.52), calls=%async_computation.2 | async-start | bytes 4718592 | tf_op jit(solution)/shard_map/all_to_all | solution.py:468
  158.9 26.8 %collective-permute-start.17 = (bf16[128,2048]{1,0:T(8,128)(2,1)S(1)}, bf16[128,2048]{1,0:T(8,128)(2,1)S(1)}, u32[]{:S(2)}, u32[]{:S(2)}) collective-permute-start(bf16[128,2048]{1,0:T(8,128)(2,1)S(1)} %get-tuple-element.43), channel_id=1, source_target_pairs={{0,2},{1,3},{2,0},{3,1},{4,6},{5,7},{6,4},{7,5},{8,10},{9,11},{10,... | collective-permute-start | bytes 1572872 | tf_op jit(solution)/shard_map/ppermute | solution.py:405
  160.8 31.9 %copy-start.27 = (f32[128,8]{0,1:T(8,128)S(1)}, f32[128,8]{0,1:T(8,128)}, u32[]{:S(2)}) copy-start(f32[128,8]{0,1:T(8,128)} %param.7) | copy-start | bytes 12292
  160.8 41.2 %collective-permute-start.15 = (bf16[128,2048]{1,0:T(8,128)(2,1)}, bf16[128,2048]{1,0:T(8,128)(2,1)}, u32[]{:S(2)}, u32[]{:S(2)}) collective-permute-start(bf16[128,2048]{1,0:T(8,128)(2,1)} %get-tuple-element.41), channel_id=1, source_target_pairs={{0,2},{1,3},{2,0},{3,1},{4,6},{5,7},{6,4},{7,5},{8,10},{9,11},{10,... | collective-permute-start | bytes 1572872 | tf_op jit(solution)/shard_map/ppermute | solution.py:405
  186.7 15.3 %collective-permute-start.18 = (bf16[128,2048]{1,0:T(8,128)(2,1)}, bf16[128,2048]{1,0:T(8,128)(2,1)}, u32[]{:S(2)}, u32[]{:S(2)}) collective-permute-start(bf16[128,2048]{1,0:T(8,128)(2,1)} %add_convert_fusion.3), channel_id=1, source_target_pairs={{0,4},{1,5},{2,6},{3,7},{12,8},{13,9},{14,10},{15,11},{16,20},{17,... | collective-permute-start | bytes 1572872 | tf_op jit(solution)/shard_map/ppermute | solution.py:400
  188.8 24.4 %collective-permute-start.13 = (bf16[128,2048]{1,0:T(8,128)(2,1)}, bf16[128,2048]{1,0:T(8,128)(2,1)}, u32[]{:S(2)}, u32[]{:S(2)}) collective-permute-start(bf16[128,2048]{1,0:T(8,128)(2,1)} %get-tuple-element.39), channel_id=1, source_target_pairs={{0,2},{1,3},{2,0},{3,1},{4,6},{5,7},{6,4},{7,5},{8,10},{9,11},{10,... | collective-permute-start | bytes 1572872 | tf_op jit(solution)/shard_map/ppermute | solution.py:405
  191.3 21.9 %collective-permute-start.20 = (bf16[128,2048]{1,0:T(8,128)(2,1)}, bf16[128,2048]{1,0:T(8,128)(2,1)}, u32[]{:S(2)}, u32[]{:S(2)}) collective-permute-start(bf16[128,2048]{1,0:T(8,128)(2,1)} %add_convert_fusion.3), channel_id=1, source_target_pairs={{4,8},{5,9},{6,10},{7,11},{8,4},{9,5},{10,6},{11,7},{20,24},{21,25... | collective-permute-start | bytes 1572872 | tf_op jit(solution)/shard_map/ppermute | solution.py:400
  193.3 46.6 %collective-permute-start.12 = (bf16[128,2048]{1,0:T(8,128)(2,1)S(1)}, bf16[128,2048]{1,0:T(8,128)(2,1)}, u32[]{:S(2)}, u32[]{:S(2)}) collective-permute-start(bf16[128,2048]{1,0:T(8,128)(2,1)S(1)} %get-tuple-element.37), channel_id=1, source_target_pairs={{0,2},{1,3},{2,0},{3,1},{4,6},{5,7},{6,4},{7,5},{8,10},{9,11},{10,... | collective-permute-start | bytes 1572872 | tf_op jit(solution)/shard_map/ppermute | solution.py:405
  204.5 35.3 %collective-permute-start.16 = (bf16[128,2048]{1,0:T(8,128)(2,1)}, bf16[128,2048]{1,0:T(8,128)(2,1)S(1)}, u32[]{:S(2)}, u32[]{:S(2)}) collective-permute-start(bf16[128,2048]{1,0:T(8,128)(2,1)} %get-tuple-element.69), channel_id=1, source_target_pairs={{0,4},{1,5},{2,6},{3,7},{12,8},{13,9},{14,10},{15,11},{16,20},{17,... | collective-permute-start | bytes 1572872 | tf_op jit(solution)/shard_map/ppermute | solution.py:400
  208.1 31.8 %collective-permute-start.19 = (bf16[128,2048]{1,0:T(8,128)(2,1)}, bf16[128,2048]{1,0:T(8,128)(2,1)}, u32[]{:S(2)}, u32[]{:S(2)}) collective-permute-start(bf16[128,2048]{1,0:T(8,128)(2,1)} %get-tuple-element.68), channel_id=1, source_target_pairs={{4,8},{5,9},{6,10},{7,11},{8,4},{9,5},{10,6},{11,7},{20,24},{21,25... | collective-permute-start | bytes 1572872 | tf_op jit(solution)/shard_map/ppermute | solution.py:400
  215.7 24.2 %collective-permute-start.14 = (bf16[128,2048]{1,0:T(8,128)(2,1)}, bf16[128,2048]{1,0:T(8,128)(2,1)}, u32[]{:S(2)}, u32[]{:S(2)}) collective-permute-start(bf16[128,2048]{1,0:T(8,128)(2,1)} %get-tuple-element.71), channel_id=1, source_target_pairs={{0,12},{1,13},{2,14},{3,15},{12,0},{13,1},{14,2},{15,3},{16,28},{1... | collective-permute-start | bytes 1572872 | tf_op jit(solution)/shard_map/ppermute | solution.py:400
  220.8 24.5 %collective-permute-start.21 = (bf16[128,2048]{1,0:T(8,128)(2,1)}, bf16[128,2048]{1,0:T(8,128)(2,1)}, u32[]{:S(2)}, u32[]{:S(2)}) collective-permute-start(bf16[128,2048]{1,0:T(8,128)(2,1)} %get-tuple-element.70), channel_id=1, source_target_pairs={{4,0},{5,1},{6,2},{7,3},{8,12},{9,13},{10,14},{11,15},{20,16},{21,... | collective-permute-start | bytes 1572872 | tf_op jit(solution)/shard_map/ppermute | solution.py:400
  231.2 1.4 copy-start.22

commit v7 on v6

--- a/solution.py
+++ b/solution.py
@@ -104,7 +104,7 @@
             jax.ShapeDtypeStruct((devices * capacity, hidden), BF16),
         ],
         scratch_shapes=[pltpu.VMEM((1, pairs), jnp.int32)],
-        compiler_params=pltpu.CompilerParams(vmem_limit_bytes=48 * MIB),
+        compiler_params=pltpu.CompilerParams(vmem_limit_bytes=60 * MIB),
         cost_estimate=pl.CostEstimate(
             flops=2 * devices * capacity * pairs * hidden, transcendentals=0,
             bytes_accessed=2 * hidden * (pairs + devices * capacity),
@@ -142,7 +142,7 @@
             jax.ShapeDtypeStruct((pairs, hidden), BF16),
             jax.ShapeDtypeStruct((pairs, 1), F32),
         ],
-        compiler_params=pltpu.CompilerParams(vmem_limit_bytes=48 * MIB),
+        compiler_params=pltpu.CompilerParams(vmem_limit_bytes=60 * MIB),
         cost_estimate=pl.CostEstimate(
             flops=2 * slots * pairs * hidden, transcendentals=0,
             bytes_accessed=2 * hidden * (2 * pairs + slots),
@@ -240,7 +240,7 @@
     hidden, width = weight.shape
     count = len(blocks)
     tokens = blocks[0].shape[0]
-    vmem, anywhere = pl.BlockSpec(memory_space=pltpu.VMEM), pl.BlockSpec(memory_space=pl.ANY)
+    vmem, anywhere = pl.BlockSpec(memory_space=pltpu.VMEM), pl.BlockSpec(memory_space=pltpu.HBM)
     return pl.pallas_call(
         functools.partial(scale_kernel, capacity, slots, len(buffers)),
         in_specs=[pl.BlockSpec(memory_space=pltpu.SMEM)] + [vmem] * (3 + count) + [anywhere] * len(buffers),
@@ -257,7 +257,7 @@
             pltpu.SemaphoreType.DMA((count,)),
         ],
         input_output_aliases={4 + count + i: i for i in range(len(buffers))},
-        compiler_params=pltpu.CompilerParams(vmem_limit_bytes=40 * MIB),
+        compiler_params=pltpu.CompilerParams(vmem_limit_bytes=60 * MIB),
         cost_estimate=pl.CostEstimate(
             flops=2 * count * capacity * width * (hidden + 2 * tokens), transcendentals=0,
             bytes_accessed=2 * count * (tokens * width + capacity * (2 * width + hidden)) + 2 * width * hidden,
@@ -266,7 +266,7 @@
     )(here, rank, gate, weight, *blocks, *buffers)
 
 
-def sibling_kernel(capacity, slots, here_ref, weight_ref, rows_ref, _z, _back, z_ref, back_ref, back_scratch, z_sem, back_sem):
+def sibling_kernel(capacity, slots, here_ref, weight_ref, rows_ref, _z, _back, z_ref, back_ref, token_ref, back_scratch, z_sem, back_sem):
     count = 2 * len(slots)
     sources = lane_sources(here_ref[0], slots, 1 - here_ref[0] % 2)
     copies = place_out([(rows_ref.at[i], z_ref.at[source]) for i, source in enumerate(sources)], z_sem)
@@ -274,6 +274,7 @@
     back = lax.dot_general(flat, weight_ref[...], (((1,), (1,)), ((), ())), preferred_element_type=F32)
     back_scratch[...] = back.astype(BF16).reshape(back_scratch.shape)
     copies += place_out([(back_scratch.at[i], back_ref.at[source]) for i, source in enumerate(sources)], back_sem)
+    token_ref[...] = jnp.zeros_like(token_ref)
     for copy in copies:
         copy.wait()
 
@@ -281,19 +282,23 @@
 def sibling_rows(here, weight, rows, slots, z_rows, back):
     count, capacity, width = rows.shape
     hidden = weight.shape[0]
-    vmem, anywhere = pl.BlockSpec(memory_space=pltpu.VMEM), pl.BlockSpec(memory_space=pl.ANY)
+    vmem, anywhere = pl.BlockSpec(memory_space=pltpu.VMEM), pl.BlockSpec(memory_space=pltpu.HBM)
     return pl.pallas_call(
         functools.partial(sibling_kernel, capacity, slots),
         in_specs=[pl.BlockSpec(memory_space=pltpu.SMEM), vmem, vmem, anywhere, anywhere],
-        out_specs=[anywhere, anywhere],
-        out_shape=[jax.ShapeDtypeStruct(z_rows.shape, BF16), jax.ShapeDtypeStruct(back.shape, BF16)],
+        out_specs=[anywhere, anywhere, vmem],
+        out_shape=[
+            jax.ShapeDtypeStruct(z_rows.shape, BF16),
+            jax.ShapeDtypeStruct(back.shape, BF16),
+            jax.ShapeDtypeStruct((8, 128), F32),
+        ],
         scratch_shapes=[
             pltpu.VMEM((count, capacity, hidden), BF16),
             pltpu.SemaphoreType.DMA((count,)),
             pltpu.SemaphoreType.DMA((count,)),
         ],
         input_output_aliases={3: 0, 4: 1},
-        compiler_params=pltpu.CompilerParams(vmem_limit_bytes=40 * MIB),
+        compiler_params=pltpu.CompilerParams(vmem_limit_bytes=60 * MIB),
         cost_estimate=pl.CostEstimate(
             flops=2 * count * capacity * width * hidden, transcendentals=0,
             bytes_accessed=2 * count * capacity * (2 * width + hidden) + 2 * width * hidden,
@@ -331,7 +336,7 @@
             out_specs=pl.BlockSpec((each, capacity, width), lambda i, here: (i, 0, 0)),
         ),
         out_shape=jax.ShapeDtypeStruct((devices // 2, capacity, width), BF16),
-        compiler_params=pltpu.CompilerParams(vmem_limit_bytes=40 * MIB),
+        compiler_params=pltpu.CompilerParams(vmem_limit_bytes=60 * MIB),
         cost_estimate=pl.CostEstimate(
             flops=devices * capacity * width * hidden, transcendentals=0,
             bytes_accessed=devices * capacity * (width + hidden) + 2 * width * hidden,
@@ -380,7 +385,7 @@
             out_specs=[pl.BlockSpec((tokens, width), lambda i, here: (0, 0))] * len(ORDER),
         ),
         out_shape=[jax.ShapeDtypeStruct((tokens, width), BF16)] * len(ORDER),
-        compiler_params=pltpu.CompilerParams(vmem_limit_bytes=40 * MIB),
+        compiler_params=pltpu.CompilerParams(vmem_limit_bytes=60 * MIB),
         cost_estimate=pl.CostEstimate(
             flops=16 * tokens * capacity * width, transcendentals=0,
             bytes_accessed=8 * width * (tokens + 2 * capacity),
@@ -422,6 +427,7 @@
         out_specs=[anywhere] * count,
         out_shape=[jax.ShapeDtypeStruct(value.shape, value.dtype) for value in values],
         input_output_aliases={i: i for i in range(count)},
+        compiler_params=pltpu.CompilerParams(vmem_limit_bytes=60 * MIB),
         cost_estimate=pl.CostEstimate(flops=0, transcendentals=0, bytes_accessed=0),
         name="after",
     )(*values, *waited)
@@ -442,11 +448,13 @@
     own_y = swapped_with(own, 2)
     routing = jnp.concatenate([slot_ids.T.astype(F32), gates.T], axis=0)
     routing = jnp.broadcast_to(routing, (devices,) + routing.shape)
+    routing, flat_ids = after(
+        (routing, slot_ids.reshape(1, -1)), from_end, from_inner, from_near_end, from_far_end, own_y
+    )
     routing = lax.all_to_all(routing, "expert", split_axis=0, concat_axis=0, tiled=True)
-    place, send_h = pack(slot_ids.reshape(1, -1), h_flat, devices, capacity)
+    place, send_h = pack(flat_ids, h_flat, devices, capacity)
     rank, gate = route(here, routing, top)
     near, last = added(from_inner, from_near_end), added(from_end, from_far_end)
-    from_end, from_inner = after((from_end, from_inner), send_h, rank, own_y)
     middle_inner, middle_end = passed(INNER, from_end), passed(ENDS, from_inner)
     near_y = swapped_with(near, 2)
     middle = added(middle_inner, middle_end)
@@ -459,15 +467,15 @@
 
     z_rows, back, sibling = scaled_rows(here, rank, gate, weight, [own, own_y, near, near_y], (0, 1), capacity, [])
     sibling = swapped_with(sibling, 1)
+    z_rows, back, early = sibling_rows(here, weight, sibling, (0, 1), z_rows, back)
     z_rows, back, sibling_last = scaled_rows(
         here, rank, gate, weight, [middle, middle_y, last, last_y], (2, 3), capacity, [z_rows, back]
     )
     sibling_last = swapped_with(sibling_last, 1)
-    z_rows, back = sibling_rows(here, weight, sibling, (0, 1), z_rows, back)
-    z_rows, back = sibling_rows(here, weight, sibling_last, (2, 3), z_rows, back)
+    z_rows, back, _ = sibling_rows(here, weight, sibling_last, (2, 3), z_rows, back)
     back_rows = lax.all_to_all(back, "expert", split_axis=0, concat_axis=0, tiled=True).reshape(-1, hidden)
 
-    rows_h, = after((rows_h,), last_y, middle_y, sibling)
+    rows_h, = after((rows_h,), last_y, middle_y, early)
     other = swapped_with(forward_rows(here, rank, gate, rows_h, weight, 1), 1)
     mine = forward_rows(here, rank, gate, rows_h, weight, 0)
     across = [swapped_with(part, 2) for part in summed(here, rank, mine, other, 1)]

time: 249 us -> 245 us (0.984)
  Pallas kernels: 42.7 us -> 60.5 us
  waiting for transfers between devices: 105 us -> 88.8 us
  local copies, waits for them, and re-layouts: 20.5 us -> 10.9 us
  starting transfers between devices: 54.8 us -> 58.8 us
    ppermute x11, waiting for transfers between devices: 74.4 us -> 58.6 us  [swapped_with(): return lax.ppermute(value, 'expert', [(i, i ^ bit) for i in range(devices)])]
    unnamed x58 -> x46, local copies, waits for them, and re-layouts: 18.5 us -> 6.6 us
    all_to_all x1, waiting for transfers between devices: 7.22 us -> 0.01 us  [dense_shards(): lax.all_to_all(routing, 'expert', split_axis=0, concat_axis=0, tiled=True)]
    pallas_call x2, Pallas kernels: 6.8 us -> 13.6 us  [scaled_rows(): pl.pallas_call(functools.partial(scale_kernel, capacity, slots, len(buffe...]
    ppermute x12, waiting for transfers between devices: 23.6 us -> 30.2 us  [passed(): lax.ppermute(value, 'expert', [(a * 4 + lane, b * 4 + lane) for a, b in p...]
    pallas_call x2, Pallas kernels: 9.18 us -> 12.2 us  [forward_rows(): pl.pallas_call(functools.partial(forward_kernel, capacity, turn), grid_sp...]
    pallas_call x2, Pallas kernels: 7.63 us -> 10.5 us  [sibling_rows(): pl.pallas_call(functools.partial(sibling_kernel, capacity, slots), in_spe...]
    ppermute x12, starting transfers between devices: 28.4 us -> 31.3 us  [passed(): lax.ppermute(value, 'expert', [(a * 4 + lane, b * 4 + lane) for a, b in p...]
  transfers between devices with their start and end apart: 26 -> 26, of which waited for: 9 -> 11; matrix products, arithmetic and copies ran while one was open for 10% -> 11% of each run, Pallas kernels for 15% -> 22%
where the time goes in v7:
time: 245 us; the launch traced here: 244 us
  waiting for transfers between devices  88.8 us (36%)
  Pallas kernels  60.5 us (25%)
  starting transfers between devices  58.8 us (24%)
  other arithmetic  14.8 us (6%)
  local copies, waits for them, and re-layouts  10.9 us (4%)
  matrix products  9.32 us (4%)
    ppermute x11, waiting for transfers between devices, swapped_with(): return lax.ppermute(value, 'expert', [(i, i ^ bit) for i in range(devices)])  58.6 us
    ppermute x12, starting transfers between devices, passed(): lax.ppermute(value, 'expert', [(a * 4 + lane, b * 4 + lane) for a, b in p...  31.3 us
    ppermute x12, waiting for transfers between devices, passed(): lax.ppermute(value, 'expert', [(a * 4 + lane, b * 4 + lane) for a, b in p...  30.2 us
    pallas_call x2, Pallas kernels, scaled_rows(): pl.pallas_call(functools.partial(scale_kernel, capacity, slots, len(buffe...  13.6 us
    pallas_call x2, Pallas kernels, forward_rows(): pl.pallas_call(functools.partial(forward_kernel, capacity, turn), grid_sp...  12.2 us
    convert_element_type x7, other arithmetic, added(): return total.astype(BF16)  12 us
    ppermute x11, starting transfers between devices, swapped_with(): return lax.ppermute(value, 'expert', [(i, i ^ bit) for i in range(devices)])  10.8 us
    pallas_call x2, Pallas kernels, sibling_rows(): pl.pallas_call(functools.partial(sibling_kernel, capacity, slots), in_spe...  10.5 us
  transfers between devices with their start and end apart: 26, of which 11 were waited for; matrix products, arithmetic and copies ran while one was open for 11% of the time, Pallas kernels for 22%

profile of v7, /device:TPU:0, one launch (start us, length us, event | category | flops | bytes accessed | tf_op | source)
XLA Modules:
  0.0 244.0 jit_solution(8048013856188376894)
XLA Ops:
  0.6 5.0 %collective-permute-start = (bf16[128,2048]{1,0:T(8,128)(2,1)}, bf16[128,2048]{1,0:T(8,128)(2,1)S(1)}, u32[]{:S(2)}, u32[]{:S(2)}) collective-permute-start(bf16[128,2048]{1,0:T(8,128)(2,1)} %refs_0_.1), channel_id=1, source_target_pairs={{0,4},{1,5},{2,6},{3,7},{12,8},{13,9},{14,10},{15,11},{16,20},{17,... | collective-permute-start | bytes 1572872 | tf_op jit(solution)/shard_map/ppermute | solution.py:405
  5.6 0.7 collective-permute-start.1
  6.3 1.3 collective-permute-start.2
  7.6 4.4 %collective-permute-start.3 = (bf16[128,2048]{1,0:T(8,128)(2,1)}, bf16[128,2048]{1,0:T(8,128)(2,1)S(1)}, u32[]{:S(2)}, u32[]{:S(2)}) collective-permute-start(bf16[128,2048]{1,0:T(8,128)(2,1)} %refs_0_.1), channel_id=1, source_target_pairs={{0,12},{1,13},{2,14},{3,15},{12,0},{13,1},{14,2},{15,3},{16,28},{1... | collective-permute-start | bytes 1572872 | tf_op jit(solution)/shard_map/ppermute | solution.py:405
  12.0 1.6 collective-permute-start.4
  13.6 0.7 gather_fusion
  14.3 0.8 select_reduce_fusion
  15.2 0.7 reshape.74.refs_1_
  15.9 0.7 pad_maximum_fusion
  16.6 1.7 collective-permute-done.refs_2_
  18.2 14.8 %collective-permute-done.2.refs_4_ = bf16[128,2048]{1,0:T(8,128)(2,1)S(1)} collective-permute-done((bf16[128,2048]{1,0:T(8,128)(2,1)}, bf16[128,2048]{1,0:T(8,128)(2,1)S(1)}, u32[]{:S(2)}, u32[]{:S(2)}) %collective-permute-start.2) | collective-permute-done | bytes 524320 | tf_op jit(solution)/shard_map/ppermute | solution.py:405
  33.1 0.7 broadcast_in_dim.19.refs_0_
  34.2 4.8 %all-to-all-start = ((f32[16,16,128]{2,1,0:T(8,128)}), f32[16,16,128]{2,1,0:T(8,128)S(1)}, u32[]{:S(2)}, u32[]{:S(2)}) async-start(f32[16,16,128]{2,1,0:T(8,128)} %get-tuple-element.31), calls=%async_computation | async-start | bytes 262144 | tf_op jit(solution)/shard_map/all_to_all | solution.py:454
  39.1 0.7 collective-permute-start.5
  39.8 1.3 collective-permute-start.6
  41.1 1.3 add_convert_fusion.7.refs_2_
  42.4 2.0 collective-permute-start.7
  44.4 5.6 %pack.1 = (s32[1,1024]{1,0:T(1,128)}, bf16[1536,768]{1,0:T(8,128)(2,1)}) custom-call(s32[1,1024]{1,0:T(1,128)} %get-tuple-element.34.ids_ref, bf16[1024,768]{1,0:T(8,128)(2,1)} %bitcast.32), custom_call_target="tpu_custom_call" | custom-call | flops 2415919104 | bytes 3932160 | tf_op jit(solution)/shard_map/pack/pallas_call | solution.py:91
  50.0 7.8 %collective-permute-done.6 = bf16[128,2048]{1,0:T(8,128)(2,1)S(1)} collective-permute-done((bf16[128,2048]{1,0:T(8,128)(2,1)}, bf16[128,2048]{1,0:T(8,128)(2,1)S(1)}, u32[]{:S(2)}, u32[]{:S(2)}) %collective-permute-start.6) | collective-permute-done | bytes 524320 | tf_op jit(solution)/shard_map/ppermute | solution.py:405
  57.8 0.9 add_convert_fusion.8.refs_1_.refs_0_
  58.7 0.8 copy-done.19
  59.5 0.7 copy-done.17
  60.2 4.6 %all-to-all-start.1 = ((bf16[16,96,768]{2,1,0:T(8,128)(2,1)}), bf16[16,96,768]{2,1,0:T(8,128)(2,1)S(1)}, u32[]{:S(2)}, u32[]{:S(2)}) async-start(bf16[16,96,768]{2,1,0:T(8,128)(2,1)} %bitcast.29), calls=%async_computation.1 | async-start | bytes 4718592 | tf_op jit(solution)/shard_map/all_to_all | solution.py:462
  64.8 1.7 route.1
  66.5 6.9 %scaled_rows.2 = (bf16[16,96,2048]{2,1,0:T(8,128)(2,1)}, bf16[16,96,768]{2,1,0:T(8,128)(2,1)}, bf16[4,96,2048]{2,1,0:T(8,128)(2,1)}) custom-call(s32[1]{0:T(128)} %bitcast.here_ref, s32[2,16,128]{2,1,0:T(8,128)} %get-tuple-element.32.rank_ref, f32[2,16,128]{2,1,0:T(8,128)} %get-tuple-element.33.gate_ref, bf16[768,2048]{1,0:T(8,128)(2,1)} %bitcast.21, ...), custom_call_target="tpu_custom_call" | custom-call | flops 1610612736 | bytes 8978432 | tf_op jit(solution)/shard_map/scaled_rows/pallas_call | solution.py:244
  73.9 1.2 add_convert_fusion.6.refs_2_
  75.1 1.7 collective-permute-start.8
  77.2 5.3 %sibling_rows.2 = (bf16[16,96,2048]{2,1,0:T(8,128)(2,1)}, bf16[16,96,768]{2,1,0:T(8,128)(2,1)}, f32[8,128]{1,0:T(8,128)}) custom-call(s32[1]{0:T(128)} %bitcast.here_ref, bf16[768,2048]{1,0:T(8,128)(2,1)} %bitcast.22, bf16[4,96,2048]{2,1,0:T(8,128)(2,1)} %collective-permute-done.10.rows_ref, ...), custom_call_target="tpu_custom_call", output_to_operand_aliasing={{0}: (3, {}), {1}: (4, {})} | custom-call | flops 1207959552 | bytes 6881280 | tf_op jit(solution)/shard_map/sibling_rows/pallas_call | solution.py:286
  82.5 18.8 %collective-permute-done.8.refs_1_.refs_3_ = bf16[128,2048]{1,0:T(8,128)(2,1)S(1)} collective-permute-done((bf16[128,2048]{1,0:T(8,128)(2,1)S(1)}, bf16[128,2048]{1,0:T(8,128)(2,1)S(1)}, u32[]{:S(2)}, u32[]{:S(2)}) %collective-permute-start.8) | collective-permute-done | bytes 524320 | tf_op jit(solution)/shard_map/ppermute | solution.py:410
  101.3 14.5 %collective-permute-done.9.refs_2_.refs_1_ = bf16[128,2048]{1,0:T(8,128)(2,1)} collective-permute-done((bf16[128,2048]{1,0:T(8,128)(2,1)S(1)}, bf16[128,2048]{1,0:T(8,128)(2,1)}, u32[]{:S(2)}, u32[]{:S(2)}) %collective-permute-start.9) | collective-permute-done | bytes 524320 | tf_op jit(solution)/shard_map/ppermute | solution.py:410
  115.8 1.4 copy-done.2
  117.2 6.1 %forward_rows.3 = bf16[8,96,2048]{2,1,0:T(8,128)(2,1)} custom-call(s32[1]{0:T(128)} %bitcast.here_ref, s32[2,16,128]{2,1,0:T(8,128)} %get-tuple-element.32.rank_ref, f32[2,16,128]{2,1,0:T(8,128)} %get-tuple-element.33.gate_ref, bf16[8,2,96,768]{3,2,1,0:T(8,128)(2,1)} %bitcast.27, bf16[768,2048]{1,0:T(8,128)(2,1)} %bitcast.23), custom_call_target="tpu_custom_call" | custom-call | flops 2415919104 | bytes 7471104 | tf_op jit(solution)/shard_map/forward_rows/pallas_call | solution.py:325
  123.3 6.8 %scaled_rows.3 = (bf16[16,96,2048]{2,1,0:T(8,128)(2,1)}, bf16[16,96,768]{2,1,0:T(8,128)(2,1)}, bf16[4,96,2048]{2,1,0:T(8,128)(2,1)}) custom-call(s32[1]{0:T(128)} %bitcast.here_ref, s32[2,16,128]{2,1,0:T(8,128)} %get-tuple-element.32.rank_ref, f32[2,16,128]{2,1,0:T(8,128)} %get-tuple-element.33.gate_ref, ...), custom_call_target="tpu_custom_call", output_to_operand_aliasing={{0}: (8, {}), {1}: (9, {})} | custom-call | flops 1610612736 | bytes 8978432 | tf_op jit(solution)/shard_map/scaled_rows/pallas_call | solution.py:244
  130.7 3.4 %collective-permute-done.22.rows_ref = bf16[4,96,2048]{2,1,0:T(8,128)(2,1)} collective-permute-done((bf16[4,96,2048]{2,1,0:T(8,128)(2,1)}, bf16[4,96,2048]{2,1,0:T(8,128)(2,1)}, u32[]{:S(2)}, u32[]{:S(2)}) %collective-permute-start.22) | collective-permute-done | bytes 1572896 | tf_op jit(solution)/shard_map/ppermute | solution.py:410
  134.1 5.3 %sibling_rows.3 = (bf16[16,96,2048]{2,1,0:T(8,128)(2,1)}, bf16[16,96,768]{2,1,0:T(8,128)(2,1)}, f32[8,128]{1,0:T(8,128)}) custom-call(s32[1]{0:T(128)} %bitcast.here_ref, bf16[768,2048]{1,0:T(8,128)(2,1)} %bitcast.25, bf16[4,96,2048]{2,1,0:T(8,128)(2,1)} %collective-permute-done.22.rows_ref, ...), custom_call_target="tpu_custom_call", output_to_operand_aliasing={{0}: (3, {}), {1}: (4, {})} | custom-call | flops 1207959552 | bytes 6881280 | tf_op jit(solution)/shard_map/sibling_rows/pallas_call | solution.py:286
  139.3 7.3 %all-to-all-start.2 = ((bf16[16,96,768]{2,1,0:T(8,128)(2,1)}), bf16[16,96,768]{2,1,0:T(8,128)(2,1)}, u32[]{:S(2)}, u32[]{:S(2)}) async-start(bf16[16,96,768]{2,1,0:T(8,128)(2,1)} %get-tuple-element.54), calls=%async_computation.2 | async-start | bytes 4718592 | tf_op jit(solution)/shard_map/all_to_all | solution.py:476
  146.6 6.1 %forward_rows.2.own_ref = bf16[8,96,2048]{2,1,0:T(8,128)(2,1)} custom-call(s32[1]{0:T(128)} %bitcast.here_ref, s32[2,16,128]{2,1,0:T(8,128)} %get-tuple-element.32.rank_ref, f32[2,16,128]{2,1,0:T(8,128)} %get-tuple-element.33.gate_ref, bf16[8,2,96,768]{3,2,1,0:T(8,128)(2,1)} %bitcast.28, bf16[768,2048]{1,0:T(8,128)(2,1)} %bitcast.26), custom_call_target="tpu_custom_call" | custom-call | flops 2415919104 | bytes 7471104 | tf_op jit(solution)/shard_map/forward_rows/pallas_call | solution.py:325
  152.8 1.7 copy-done.1
  154.5 4.9 %summed.3 = (bf16[128,2048]{1,0:T(8,128)(2,1)}, bf16[128,2048]{1,0:T(8,128)(2,1)}, bf16[128,2048]{1,0:T(8,128)(2,1)}, bf16[128,2048]{1,0:T(8,128)(2,1)}) custom-call(s32[1]{0:T(128)} %bitcast.here_ref, s32[2,16,128]{2,1,0:T(8,128)} %get-tuple-element.32.rank_ref, bf16[8,96,2048]{2,1,0:T(8,128)(2,1)} %forward_rows.2.own_ref, bf16[8,96,2048]{2,1,0:T(8,128)(2,1)} %copy-done.1), custom_call_target="tpu_custom_call" | custom-call | flops 402653184 | bytes 5242880 | tf_op jit(solution)/shard_map/summed/pallas_call | solution.py:375
  159.4 1.9 collective-permute-start.17
  161.4 4.9 %summed.2 = (bf16[128,2048]{1,0:T(8,128)(2,1)}, bf16[128,2048]{1,0:T(8,128)(2,1)}, bf16[128,2048]{1,0:T(8,128)(2,1)}, bf16[128,2048]{1,0:T(8,128)(2,1)}) custom-call(s32[1]{0:T(128)} %bitcast.here_ref, s32[2,16,128]{2,1,0:T(8,128)} %get-tuple-element.32.rank_ref, bf16[8,96,2048]{2,1,0:T(8,128)(2,1)} %forward_rows.2.own_ref, bf16[8,96,2048]{2,1,0:T(8,128)(2,1)} %copy-done.1), custom_call_target="tpu_custom_call" | custom-call | flops 402653184 | bytes 5242880 | tf_op jit(solution)/shard_map/summed/pallas_call | solution.py:375
  166.4 17.1 %collective-permute-done.17 = bf16[128,2048]{1,0:T(8,128)(2,1)S(1)} collective-permute-done((bf16[128,2048]{1,0:T(8,128)(2,1)}, bf16[128,2048]{1,0:T(8,128)(2,1)S(1)}, u32[]{:S(2)}, u32[]{:S(2)}) %collective-permute-start.17) | collective-permute-done | bytes 524320 | tf_op jit(solution)/shard_map/ppermute | solution.py:410
  183.5 2.1 add_convert_fusion.3
  185.6 4.1 %collective-permute-start.18 = (bf16[128,2048]{1,0:T(8,128)(2,1)}, bf16[128,2048]{1,0:T(8,128)(2,1)S(1)}, u32[]{:S(2)}, u32[]{:S(2)}) collective-permute-start(bf16[128,2048]{1,0:T(8,128)(2,1)} %add_convert_fusion.3), channel_id=1, source_target_pairs={{0,4},{1,5},{2,6},{3,7},{12,8},{13,9},{14,10},{15,11},{16,20},{17,... | collective-permute-start | bytes 1572872 | tf_op jit(solution)/shard_map/ppermute | solution.py:405
  189.8 1.5 collective-permute-start.20
  191.4 1.0 reshape.92.gate_ref
  192.4 1.0 copy.32.place_ref
  193.4 2.0 collective-permute-start.12
  195.4 3.1 %collective-permute-done.15 = bf16[128,2048]{1,0:T(8,128)(2,1)S(1)} collective-permute-done((bf16[128,2048]{1,0:T(8,128)(2,1)}, bf16[128,2048]{1,0:T(8,128)(2,1)S(1)}, u32[]{:S(2)}, u32[]{:S(2)}) %collective-permute-start.15) | collective-permute-done | bytes 524320 | tf_op jit(solution)/shard_map/ppermute | solution.py:410
  198.5 1.2 collective-permute-done.18
  199.8 0.8 copy-done.16
  200.6 1.5 add_convert_fusion.2
  202.0 5.5 %collective-permute-start.16 = (bf16[128,2048]{1,0:T(8,128)(2,1)S(1)}, bf16[128,2048]{1,0:T(8,128)(2,1)S(1)}, u32[]{:S(2)}, u32[]{:S(2)}) collective-permute-start(bf16[128,2048]{1,0:T(8,128)(2,1)S(1)} %get-tuple-element.71), channel_id=1, source_target_pairs={{0,4},{1,5},{2,6},{3,7},{12,8},{13,9},{14,10},{15,11},{16,20},{17,... | collective-permute-start | bytes 1572872 | tf_op jit(solution)/shard_map/ppermute | solution.py:405
  207.5 0.7 collective-permute-start.19
  208.2 1.7 collective-permute-done.13
  209.9 2.5 %add_convert_fusion.1 = (bf16[128,2048]{1,0:T(8,128)(2,1)}, bf16[128,2048]{1,0:T(8,128)(2,1)}) fusion(bf16[128,2048]{1,0:T(8,128)(2,1)} %collective-permute-done.20, bf16[128,2048]{1,0:T(8,128)(2,1)} %collective-permute-done.13, bf16[128,2048]{1,0:T(8,128)(2,1)S(1)} %copy-done.13), kind=kLoop, calls=%fused_computation.4 | loop fusion | flops 2097152 | bytes 2621440 | tf_op jit(solution)/shard_map/convert_element_type | solution.py:401
  212.3 4.8 %collective-permute-start.14 = (bf16[128,2048]{1,0:T(8,128)(2,1)}, bf16[128,2048]{1,0:T(8,128)(2,1)}, u32[]{:S(2)}, u32[]{:S(2)}) collective-permute-start(bf16[128,2048]{1,0:T(8,128)(2,1)} %get-tuple-element.73), channel_id=1, source_target_pairs={{0,12},{1,13},{2,14},{3,15},{12,0},{13,1},{14,2},{15,3},{16,28},{1... | collective-permute-start | bytes 1572872 | tf_op jit(solution)/shard_map/ppermute | solution.py:405
  217.2 1.3 collective-permute-start.21
  218.5 9.3 %fusion = bf16[1,768,2048]{2,1,0:T(8,128)(2,1)} fusion(bf16[16,96,768]{2,1,0:T(8,128)(2,1)S(1)} %copy-done.3, bf16[16,96,2048]{2,1,0:T(8,128)(2,1)} %get-tuple-element.57), kind=kOutput, calls=%fused_computation.2 | convolution fusion | flops 4833411072 | bytes 11796480 | tf_op jit(solution)/shard_map/dot_general | solution.py:492
  227.8 7.0 %unpack.1 = (bf16[1024,768]{1,0:T(8,128)(2,1)}, f32[1024,1]{1,0:T(8,128)}) custom-call(s32[1024,1]{1,0:T(8,128)} %copy.32.place_ref, f32[1024,1]{1,0:T(8,128)} %reshape.92.gate_ref, bf16[1024,768]{1,0:T(8,128)(2,1)} %bitcast.33, bf16[1536,768]{1,0:T(8,128)(2,1)} %bitcast.9.back_ref), custom_call_target="tpu_custom_call" | custom-call | flops 2415919104 | bytes 5505024 | tf_op jit(solution)/shard_map/unpack/pallas_call | solution.py:128
  234.7 1.2 reduce
  236.1 0.7 copy.34
  236.8 4.7 %collective-permute-done.21 = bf16[128,2048]{1,0:T(8,128)(2,1)} collective-permute-done((bf16[128,2048]{1,0:T(8,128)(2,1)}, bf16[128,2048]{1,0:T(8,128)(2,1)}, u32[]{:S(2)}, u32[]{:S(2)}) %collective-permute-start.21) | collective-permute-done | bytes 524320 | tf_op jit(solution)/shard_map/ppermute | solution.py:405
  241.5 2.5 %add_convert_fusion = bf16[128,2048]{1,0:T(8,128)(2,1)} fusion(bf16[128,2048]{1,0:T(8,128)(2,1)} %collective-permute-done.21, bf16[128,2048]{1,0:T(8,128)(2,1)S(1)} %collective-permute-done.19, bf16[128,2048]{1,0:T(8,128)(2,1)S(1)} %collective-permute-done.16, bf16[128,2048]{1,0:T(8,128)(2,1)} %collective-permute-done.14, ...), kind=kLoop, calls=%fused_computation.3 | loop fusion | flops 3145728 | bytes 3670016 | tf_op jit(solution)/shard_map/convert_element_type | solution.py:401
  (70 shorter events, 2.6 us)
Async XLA Ops:
  0.6 13.0 %copy-start = (s32[8]{0:T(128)S(1)}, s32[8]{0:T(128)}, u32[]{:S(2)}) copy-start(s32[8]{0:T(128)} %param.11) | copy-start | bytes 100
  0.6 17.6 %collective-permute-start = (bf16[128,2048]{1,0:T(8,128)(2,1)}, bf16[128,2048]{1,0:T(8,128)(2,1)S(1)}, u32[]{:S(2)}, u32[]{:S(2)}) collective-permute-start(bf16[128,2048]{1,0:T(8,128)(2,1)} %refs_0_.1), channel_id=1, source_target_pairs={{0,4},{1,5},{2,6},{3,7},{12,8},{13,9},{14,10},{15,11},{16,20},{17,... | collective-permute-start | bytes 1572872 | tf_op jit(solution)/shard_map/ppermute | solution.py:405
  5.6 12.6 %collective-permute-start.1 = (bf16[128,2048]{1,0:T(8,128)(2,1)}, bf16[128,2048]{1,0:T(8,128)(2,1)S(1)}, u32[]{:S(2)}, u32[]{:S(2)}) collective-permute-start(bf16[128,2048]{1,0:T(8,128)(2,1)} %refs_0_.1), channel_id=1, source_target_pairs={{4,8},{5,9},{6,10},{7,11},{8,4},{9,5},{10,6},{11,7},{20,24},{21,25... | collective-permute-start | bytes 1572872 | tf_op jit(solution)/shard_map/ppermute | solution.py:405
  6.3 26.7 %collective-permute-start.2 = (bf16[128,2048]{1,0:T(8,128)(2,1)}, bf16[128,2048]{1,0:T(8,128)(2,1)S(1)}, u32[]{:S(2)}, u32[]{:S(2)}) collective-permute-start(bf16[128,2048]{1,0:T(8,128)(2,1)} %refs_0_.1), channel_id=1, source_target_pairs={{4,0},{5,1},{6,2},{7,3},{8,12},{9,13},{10,14},{11,15},{20,16},{21,... | collective-permute-start | bytes 1572872 | tf_op jit(solution)/shard_map/ppermute | solution.py:405
  7.6 25.4 %collective-permute-start.3 = (bf16[128,2048]{1,0:T(8,128)(2,1)}, bf16[128,2048]{1,0:T(8,128)(2,1)S(1)}, u32[]{:S(2)}, u32[]{:S(2)}) collective-permute-start(bf16[128,2048]{1,0:T(8,128)(2,1)} %refs_0_.1), channel_id=1, source_target_pairs={{0,12},{1,13},{2,14},{3,15},{12,0},{13,1},{14,2},{15,3},{16,28},{1... | collective-permute-start | bytes 1572872 | tf_op jit(solution)/shard_map/ppermute | solution.py:405
  12.0 21.0 %collective-permute-start.4 = (bf16[128,2048]{1,0:T(8,128)(2,1)}, bf16[128,2048]{1,0:T(8,128)(2,1)S(1)}, u32[]{:S(2)}, u32[]{:S(2)}) collective-permute-start(bf16[128,2048]{1,0:T(8,128)(2,1)} %refs_0_.1), channel_id=1, source_target_pairs={{0,2},{1,3},{2,0},{3,1},{4,6},{5,7},{6,4},{7,5},{8,10},{9,11},{10,... | collective-permute-start | bytes 1572872 | tf_op jit(solution)/shard_map/ppermute | solution.py:410
  18.2 15.6 %copy-start.7 = (bf16[128,2048]{1,0:T(8,128)(2,1)}, bf16[128,2048]{1,0:T(8,128)(2,1)S(1)}, u32[]{:S(2)}) copy-start(bf16[128,2048]{1,0:T(8,128)(2,1)S(1)} %collective-permute-done.refs_2_) | copy-start | bytes 1572868
  18.2 15.6 %copy-start.10 = (bf16[128,2048]{1,0:T(8,128)(2,1)}, bf16[128,2048]{1,0:T(8,128)(2,1)S(1)}, u32[]{:S(2)}) copy-start(bf16[128,2048]{1,0:T(8,128)(2,1)S(1)} %collective-permute-done.1.refs_3_) | copy-start | bytes 1572868
  33.0 0.8 copy-start.11
  33.0 1.1 copy-start.9
  33.1 1.2 copy-start.18
  34.2 25.3 %all-to-all-start = ((f32[16,16,128]{2,1,0:T(8,128)}), f32[16,16,128]{2,1,0:T(8,128)S(1)}, u32[]{:S(2)}, u32[]{:S(2)}) async-start(f32[16,16,128]{2,1,0:T(8,128)} %get-tuple-element.31), calls=%async_computation | async-start | bytes 262144 | tf_op jit(solution)/shard_map/all_to_all | solution.py:454
  39.1 11.0 %collective-permute-start.5 = (bf16[128,2048]{1,0:T(8,128)(2,1)}, bf16[128,2048]{1,0:T(8,128)(2,1)S(1)}, u32[]{:S(2)}, u32[]{:S(2)}) collective-permute-start(bf16[128,2048]{1,0:T(8,128)(2,1)} %copy-done.7), channel_id=1, source_target_pairs={{4,8},{5,9},{6,10},{7,11},{8,4},{9,5},{10,6},{11,7},{20,24},{21,25... | collective-permute-start | bytes 1572872 | tf_op jit(solution)/shard_map/ppermute | solution.py:405
  39.8 18.0 %collective-permute-start.6 = (bf16[128,2048]{1,0:T(8,128)(2,1)}, bf16[128,2048]{1,0:T(8,128)(2,1)S(1)}, u32[]{:S(2)}, u32[]{:S(2)}) collective-permute-start(bf16[128,2048]{1,0:T(8,128)(2,1)} %copy-done.10), channel_id=1, source_target_pairs={{4,0},{5,1},{6,2},{7,3},{8,12},{9,13},{10,14},{11,15},{20,16},{21,... | collective-permute-start | bytes 1572872 | tf_op jit(solution)/shard_map/ppermute | solution.py:405
  42.4 7.6 %copy-start.14 = (bf16[128,2048]{1,0:T(8,128)(2,1)}, bf16[128,2048]{1,0:T(8,128)(2,1)S(1)}, u32[]{:S(2)}) copy-start(bf16[128,2048]{1,0:T(8,128)(2,1)S(1)} %add_convert_fusion.7.refs_2_) | copy-start | bytes 1572868
  42.4 16.3 %collective-permute-start.7 = (bf16[128,2048]{1,0:T(8,128)(2,1)S(1)}, bf16[128,2048]{1,0:T(8,128)(2,1)S(1)}, u32[]{:S(2)}, u32[]{:S(2)}) collective-permute-start(bf16[128,2048]{1,0:T(8,128)(2,1)S(1)} %add_convert_fusion.7.refs_2_), channel_id=1, source_target_pairs={{0,2},{1,3},{2,0},{3,1},{4,6},{5,7},{6,4},{7,5},{8,10},{9,11},{10,... | collective-permute-start | bytes 1572872 | tf_op jit(solution)/shard_map/ppermute | solution.py:410
  58.7 0.8 copy-start.19
  59.5 0.7 copy-start.17
  60.2 55.6 %all-to-all-start.1 = ((bf16[16,96,768]{2,1,0:T(8,128)(2,1)}), bf16[16,96,768]{2,1,0:T(8,128)(2,1)S(1)}, u32[]{:S(2)}, u32[]{:S(2)}) async-start(bf16[16,96,768]{2,1,0:T(8,128)(2,1)} %bitcast.29), calls=%async_computation.1 | async-start | bytes 4718592 | tf_op jit(solution)/shard_map/all_to_all | solution.py:462
  66.5 7.4 %copy-start.8 = (bf16[128,2048]{1,0:T(8,128)(2,1)S(1)}, bf16[128,2048]{1,0:T(8,128)(2,1)}, u32[]{:S(2)}) copy-start(bf16[128,2048]{1,0:T(8,128)(2,1)} %copy-done.7) | copy-start | bytes 1572868
  66.5 10.3 %copy-start.4 = (bf16[128,2048]{1,0:T(8,128)(2,1)S(1)}, bf16[128,2048]{1,0:T(8,128)(2,1)}, u32[]{:S(2)}) copy-start(bf16[128,2048]{1,0:T(8,128)(2,1)} %add_convert_fusion.8.refs_1_.refs_0_) | copy-start | bytes 1572868
  73.4 3.9 %collective-permute-start.10 = (bf16[4,96,2048]{2,1,0:T(8,128)(2,1)}, bf16[4,96,2048]{2,1,0:T(8,128)(2,1)}, u32[]{:S(2)}, u32[]{:S(2)}) collective-permute-start(bf16[4,96,2048]{2,1,0:T(8,128)(2,1)} %get-tuple-element.36), channel_id=1, source_target_pairs={{0,1},{1,0},{2,3},{3,2},{4,5},{5,4},{6,7},{7,6},{8,9},{9,8},{10,11... | collective-permute-start | bytes 4718600 | tf_op jit(solution)/shard_map/ppermute | solution.py:410
  75.1 7.4 %copy-start.5 = (bf16[128,2048]{1,0:T(8,128)(2,1)}, bf16[128,2048]{1,0:T(8,128)(2,1)S(1)}, u32[]{:S(2)}) copy-start(bf16[128,2048]{1,0:T(8,128)(2,1)S(1)} %add_convert_fusion.6.refs_2_) | copy-start | bytes 1572868
  75.1 26.2 %collective-permute-start.8 = (bf16[128,2048]{1,0:T(8,128)(2,1)S(1)}, bf16[128,2048]{1,0:T(8,128)(2,1)S(1)}, u32[]{:S(2)}, u32[]{:S(2)}) collective-permute-start(bf16[128,2048]{1,0:T(8,128)(2,1)S(1)} %add_convert_fusion.6.refs_2_), channel_id=1, source_target_pairs={{0,2},{1,3},{2,0},{3,1},{4,6},{5,7},{6,4},{7,5},{8,10},{9,11},{10,... | collective-permute-start | bytes 1572872 | tf_op jit(solution)/shard_map/ppermute | solution.py:410
  76.8 39.0 %collective-permute-start.9 = (bf16[128,2048]{1,0:T(8,128)(2,1)S(1)}, bf16[128,2048]{1,0:T(8,128)(2,1)}, u32[]{:S(2)}, u32[]{:S(2)}) collective-permute-start(bf16[128,2048]{1,0:T(8,128)(2,1)S(1)} %copy-done.4), channel_id=1, source_target_pairs={{0,2},{1,3},{2,0},{3,1},{4,6},{5,7},{6,4},{7,5},{8,10},{9,11},{10,... | collective-permute-start | bytes 1572872 | tf_op jit(solution)/shard_map/ppermute | solution.py:410
  101.3 14.5 %copy-start.6 = (bf16[128,2048]{1,0:T(8,128)(2,1)}, bf16[128,2048]{1,0:T(8,128)(2,1)S(1)}, u32[]{:S(2)}) copy-start(bf16[128,2048]{1,0:T(8,128)(2,1)S(1)} %collective-permute-done.8.refs_1_.refs_3_) | copy-start | bytes 1572868
  115.8 1.4 copy-start.2
  123.3 29.4 %collective-permute-start.11 = (bf16[8,96,2048]{2,1,0:T(8,128)(2,1)}, bf16[8,96,2048]{2,1,0:T(8,128)(2,1)S(1)}, u32[]{:S(2)}, u32[]{:S(2)}) collective-permute-start(bf16[8,96,2048]{2,1,0:T(8,128)(2,1)} %forward_rows.3), channel_id=1, source_target_pairs={{0,1},{1,0},{2,3},{3,2},{4,5},{5,4},{6,7},{7,6},{8,9},{9,8},{10,11... | collective-permute-start | bytes 9437192 | tf_op jit(solution)/shard_map/ppermute | solution.py:410
  130.1 4.0 %collective-permute-start.22 = (bf16[4,96,2048]{2,1,0:T(8,128)(2,1)}, bf16[4,96,2048]{2,1,0:T(8,128)(2,1)}, u32[]{:S(2)}, u32[]{:S(2)}) collective-permute-start(bf16[4,96,2048]{2,1,0:T(8,128)(2,1)} %get-tuple-element.51), channel_id=1, source_target_pairs={{0,1},{1,0},{2,3},{3,2},{4,5},{5,4},{6,7},{7,6},{8,9},{9,8},{10,11... | collective-permute-start | bytes 4718600 | tf_op jit(solution)/shard_map/ppermute | solution.py:410
  139.3 88.5 %all-to-all-start.2 = ((bf16[16,96,768]{2,1,0:T(8,128)(2,1)}), bf16[16,96,768]{2,1,0:T(8,128)(2,1)}, u32[]{:S(2)}, u32[]{:S(2)}) async-start(bf16[16,96,768]{2,1,0:T(8,128)(2,1)} %get-tuple-element.54), calls=%async_computation.2 | async-start | bytes 4718592 | tf_op jit(solution)/shard_map/all_to_all | solution.py:476
  152.8 1.7 copy-start.1
  159.4 24.1 %collective-permute-start.17 = (bf16[128,2048]{1,0:T(8,128)(2,1)}, bf16[128,2048]{1,0:T(8,128)(2,1)S(1)}, u32[]{:S(2)}, u32[]{:S(2)}) collective-permute-start(bf16[128,2048]{1,0:T(8,128)(2,1)} %get-tuple-element.47), channel_id=1, source_target_pairs={{0,2},{1,3},{2,0},{3,1},{4,6},{5,7},{6,4},{7,5},{8,10},{9,11},{10,... | collective-permute-start | bytes 1572872 | tf_op jit(solution)/shard_map/ppermute | solution.py:410
  161.3 30.1 %copy-start.20 = (f32[128,8]{0,1:T(8,128)S(1)}, f32[128,8]{0,1:T(8,128)}, u32[]{:S(2)}) copy-start(f32[128,8]{0,1:T(8,128)} %param.7) | copy-start | bytes 12292
  161.3 31.2 %copy-start.21 = (s32[1,1024]{1,0:T(1,128)S(1)}, s32[1,1024]{1,0:T(1,128)}, u32[]{:S(2)}) copy-start(s32[1,1024]{1,0:T(1,128)} %get-tuple-element.48) | copy-start | bytes 12292
  161.3 37.3 %collective-permute-start.15 = (bf16[128,2048]{1,0:T(8,128)(2,1)}, bf16[128,2048]{1,0:T(8,128)(2,1)S(1)}, u32[]{:S(2)}, u32[]{:S(2)}) collective-permute-start(bf16[128,2048]{1,0:T(8,128)(2,1)} %get-tuple-element.45), channel_id=1, source_target_pairs={{0,2},{1,3},{2,0},{3,1},{4,6},{5,7},{6,4},{7,5},{8,10},{9,11},{10,... | collective-permute-start | bytes 1572872 | tf_op jit(solution)/shard_map/ppermute | solution.py:410
  166.3 34.2 %copy-start.15 = (bf16[128,2048]{1,0:T(8,128)(2,1)S(1)}, bf16[128,2048]{1,0:T(8,128)(2,1)}, u32[]{:S(2)}) copy-start(bf16[128,2048]{1,0:T(8,128)(2,1)} %get-tuple-element.44) | copy-start | bytes 1572868
  183.5 26.4 %copy-start.13 = (bf16[128,2048]{1,0:T(8,128)(2,1)S(1)}, bf16[128,2048]{1,0:T(8,128)(2,1)}, u32[]{:S(2)}) copy-start(bf16[128,2048]{1,0:T(8,128)(2,1)} %get-tuple-element.42) | copy-start | bytes 1572868
  185.6 14.2 %collective-permute-start.18 = (bf16[128,2048]{1,0:T(8,128)(2,1)}, bf16[128,2048]{1,0:T(8,128)(2,1)S(1)}, u32[]{:S(2)}, u32[]{:S(2)}) collective-permute-start(bf16[128,2048]{1,0:T(8,128)(2,1)} %add_convert_fusion.3), channel_id=1, source_target_pairs={{0,4},{1,5},{2,6},{3,7},{12,8},{13,9},{14,10},{15,11},{16,20},{17,... | collective-permute-start | bytes 1572872 | tf_op jit(solution)/shard_map/ppermute | solution.py:405
  189.7 20.1 %collective-permute-start.13 = (bf16[128,2048]{1,0:T(8,128)(2,1)}, bf16[128,2048]{1,0:T(8,128)(2,1)}, u32[]{:S(2)}, u32[]{:S(2)}) collective-permute-start(bf16[128,2048]{1,0:T(8,128)(2,1)} %get-tuple-element.43), channel_id=1, source_target_pairs={{0,2},{1,3},{2,0},{3,1},{4,6},{5,7},{6,4},{7,5},{8,10},{9,11},{10,... | collective-permute-start | bytes 1572872 | tf_op jit(solution)/shard_map/ppermute | solution.py:410
  189.8 20.1 %collective-permute-start.20 = (bf16[128,2048]{1,0:T(8,128)(2,1)}, bf16[128,2048]{1,0:T(8,128)(2,1)}, u32[]{:S(2)}, u32[]{:S(2)}) collective-permute-start(bf16[128,2048]{1,0:T(8,128)(2,1)} %add_convert_fusion.3), channel_id=1, source_target_pairs={{4,8},{5,9},{6,10},{7,11},{8,4},{9,5},{10,6},{11,7},{20,24},{21,25... | collective-permute-start | bytes 1572872 | tf_op jit(solution)/shard_map/ppermute | solution.py:405
  193.4 43.3 %collective-permute-start.12 = (bf16[128,2048]{1,0:T(8,128)(2,1)}, bf16[128,2048]{1,0:T(8,128)(2,1)S(1)}, u32[]{:S(2)}, u32[]{:S(2)}) collective-permute-start(bf16[128,2048]{1,0:T(8,128)(2,1)} %get-tuple-element.41), channel_id=1, source_target_pairs={{0,2},{1,3},{2,0},{3,1},{4,6},{5,7},{6,4},{7,5},{8,10},{9,11},{10,... | collective-permute-start | bytes 1572872 | tf_op jit(solution)/shard_map/ppermute | solution.py:410
  199.8 0.8 copy-start.16
  200.5 17.9 %copy-start.3 = (bf16[16,96,768]{2,1,0:T(8,128)(2,1)S(1)}, bf16[16,96,768]{2,1,0:T(8,128)(2,1)}, u32[]{:S(2)}) copy-start(bf16[16,96,768]{2,1,0:T(8,128)(2,1)} %after.5) | copy-start | bytes 7077892
  202.0 34.7 %collective-permute-start.16 = (bf16[128,2048]{1,0:T(8,128)(2,1)S(1)}, bf16[128,2048]{1,0:T(8,128)(2,1)S(1)}, u32[]{:S(2)}, u32[]{:S(2)}) collective-permute-start(bf16[128,2048]{1,0:T(8,128)(2,1)S(1)} %get-tuple-element.71), channel_id=1, source_target_pairs={{0,4},{1,5},{2,6},{3,7},{12,8},{13,9},{14,10},{15,11},{16,20},{17,... | collective-permute-start | bytes 1572872 | tf_op jit(solution)/shard_map/ppermute | solution.py:405
  207.5 29.3 %collective-permute-start.19 = (bf16[128,2048]{1,0:T(8,128)(2,1)S(1)}, bf16[128,2048]{1,0:T(8,128)(2,1)S(1)}, u32[]{:S(2)}, u32[]{:S(2)}) collective-permute-start(bf16[128,2048]{1,0:T(8,128)(2,1)S(1)} %get-tuple-element.70), channel_id=1, source_target_pairs={{4,8},{5,9},{6,10},{7,11},{8,4},{9,5},{10,6},{11,7},{20,24},{21,25... | collective-permute-start | bytes 1572872 | tf_op jit(solution)/shard_map/ppermute | solution.py:405
  212.3 24.4 %collective-permute-start.14 = (bf16[128,2048]{1,0:T(8,128)(2,1)}, bf16[128,2048]{1,0:T(8,128)(2,1)}, u32[]{:S(2)}, u32[]{:S(2)}) collective-permute-start(bf16[128,2048]{1,0:T(8,128)(2,1)} %get-tuple-element.73), channel_id=1, source_target_pairs={{0,12},{1,13},{2,14},{3,15},{12,0},{13,1},{14,2},{15,3},{16,28},{1... | collective-permute-start | bytes 1572872 | tf_op jit(solution)/shard_map/ppermute | solution.py:405
  217.2 24.3 %collective-permute-start.21 = (bf16[128,2048]{1,0:T(8,128)(2,1)}, bf16[128,2048]{1,0:T(8,128)(2,1)}, u32[]{:S(2)}, u32[]{:S(2)}) collective-permute-start(bf16[128,2048]{1,0:T(8,128)(2,1)} %get-tuple-element.72), channel_id=1, source_target_pairs={{4,0},{5,1},{6,2},{7,3},{8,12},{9,13},{10,14},{11,15},{20,16},{21,... | collective-permute-start | bytes 1572872 | tf_op jit(solution)/shard_map/ppermute | solution.py:405
  227.8 13.7 %copy-start.12 = (bf16[128,2048]{1,0:T(8,128)(2,1)S(1)}, bf16[128,2048]{1,0:T(8,128)(2,1)}, u32[]{:S(2)}) copy-start(bf16[128,2048]{1,0:T(8,128)(2,1)} %get-tuple-element.40) | copy-start | bytes 1572868

commit v8 on v7

--- a/solution.py
+++ b/solution.py
@@ -10,6 +10,7 @@
 F32 = jnp.float32
 BF16 = jnp.bfloat16
 MIB = 1 << 20
+BRIEF = pl.CostEstimate(flops=0, transcendentals=0, bytes_accessed=0)
 
 
 def slots_of(ids, swapped, devices):
@@ -105,10 +106,7 @@
         ],
         scratch_shapes=[pltpu.VMEM((1, pairs), jnp.int32)],
         compiler_params=pltpu.CompilerParams(vmem_limit_bytes=60 * MIB),
-        cost_estimate=pl.CostEstimate(
-            flops=2 * devices * capacity * pairs * hidden, transcendentals=0,
-            bytes_accessed=2 * hidden * (pairs + devices * capacity),
-        ),
+        cost_estimate=BRIEF,
         name="pack",
     )(ids, h_flat)
 
@@ -143,10 +141,7 @@
             jax.ShapeDtypeStruct((pairs, 1), F32),
         ],
         compiler_params=pltpu.CompilerParams(vmem_limit_bytes=60 * MIB),
-        cost_estimate=pl.CostEstimate(
-            flops=2 * slots * pairs * hidden, transcendentals=0,
-            bytes_accessed=2 * hidden * (2 * pairs + slots),
-        ),
+        cost_estimate=BRIEF,
         name="unpack",
     )(place, gates, h_flat, back_rows)
 
@@ -183,7 +178,7 @@
             jax.ShapeDtypeStruct((2, devices, tokens), jnp.int32),
             jax.ShapeDtypeStruct((2, devices, tokens), F32),
         ],
-        cost_estimate=pl.CostEstimate(flops=1 << 21, transcendentals=0, bytes_accessed=1 << 19),
+        cost_estimate=BRIEF,
         name="route",
     )(here, routing)
 
@@ -258,10 +253,7 @@
         ],
         input_output_aliases={4 + count + i: i for i in range(len(buffers))},
         compiler_params=pltpu.CompilerParams(vmem_limit_bytes=60 * MIB),
-        cost_estimate=pl.CostEstimate(
-            flops=2 * count * capacity * width * (hidden + 2 * tokens), transcendentals=0,
-            bytes_accessed=2 * count * (tokens * width + capacity * (2 * width + hidden)) + 2 * width * hidden,
-        ),
+        cost_estimate=BRIEF,
         name="scaled_rows",
     )(here, rank, gate, weight, *blocks, *buffers)
 
@@ -299,10 +291,7 @@
         ],
         input_output_aliases={3: 0, 4: 1},
         compiler_params=pltpu.CompilerParams(vmem_limit_bytes=60 * MIB),
-        cost_estimate=pl.CostEstimate(
-            flops=2 * count * capacity * width * hidden, transcendentals=0,
-            bytes_accessed=2 * count * capacity * (2 * width + hidden) + 2 * width * hidden,
-        ),
+        cost_estimate=BRIEF,
         name="sibling_rows",
     )(here, weight, rows, z_rows, back)
 
@@ -337,10 +326,7 @@
         ),
         out_shape=jax.ShapeDtypeStruct((devices // 2, capacity, width), BF16),
         compiler_params=pltpu.CompilerParams(vmem_limit_bytes=60 * MIB),
-        cost_estimate=pl.CostEstimate(
-            flops=devices * capacity * width * hidden, transcendentals=0,
-            bytes_accessed=devices * capacity * (width + hidden) + 2 * width * hidden,
-        ),
+        cost_estimate=BRIEF,
         name="forward_rows",
     )(here, rank, gate, rows_h.reshape(devices // 2, 2, capacity, hidden), weight)
 
@@ -386,10 +372,7 @@
         ),
         out_shape=[jax.ShapeDtypeStruct((tokens, width), BF16)] * len(ORDER),
         compiler_params=pltpu.CompilerParams(vmem_limit_bytes=60 * MIB),
-        cost_estimate=pl.CostEstimate(
-            flops=16 * tokens * capacity * width, transcendentals=0,
-            bytes_accessed=8 * width * (tokens + 2 * capacity),
-        ),
+        cost_estimate=BRIEF,
         name="summed",
     )(here, rank, own, other)
 
@@ -428,7 +411,7 @@
         out_shape=[jax.ShapeDtypeStruct(value.shape, value.dtype) for value in values],
         input_output_aliases={i: i for i in range(count)},
         compiler_params=pltpu.CompilerParams(vmem_limit_bytes=60 * MIB),
-        cost_estimate=pl.CostEstimate(flops=0, transcendentals=0, bytes_accessed=0),
+        cost_estimate=BRIEF,
         name="after",
     )(*values, *waited)
 
@@ -448,26 +431,29 @@
     own_y = swapped_with(own, 2)
     routing = jnp.concatenate([slot_ids.T.astype(F32), gates.T], axis=0)
     routing = jnp.broadcast_to(routing, (devices,) + routing.shape)
-    routing, flat_ids = after(
-        (routing, slot_ids.reshape(1, -1)), from_end, from_inner, from_near_end, from_far_end, own_y
-    )
+    place, send_h = pack(slot_ids.reshape(1, -1), h_flat, devices, capacity)
     routing = lax.all_to_all(routing, "expert", split_axis=0, concat_axis=0, tiled=True)
-    place, send_h = pack(flat_ids, h_flat, devices, capacity)
     rank, gate = route(here, routing, top)
+    send_h, = after((send_h,), from_end, from_inner, from_near_end, from_far_end, own_y, rank)
+    rows_h = lax.all_to_all(
+        send_h.reshape(devices, capacity, hidden), "expert", split_axis=0, concat_axis=0, tiled=True
+    )
     near, last = added(from_inner, from_near_end), added(from_end, from_far_end)
     middle_inner, middle_end = passed(INNER, from_end), passed(ENDS, from_inner)
     near_y = swapped_with(near, 2)
     middle = added(middle_inner, middle_end)
-    send_h, = after((send_h,), middle, near_y)
-    rows_h = lax.all_to_all(
-        send_h.reshape(devices, capacity, hidden), "expert", split_axis=0, concat_axis=0, tiled=True
-    )
     last_y = swapped_with(last, 2)
     middle_y = swapped_with(middle, 2)
 
     z_rows, back, sibling = scaled_rows(here, rank, gate, weight, [own, own_y, near, near_y], (0, 1), capacity, [])
     sibling = swapped_with(sibling, 1)
     z_rows, back, early = sibling_rows(here, weight, sibling, (0, 1), z_rows, back)
+    rows_h, = after((rows_h,), early, middle, last_y)
+    other = swapped_with(forward_rows(here, rank, gate, rows_h, weight, 1), 1)
+    mine = forward_rows(here, rank, gate, rows_h, weight, 0)
+    leaving = summed(here, rank, mine, other, 1)
+    across = [swapped_with(part, 2) for part in leaving]
+    last_y, = after((last_y,), leaving[0])
     z_rows, back, sibling_last = scaled_rows(
         here, rank, gate, weight, [middle, middle_y, last, last_y], (2, 3), capacity, [z_rows, back]
     )
@@ -475,10 +461,6 @@
     z_rows, back, _ = sibling_rows(here, weight, sibling_last, (2, 3), z_rows, back)
     back_rows = lax.all_to_all(back, "expert", split_axis=0, concat_axis=0, tiled=True).reshape(-1, hidden)
 
-    rows_h, = after((rows_h,), last_y, middle_y, early)
-    other = swapped_with(forward_rows(here, rank, gate, rows_h, weight, 1), 1)
-    mine = forward_rows(here, rank, gate, rows_h, weight, 0)
-    across = [swapped_with(part, 2) for part in summed(here, rank, mine, other, 1)]
     beside = summed(here, rank, mine, other, 0)
     far, mid, close, kept = zip(beside, across)
     far, mid, close = added(*far), added(*mid), added(*close)

time: 245 us -> 271 us (1.11)
  starting transfers between devices: 58.8 us -> 80.3 us
  waiting for transfers between devices: 88.8 us -> 93.1 us
  local copies, waits for them, and re-layouts: 10.9 us -> 14.5 us
  other arithmetic: 14.8 us -> 11.5 us
    ppermute x12, starting transfers between devices: 31.3 us -> 50.2 us  [passed(): lax.ppermute(value, 'expert', [(a * 4 + lane, b * 4 + lane) for a, b in p...]
    all_to_all x1, waiting for transfers between devices: 0.01 us -> 9.45 us  [dense_shards(): lax.all_to_all(routing, 'expert', split_axis=0, concat_axis=0, tiled=True)]
    ppermute x12, waiting for transfers between devices: 30.2 us -> 22.7 us  [passed(): lax.ppermute(value, 'expert', [(a * 4 + lane, b * 4 + lane) for a, b in p...]
    unnamed x46 -> x54, local copies, waits for them, and re-layouts: 6.6 us -> 10.3 us
    convert_element_type x7, other arithmetic: 12 us -> 8.77 us  [added(): return total.astype(BF16)]
  transfers between devices with their start and end apart: 26 -> 26, of which waited for: 11 -> 8; matrix products, arithmetic and copies ran while one was open for 11% -> 9% of each run, Pallas kernels for 22% -> 15%
where the time goes in v8:
time: 271 us; the launch traced here: 270 us
  waiting for transfers between devices  93.1 us (34%)
  starting transfers between devices  80.3 us (30%)
  Pallas kernels  60.5 us (22%)
  local copies, waits for them, and re-layouts  14.5 us (5%)
  other arithmetic  11.5 us (4%)
  matrix products  9.37 us (3%)
    ppermute x11, waiting for transfers between devices, swapped_with(): return lax.ppermute(value, 'expert', [(i, i ^ bit) for i in range(devices)])  60.9 us
    ppermute x12, starting transfers between devices, passed(): lax.ppermute(value, 'expert', [(a * 4 + lane, b * 4 + lane) for a, b in p...  50.2 us
    ppermute x12, waiting for transfers between devices, passed(): lax.ppermute(value, 'expert', [(a * 4 + lane, b * 4 + lane) for a, b in p...  22.7 us
    pallas_call x2, Pallas kernels, scaled_rows(): pl.pallas_call(functools.partial(scale_kernel, capacity, slots, len(buffe...  13.7 us
    ppermute x11, starting transfers between devices, swapped_with(): return lax.ppermute(value, 'expert', [(i, i ^ bit) for i in range(devices)])  13 us
    pallas_call x2, Pallas kernels, forward_rows(): pl.pallas_call(functools.partial(forward_kernel, capacity, turn), grid_sp...  12.3 us
    pallas_call x2, Pallas kernels, sibling_rows(): pl.pallas_call(functools.partial(sibling_kernel, capacity, slots), in_spe...  10.5 us
    unnamed x54, local copies, waits for them, and re-layouts  10.3 us
  transfers between devices with their start and end apart: 26, of which 8 were waited for; matrix products, arithmetic and copies ran while one was open for 9% of the time, Pallas kernels for 15%

profile of v8, /device:TPU:0, one launch (start us, length us, event | category | flops | bytes accessed | tf_op | source)
XLA Modules:
  0.0 270.5 jit_solution(16599021108780662701)
XLA Ops:
  0.6 5.0 %collective-permute-start = (bf16[128,2048]{1,0:T(8,128)(2,1)}, bf16[128,2048]{1,0:T(8,128)(2,1)S(1)}, u32[]{:S(2)}, u32[]{:S(2)}) collective-permute-start(bf16[128,2048]{1,0:T(8,128)(2,1)} %refs_0_.1), channel_id=1, source_target_pairs={{0,4},{1,5},{2,6},{3,7},{12,8},{13,9},{14,10},{15,11},{16,20},{17,... | collective-permute-start | bytes 1572872 | tf_op jit(solution)/shard_map/ppermute | solution.py:388
  5.6 0.7 collective-permute-start.1
  6.3 1.3 collective-permute-start.2
  7.6 4.4 %collective-permute-start.3 = (bf16[128,2048]{1,0:T(8,128)(2,1)}, bf16[128,2048]{1,0:T(8,128)(2,1)S(1)}, u32[]{:S(2)}, u32[]{:S(2)}) collective-permute-start(bf16[128,2048]{1,0:T(8,128)(2,1)} %refs_0_.1), channel_id=1, source_target_pairs={{0,12},{1,13},{2,14},{3,15},{12,0},{13,1},{14,2},{15,3},{16,28},{1... | collective-permute-start | bytes 1572872 | tf_op jit(solution)/shard_map/ppermute | solution.py:388
  12.0 1.6 collective-permute-start.4
  13.6 0.7 gather_fusion
  14.3 0.8 select_reduce_fusion
  15.1 0.7 pad_maximum_fusion
  15.8 0.7 broadcast_in_dim.19
  16.4 3.5 %all-to-all-start = ((f32[16,16,128]{2,1,0:T(8,128)}), f32[16,16,128]{2,1,0:T(8,128)S(1)}, u32[]{:S(2)}, u32[]{:S(2)}) async-start(f32[16,16,128]{2,1,0:T(8,128)} %broadcast_in_dim.19), calls=%async_computation | async-start | bytes 262144 | tf_op jit(solution)/shard_map/all_to_all | solution.py:435
  20.1 0.7 reshape.74.ids_ref
  20.8 5.6 %pack.1 = (s32[1,1024]{1,0:T(1,128)}, bf16[1536,768]{1,0:T(8,128)(2,1)}) custom-call(s32[1,1024]{1,0:T(1,128)} %reshape.74.ids_ref, bf16[1024,768]{1,0:T(8,128)(2,1)} %bitcast.31), custom_call_target="tpu_custom_call" | custom-call | tf_op jit(solution)/shard_map/pack/pallas_call | solution.py:92
  26.4 9.5 %all-to-all-done.routing_ref = f32[16,16,128]{2,1,0:T(8,128)S(1)} async-done(((f32[16,16,128]{2,1,0:T(8,128)}), f32[16,16,128]{2,1,0:T(8,128)S(1)}, u32[]{:S(2)}, u32[]{:S(2)}) %all-to-all-start) | async-done | bytes 131104 | tf_op jit(solution)/shard_map/all_to_all | solution.py:435
  36.5 1.7 route.1
  38.3 0.7 copy-done.7
  39.7 4.3 %all-to-all-start.1 = ((bf16[16,96,768]{2,1,0:T(8,128)(2,1)}), bf16[16,96,768]{2,1,0:T(8,128)(2,1)S(1)}, u32[]{:S(2)}, u32[]{:S(2)}) async-start(bf16[16,96,768]{2,1,0:T(8,128)(2,1)} %bitcast.29), calls=%async_computation.1 | async-start | bytes 4718592 | tf_op jit(solution)/shard_map/all_to_all | solution.py:438
  44.1 2.0 collective-permute-start.5
  46.1 32.2 %collective-permute-done.5.refs_3_ = bf16[128,2048]{1,0:T(8,128)(2,1)S(1)} collective-permute-done((bf16[128,2048]{1,0:T(8,128)(2,1)S(1)}, bf16[128,2048]{1,0:T(8,128)(2,1)S(1)}, u32[]{:S(2)}, u32[]{:S(2)}) %collective-permute-start.5) | collective-permute-done | bytes 524320 | tf_op jit(solution)/shard_map/ppermute | solution.py:393
  78.3 0.8 copy-done.23
  79.1 6.9 %scaled_rows.2 = (bf16[16,96,2048]{2,1,0:T(8,128)(2,1)}, bf16[16,96,768]{2,1,0:T(8,128)(2,1)}, bf16[4,96,2048]{2,1,0:T(8,128)(2,1)}) custom-call(s32[1]{0:T(128)} %bitcast.here_ref, s32[2,16,128]{2,1,0:T(8,128)} %get-tuple-element.29.refs_6_.rank_ref, f32[2,16,128]{2,1,0:T(8,128)} %get-tuple-element.30.gate_ref, bf16[768,2048]{1,0:T(8,128)(2,1)} %bitcast.21, ...), custom_call_target="tpu_custom_call" | custom-call | tf_op jit(solution)/shard_map/scaled_rows/pallas_call | solution.py:239
  86.1 1.3 collective-permute-start.8
  87.4 0.9 collective-permute-start.7
  88.3 0.9 add_convert_fusion.6.refs_2_
  89.2 2.4 collective-permute-start.9
  91.7 11.9 %collective-permute-done.8 = bf16[128,2048]{1,0:T(8,128)(2,1)S(1)} collective-permute-done((bf16[128,2048]{1,0:T(8,128)(2,1)S(1)}, bf16[128,2048]{1,0:T(8,128)(2,1)S(1)}, u32[]{:S(2)}, u32[]{:S(2)}) %collective-permute-start.8) | collective-permute-done | bytes 524320 | tf_op jit(solution)/shard_map/ppermute | solution.py:388
  103.6 0.9 add_convert_fusion.7.refs_2_.refs_0_
  104.5 5.3 %sibling_rows.2 = (bf16[16,96,2048]{2,1,0:T(8,128)(2,1)}, bf16[16,96,768]{2,1,0:T(8,128)(2,1)}, f32[8,128]{1,0:T(8,128)}) custom-call(s32[1]{0:T(128)} %bitcast.here_ref, bf16[768,2048]{1,0:T(8,128)(2,1)} %bitcast.22, bf16[4,96,2048]{2,1,0:T(8,128)(2,1)} %collective-permute-done.6.rows_ref, ...), custom_call_target="tpu_custom_call", output_to_operand_aliasing={{0}: (3, {}), {1}: (4, {})} | custom-call | tf_op jit(solution)/shard_map/sibling_rows/pallas_call | solution.py:278
  109.9 0.8 copy-done.6
  110.6 0.8 copy-done.1
  111.4 6.2 %forward_rows.3 = bf16[8,96,2048]{2,1,0:T(8,128)(2,1)} custom-call(s32[1]{0:T(128)} %bitcast.here_ref, s32[2,16,128]{2,1,0:T(8,128)} %get-tuple-element.29.refs_6_.rank_ref, f32[2,16,128]{2,1,0:T(8,128)} %get-tuple-element.30.gate_ref, bf16[8,2,96,768]{3,2,1,0:T(8,128)(2,1)} %bitcast.27, bf16[768,2048]{1,0:T(8,128)(2,1)} %bitcast.23), custom_call_target="tpu_custom_call" | custom-call | tf_op jit(solution)/shard_map/forward_rows/pallas_call | solution.py:314
  117.7 1.5 collective-permute-start.21
  119.2 6.1 %forward_rows.2.own_ref = bf16[8,96,2048]{2,1,0:T(8,128)(2,1)} custom-call(s32[1]{0:T(128)} %bitcast.here_ref, s32[2,16,128]{2,1,0:T(8,128)} %get-tuple-element.29.refs_6_.rank_ref, f32[2,16,128]{2,1,0:T(8,128)} %get-tuple-element.30.gate_ref, bf16[8,2,96,768]{3,2,1,0:T(8,128)(2,1)} %bitcast.28, bf16[768,2048]{1,0:T(8,128)(2,1)} %bitcast.24), custom_call_target="tpu_custom_call" | custom-call | tf_op jit(solution)/shard_map/forward_rows/pallas_call | solution.py:314
  125.3 1.7 copy-done.3
  127.0 4.9 %summed.3 = (bf16[128,2048]{1,0:T(8,128)(2,1)}, bf16[128,2048]{1,0:T(8,128)(2,1)}, bf16[128,2048]{1,0:T(8,128)(2,1)}, bf16[128,2048]{1,0:T(8,128)(2,1)}) custom-call(s32[1]{0:T(128)} %bitcast.here_ref, s32[2,16,128]{2,1,0:T(8,128)} %get-tuple-element.29.refs_6_.rank_ref, bf16[8,96,2048]{2,1,0:T(8,128)(2,1)} %forward_rows.2.own_ref, ...), custom_call_target="tpu_custom_call" | custom-call | tf_op jit(solution)/shard_map/summed/pallas_call | solution.py:361
  132.1 6.8 %scaled_rows.3 = (bf16[16,96,2048]{2,1,0:T(8,128)(2,1)}, bf16[16,96,768]{2,1,0:T(8,128)(2,1)}, bf16[4,96,2048]{2,1,0:T(8,128)(2,1)}) custom-call(s32[1]{0:T(128)} %bitcast.here_ref, s32[2,16,128]{2,1,0:T(8,128)} %get-tuple-element.29.refs_6_.rank_ref, f32[2,16,128]{2,1,0:T(8,128)} %get-tuple-element.30.gate_ref, ...), custom_call_target="tpu_custom_call", output_to_operand_aliasing={{0}: (8, {}), {1}: (9, {})} | custom-call | tf_op jit(solution)/shard_map/scaled_rows/pallas_call | solution.py:239
  139.0 1.6 collective-permute-start.16
  140.5 2.0 collective-permute-done.22.rows_ref
  142.5 1.1 copy-done.17
  143.7 5.3 %sibling_rows.3 = (bf16[16,96,2048]{2,1,0:T(8,128)(2,1)}, bf16[16,96,768]{2,1,0:T(8,128)(2,1)}, f32[8,128]{1,0:T(8,128)}) custom-call(s32[1]{0:T(128)} %bitcast.here_ref, bf16[768,2048]{1,0:T(8,128)(2,1)} %bitcast.26, bf16[4,96,2048]{2,1,0:T(8,128)(2,1)} %copy-done.17, ...), custom_call_target="tpu_custom_call", output_to_operand_aliasing={{0}: (3, {}), {1}: (4, {})} | custom-call | tf_op jit(solution)/shard_map/sibling_rows/pallas_call | solution.py:278
  149.0 9.3 %all-to-all-start.2 = ((bf16[16,96,768]{2,1,0:T(8,128)(2,1)}), bf16[16,96,768]{2,1,0:T(8,128)(2,1)S(1)}, u32[]{:S(2)}, u32[]{:S(2)}) async-start(bf16[16,96,768]{2,1,0:T(8,128)(2,1)} %get-tuple-element.50), calls=%async_computation.2 | async-start | bytes 4718592 | tf_op jit(solution)/shard_map/all_to_all | solution.py:462
  158.3 2.0 collective-permute-start.12
  160.3 4.9 %summed.2 = (bf16[128,2048]{1,0:T(8,128)(2,1)}, bf16[128,2048]{1,0:T(8,128)(2,1)}, bf16[128,2048]{1,0:T(8,128)(2,1)}, bf16[128,2048]{1,0:T(8,128)(2,1)}) custom-call(s32[1]{0:T(128)} %bitcast.here_ref, s32[2,16,128]{2,1,0:T(8,128)} %get-tuple-element.29.refs_6_.rank_ref, bf16[8,96,2048]{2,1,0:T(8,128)(2,1)} %forward_rows.2.own_ref, ...), custom_call_target="tpu_custom_call" | custom-call | tf_op jit(solution)/shard_map/summed/pallas_call | solution.py:361
  165.2 0.8 copy-done.21
  166.0 2.2 add_convert_fusion.3
  168.2 1.5 collective-permute-start.19
  169.9 6.5 %collective-permute-start.17 = (bf16[128,2048]{1,0:T(8,128)(2,1)}, bf16[128,2048]{1,0:T(8,128)(2,1)}, u32[]{:S(2)}, u32[]{:S(2)}) collective-permute-start(bf16[128,2048]{1,0:T(8,128)(2,1)} %add_convert_fusion.3), channel_id=1, source_target_pairs={{0,4},{1,5},{2,6},{3,7},{12,8},{13,9},{14,10},{15,11},{16,20},{17,... | collective-permute-start | bytes 1572872 | tf_op jit(solution)/shard_map/ppermute | solution.py:388
  176.5 1.1 copy.31.place_ref
  177.6 1.0 reshape.92.gate_ref
  178.6 1.5 collective-permute-start.11
  180.0 12.7 %collective-permute-done.12 = bf16[128,2048]{1,0:T(8,128)(2,1)} collective-permute-done((bf16[128,2048]{1,0:T(8,128)(2,1)S(1)}, bf16[128,2048]{1,0:T(8,128)(2,1)}, u32[]{:S(2)}, u32[]{:S(2)}) %collective-permute-start.12) | collective-permute-done | bytes 524320 | tf_op jit(solution)/shard_map/ppermute | solution.py:393
  192.7 1.8 add_convert_fusion.1
  194.5 1.3 collective-permute-start.20
  195.8 13.9 %collective-permute-done.14 = bf16[128,2048]{1,0:T(8,128)(2,1)} collective-permute-done((bf16[128,2048]{1,0:T(8,128)(2,1)}, bf16[128,2048]{1,0:T(8,128)(2,1)}, u32[]{:S(2)}, u32[]{:S(2)}) %collective-permute-start.14) | collective-permute-done | bytes 524320 | tf_op jit(solution)/shard_map/ppermute | solution.py:393
  209.7 1.5 add_convert_fusion.2
  211.2 0.7 collective-permute-start.18
  211.9 22.2 %collective-permute-start.15 = (bf16[128,2048]{1,0:T(8,128)(2,1)S(1)}, bf16[128,2048]{1,0:T(8,128)(2,1)S(1)}, u32[]{:S(2)}, u32[]{:S(2)}) collective-permute-start(bf16[128,2048]{1,0:T(8,128)(2,1)S(1)} %get-tuple-element.67), channel_id=1, source_target_pairs={{0,4},{1,5},{2,6},{3,7},{12,8},{13,9},{14,10},{15,11},{16,20},{17,... | collective-permute-start | bytes 1572872 | tf_op jit(solution)/shard_map/ppermute | solution.py:388
  234.1 4.5 %collective-permute-start.13 = (bf16[128,2048]{1,0:T(8,128)(2,1)S(1)}, bf16[128,2048]{1,0:T(8,128)(2,1)S(1)}, u32[]{:S(2)}, u32[]{:S(2)}) collective-permute-start(bf16[128,2048]{1,0:T(8,128)(2,1)S(1)} %get-tuple-element.69), channel_id=1, source_target_pairs={{0,12},{1,13},{2,14},{3,15},{12,0},{13,1},{14,2},{15,3},{16,28},{1... | collective-permute-start | bytes 1572872 | tf_op jit(solution)/shard_map/ppermute | solution.py:388
  238.7 9.4 %fusion = bf16[1,768,2048]{2,1,0:T(8,128)(2,1)} fusion(bf16[16,96,768]{2,1,0:T(8,128)(2,1)S(1)} %copy-done.2, bf16[16,96,2048]{2,1,0:T(8,128)(2,1)} %get-tuple-element.53), kind=kOutput, calls=%fused_computation.2 | convolution fusion | flops 4833411072 | bytes 11796480 | tf_op jit(solution)/shard_map/dot_general | solution.py:474
  248.1 10.8 %collective-permute-done.13 = bf16[128,2048]{1,0:T(8,128)(2,1)S(1)} collective-permute-done((bf16[128,2048]{1,0:T(8,128)(2,1)S(1)}, bf16[128,2048]{1,0:T(8,128)(2,1)S(1)}, u32[]{:S(2)}, u32[]{:S(2)}) %collective-permute-start.13) | collective-permute-done | bytes 524320 | tf_op jit(solution)/shard_map/ppermute | solution.py:388
  258.9 1.3 add_convert_fusion
  260.2 1.4 copy-done.4
  261.6 6.9 %unpack.1 = (bf16[1024,768]{1,0:T(8,128)(2,1)}, f32[1024,1]{1,0:T(8,128)}) custom-call(s32[1024,1]{1,0:T(8,128)} %copy.31.place_ref, f32[1024,1]{1,0:T(8,128)} %reshape.92.gate_ref, bf16[1024,768]{1,0:T(8,128)(2,1)} %bitcast.32, bf16[1536,768]{1,0:T(8,128)(2,1)} %bitcast.30), custom_call_target="tpu_custom_call" | custom-call | tf_op jit(solution)/shard_map/unpack/pallas_call | solution.py:126
  268.5 1.2 reduce
  269.8 0.7 copy.33
  (78 shorter events, 2.4 us)
Async XLA Ops:
  0.6 13.0 %copy-start = (s32[8]{0:T(128)S(1)}, s32[8]{0:T(128)}, u32[]{:S(2)}) copy-start(s32[8]{0:T(128)} %param.11) | copy-start | bytes 100
  0.6 37.5 %collective-permute-start = (bf16[128,2048]{1,0:T(8,128)(2,1)}, bf16[128,2048]{1,0:T(8,128)(2,1)S(1)}, u32[]{:S(2)}, u32[]{:S(2)}) collective-permute-start(bf16[128,2048]{1,0:T(8,128)(2,1)} %refs_0_.1), channel_id=1, source_target_pairs={{0,4},{1,5},{2,6},{3,7},{12,8},{13,9},{14,10},{15,11},{16,20},{17,... | collective-permute-start | bytes 1572872 | tf_op jit(solution)/shard_map/ppermute | solution.py:388
  5.6 32.6 %collective-permute-start.1 = (bf16[128,2048]{1,0:T(8,128)(2,1)}, bf16[128,2048]{1,0:T(8,128)(2,1)S(1)}, u32[]{:S(2)}, u32[]{:S(2)}) collective-permute-start(bf16[128,2048]{1,0:T(8,128)(2,1)} %refs_0_.1), channel_id=1, source_target_pairs={{4,8},{5,9},{6,10},{7,11},{8,4},{9,5},{10,6},{11,7},{20,24},{21,25... | collective-permute-start | bytes 1572872 | tf_op jit(solution)/shard_map/ppermute | solution.py:388
  6.3 31.9 %collective-permute-start.2 = (bf16[128,2048]{1,0:T(8,128)(2,1)}, bf16[128,2048]{1,0:T(8,128)(2,1)S(1)}, u32[]{:S(2)}, u32[]{:S(2)}) collective-permute-start(bf16[128,2048]{1,0:T(8,128)(2,1)} %refs_0_.1), channel_id=1, source_target_pairs={{4,0},{5,1},{6,2},{7,3},{8,12},{9,13},{10,14},{11,15},{20,16},{21,... | collective-permute-start | bytes 1572872 | tf_op jit(solution)/shard_map/ppermute | solution.py:388
  7.6 30.6 %collective-permute-start.3 = (bf16[128,2048]{1,0:T(8,128)(2,1)}, bf16[128,2048]{1,0:T(8,128)(2,1)S(1)}, u32[]{:S(2)}, u32[]{:S(2)}) collective-permute-start(bf16[128,2048]{1,0:T(8,128)(2,1)} %refs_0_.1), channel_id=1, source_target_pairs={{0,12},{1,13},{2,14},{3,15},{12,0},{13,1},{14,2},{15,3},{16,28},{1... | collective-permute-start | bytes 1572872 | tf_op jit(solution)/shard_map/ppermute | solution.py:388
  12.0 26.2 %collective-permute-start.4 = (bf16[128,2048]{1,0:T(8,128)(2,1)}, bf16[128,2048]{1,0:T(8,128)(2,1)S(1)}, u32[]{:S(2)}, u32[]{:S(2)}) collective-permute-start(bf16[128,2048]{1,0:T(8,128)(2,1)} %refs_0_.1), channel_id=1, source_target_pairs={{0,2},{1,3},{2,0},{3,1},{4,6},{5,7},{6,4},{7,5},{8,10},{9,11},{10,... | collective-permute-start | bytes 1572872 | tf_op jit(solution)/shard_map/ppermute | solution.py:393
  16.4 19.4 %all-to-all-start = ((f32[16,16,128]{2,1,0:T(8,128)}), f32[16,16,128]{2,1,0:T(8,128)S(1)}, u32[]{:S(2)}, u32[]{:S(2)}) async-start(f32[16,16,128]{2,1,0:T(8,128)} %broadcast_in_dim.19), calls=%async_computation | async-start | bytes 262144 | tf_op jit(solution)/shard_map/all_to_all | solution.py:435
  35.8 0.7 copy-start.22
  38.2 0.8 copy-start.7
  38.2 1.0 copy-start.9
  38.2 1.1 copy-start.13
  38.2 1.3 copy-start.11
  38.2 1.4 copy-start.15
  39.7 4.3 %copy-start.10 = (bf16[128,2048]{1,0:T(8,128)(2,1)S(1)}, bf16[128,2048]{1,0:T(8,128)(2,1)}, u32[]{:S(2)}) copy-start(bf16[128,2048]{1,0:T(8,128)(2,1)} %copy-done.9) | copy-start | bytes 1572868
  39.7 4.3 %copy-start.14 = (bf16[128,2048]{1,0:T(8,128)(2,1)S(1)}, bf16[128,2048]{1,0:T(8,128)(2,1)}, u32[]{:S(2)}) copy-start(bf16[128,2048]{1,0:T(8,128)(2,1)} %copy-done.13) | copy-start | bytes 1572868
  39.7 70.2 %all-to-all-start.1 = ((bf16[16,96,768]{2,1,0:T(8,128)(2,1)}), bf16[16,96,768]{2,1,0:T(8,128)(2,1)S(1)}, u32[]{:S(2)}, u32[]{:S(2)}) async-start(bf16[16,96,768]{2,1,0:T(8,128)(2,1)} %bitcast.29), calls=%async_computation.1 | async-start | bytes 4718592 | tf_op jit(solution)/shard_map/all_to_all | solution.py:438
  44.1 34.2 %copy-start.16 = (bf16[128,2048]{1,0:T(8,128)(2,1)}, bf16[128,2048]{1,0:T(8,128)(2,1)S(1)}, u32[]{:S(2)}) copy-start(bf16[128,2048]{1,0:T(8,128)(2,1)S(1)} %add_convert_fusion.8.refs_2_) | copy-start | bytes 1572868
  44.1 34.2 %collective-permute-start.5 = (bf16[128,2048]{1,0:T(8,128)(2,1)S(1)}, bf16[128,2048]{1,0:T(8,128)(2,1)S(1)}, u32[]{:S(2)}, u32[]{:S(2)}) collective-permute-start(bf16[128,2048]{1,0:T(8,128)(2,1)S(1)} %add_convert_fusion.8.refs_2_), channel_id=1, source_target_pairs={{0,2},{1,3},{2,0},{3,1},{4,6},{5,7},{6,4},{7,5},{8,10},{9,11},{10,... | collective-permute-start | bytes 1572872 | tf_op jit(solution)/shard_map/ppermute | solution.py:393
  78.3 0.8 copy-start.23
  79.1 8.3 %copy-start.8 = (bf16[128,2048]{1,0:T(8,128)(2,1)S(1)}, bf16[128,2048]{1,0:T(8,128)(2,1)}, u32[]{:S(2)}) copy-start(bf16[128,2048]{1,0:T(8,128)(2,1)} %copy-done.7) | copy-start | bytes 1572868
  79.1 9.2 %copy-start.12 = (bf16[128,2048]{1,0:T(8,128)(2,1)S(1)}, bf16[128,2048]{1,0:T(8,128)(2,1)}, u32[]{:S(2)}) copy-start(bf16[128,2048]{1,0:T(8,128)(2,1)} %copy-done.11) | copy-start | bytes 1572868
  86.0 18.5 %collective-permute-start.6 = (bf16[4,96,2048]{2,1,0:T(8,128)(2,1)}, bf16[4,96,2048]{2,1,0:T(8,128)(2,1)}, u32[]{:S(2)}, u32[]{:S(2)}) collective-permute-start(bf16[4,96,2048]{2,1,0:T(8,128)(2,1)} %get-tuple-element.32), channel_id=1, source_target_pairs={{0,1},{1,0},{2,3},{3,2},{4,5},{5,4},{6,7},{7,6},{8,9},{9,8},{10,11... | collective-permute-start | bytes 4718600 | tf_op jit(solution)/shard_map/ppermute | solution.py:393
  86.1 17.5 %collective-permute-start.8 = (bf16[128,2048]{1,0:T(8,128)(2,1)S(1)}, bf16[128,2048]{1,0:T(8,128)(2,1)S(1)}, u32[]{:S(2)}, u32[]{:S(2)}) collective-permute-start(bf16[128,2048]{1,0:T(8,128)(2,1)S(1)} %copy-done.10), channel_id=1, source_target_pairs={{4,0},{5,1},{6,2},{7,3},{8,12},{9,13},{10,14},{11,15},{20,16},{21,... | collective-permute-start | bytes 1572872 | tf_op jit(solution)/shard_map/ppermute | solution.py:388
  87.4 16.2 %collective-permute-start.7 = (bf16[128,2048]{1,0:T(8,128)(2,1)S(1)}, bf16[128,2048]{1,0:T(8,128)(2,1)S(1)}, u32[]{:S(2)}, u32[]{:S(2)}) collective-permute-start(bf16[128,2048]{1,0:T(8,128)(2,1)S(1)} %copy-done.8), channel_id=1, source_target_pairs={{4,8},{5,9},{6,10},{7,11},{8,4},{9,5},{10,6},{11,7},{20,24},{21,25... | collective-permute-start | bytes 1572872 | tf_op jit(solution)/shard_map/ppermute | solution.py:388
  89.2 20.6 %collective-permute-start.9 = (bf16[128,2048]{1,0:T(8,128)(2,1)}, bf16[128,2048]{1,0:T(8,128)(2,1)S(1)}, u32[]{:S(2)}, u32[]{:S(2)}) collective-permute-start(bf16[128,2048]{1,0:T(8,128)(2,1)} %add_convert_fusion.6.refs_2_), channel_id=1, source_target_pairs={{0,2},{1,3},{2,0},{3,1},{4,6},{5,7},{6,4},{7,5},{8,10},{9,11},{10,... | collective-permute-start | bytes 1572872 | tf_op jit(solution)/shard_map/ppermute | solution.py:393
  109.8 0.8 copy-start.6
  109.9 1.6 copy-start.1
  111.4 6.3 %copy-start.5 = (bf16[128,2048]{1,0:T(8,128)(2,1)S(1)}, bf16[128,2048]{1,0:T(8,128)(2,1)}, u32[]{:S(2)}) copy-start(bf16[128,2048]{1,0:T(8,128)(2,1)} %add_convert_fusion.7.refs_2_.refs_0_) | copy-start | bytes 1572868
  117.6 7.7 %collective-permute-start.10 = (bf16[8,96,2048]{2,1,0:T(8,128)(2,1)}, bf16[8,96,2048]{2,1,0:T(8,128)(2,1)S(1)}, u32[]{:S(2)}, u32[]{:S(2)}) collective-permute-start(bf16[8,96,2048]{2,1,0:T(8,128)(2,1)} %forward_rows.3), channel_id=1, source_target_pairs={{0,1},{1,0},{2,3},{3,2},{4,5},{5,4},{6,7},{7,6},{8,9},{9,8},{10,11... | collective-permute-start | bytes 9437192 | tf_op jit(solution)/shard_map/ppermute | solution.py:393
  117.7 14.4 %collective-permute-start.21 = (bf16[128,2048]{1,0:T(8,128)(2,1)S(1)}, bf16[128,2048]{1,0:T(8,128)(2,1)}, u32[]{:S(2)}, u32[]{:S(2)}) collective-permute-start(bf16[128,2048]{1,0:T(8,128)(2,1)S(1)} %copy-done.5), channel_id=1, source_target_pairs={{0,2},{1,3},{2,0},{3,1},{4,6},{5,7},{6,4},{7,5},{8,10},{9,11},{10,... | collective-permute-start | bytes 1572872 | tf_op jit(solution)/shard_map/ppermute | solution.py:393
  125.3 1.7 copy-start.3
  138.9 3.7 %collective-permute-start.22 = (bf16[4,96,2048]{2,1,0:T(8,128)(2,1)}, bf16[4,96,2048]{2,1,0:T(8,128)(2,1)S(1)}, u32[]{:S(2)}, u32[]{:S(2)}) collective-permute-start(bf16[4,96,2048]{2,1,0:T(8,128)(2,1)} %get-tuple-element.47), channel_id=1, source_target_pairs={{0,1},{1,0},{2,3},{3,2},{4,5},{5,4},{6,7},{7,6},{8,9},{9,8},{10,11... | collective-permute-start | bytes 4718600 | tf_op jit(solution)/shard_map/ppermute | solution.py:393
  139.0 26.3 %collective-permute-start.16 = (bf16[128,2048]{1,0:T(8,128)(2,1)}, bf16[128,2048]{1,0:T(8,128)(2,1)S(1)}, u32[]{:S(2)}, u32[]{:S(2)}) collective-permute-start(bf16[128,2048]{1,0:T(8,128)(2,1)} %get-tuple-element.43), channel_id=1, source_target_pairs={{0,2},{1,3},{2,0},{3,1},{4,6},{5,7},{6,4},{7,5},{8,10},{9,11},{10,... | collective-permute-start | bytes 1572872 | tf_op jit(solution)/shard_map/ppermute | solution.py:393
  142.5 1.1 copy-start.17
  148.9 9.3 %copy-start.19 = (bf16[128,2048]{1,0:T(8,128)(2,1)S(1)}, bf16[128,2048]{1,0:T(8,128)(2,1)}, u32[]{:S(2)}) copy-start(bf16[128,2048]{1,0:T(8,128)(2,1)} %get-tuple-element.39.refs_1_) | copy-start | bytes 1572868
  149.0 111.2 %all-to-all-start.2 = ((bf16[16,96,768]{2,1,0:T(8,128)(2,1)}), bf16[16,96,768]{2,1,0:T(8,128)(2,1)S(1)}, u32[]{:S(2)}, u32[]{:S(2)}) async-start(bf16[16,96,768]{2,1,0:T(8,128)(2,1)} %get-tuple-element.50), calls=%async_computation.2 | async-start | bytes 4718592 | tf_op jit(solution)/shard_map/all_to_all | solution.py:462
  158.3 18.1 %copy-start.24 = (f32[128,8]{0,1:T(8,128)S(1)}, f32[128,8]{0,1:T(8,128)}, u32[]{:S(2)}) copy-start(f32[128,8]{0,1:T(8,128)} %param.7) | copy-start | bytes 12292
  158.3 18.2 %copy-start.25 = (s32[1,1024]{1,0:T(1,128)S(1)}, s32[1,1024]{1,0:T(1,128)}, u32[]{:S(2)}) copy-start(s32[1,1024]{1,0:T(1,128)} %get-tuple-element.44) | copy-start | bytes 12292
  158.3 34.4 %collective-permute-start.12 = (bf16[128,2048]{1,0:T(8,128)(2,1)S(1)}, bf16[128,2048]{1,0:T(8,128)(2,1)}, u32[]{:S(2)}, u32[]{:S(2)}) collective-permute-start(bf16[128,2048]{1,0:T(8,128)(2,1)S(1)} %copy-done.19), channel_id=1, source_target_pairs={{0,2},{1,3},{2,0},{3,1},{4,6},{5,7},{6,4},{7,5},{8,10},{9,11},{10,... | collective-permute-start | bytes 1572872 | tf_op jit(solution)/shard_map/ppermute | solution.py:393
  165.2 0.8 copy-start.21
  166.0 43.7 %copy-start.20 = (bf16[128,2048]{1,0:T(8,128)(2,1)S(1)}, bf16[128,2048]{1,0:T(8,128)(2,1)}, u32[]{:S(2)}) copy-start(bf16[128,2048]{1,0:T(8,128)(2,1)} %get-tuple-element.40) | copy-start | bytes 1572868
  168.2 24.5 %collective-permute-start.19 = (bf16[128,2048]{1,0:T(8,128)(2,1)}, bf16[128,2048]{1,0:T(8,128)(2,1)}, u32[]{:S(2)}, u32[]{:S(2)}) collective-permute-start(bf16[128,2048]{1,0:T(8,128)(2,1)} %add_convert_fusion.3), channel_id=1, source_target_pairs={{4,8},{5,9},{6,10},{7,11},{8,4},{9,5},{10,6},{11,7},{20,24},{21,25... | collective-permute-start | bytes 1572872 | tf_op jit(solution)/shard_map/ppermute | solution.py:388
  169.7 40.0 %collective-permute-start.14 = (bf16[128,2048]{1,0:T(8,128)(2,1)}, bf16[128,2048]{1,0:T(8,128)(2,1)}, u32[]{:S(2)}, u32[]{:S(2)}) collective-permute-start(bf16[128,2048]{1,0:T(8,128)(2,1)} %get-tuple-element.41), channel_id=1, source_target_pairs={{0,2},{1,3},{2,0},{3,1},{4,6},{5,7},{6,4},{7,5},{8,10},{9,11},{10,... | collective-permute-start | bytes 1572872 | tf_op jit(solution)/shard_map/ppermute | solution.py:393
  169.9 39.9 %collective-permute-start.17 = (bf16[128,2048]{1,0:T(8,128)(2,1)}, bf16[128,2048]{1,0:T(8,128)(2,1)}, u32[]{:S(2)}, u32[]{:S(2)}) collective-permute-start(bf16[128,2048]{1,0:T(8,128)(2,1)} %add_convert_fusion.3), channel_id=1, source_target_pairs={{0,4},{1,5},{2,6},{3,7},{12,8},{13,9},{14,10},{15,11},{16,20},{17,... | collective-permute-start | bytes 1572872 | tf_op jit(solution)/shard_map/ppermute | solution.py:388
  178.6 69.5 %collective-permute-start.11 = (bf16[128,2048]{1,0:T(8,128)(2,1)}, bf16[128,2048]{1,0:T(8,128)(2,1)S(1)}, u32[]{:S(2)}, u32[]{:S(2)}) collective-permute-start(bf16[128,2048]{1,0:T(8,128)(2,1)} %get-tuple-element.37), channel_id=1, source_target_pairs={{0,2},{1,3},{2,0},{3,1},{4,6},{5,7},{6,4},{7,5},{8,10},{9,11},{10,... | collective-permute-start | bytes 1572872 | tf_op jit(solution)/shard_map/ppermute | solution.py:393
  192.7 45.9 %copy-start.2 = (bf16[16,96,768]{2,1,0:T(8,128)(2,1)S(1)}, bf16[16,96,768]{2,1,0:T(8,128)(2,1)}, u32[]{:S(2)}) copy-start(bf16[16,96,768]{2,1,0:T(8,128)(2,1)} %after.4) | copy-start | bytes 7077892
  194.5 53.5 %collective-permute-start.20 = (bf16[128,2048]{1,0:T(8,128)(2,1)S(1)}, bf16[128,2048]{1,0:T(8,128)(2,1)S(1)}, u32[]{:S(2)}, u32[]{:S(2)}) collective-permute-start(bf16[128,2048]{1,0:T(8,128)(2,1)S(1)} %get-tuple-element.68), channel_id=1, source_target_pairs={{4,0},{5,1},{6,2},{7,3},{8,12},{9,13},{10,14},{11,15},{20,16},{21,... | collective-permute-start | bytes 1572872 | tf_op jit(solution)/shard_map/ppermute | solution.py:388
  211.2 36.8 %collective-permute-start.18 = (bf16[128,2048]{1,0:T(8,128)(2,1)S(1)}, bf16[128,2048]{1,0:T(8,128)(2,1)S(1)}, u32[]{:S(2)}, u32[]{:S(2)}) collective-permute-start(bf16[128,2048]{1,0:T(8,128)(2,1)S(1)} %get-tuple-element.66), channel_id=1, source_target_pairs={{4,8},{5,9},{6,10},{7,11},{8,4},{9,5},{10,6},{11,7},{20,24},{21,25... | collective-permute-start | bytes 1572872 | tf_op jit(solution)/shard_map/ppermute | solution.py:388
  211.9 36.1 %collective-permute-start.15 = (bf16[128,2048]{1,0:T(8,128)(2,1)S(1)}, bf16[128,2048]{1,0:T(8,128)(2,1)S(1)}, u32[]{:S(2)}, u32[]{:S(2)}) collective-permute-start(bf16[128,2048]{1,0:T(8,128)(2,1)S(1)} %get-tuple-element.67), channel_id=1, source_target_pairs={{0,4},{1,5},{2,6},{3,7},{12,8},{13,9},{14,10},{15,11},{16,20},{17,... | collective-permute-start | bytes 1572872 | tf_op jit(solution)/shard_map/ppermute | solution.py:388
  234.1 24.8 %collective-permute-start.13 = (bf16[128,2048]{1,0:T(8,128)(2,1)S(1)}, bf16[128,2048]{1,0:T(8,128)(2,1)S(1)}, u32[]{:S(2)}, u32[]{:S(2)}) collective-permute-start(bf16[128,2048]{1,0:T(8,128)(2,1)S(1)} %get-tuple-element.69), channel_id=1, source_target_pairs={{0,12},{1,13},{2,14},{3,15},{12,0},{13,1},{14,2},{15,3},{16,28},{1... | collective-permute-start | bytes 1572872 | tf_op jit(solution)/shard_map/ppermute | solution.py:388
  238.7 20.2 %copy-start.18 = (bf16[128,2048]{1,0:T(8,128)(2,1)S(1)}, bf16[128,2048]{1,0:T(8,128)(2,1)}, u32[]{:S(2)}) copy-start(bf16[128,2048]{1,0:T(8,128)(2,1)} %get-tuple-element.36) | copy-start | bytes 1572868
  260.2 1.4 copy-start.4

commit v9 on v8

--- a/solution.py
+++ b/solution.py
@@ -394,7 +394,7 @@
 
 
 OUTER, INNER = ((0, 1), (3, 2)), ((1, 2), (2, 1))
-ENDS, ENDS_SWAP = ((1, 0), (2, 3)), ((0, 3), (3, 0))
+ENDS = ((1, 0), (2, 3))
 
 
 def gate_kernel(*refs):
@@ -425,51 +425,52 @@
     slot_ids = slots_of(expert_ids, swapped, devices)
     h_flat = h_rows.reshape(-1, hidden)
 
+    routing = jnp.concatenate([slot_ids.T.astype(F32), gates.T], axis=0)
+    routing = jnp.broadcast_to(routing, (devices,) + routing.shape)
+    routing = lax.all_to_all(routing, "expert", split_axis=0, concat_axis=0, tiled=True)
+    rank, gate = route(here, routing, top)
+    place, send_h = pack(slot_ids.reshape(1, -1), h_flat, devices, capacity)
+
     own = cotangent
     from_end, from_inner, from_near_end = passed(OUTER, own), passed(INNER, own), passed(ENDS, own)
-    from_far_end = passed(ENDS_SWAP, own)
     own_y = swapped_with(own, 2)
-    routing = jnp.concatenate([slot_ids.T.astype(F32), gates.T], axis=0)
-    routing = jnp.broadcast_to(routing, (devices,) + routing.shape)
-    place, send_h = pack(slot_ids.reshape(1, -1), h_flat, devices, capacity)
-    routing = lax.all_to_all(routing, "expert", split_axis=0, concat_axis=0, tiled=True)
-    rank, gate = route(here, routing, top)
-    send_h, = after((send_h,), from_end, from_inner, from_near_end, from_far_end, own_y, rank)
+    near = added(from_inner, from_near_end)
+    start_end, start_inner, near = after((from_end, from_inner, near), own_y)
+    from_far, from_middle = passed(INNER, start_end), passed(ENDS, start_inner)
+    near_y = swapped_with(near, 2)
+    middle = added(from_far, from_middle)
+    start_far, middle = after((from_far, middle), near_y, rank)
+    last = added(from_end, passed(ENDS, start_far))
+    middle_y = swapped_with(middle, 2)
+    z_rows, back, sibling = scaled_rows(here, rank, gate, weight, [own, own_y, near, near_y], (0, 1), capacity, [])
+    send_h, last = after((send_h, last), middle_y, sibling)
+    sibling = swapped_with(sibling, 1)
     rows_h = lax.all_to_all(
         send_h.reshape(devices, capacity, hidden), "expert", split_axis=0, concat_axis=0, tiled=True
     )
-    near, last = added(from_inner, from_near_end), added(from_end, from_far_end)
-    middle_inner, middle_end = passed(INNER, from_end), passed(ENDS, from_inner)
-    near_y = swapped_with(near, 2)
-    middle = added(middle_inner, middle_end)
     last_y = swapped_with(last, 2)
-    middle_y = swapped_with(middle, 2)
-
-    z_rows, back, sibling = scaled_rows(here, rank, gate, weight, [own, own_y, near, near_y], (0, 1), capacity, [])
-    sibling = swapped_with(sibling, 1)
-    z_rows, back, early = sibling_rows(here, weight, sibling, (0, 1), z_rows, back)
-    rows_h, = after((rows_h,), early, middle, last_y)
+
+    z_rows, back, _ = sibling_rows(here, weight, sibling, (0, 1), z_rows, back)
+    z_rows, back, sibling_last = scaled_rows(
+        here, rank, gate, weight, [middle, middle_y, last, last_y], (2, 3), capacity, [z_rows, back]
+    )
+    sibling_last = swapped_with(sibling_last, 1)
+    z_rows, back, ready = sibling_rows(here, weight, sibling_last, (2, 3), z_rows, back)
+    back_rows = lax.all_to_all(back, "expert", split_axis=0, concat_axis=0, tiled=True).reshape(-1, hidden)
+
+    rows_h, = after((rows_h,), ready)
     other = swapped_with(forward_rows(here, rank, gate, rows_h, weight, 1), 1)
     mine = forward_rows(here, rank, gate, rows_h, weight, 0)
-    leaving = summed(here, rank, mine, other, 1)
-    across = [swapped_with(part, 2) for part in leaving]
-    last_y, = after((last_y,), leaving[0])
-    z_rows, back, sibling_last = scaled_rows(
-        here, rank, gate, weight, [middle, middle_y, last, last_y], (2, 3), capacity, [z_rows, back]
-    )
-    sibling_last = swapped_with(sibling_last, 1)
-    z_rows, back, _ = sibling_rows(here, weight, sibling_last, (2, 3), z_rows, back)
-    back_rows = lax.all_to_all(back, "expert", split_axis=0, concat_axis=0, tiled=True).reshape(-1, hidden)
-
+    across = [swapped_with(part, 2) for part in summed(here, rank, mine, other, 1)]
     beside = summed(here, rank, mine, other, 0)
     far, mid, close, kept = zip(beside, across)
-    far, mid, close = added(*far), added(*mid), added(*close)
-    ends = passed(ENDS_SWAP, far)
-    mid_outer, mid_inner = passed(OUTER, mid), passed(INNER, mid)
-    close_outer = passed(OUTER, close)
-    close_inner = passed(INNER, added(close, mid_outer))
-    far_ends = passed(ENDS, added(far, mid_inner))
-    mixed = added(*kept, ends, close_outer, close_inner, far_ends)
+    outer1 = passed(OUTER, added(*far))
+    mid = added(*mid, outer1)
+    outer2, inner2 = passed(OUTER, mid), passed(INNER, mid)
+    close, = after((added(*close, outer2),), back_rows)
+    outer3, inner3 = passed(OUTER, close), passed(INNER, close)
+    ends3 = passed(ENDS, added(*far, inner2))
+    mixed = added(*kept, outer3, inner3, ends3)
 
     grad_sum = lax.dot_general(
         rows_h.reshape(-1, hidden), z_rows.reshape(devices * capacity, -1), (((0,), (0,)), ((), ())),

time: 271 us -> 245 us (0.904)
  starting transfers between devices: 80.3 us -> 61.6 us
  waiting for transfers between devices: 93.1 us -> 83.6 us
  other arithmetic: 11.5 us -> 15.3 us
    ppermute x12, starting transfers between devices: 50.2 us -> 30.4 us  [passed(): lax.ppermute(value, 'expert', [(a * 4 + lane, b * 4 + lane) for a, b in p...]
    ppermute x12, waiting for transfers between devices: 22.7 us -> 13.4 us  [passed(): lax.ppermute(value, 'expert', [(a * 4 + lane, b * 4 + lane) for a, b in p...]
    convert_element_type x7 -> x8, other arithmetic: 8.77 us -> 13.3 us  [added(): return total.astype(BF16)]
    all_to_all x1, starting transfers between devices: 3.51 us -> 7.01 us  [dense_shards(): lax.all_to_all(routing, 'expert', split_axis=0, concat_axis=0, tiled=True)]
    unnamed x54 -> x37, local copies, waits for them, and re-layouts: 10.3 us -> 8.38 us
  transfers between devices with their start and end apart: 26 -> 26, of which waited for: 8 -> 10; matrix products, arithmetic and copies ran while one was open for 9% -> 11% of each run, Pallas kernels for 15% -> 22%
where the time goes in v9:
time: 245 us; the launch traced here: 244 us
  waiting for transfers between devices  83.6 us (34%)
  starting transfers between devices  61.6 us (25%)
  Pallas kernels  60.7 us (25%)
  other arithmetic  15.3 us (6%)
  local copies, waits for them, and re-layouts  12.6 us (5%)
  matrix products  9.32 us (4%)
    ppermute x11, waiting for transfers between devices, swapped_with(): return lax.ppermute(value, 'expert', [(i, i ^ bit) for i in range(devices)])  62.3 us
    ppermute x12, starting transfers between devices, passed(): lax.ppermute(value, 'expert', [(a * 4 + lane, b * 4 + lane) for a, b in p...  30.4 us
    pallas_call x2, Pallas kernels, scaled_rows(): pl.pallas_call(functools.partial(scale_kernel, capacity, slots, len(buffe...  13.6 us
    ppermute x12, waiting for transfers between devices, passed(): lax.ppermute(value, 'expert', [(a * 4 + lane, b * 4 + lane) for a, b in p...  13.4 us
    convert_element_type x8, other arithmetic, added(): return total.astype(BF16)  13.3 us
    pallas_call x2, Pallas kernels, forward_rows(): pl.pallas_call(functools.partial(forward_kernel, capacity, turn), grid_sp...  12.3 us
    ppermute x11, starting transfers between devices, swapped_with(): return lax.ppermute(value, 'expert', [(i, i ^ bit) for i in range(devices)])  10.9 us
    pallas_call x2, Pallas kernels, sibling_rows(): pl.pallas_call(functools.partial(sibling_kernel, capacity, slots), in_spe...  10.6 us
  transfers between devices with their start and end apart: 26, of which 10 were waited for; matrix products, arithmetic and copies ran while one was open for 11% of the time, Pallas kernels for 22%

profile of v9, /device:TPU:0, one launch (start us, length us, event | category | flops | bytes accessed | tf_op | source)
XLA Modules:
  0.0 244.1 jit_solution(16551669001010893862)
XLA Ops:
  0.6 0.7 collective-permute-start.1
  1.3 1.3 collective-permute-start.2
  2.6 7.8 %collective-permute-start = (bf16[128,2048]{1,0:T(8,128)(2,1)}, bf16[128,2048]{1,0:T(8,128)(2,1)S(1)}, u32[]{:S(2)}, u32[]{:S(2)}) collective-permute-start(bf16[128,2048]{1,0:T(8,128)(2,1)} %refs_0_.1), channel_id=1, source_target_pairs={{0,4},{1,5},{2,6},{3,7},{12,8},{13,9},{14,10},{15,11},{16,20},{17,... | collective-permute-start | bytes 1572872 | tf_op jit(solution)/shard_map/ppermute | solution.py:388
  10.4 1.6 collective-permute-start.3
  12.7 0.8 select_reduce_fusion
  13.5 8.1 %collective-permute-done = bf16[128,2048]{1,0:T(8,128)(2,1)S(1)} collective-permute-done((bf16[128,2048]{1,0:T(8,128)(2,1)}, bf16[128,2048]{1,0:T(8,128)(2,1)S(1)}, u32[]{:S(2)}, u32[]{:S(2)}) %collective-permute-start) | collective-permute-done | bytes 524320 | tf_op jit(solution)/shard_map/ppermute | solution.py:388
  21.6 0.8 copy.40.refs_0_
  22.4 1.0 add_convert_fusion.6.refs_2_
  23.8 0.8 copy-done.10
  24.6 0.7 collective-permute-start.4
  25.3 1.3 collective-permute-start.5
  26.7 0.7 broadcast_in_dim.19
  27.3 7.0 %all-to-all-start = ((f32[16,16,128]{2,1,0:T(8,128)}), f32[16,16,128]{2,1,0:T(8,128)S(1)}, u32[]{:S(2)}, u32[]{:S(2)}) async-start(f32[16,16,128]{2,1,0:T(8,128)} %broadcast_in_dim.19), calls=%async_computation | async-start | bytes 262144 | tf_op jit(solution)/shard_map/all_to_all | solution.py:430
  34.3 1.9 collective-permute-start.6
  36.3 8.0 %all-to-all-done.routing_ref = f32[16,16,128]{2,1,0:T(8,128)S(1)} async-done(((f32[16,16,128]{2,1,0:T(8,128)}), f32[16,16,128]{2,1,0:T(8,128)S(1)}, u32[]{:S(2)}, u32[]{:S(2)}) %all-to-all-start) | async-done | bytes 131104 | tf_op jit(solution)/shard_map/all_to_all | solution.py:430
  44.9 1.7 route.1
  46.6 1.0 add_convert_fusion.5.refs_1_
  47.5 2.6 %collective-permute-done.6.refs_2_.refs_3_ = bf16[128,2048]{1,0:T(8,128)(2,1)S(1)} collective-permute-done((bf16[128,2048]{1,0:T(8,128)(2,1)}, bf16[128,2048]{1,0:T(8,128)(2,1)S(1)}, u32[]{:S(2)}, u32[]{:S(2)}) %collective-permute-start.6) | collective-permute-done | bytes 524320 | tf_op jit(solution)/shard_map/ppermute | solution.py:393
  50.1 0.8 copy-done.9
  50.9 1.3 collective-permute-start.7
  52.2 1.5 collective-permute-start.8
  53.8 0.7 reshape.74.ids_ref
  54.5 5.6 %pack.1 = (s32[1,1024]{1,0:T(1,128)}, bf16[1536,768]{1,0:T(8,128)(2,1)}) custom-call(s32[1,1024]{1,0:T(1,128)} %reshape.74.ids_ref, bf16[1024,768]{1,0:T(8,128)(2,1)} %bitcast.32), custom_call_target="tpu_custom_call" | custom-call | tf_op jit(solution)/shard_map/pack/pallas_call | solution.py:92
  60.1 6.8 %scaled_rows.2 = (bf16[16,96,2048]{2,1,0:T(8,128)(2,1)}, bf16[16,96,768]{2,1,0:T(8,128)(2,1)}, bf16[4,96,2048]{2,1,0:T(8,128)(2,1)}) custom-call(s32[1]{0:T(128)} %bitcast.here_ref, s32[2,16,128]{2,1,0:T(8,128)} %get-tuple-element.36.refs_3_.rank_ref, f32[2,16,128]{2,1,0:T(8,128)} %get-tuple-element.37.gate_ref, bf16[768,2048]{1,0:T(8,128)(2,1)} %bitcast.21, ...), custom_call_target="tpu_custom_call" | custom-call | tf_op jit(solution)/shard_map/scaled_rows/pallas_call | solution.py:239
  66.9 0.9 add_convert_fusion.4.refs_1_
  67.8 0.9 copy-done.5
  68.7 6.1 %all-to-all-start.1 = ((bf16[16,96,768]{2,1,0:T(8,128)(2,1)}), bf16[16,96,768]{2,1,0:T(8,128)(2,1)S(1)}, u32[]{:S(2)}, u32[]{:S(2)}) async-start(bf16[16,96,768]{2,1,0:T(8,128)(2,1)} %bitcast.31), calls=%async_computation.1 | async-start | bytes 4718592 | tf_op jit(solution)/shard_map/all_to_all | solution.py:448
  75.3 1.7 collective-permute-start.9
  76.9 1.8 collective-permute-done.10.rows_ref
  78.7 5.3 %sibling_rows.2 = (bf16[16,96,2048]{2,1,0:T(8,128)(2,1)}, bf16[16,96,768]{2,1,0:T(8,128)(2,1)}, f32[8,128]{1,0:T(8,128)}) custom-call(s32[1]{0:T(128)} %bitcast.here_ref, bf16[768,2048]{1,0:T(8,128)(2,1)} %bitcast.22, bf16[4,96,2048]{2,1,0:T(8,128)(2,1)} %collective-permute-done.10.rows_ref, ...), custom_call_target="tpu_custom_call", output_to_operand_aliasing={{0}: (3, {}), {1}: (4, {})} | custom-call | tf_op jit(solution)/shard_map/sibling_rows/pallas_call | solution.py:278
  84.0 25.2 %collective-permute-done.9.refs_3_ = bf16[128,2048]{1,0:T(8,128)(2,1)S(1)} collective-permute-done((bf16[128,2048]{1,0:T(8,128)(2,1)S(1)}, bf16[128,2048]{1,0:T(8,128)(2,1)S(1)}, u32[]{:S(2)}, u32[]{:S(2)}) %collective-permute-start.9) | collective-permute-done | bytes 524320 | tf_op jit(solution)/shard_map/ppermute | solution.py:393
  109.2 0.8 copy-done.11
  110.0 6.8 %scaled_rows.3 = (bf16[16,96,2048]{2,1,0:T(8,128)(2,1)}, bf16[16,96,768]{2,1,0:T(8,128)(2,1)}, bf16[4,96,2048]{2,1,0:T(8,128)(2,1)}) custom-call(s32[1]{0:T(128)} %bitcast.here_ref, s32[2,16,128]{2,1,0:T(8,128)} %get-tuple-element.36.refs_3_.rank_ref, f32[2,16,128]{2,1,0:T(8,128)} %get-tuple-element.37.gate_ref, ...), custom_call_target="tpu_custom_call", output_to_operand_aliasing={{0}: (8, {}), {1}: (9, {})} | custom-call | tf_op jit(solution)/shard_map/scaled_rows/pallas_call | solution.py:239
  116.9 3.7 %collective-permute-done.11.rows_ref = bf16[4,96,2048]{2,1,0:T(8,128)(2,1)} collective-permute-done((bf16[4,96,2048]{2,1,0:T(8,128)(2,1)}, bf16[4,96,2048]{2,1,0:T(8,128)(2,1)}, u32[]{:S(2)}, u32[]{:S(2)}) %collective-permute-start.11) | collective-permute-done | bytes 1572896 | tf_op jit(solution)/shard_map/ppermute | solution.py:393
  120.7 5.3 %sibling_rows.3 = (bf16[16,96,2048]{2,1,0:T(8,128)(2,1)}, bf16[16,96,768]{2,1,0:T(8,128)(2,1)}, f32[8,128]{1,0:T(8,128)}) custom-call(s32[1]{0:T(128)} %bitcast.here_ref, bf16[768,2048]{1,0:T(8,128)(2,1)} %bitcast.24, bf16[4,96,2048]{2,1,0:T(8,128)(2,1)} %collective-permute-done.11.rows_ref, ...), custom_call_target="tpu_custom_call", output_to_operand_aliasing={{0}: (3, {}), {1}: (4, {})} | custom-call | tf_op jit(solution)/shard_map/sibling_rows/pallas_call | solution.py:278
  126.0 1.4 copy-done.1
  127.4 6.2 %forward_rows.3 = bf16[8,96,2048]{2,1,0:T(8,128)(2,1)} custom-call(s32[1]{0:T(128)} %bitcast.here_ref, s32[2,16,128]{2,1,0:T(8,128)} %get-tuple-element.36.refs_3_.rank_ref, f32[2,16,128]{2,1,0:T(8,128)} %get-tuple-element.37.gate_ref, bf16[8,2,96,768]{3,2,1,0:T(8,128)(2,1)} %bitcast.27, bf16[768,2048]{1,0:T(8,128)(2,1)} %bitcast.25), custom_call_target="tpu_custom_call" | custom-call | tf_op jit(solution)/shard_map/forward_rows/pallas_call | solution.py:314
  133.6 7.1 %all-to-all-start.2 = ((bf16[16,96,768]{2,1,0:T(8,128)(2,1)}), bf16[16,96,768]{2,1,0:T(8,128)(2,1)S(1)}, u32[]{:S(2)}, u32[]{:S(2)}) async-start(bf16[16,96,768]{2,1,0:T(8,128)(2,1)} %get-tuple-element.63), calls=%async_computation.2 | async-start | bytes 4718592 | tf_op jit(solution)/shard_map/all_to_all | solution.py:459
  140.8 6.1 %forward_rows.2.own_ref = bf16[8,96,2048]{2,1,0:T(8,128)(2,1)} custom-call(s32[1]{0:T(128)} %bitcast.here_ref, s32[2,16,128]{2,1,0:T(8,128)} %get-tuple-element.36.refs_3_.rank_ref, f32[2,16,128]{2,1,0:T(8,128)} %get-tuple-element.37.gate_ref, bf16[8,2,96,768]{3,2,1,0:T(8,128)(2,1)} %bitcast.28, bf16[768,2048]{1,0:T(8,128)(2,1)} %bitcast.26), custom_call_target="tpu_custom_call" | custom-call | tf_op jit(solution)/shard_map/forward_rows/pallas_call | solution.py:314
  146.9 5.1 %summed.3 = (bf16[128,2048]{1,0:T(8,128)(2,1)}, bf16[128,2048]{1,0:T(8,128)(2,1)}, bf16[128,2048]{1,0:T(8,128)(2,1)}, bf16[128,2048]{1,0:T(8,128)(2,1)}) custom-call(s32[1]{0:T(128)} %bitcast.here_ref, s32[2,16,128]{2,1,0:T(8,128)} %get-tuple-element.36.refs_3_.rank_ref, bf16[8,96,2048]{2,1,0:T(8,128)(2,1)} %forward_rows.2.own_ref, ...), custom_call_target="tpu_custom_call" | custom-call | tf_op jit(solution)/shard_map/summed/pallas_call | solution.py:361
  152.0 1.9 collective-permute-start.16
  154.0 5.0 %summed.2 = (bf16[128,2048]{1,0:T(8,128)(2,1)}, bf16[128,2048]{1,0:T(8,128)(2,1)}, bf16[128,2048]{1,0:T(8,128)(2,1)}, bf16[128,2048]{1,0:T(8,128)(2,1)}) custom-call(s32[1]{0:T(128)} %bitcast.here_ref, s32[2,16,128]{2,1,0:T(8,128)} %get-tuple-element.36.refs_3_.rank_ref, bf16[8,96,2048]{2,1,0:T(8,128)(2,1)} %forward_rows.2.own_ref, ...), custom_call_target="tpu_custom_call" | custom-call | tf_op jit(solution)/shard_map/summed/pallas_call | solution.py:361
  159.0 18.4 %collective-permute-done.16 = bf16[128,2048]{1,0:T(8,128)(2,1)S(1)} collective-permute-done((bf16[128,2048]{1,0:T(8,128)(2,1)}, bf16[128,2048]{1,0:T(8,128)(2,1)S(1)}, u32[]{:S(2)}, u32[]{:S(2)}) %collective-permute-start.16) | collective-permute-done | bytes 524320 | tf_op jit(solution)/shard_map/ppermute | solution.py:393
  177.4 1.2 fusion.1
  178.6 2.6 %collective-permute-start.17 = (bf16[128,2048]{1,0:T(8,128)(2,1)S(1)}, bf16[128,2048]{1,0:T(8,128)(2,1)S(1)}, u32[]{:S(2)}, u32[]{:S(2)}) collective-permute-start(bf16[128,2048]{1,0:T(8,128)(2,1)S(1)} %fusion.1), channel_id=1, source_target_pairs={{0,4},{1,5},{2,6},{3,7},{12,8},{13,9},{14,10},{15,11},{16,20},{17,... | collective-permute-start | bytes 1572872 | tf_op jit(solution)/shard_map/ppermute | solution.py:388
  181.2 1.2 collective-permute-start.14
  182.4 10.2 %collective-permute-done.15 = bf16[128,2048]{1,0:T(8,128)(2,1)S(1)} collective-permute-done((bf16[128,2048]{1,0:T(8,128)(2,1)}, bf16[128,2048]{1,0:T(8,128)(2,1)S(1)}, u32[]{:S(2)}, u32[]{:S(2)}) %collective-permute-start.15) | collective-permute-done | bytes 524320 | tf_op jit(solution)/shard_map/ppermute | solution.py:393
  192.6 2.1 add_convert_fusion.3
  194.7 6.0 %collective-permute-start.18 = (bf16[128,2048]{1,0:T(8,128)(2,1)}, bf16[128,2048]{1,0:T(8,128)(2,1)}, u32[]{:S(2)}, u32[]{:S(2)}) collective-permute-start(bf16[128,2048]{1,0:T(8,128)(2,1)} %add_convert_fusion.3), channel_id=1, source_target_pairs={{0,4},{1,5},{2,6},{3,7},{12,8},{13,9},{14,10},{15,11},{16,20},{17,... | collective-permute-start | bytes 1572872 | tf_op jit(solution)/shard_map/ppermute | solution.py:388
  200.7 1.5 collective-permute-start.21
  202.3 1.0 copy.37.place_ref
  203.3 1.0 reshape.92.gate_ref
  204.8 5.2 %collective-permute-done.18 = bf16[128,2048]{1,0:T(8,128)(2,1)} collective-permute-done((bf16[128,2048]{1,0:T(8,128)(2,1)}, bf16[128,2048]{1,0:T(8,128)(2,1)}, u32[]{:S(2)}, u32[]{:S(2)}) %collective-permute-start.18) | collective-permute-done | bytes 524320 | tf_op jit(solution)/shard_map/ppermute | solution.py:388
  210.0 2.5 %add_convert_fusion.2.refs_0_ = bf16[128,2048]{1,0:T(8,128)(2,1)} fusion(bf16[128,2048]{1,0:T(8,128)(2,1)} %collective-permute-done.18, bf16[128,2048]{1,0:T(8,128)(2,1)} %copy-done.14, bf16[128,2048]{1,0:T(8,128)(2,1)} %get-tuple-element.57), kind=kLoop, calls=%fused_computation.5 | loop fusion | flops 1572864 | bytes 2097152 | tf_op jit(solution)/shard_map/convert_element_type | solution.py:384
  212.5 1.5 copy-done.3
  214.0 4.5 %collective-permute-start.19 = (bf16[128,2048]{1,0:T(8,128)(2,1)}, bf16[128,2048]{1,0:T(8,128)(2,1)S(1)}, u32[]{:S(2)}, u32[]{:S(2)}) collective-permute-start(bf16[128,2048]{1,0:T(8,128)(2,1)} %after.9), channel_id=1, source_target_pairs={{0,4},{1,5},{2,6},{3,7},{12,8},{13,9},{14,10},{15,11},{16,20},{17,... | collective-permute-start | bytes 1572872 | tf_op jit(solution)/shard_map/ppermute | solution.py:388
  218.5 1.5 collective-permute-start.20
  220.0 2.1 add_convert_fusion.1
  222.1 1.3 collective-permute-start.22
  223.4 9.3 %fusion = bf16[1,768,2048]{2,1,0:T(8,128)(2,1)} fusion(bf16[16,96,768]{2,1,0:T(8,128)(2,1)S(1)} %copy-done.2, bf16[16,96,2048]{2,1,0:T(8,128)(2,1)} %get-tuple-element.67), kind=kOutput, calls=%fused_computation.2 | convolution fusion | flops 4833411072 | bytes 11796480 | tf_op jit(solution)/shard_map/dot_general | solution.py:475
  232.7 6.9 %unpack.1 = (bf16[1024,768]{1,0:T(8,128)(2,1)}, f32[1024,1]{1,0:T(8,128)}) custom-call(s32[1024,1]{1,0:T(8,128)} %copy.37.place_ref, f32[1024,1]{1,0:T(8,128)} %reshape.92.gate_ref, bf16[1024,768]{1,0:T(8,128)(2,1)} %bitcast.33, bf16[1536,768]{1,0:T(8,128)(2,1)} %bitcast.30), custom_call_target="tpu_custom_call" | custom-call | tf_op jit(solution)/shard_map/unpack/pallas_call | solution.py:126
  239.6 1.2 reduce
  241.0 0.7 copy.39
  241.7 2.4 %add_convert_fusion = bf16[128,2048]{1,0:T(8,128)(2,1)} fusion(bf16[128,2048]{1,0:T(8,128)(2,1)S(1)} %collective-permute-done.22, bf16[128,2048]{1,0:T(8,128)(2,1)} %collective-permute-done.20, bf16[128,2048]{1,0:T(8,128)(2,1)S(1)} %collective-permute-done.19, bf16[128,2048]{1,0:T(8,128)(2,1)} %collective-permute-done.13, bf16[128,2048]{1,0:T(8,128)(2,1)S(1)} %copy-done.13), kind=kLoop, calls=%fused_computation.3 | loop fusion | flops 2621440 | bytes 3145728 | tf_op jit(solution)/shard_map/convert_element_type | solution.py:384
  (64 shorter events, 3.3 us)
Async XLA Ops:
  0.6 11.4 %copy-start = (s32[8]{0:T(128)S(1)}, s32[8]{0:T(128)}, u32[]{:S(2)}) copy-start(s32[8]{0:T(128)} %param.11) | copy-start | bytes 100
  0.6 21.8 %collective-permute-start.1 = (bf16[128,2048]{1,0:T(8,128)(2,1)}, bf16[128,2048]{1,0:T(8,128)(2,1)S(1)}, u32[]{:S(2)}, u32[]{:S(2)}) collective-permute-start(bf16[128,2048]{1,0:T(8,128)(2,1)} %refs_0_.1), channel_id=1, source_target_pairs={{4,8},{5,9},{6,10},{7,11},{8,4},{9,5},{10,6},{11,7},{20,24},{21,25... | collective-permute-start | bytes 1572872 | tf_op jit(solution)/shard_map/ppermute | solution.py:388
  1.3 21.1 %collective-permute-start.2 = (bf16[128,2048]{1,0:T(8,128)(2,1)}, bf16[128,2048]{1,0:T(8,128)(2,1)S(1)}, u32[]{:S(2)}, u32[]{:S(2)}) collective-permute-start(bf16[128,2048]{1,0:T(8,128)(2,1)} %refs_0_.1), channel_id=1, source_target_pairs={{4,0},{5,1},{6,2},{7,3},{8,12},{9,13},{10,14},{11,15},{20,16},{21,... | collective-permute-start | bytes 1572872 | tf_op jit(solution)/shard_map/ppermute | solution.py:388
  2.6 19.0 %collective-permute-start = (bf16[128,2048]{1,0:T(8,128)(2,1)}, bf16[128,2048]{1,0:T(8,128)(2,1)S(1)}, u32[]{:S(2)}, u32[]{:S(2)}) collective-permute-start(bf16[128,2048]{1,0:T(8,128)(2,1)} %refs_0_.1), channel_id=1, source_target_pairs={{0,4},{1,5},{2,6},{3,7},{12,8},{13,9},{14,10},{15,11},{16,20},{17,... | collective-permute-start | bytes 1572872 | tf_op jit(solution)/shard_map/ppermute | solution.py:388
  10.4 13.4 %collective-permute-start.3 = (bf16[128,2048]{1,0:T(8,128)(2,1)}, bf16[128,2048]{1,0:T(8,128)(2,1)S(1)}, u32[]{:S(2)}, u32[]{:S(2)}) collective-permute-start(bf16[128,2048]{1,0:T(8,128)(2,1)} %refs_0_.1), channel_id=1, source_target_pairs={{0,2},{1,3},{2,0},{3,1},{4,6},{5,7},{6,4},{7,5},{8,10},{9,11},{10,... | collective-permute-start | bytes 1572872 | tf_op jit(solution)/shard_map/ppermute | solution.py:393
  13.5 13.1 %copy-start.15 = (f32[128,8]{0,1:T(8,128)S(1)}, f32[128,8]{0,1:T(8,128)}, u32[]{:S(2)}) copy-start(f32[128,8]{0,1:T(8,128)} %param.7) | copy-start | bytes 12292
  22.4 1.4 copy-start.8
  23.8 0.8 copy-start.10
  24.6 21.9 %collective-permute-start.4 = (bf16[128,2048]{1,0:T(8,128)(2,1)}, bf16[128,2048]{1,0:T(8,128)(2,1)S(1)}, u32[]{:S(2)}, u32[]{:S(2)}) collective-permute-start(bf16[128,2048]{1,0:T(8,128)(2,1)} %get-tuple-element.39), channel_id=1, source_target_pairs={{4,8},{5,9},{6,10},{7,11},{8,4},{9,5},{10,6},{11,7},{20,24},{21,25... | collective-permute-start | bytes 1572872 | tf_op jit(solution)/shard_map/ppermute | solution.py:388
  25.3 21.2 %collective-permute-start.5 = (bf16[128,2048]{1,0:T(8,128)(2,1)}, bf16[128,2048]{1,0:T(8,128)(2,1)S(1)}, u32[]{:S(2)}, u32[]{:S(2)}) collective-permute-start(bf16[128,2048]{1,0:T(8,128)(2,1)} %get-tuple-element.40), channel_id=1, source_target_pairs={{4,0},{5,1},{6,2},{7,3},{8,12},{9,13},{10,14},{11,15},{20,16},{21,... | collective-permute-start | bytes 1572872 | tf_op jit(solution)/shard_map/ppermute | solution.py:388
  27.3 16.9 %all-to-all-start = ((f32[16,16,128]{2,1,0:T(8,128)}), f32[16,16,128]{2,1,0:T(8,128)S(1)}, u32[]{:S(2)}, u32[]{:S(2)}) async-start(f32[16,16,128]{2,1,0:T(8,128)} %broadcast_in_dim.19), calls=%async_computation | async-start | bytes 262144 | tf_op jit(solution)/shard_map/all_to_all | solution.py:430
  34.3 15.8 %collective-permute-start.6 = (bf16[128,2048]{1,0:T(8,128)(2,1)}, bf16[128,2048]{1,0:T(8,128)(2,1)S(1)}, u32[]{:S(2)}, u32[]{:S(2)}) collective-permute-start(bf16[128,2048]{1,0:T(8,128)(2,1)} %get-tuple-element.41.refs_2_), channel_id=1, source_target_pairs={{0,2},{1,3},{2,0},{3,1},{4,6},{5,7},{6,4},{7,5},{8,10},{9,11},{10,... | collective-permute-start | bytes 1572872 | tf_op jit(solution)/shard_map/ppermute | solution.py:393
  44.2 0.7 copy-start.12
  46.5 3.6 %copy-start.6 = (bf16[128,2048]{1,0:T(8,128)(2,1)}, bf16[128,2048]{1,0:T(8,128)(2,1)S(1)}, u32[]{:S(2)}) copy-start(bf16[128,2048]{1,0:T(8,128)(2,1)S(1)} %collective-permute-done.4.refs_0_) | copy-start | bytes 1572868
  50.1 0.8 copy-start.9
  50.9 16.0 %collective-permute-start.7 = (bf16[128,2048]{1,0:T(8,128)(2,1)}, bf16[128,2048]{1,0:T(8,128)(2,1)S(1)}, u32[]{:S(2)}, u32[]{:S(2)}) collective-permute-start(bf16[128,2048]{1,0:T(8,128)(2,1)} %get-tuple-element.42), channel_id=1, source_target_pairs={{4,0},{5,1},{6,2},{7,3},{8,12},{9,13},{10,14},{11,15},{20,16},{21,... | collective-permute-start | bytes 1572872 | tf_op jit(solution)/shard_map/ppermute | solution.py:388
  52.2 15.6 %collective-permute-start.8 = (bf16[128,2048]{1,0:T(8,128)(2,1)}, bf16[128,2048]{1,0:T(8,128)(2,1)S(1)}, u32[]{:S(2)}, u32[]{:S(2)}) collective-permute-start(bf16[128,2048]{1,0:T(8,128)(2,1)} %get-tuple-element.43.refs_0_), channel_id=1, source_target_pairs={{0,2},{1,3},{2,0},{3,1},{4,6},{5,7},{6,4},{7,5},{8,10},{9,11},{10,... | collective-permute-start | bytes 1572872 | tf_op jit(solution)/shard_map/ppermute | solution.py:393
  67.8 0.9 copy-start.5
  68.7 6.6 %copy-start.4 = (bf16[128,2048]{1,0:T(8,128)(2,1)S(1)}, bf16[128,2048]{1,0:T(8,128)(2,1)}, u32[]{:S(2)}) copy-start(bf16[128,2048]{1,0:T(8,128)(2,1)} %get-tuple-element.46.refs_2_) | copy-start | bytes 1572868
  68.7 57.3 %all-to-all-start.1 = ((bf16[16,96,768]{2,1,0:T(8,128)(2,1)}), bf16[16,96,768]{2,1,0:T(8,128)(2,1)S(1)}, u32[]{:S(2)}, u32[]{:S(2)}) async-start(bf16[16,96,768]{2,1,0:T(8,128)(2,1)} %bitcast.31), calls=%async_computation.1 | async-start | bytes 4718592 | tf_op jit(solution)/shard_map/all_to_all | solution.py:448
  74.8 3.9 %collective-permute-start.10 = (bf16[4,96,2048]{2,1,0:T(8,128)(2,1)}, bf16[4,96,2048]{2,1,0:T(8,128)(2,1)}, u32[]{:S(2)}, u32[]{:S(2)}) collective-permute-start(bf16[4,96,2048]{2,1,0:T(8,128)(2,1)} %get-tuple-element.44.refs_3_), channel_id=1, source_target_pairs={{0,1},{1,0},{2,3},{3,2},{4,5},{5,4},{6,7},{7,6},{8,9},{9,8},{10,11... | collective-permute-start | bytes 4718600 | tf_op jit(solution)/shard_map/ppermute | solution.py:393
  75.3 34.0 %collective-permute-start.9 = (bf16[128,2048]{1,0:T(8,128)(2,1)S(1)}, bf16[128,2048]{1,0:T(8,128)(2,1)S(1)}, u32[]{:S(2)}, u32[]{:S(2)}) collective-permute-start(bf16[128,2048]{1,0:T(8,128)(2,1)S(1)} %copy-done.4), channel_id=1, source_target_pairs={{0,2},{1,3},{2,0},{3,1},{4,6},{5,7},{6,4},{7,5},{8,10},{9,11},{10,... | collective-permute-start | bytes 1572872 | tf_op jit(solution)/shard_map/ppermute | solution.py:393
  109.2 0.8 copy-start.11
  116.8 3.8 %collective-permute-start.11 = (bf16[4,96,2048]{2,1,0:T(8,128)(2,1)}, bf16[4,96,2048]{2,1,0:T(8,128)(2,1)}, u32[]{:S(2)}, u32[]{:S(2)}) collective-permute-start(bf16[4,96,2048]{2,1,0:T(8,128)(2,1)} %get-tuple-element.51), channel_id=1, source_target_pairs={{0,1},{1,0},{2,3},{3,2},{4,5},{5,4},{6,7},{7,6},{8,9},{9,8},{10,11... | collective-permute-start | bytes 4718600 | tf_op jit(solution)/shard_map/ppermute | solution.py:393
  126.0 1.4 copy-start.1
  133.5 13.4 %collective-permute-start.12 = (bf16[8,96,2048]{2,1,0:T(8,128)(2,1)}, bf16[8,96,2048]{2,1,0:T(8,128)(2,1)}, u32[]{:S(2)}, u32[]{:S(2)}) collective-permute-start(bf16[8,96,2048]{2,1,0:T(8,128)(2,1)} %forward_rows.3), channel_id=1, source_target_pairs={{0,1},{1,0},{2,3},{3,2},{4,5},{5,4},{6,7},{7,6},{8,9},{9,8},{10,11... | collective-permute-start | bytes 9437192 | tf_op jit(solution)/shard_map/ppermute | solution.py:393
  133.6 78.8 %all-to-all-start.2 = ((bf16[16,96,768]{2,1,0:T(8,128)(2,1)}), bf16[16,96,768]{2,1,0:T(8,128)(2,1)S(1)}, u32[]{:S(2)}, u32[]{:S(2)}) async-start(bf16[16,96,768]{2,1,0:T(8,128)(2,1)} %get-tuple-element.63), calls=%async_computation.2 | async-start | bytes 4718592 | tf_op jit(solution)/shard_map/all_to_all | solution.py:459
  152.0 25.4 %collective-permute-start.16 = (bf16[128,2048]{1,0:T(8,128)(2,1)}, bf16[128,2048]{1,0:T(8,128)(2,1)S(1)}, u32[]{:S(2)}, u32[]{:S(2)}) collective-permute-start(bf16[128,2048]{1,0:T(8,128)(2,1)} %get-tuple-element.62), channel_id=1, source_target_pairs={{0,2},{1,3},{2,0},{3,1},{4,6},{5,7},{6,4},{7,5},{8,10},{9,11},{10,... | collective-permute-start | bytes 1572872 | tf_op jit(solution)/shard_map/ppermute | solution.py:393
  153.9 38.7 %collective-permute-start.15 = (bf16[128,2048]{1,0:T(8,128)(2,1)}, bf16[128,2048]{1,0:T(8,128)(2,1)S(1)}, u32[]{:S(2)}, u32[]{:S(2)}) collective-permute-start(bf16[128,2048]{1,0:T(8,128)(2,1)} %get-tuple-element.60), channel_id=1, source_target_pairs={{0,2},{1,3},{2,0},{3,1},{4,6},{5,7},{6,4},{7,5},{8,10},{9,11},{10,... | collective-permute-start | bytes 1572872 | tf_op jit(solution)/shard_map/ppermute | solution.py:393
  159.0 43.3 %copy-start.16 = (s32[1,1024]{1,0:T(1,128)S(1)}, s32[1,1024]{1,0:T(1,128)}, u32[]{:S(2)}) copy-start(s32[1,1024]{1,0:T(1,128)} %get-tuple-element.64) | copy-start | bytes 12292
  178.6 13.9 %collective-permute-start.17 = (bf16[128,2048]{1,0:T(8,128)(2,1)S(1)}, bf16[128,2048]{1,0:T(8,128)(2,1)S(1)}, u32[]{:S(2)}, u32[]{:S(2)}) collective-permute-start(bf16[128,2048]{1,0:T(8,128)(2,1)S(1)} %fusion.1), channel_id=1, source_target_pairs={{0,4},{1,5},{2,6},{3,7},{12,8},{13,9},{14,10},{15,11},{16,20},{17,... | collective-permute-start | bytes 1572872 | tf_op jit(solution)/shard_map/ppermute | solution.py:388
  181.2 23.5 %collective-permute-start.14 = (bf16[128,2048]{1,0:T(8,128)(2,1)}, bf16[128,2048]{1,0:T(8,128)(2,1)S(1)}, u32[]{:S(2)}, u32[]{:S(2)}) collective-permute-start(bf16[128,2048]{1,0:T(8,128)(2,1)} %get-tuple-element.58), channel_id=1, source_target_pairs={{0,2},{1,3},{2,0},{3,1},{4,6},{5,7},{6,4},{7,5},{8,10},{9,11},{10,... | collective-permute-start | bytes 1572872 | tf_op jit(solution)/shard_map/ppermute | solution.py:393
  194.7 15.3 %collective-permute-start.18 = (bf16[128,2048]{1,0:T(8,128)(2,1)}, bf16[128,2048]{1,0:T(8,128)(2,1)}, u32[]{:S(2)}, u32[]{:S(2)}) collective-permute-start(bf16[128,2048]{1,0:T(8,128)(2,1)} %add_convert_fusion.3), channel_id=1, source_target_pairs={{0,4},{1,5},{2,6},{3,7},{12,8},{13,9},{14,10},{15,11},{16,20},{17,... | collective-permute-start | bytes 1572872 | tf_op jit(solution)/shard_map/ppermute | solution.py:388
  200.7 19.3 %collective-permute-start.21 = (bf16[128,2048]{1,0:T(8,128)(2,1)}, bf16[128,2048]{1,0:T(8,128)(2,1)}, u32[]{:S(2)}, u32[]{:S(2)}) collective-permute-start(bf16[128,2048]{1,0:T(8,128)(2,1)} %add_convert_fusion.3), channel_id=1, source_target_pairs={{4,8},{5,9},{6,10},{7,11},{8,4},{9,5},{10,6},{11,7},{20,24},{21,25... | collective-permute-start | bytes 1572872 | tf_op jit(solution)/shard_map/ppermute | solution.py:388
  204.3 37.4 %collective-permute-start.13 = (bf16[128,2048]{1,0:T(8,128)(2,1)}, bf16[128,2048]{1,0:T(8,128)(2,1)}, u32[]{:S(2)}, u32[]{:S(2)}) collective-permute-start(bf16[128,2048]{1,0:T(8,128)(2,1)} %get-tuple-element.56), channel_id=1, source_target_pairs={{0,2},{1,3},{2,0},{3,1},{4,6},{5,7},{6,4},{7,5},{8,10},{9,11},{10,... | collective-permute-start | bytes 1572872 | tf_op jit(solution)/shard_map/ppermute | solution.py:393
  204.7 5.2 %copy-start.14 = (bf16[128,2048]{1,0:T(8,128)(2,1)}, bf16[128,2048]{1,0:T(8,128)(2,1)S(1)}, u32[]{:S(2)}) copy-start(bf16[128,2048]{1,0:T(8,128)(2,1)S(1)} %collective-permute-done.14) | copy-start | bytes 1572868
  210.0 10.0 %copy-start.7 = (bf16[128,2048]{1,0:T(8,128)(2,1)S(1)}, bf16[128,2048]{1,0:T(8,128)(2,1)}, u32[]{:S(2)}) copy-start(bf16[128,2048]{1,0:T(8,128)(2,1)} %get-tuple-element.61) | copy-start | bytes 1572868
  212.5 1.5 copy-start.3
  213.9 9.4 %copy-start.2 = (bf16[16,96,768]{2,1,0:T(8,128)(2,1)S(1)}, bf16[16,96,768]{2,1,0:T(8,128)(2,1)}, u32[]{:S(2)}) copy-start(bf16[16,96,768]{2,1,0:T(8,128)(2,1)} %after.8) | copy-start | bytes 7077892
  214.0 27.7 %collective-permute-start.19 = (bf16[128,2048]{1,0:T(8,128)(2,1)}, bf16[128,2048]{1,0:T(8,128)(2,1)S(1)}, u32[]{:S(2)}, u32[]{:S(2)}) collective-permute-start(bf16[128,2048]{1,0:T(8,128)(2,1)} %after.9), channel_id=1, source_target_pairs={{0,4},{1,5},{2,6},{3,7},{12,8},{13,9},{14,10},{15,11},{16,20},{17,... | collective-permute-start | bytes 1572872 | tf_op jit(solution)/shard_map/ppermute | solution.py:388
  218.5 23.2 %collective-permute-start.20 = (bf16[128,2048]{1,0:T(8,128)(2,1)}, bf16[128,2048]{1,0:T(8,128)(2,1)}, u32[]{:S(2)}, u32[]{:S(2)}) collective-permute-start(bf16[128,2048]{1,0:T(8,128)(2,1)} %after.9), channel_id=1, source_target_pairs={{4,8},{5,9},{6,10},{7,11},{8,4},{9,5},{10,6},{11,7},{20,24},{21,25... | collective-permute-start | bytes 1572872 | tf_op jit(solution)/shard_map/ppermute | solution.py:388
  222.1 19.6 %collective-permute-start.22 = (bf16[128,2048]{1,0:T(8,128)(2,1)}, bf16[128,2048]{1,0:T(8,128)(2,1)S(1)}, u32[]{:S(2)}, u32[]{:S(2)}) collective-permute-start(bf16[128,2048]{1,0:T(8,128)(2,1)} %add_convert_fusion.1), channel_id=1, source_target_pairs={{4,0},{5,1},{6,2},{7,3},{8,12},{9,13},{10,14},{11,15},{20,16},{21,... | collective-permute-start | bytes 1572872 | tf_op jit(solution)/shard_map/ppermute | solution.py:388
  232.7 9.0 %copy-start.13 = (bf16[128,2048]{1,0:T(8,128)(2,1)S(1)}, bf16[128,2048]{1,0:T(8,128)(2,1)}, u32[]{:S(2)}) copy-start(bf16[128,2048]{1,0:T(8,128)(2,1)} %get-tuple-element.55) | copy-start | bytes 1572868

commit v10 on v9

--- a/solution.py
+++ b/solution.py
@@ -296,46 +296,44 @@
     )(here, weight, rows, z_rows, back)
 
 
-def forward_kernel(capacity, turn, here_ref, rank_ref, gate_ref, h_ref, weight_ref, out_ref):
-    each = out_ref.shape[0]
-    lane = (here_ref[0] % 2) ^ turn
-    flat = h_ref[...].reshape(each * capacity, h_ref.shape[3])
+def forward_kernel(capacity, slots, turn, here_ref, rank_ref, gate_ref, weight_ref, *refs):
+    blocks, out_ref = refs[:-1], refs[-1]
+    sources = lane_sources(here_ref[0], slots, (here_ref[0] % 2) ^ turn)
+    flat = jnp.concatenate([block[0, 0] for block in blocks], axis=0)
     out = jnp.dot(flat, weight_ref[...], preferred_element_type=F32).astype(BF16).astype(F32)
-    for j in range(each):
-        source = (pl.program_id(0) * each + j) * 2 + lane
+    for j, source in enumerate(sources):
         gate = gate_column(gate_ref, chosen_rows(rank_ref, 0, source, capacity), 0, source)
         out_ref[j] = (out[j * capacity:(j + 1) * capacity, :] * gate).astype(BF16)
 
 
-def forward_rows(here, rank, gate, rows_h, weight, turn, each=4):
+def forward_rows(here, rank, gate, rows_h, weight, slots, turn):
     devices, capacity, hidden = rows_h.shape
     width = weight.shape[1]
+    count = 2 * len(slots)
+
+    def block(j):
+        return lambda i, here: (lane_sources(here[0], slots, 0)[j] // 2, (here[0] % 2) ^ turn, 0, 0)
+
     whole = pl.BlockSpec(rank.shape, lambda i, here: (0, 0, 0))
-    return pl.pallas_call(
-        functools.partial(forward_kernel, capacity, turn),
+    rows = rows_h.reshape(devices // 2, 2, capacity, hidden)
+    return pl.pallas_call(
+        functools.partial(forward_kernel, capacity, slots, turn),
         grid_spec=pltpu.PrefetchScalarGridSpec(
             num_scalar_prefetch=1,
-            grid=(devices // 2 // each,),
-            in_specs=[
-                whole,
-                whole,
-                pl.BlockSpec((each, 1, capacity, hidden), lambda i, here: (i, (here[0] % 2) ^ turn, 0, 0)),
-                pl.BlockSpec((hidden, width), lambda i, here: (0, 0)),
-            ],
-            out_specs=pl.BlockSpec((each, capacity, width), lambda i, here: (i, 0, 0)),
+            grid=(1,),
+            in_specs=[whole, whole, pl.BlockSpec((hidden, width), lambda i, here: (0, 0))]
+            + [pl.BlockSpec((1, 1, capacity, hidden), block(j)) for j in range(count)],
+            out_specs=pl.BlockSpec((count, capacity, width), lambda i, here: (0, 0, 0)),
         ),
-        out_shape=jax.ShapeDtypeStruct((devices // 2, capacity, width), BF16),
+        out_shape=jax.ShapeDtypeStruct((count, capacity, width), BF16),
         compiler_params=pltpu.CompilerParams(vmem_limit_bytes=60 * MIB),
         cost_estimate=BRIEF,
         name="forward_rows",
-    )(here, rank, gate, rows_h.reshape(devices // 2, 2, capacity, hidden), weight)
-
-
-ORDER = (3, 2, 1, 0)
-
-
-def sum_kernel(capacity, turn, here_ref, rank_ref, own_ref, other_ref, *part_refs):
-    for step, slot in enumerate(ORDER):
+    )(here, rank, gate, weight, *[rows] * count)
+
+
+def sum_kernel(capacity, slots, turn, here_ref, rank_ref, own_ref, other_ref, *part_refs):
+    for step, slot in enumerate(slots):
 
         @pl.when(pl.program_id(0) == step)
         def _():
@@ -348,29 +346,19 @@
             part_refs[step][...] = part.astype(BF16)
 
 
-def summed(here, rank, own, other, turn):
+def summed(here, rank, own, other, slots, turn):
     _, capacity, width = own.shape
     tokens = rank.shape[2]
-
-    def block(i, here):
-        place = jnp.int32(0)
-        for step, slot in enumerate(ORDER):
-            place = jnp.where(i == step, lane_sources(here[0], (slot,), 0)[turn] // 2, place)
-        return (place, 0, 0)
-
-    return pl.pallas_call(
-        functools.partial(sum_kernel, capacity, turn),
+    block = pl.BlockSpec((1, capacity, width), lambda i, here: (2 * i + turn, 0, 0))
+    return pl.pallas_call(
+        functools.partial(sum_kernel, capacity, slots, turn),
         grid_spec=pltpu.PrefetchScalarGridSpec(
             num_scalar_prefetch=1,
-            grid=(len(ORDER),),
-            in_specs=[
-                pl.BlockSpec(rank.shape, lambda i, here: (0, 0, 0)),
-                pl.BlockSpec((1, capacity, width), block),
-                pl.BlockSpec((1, capacity, width), block),
-            ],
-            out_specs=[pl.BlockSpec((tokens, width), lambda i, here: (0, 0))] * len(ORDER),
+            grid=(len(slots),),
+            in_specs=[pl.BlockSpec(rank.shape, lambda i, here: (0, 0, 0)), block, block],
+            out_specs=[pl.BlockSpec((tokens, width), lambda i, here: (0, 0))] * len(slots),
         ),
-        out_shape=[jax.ShapeDtypeStruct((tokens, width), BF16)] * len(ORDER),
+        out_shape=[jax.ShapeDtypeStruct((tokens, width), BF16)] * len(slots),
         compiler_params=pltpu.CompilerParams(vmem_limit_bytes=60 * MIB),
         cost_estimate=BRIEF,
         name="summed",
@@ -427,8 +415,6 @@
 
     routing = jnp.concatenate([slot_ids.T.astype(F32), gates.T], axis=0)
     routing = jnp.broadcast_to(routing, (devices,) + routing.shape)
-    routing = lax.all_to_all(routing, "expert", split_axis=0, concat_axis=0, tiled=True)
-    rank, gate = route(here, routing, top)
     place, send_h = pack(slot_ids.reshape(1, -1), h_flat, devices, capacity)
 
     own = cotangent
@@ -439,17 +425,19 @@
     from_far, from_middle = passed(INNER, start_end), passed(ENDS, start_inner)
     near_y = swapped_with(near, 2)
     middle = added(from_far, from_middle)
-    start_far, middle = after((from_far, middle), near_y, rank)
+    start_far, middle, routing = after((from_far, middle, routing), near_y, send_h)
     last = added(from_end, passed(ENDS, start_far))
     middle_y = swapped_with(middle, 2)
-    z_rows, back, sibling = scaled_rows(here, rank, gate, weight, [own, own_y, near, near_y], (0, 1), capacity, [])
-    send_h, last = after((send_h, last), middle_y, sibling)
-    sibling = swapped_with(sibling, 1)
+    routing = lax.all_to_all(routing, "expert", split_axis=0, concat_axis=0, tiled=True)
+    rank, gate = route(here, routing, top)
+    send_h, last = after((send_h, last), middle_y, rank)
     rows_h = lax.all_to_all(
         send_h.reshape(devices, capacity, hidden), "expert", split_axis=0, concat_axis=0, tiled=True
     )
     last_y = swapped_with(last, 2)
 
+    z_rows, back, sibling = scaled_rows(here, rank, gate, weight, [own, own_y, near, near_y], (0, 1), capacity, [])
+    sibling = swapped_with(sibling, 1)
     z_rows, back, _ = sibling_rows(here, weight, sibling, (0, 1), z_rows, back)
     z_rows, back, sibling_last = scaled_rows(
         here, rank, gate, weight, [middle, middle_y, last, last_y], (2, 3), capacity, [z_rows, back]
@@ -459,11 +447,19 @@
     back_rows = lax.all_to_all(back, "expert", split_axis=0, concat_axis=0, tiled=True).reshape(-1, hidden)
 
     rows_h, = after((rows_h,), ready)
-    other = swapped_with(forward_rows(here, rank, gate, rows_h, weight, 1), 1)
-    mine = forward_rows(here, rank, gate, rows_h, weight, 0)
-    across = [swapped_with(part, 2) for part in summed(here, rank, mine, other, 1)]
-    beside = summed(here, rank, mine, other, 0)
+    beside, across = [], []
+    for slots in ((3, 2), (1, 0)):
+        other = swapped_with(forward_rows(here, rank, gate, rows_h, weight, slots, 1), 1)
+        mine = forward_rows(here, rank, gate, rows_h, weight, slots, 0)
+        across += [swapped_with(part, 2) for part in summed(here, rank, mine, other, slots, 1)]
+        beside += summed(here, rank, mine, other, slots, 0)
+    grad_sum = lax.dot_general(
+        rows_h.reshape(-1, hidden), z_rows.reshape(devices * capacity, -1), (((0,), (0,)), ((), ())),
+        preferred_element_type=F32,
+    )
+    weight_grad = grad_sum.astype(BF16)[None]
     far, mid, close, kept = zip(beside, across)
+    far = (*after((far[0],), weight_grad), far[1])
     outer1 = passed(OUTER, added(*far))
     mid = added(*mid, outer1)
     outer2, inner2 = passed(OUTER, mid), passed(INNER, mid)
@@ -472,16 +468,12 @@
     ends3 = passed(ENDS, added(*far, inner2))
     mixed = added(*kept, outer3, inner3, ends3)
 
-    grad_sum = lax.dot_general(
-        rows_h.reshape(-1, hidden), z_rows.reshape(devices * capacity, -1), (((0,), (0,)), ((), ())),
-        preferred_element_type=F32,
-    )
     h_grad, gate_grad = unpack(place.reshape(-1, 1), gates.reshape(-1, 1), h_flat, back_rows)
     return (
         mixed,
         gate_grad.reshape(tokens, top),
         h_grad.reshape(tokens, top, hidden),
-        grad_sum.astype(BF16)[None],
+        weight_grad,
     )
 
 

time: 245 us -> 230 us (0.939)
  waiting for transfers between devices: 83.6 us -> 71.5 us
  Pallas kernels: 60.7 us -> 68.3 us
  starting transfers between devices: 61.6 us -> 54.6 us
  other arithmetic: 15.3 us -> 12.3 us
    ppermute x11 -> x12, waiting for transfers between devices: 62.3 us -> 38.3 us  [swapped_with(): return lax.ppermute(value, 'expert', [(i, i ^ bit) for i in range(devices)])]
    ppermute x12, waiting for transfers between devices: 13.4 us -> 25.5 us  [passed(): lax.ppermute(value, 'expert', [(a * 4 + lane, b * 4 + lane) for a, b in p...]
    pallas_call x4 -> x8, Pallas kernels: 22.3 us -> 30 us  [the longest x4 18.5 us: forward_rows(): pl.pallas_call(functools.partial(forward_kernel, capacity, slots, turn),...]
    ppermute x12, starting transfers between devices: 30.4 us -> 27.1 us  [passed(): lax.ppermute(value, 'expert', [(a * 4 + lane, b * 4 + lane) for a, b in p...]
    ppermute x11 -> x12, starting transfers between devices: 10.9 us -> 9.89 us  [swapped_with(): return lax.ppermute(value, 'expert', [(i, i ^ bit) for i in range(devices)])]
    unnamed x37 -> x41, local copies, waits for them, and re-layouts: 8.38 us -> 8.27 us
  transfers between devices with their start and end apart: 26 -> 27, of which waited for: 10 -> 14; matrix products, arithmetic and copies ran while one was open for 11% -> 11% of each run, Pallas kernels for 22% -> 28%
where the time goes in v10:
time: 230 us
  waiting for transfers between devices  71.5 us (31%)
  Pallas kernels  68.3 us (30%)
  starting transfers between devices  54.6 us (24%)
  local copies, waits for them, and re-layouts  12.6 us (5%)
  other arithmetic  12.3 us (5%)
  matrix products  9.3 us (4%)
    ppermute x12, waiting for transfers between devices, swapped_with(): return lax.ppermute(value, 'expert', [(i, i ^ bit) for i in range(devices)])  38.3 us
    ppermute x12, starting transfers between devices, passed(): lax.ppermute(value, 'expert', [(a * 4 + lane, b * 4 + lane) for a, b in p...  27.1 us
    ppermute x12, waiting for transfers between devices, passed(): lax.ppermute(value, 'expert', [(a * 4 + lane, b * 4 + lane) for a, b in p...  25.5 us
    pallas_call x4, Pallas kernels, forward_rows(): pl.pallas_call(functools.partial(forward_kernel, capacity, slots, turn),...  18.5 us
    pallas_call x2, Pallas kernels, scaled_rows(): pl.pallas_call(functools.partial(scale_kernel, capacity, slots, len(buffe...  13.6 us
    pallas_call x4, Pallas kernels, summed(): pl.pallas_call(functools.partial(sum_kernel, capacity, slots, turn), grid...  11.4 us
    convert_element_type x8, other arithmetic, added(): return total.astype(BF16)  10.9 us
    pallas_call x2, Pallas kernels, sibling_rows(): pl.pallas_call(functools.partial(sibling_kernel, capacity, slots), in_spe...  10.5 us
  transfers between devices with their start and end apart: 27, of which 14 were waited for; matrix products, arithmetic and copies ran while one was open for 11% of the time, Pallas kernels for 28%

profile of v10, /device:TPU:0, one launch (start us, length us, event | category | flops | bytes accessed | tf_op | source)
XLA Modules:
  0.0 229.6 jit_solution(12020899764172301228)
XLA Ops:
  0.6 5.0 %collective-permute-start = (bf16[128,2048]{1,0:T(8,128)(2,1)}, bf16[128,2048]{1,0:T(8,128)(2,1)S(1)}, u32[]{:S(2)}, u32[]{:S(2)}) collective-permute-start(bf16[128,2048]{1,0:T(8,128)(2,1)} %refs_0_.1), channel_id=1, source_target_pairs={{0,4},{1,5},{2,6},{3,7},{12,8},{13,9},{14,10},{15,11},{16,20},{17,... | collective-permute-start | bytes 1572872 | tf_op jit(solution)/shard_map/ppermute | solution.py:376
  6.3 1.3 collective-permute-start.2
  7.6 1.6 collective-permute-start.3
  9.9 7.2 %collective-permute-done = bf16[128,2048]{1,0:T(8,128)(2,1)S(1)} collective-permute-done((bf16[128,2048]{1,0:T(8,128)(2,1)}, bf16[128,2048]{1,0:T(8,128)(2,1)S(1)}, u32[]{:S(2)}, u32[]{:S(2)}) %collective-permute-start) | collective-permute-done | bytes 524320 | tf_op jit(solution)/shard_map/ppermute | solution.py:376
  17.1 0.8 copy.42.refs_0_
  17.9 3.9 %collective-permute-done.2 = bf16[128,2048]{1,0:T(8,128)(2,1)S(1)} collective-permute-done((bf16[128,2048]{1,0:T(8,128)(2,1)}, bf16[128,2048]{1,0:T(8,128)(2,1)S(1)}, u32[]{:S(2)}, u32[]{:S(2)}) %collective-permute-start.2) | collective-permute-done | bytes 524320 | tf_op jit(solution)/shard_map/ppermute | solution.py:376
  21.8 1.0 add_convert_fusion.6.refs_2_
  22.8 0.8 copy-done.9
  24.3 1.3 collective-permute-start.5
  25.7 1.6 collective-permute-start.6
  28.1 5.6 %pack.1 = (s32[1,1024]{1,0:T(1,128)}, bf16[1536,768]{1,0:T(8,128)(2,1)}) custom-call(s32[1,1024]{1,0:T(1,128)} %reshape.76.ids_ref, bf16[1024,768]{1,0:T(8,128)(2,1)} %bitcast.46), custom_call_target="tpu_custom_call" | custom-call | tf_op jit(solution)/shard_map/pack/pallas_call | solution.py:92
  33.7 5.9 %collective-permute-done.5 = bf16[128,2048]{1,0:T(8,128)(2,1)S(1)} collective-permute-done((bf16[128,2048]{1,0:T(8,128)(2,1)}, bf16[128,2048]{1,0:T(8,128)(2,1)S(1)}, u32[]{:S(2)}, u32[]{:S(2)}) %collective-permute-start.5) | collective-permute-done | bytes 524320 | tf_op jit(solution)/shard_map/ppermute | solution.py:376
  39.6 0.9 add_convert_fusion.5.refs_1_
  40.5 0.7 broadcast_in_dim.19.refs_2_
  41.4 1.3 collective-permute-start.7
  42.6 5.3 %all-to-all-start = ((f32[16,16,128]{2,1,0:T(8,128)}), f32[16,16,128]{2,1,0:T(8,128)S(1)}, u32[]{:S(2)}, u32[]{:S(2)}) async-start(f32[16,16,128]{2,1,0:T(8,128)} %get-tuple-element.41), calls=%async_computation | async-start | bytes 262144 | tf_op jit(solution)/shard_map/all_to_all | solution.py:431
  47.9 1.9 collective-permute-start.8
  49.9 7.7 %all-to-all-done.routing_ref = f32[16,16,128]{2,1,0:T(8,128)S(1)} async-done(((f32[16,16,128]{2,1,0:T(8,128)}), f32[16,16,128]{2,1,0:T(8,128)S(1)}, u32[]{:S(2)}, u32[]{:S(2)}) %all-to-all-start) | async-done | bytes 131104 | tf_op jit(solution)/shard_map/all_to_all | solution.py:431
  58.3 1.7 route.1
  59.9 0.9 add_convert_fusion.4.refs_1_
  60.9 2.9 %collective-permute-done.8.refs_2_.refs_1_ = bf16[128,2048]{1,0:T(8,128)(2,1)S(1)} collective-permute-done((bf16[128,2048]{1,0:T(8,128)(2,1)}, bf16[128,2048]{1,0:T(8,128)(2,1)S(1)}, u32[]{:S(2)}, u32[]{:S(2)}) %collective-permute-start.8) | collective-permute-done | bytes 524320 | tf_op jit(solution)/shard_map/ppermute | solution.py:381
  63.7 0.9 copy-done.6
  64.6 5.1 %all-to-all-start.1 = ((bf16[16,96,768]{2,1,0:T(8,128)(2,1)}), bf16[16,96,768]{2,1,0:T(8,128)(2,1)S(1)}, u32[]{:S(2)}, u32[]{:S(2)}) async-start(bf16[16,96,768]{2,1,0:T(8,128)(2,1)} %bitcast.45), calls=%async_computation.1 | async-start | bytes 4718592 | tf_op jit(solution)/shard_map/all_to_all | solution.py:434
  69.7 6.8 %scaled_rows.2 = (bf16[16,96,2048]{2,1,0:T(8,128)(2,1)}, bf16[16,96,768]{2,1,0:T(8,128)(2,1)}, bf16[4,96,2048]{2,1,0:T(8,128)(2,1)}) custom-call(s32[1]{0:T(128)} %bitcast.here_ref, s32[2,16,128]{2,1,0:T(8,128)} %get-tuple-element.42.refs_3_.rank_ref, f32[2,16,128]{2,1,0:T(8,128)} %get-tuple-element.43.gate_ref, bf16[768,2048]{1,0:T(8,128)(2,1)} %bitcast.37, ...), custom_call_target="tpu_custom_call" | custom-call | tf_op jit(solution)/shard_map/scaled_rows/pallas_call | solution.py:239
  77.0 1.7 collective-permute-start.9
  78.7 1.7 collective-permute-done.10.rows_ref
  80.4 5.3 %sibling_rows.2 = (bf16[16,96,2048]{2,1,0:T(8,128)(2,1)}, bf16[16,96,768]{2,1,0:T(8,128)(2,1)}, f32[8,128]{1,0:T(8,128)}) custom-call(s32[1]{0:T(128)} %bitcast.here_ref, bf16[768,2048]{1,0:T(8,128)(2,1)} %bitcast.38, bf16[4,96,2048]{2,1,0:T(8,128)(2,1)} %collective-permute-done.10.rows_ref, ...), custom_call_target="tpu_custom_call", output_to_operand_aliasing={{0}: (3, {}), {1}: (4, {})} | custom-call | tf_op jit(solution)/shard_map/sibling_rows/pallas_call | solution.py:278
  85.6 18.4 %collective-permute-done.9.refs_3_ = bf16[128,2048]{1,0:T(8,128)(2,1)S(1)} collective-permute-done((bf16[128,2048]{1,0:T(8,128)(2,1)S(1)}, bf16[128,2048]{1,0:T(8,128)(2,1)S(1)}, u32[]{:S(2)}, u32[]{:S(2)}) %collective-permute-start.9) | collective-permute-done | bytes 524320 | tf_op jit(solution)/shard_map/ppermute | solution.py:381
  104.1 0.8 copy-done.11
  104.9 6.8 %scaled_rows.3 = (bf16[16,96,2048]{2,1,0:T(8,128)(2,1)}, bf16[16,96,768]{2,1,0:T(8,128)(2,1)}, bf16[4,96,2048]{2,1,0:T(8,128)(2,1)}) custom-call(s32[1]{0:T(128)} %bitcast.here_ref, s32[2,16,128]{2,1,0:T(8,128)} %get-tuple-element.42.refs_3_.rank_ref, f32[2,16,128]{2,1,0:T(8,128)} %get-tuple-element.43.gate_ref, ...), custom_call_target="tpu_custom_call", output_to_operand_aliasing={{0}: (8, {}), {1}: (9, {})} | custom-call | tf_op jit(solution)/shard_map/scaled_rows/pallas_call | solution.py:239
  111.7 3.7 %collective-permute-done.11.rows_ref = bf16[4,96,2048]{2,1,0:T(8,128)(2,1)} collective-permute-done((bf16[4,96,2048]{2,1,0:T(8,128)(2,1)}, bf16[4,96,2048]{2,1,0:T(8,128)(2,1)}, u32[]{:S(2)}, u32[]{:S(2)}) %collective-permute-start.11) | collective-permute-done | bytes 1572896 | tf_op jit(solution)/shard_map/ppermute | solution.py:381
  115.5 5.3 %sibling_rows.3 = (bf16[16,96,2048]{2,1,0:T(8,128)(2,1)}, bf16[16,96,768]{2,1,0:T(8,128)(2,1)}, f32[8,128]{1,0:T(8,128)}) custom-call(s32[1]{0:T(128)} %bitcast.here_ref, bf16[768,2048]{1,0:T(8,128)(2,1)} %bitcast.40, bf16[4,96,2048]{2,1,0:T(8,128)(2,1)} %collective-permute-done.11.rows_ref, ...), custom_call_target="tpu_custom_call", output_to_operand_aliasing={{0}: (3, {}), {1}: (4, {})} | custom-call | tf_op jit(solution)/shard_map/sibling_rows/pallas_call | solution.py:278
  120.8 1.5 copy-done.1
  122.2 4.6 %forward_rows.7 = bf16[4,96,2048]{2,1,0:T(8,128)(2,1)} custom-call(s32[1]{0:T(128)} %bitcast.here_ref, s32[2,16,128]{2,1,0:T(8,128)} %get-tuple-element.42.refs_3_.rank_ref, f32[2,16,128]{2,1,0:T(8,128)} %get-tuple-element.43.gate_ref, bf16[768,2048]{1,0:T(8,128)(2,1)} %bitcast.41, bf16[8,2,96,768]{3,2,1,0:T(8,128)(2,1)} %bitcast.21, ...), custom_call_target="tpu_custom_call" | custom-call | tf_op jit(solution)/shard_map/forward_rows/pallas_call | solution.py:319
  127.0 7.2 %all-to-all-start.2 = ((bf16[16,96,768]{2,1,0:T(8,128)(2,1)}), bf16[16,96,768]{2,1,0:T(8,128)(2,1)}, u32[]{:S(2)}, u32[]{:S(2)}) async-start(bf16[16,96,768]{2,1,0:T(8,128)(2,1)} %get-tuple-element.66), calls=%async_computation.2 | async-start | bytes 4718592 | tf_op jit(solution)/shard_map/all_to_all | solution.py:447
  134.2 4.6 %forward_rows.5 = bf16[4,96,2048]{2,1,0:T(8,128)(2,1)} custom-call(s32[1]{0:T(128)} %bitcast.here_ref, s32[2,16,128]{2,1,0:T(8,128)} %get-tuple-element.42.refs_3_.rank_ref, f32[2,16,128]{2,1,0:T(8,128)} %get-tuple-element.43.gate_ref, bf16[768,2048]{1,0:T(8,128)(2,1)} %bitcast.42, bf16[8,2,96,768]{3,2,1,0:T(8,128)(2,1)} %bitcast.25, ...), custom_call_target="tpu_custom_call" | custom-call | tf_op jit(solution)/shard_map/forward_rows/pallas_call | solution.py:319
  138.8 4.6 %forward_rows.6.own_ref = bf16[4,96,2048]{2,1,0:T(8,128)(2,1)} custom-call(s32[1]{0:T(128)} %bitcast.here_ref, s32[2,16,128]{2,1,0:T(8,128)} %get-tuple-element.42.refs_3_.rank_ref, f32[2,16,128]{2,1,0:T(8,128)} %get-tuple-element.43.gate_ref, bf16[768,2048]{1,0:T(8,128)(2,1)} %bitcast.43, bf16[8,2,96,768]{3,2,1,0:T(8,128)(2,1)} %bitcast.29, ...), custom_call_target="tpu_custom_call" | custom-call | tf_op jit(solution)/shard_map/forward_rows/pallas_call | solution.py:319
  143.8 3.0 %summed.7 = (bf16[128,2048]{1,0:T(8,128)(2,1)}, bf16[128,2048]{1,0:T(8,128)(2,1)}) custom-call(s32[1]{0:T(128)} %bitcast.here_ref, s32[2,16,128]{2,1,0:T(8,128)} %get-tuple-element.42.refs_3_.rank_ref, bf16[4,96,2048]{2,1,0:T(8,128)(2,1)} %forward_rows.6.own_ref, bf16[4,96,2048]{2,1,0:T(8,128)(2,1)} %collective-permute-done.15.other_ref), custom_call_target="tpu_custom_call" | custom-call | tf_op jit(solution)/shard_map/summed/pallas_call | solution.py:353
  146.8 1.6 collective-permute-start.17
  148.4 9.3 %fusion.refs_1_ = bf16[1,768,2048]{2,1,0:T(8,128)(2,1)} fusion(bf16[16,96,768]{2,1,0:T(8,128)(2,1)S(1)} %copy-done.2, bf16[16,96,2048]{2,1,0:T(8,128)(2,1)} %get-tuple-element.64), kind=kOutput, calls=%fused_computation.2 | convolution fusion | flops 4833411072 | bytes 11796480 | tf_op jit(solution)/shard_map/dot_general | solution.py:456
  158.2 2.8 %summed.6 = (bf16[128,2048]{1,0:T(8,128)(2,1)}, bf16[128,2048]{1,0:T(8,128)(2,1)}) custom-call(s32[1]{0:T(128)} %bitcast.here_ref, s32[2,16,128]{2,1,0:T(8,128)} %get-tuple-element.42.refs_3_.rank_ref, bf16[4,96,2048]{2,1,0:T(8,128)(2,1)} %forward_rows.6.own_ref, bf16[4,96,2048]{2,1,0:T(8,128)(2,1)} %collective-permute-done.15.other_ref), custom_call_target="tpu_custom_call" | custom-call | tf_op jit(solution)/shard_map/summed/pallas_call | solution.py:353
  160.9 9.9 %collective-permute-done.17 = bf16[128,2048]{1,0:T(8,128)(2,1)} collective-permute-done((bf16[128,2048]{1,0:T(8,128)(2,1)}, bf16[128,2048]{1,0:T(8,128)(2,1)}, u32[]{:S(2)}, u32[]{:S(2)}) %collective-permute-start.17) | collective-permute-done | bytes 524320 | tf_op jit(solution)/shard_map/ppermute | solution.py:381
  170.9 1.3 fusion.1
  172.2 4.0 %collective-permute-start.18 = (bf16[128,2048]{1,0:T(8,128)(2,1)S(1)}, bf16[128,2048]{1,0:T(8,128)(2,1)S(1)}, u32[]{:S(2)}, u32[]{:S(2)}) collective-permute-start(bf16[128,2048]{1,0:T(8,128)(2,1)S(1)} %fusion.1), channel_id=1, source_target_pairs={{0,4},{1,5},{2,6},{3,7},{12,8},{13,9},{14,10},{15,11},{16,20},{17,... | collective-permute-start | bytes 1572872 | tf_op jit(solution)/shard_map/ppermute | solution.py:376
  176.2 4.6 %forward_rows.4.own_ref = bf16[4,96,2048]{2,1,0:T(8,128)(2,1)} custom-call(s32[1]{0:T(128)} %bitcast.here_ref, s32[2,16,128]{2,1,0:T(8,128)} %get-tuple-element.42.refs_3_.rank_ref, f32[2,16,128]{2,1,0:T(8,128)} %get-tuple-element.43.gate_ref, bf16[768,2048]{1,0:T(8,128)(2,1)} %bitcast.44, bf16[8,2,96,768]{3,2,1,0:T(8,128)(2,1)} %bitcast.33, ...), custom_call_target="tpu_custom_call" | custom-call | tf_op jit(solution)/shard_map/forward_rows/pallas_call | solution.py:319
  180.9 1.2 copy-done.3
  182.1 2.8 %summed.5 = (bf16[128,2048]{1,0:T(8,128)(2,1)}, bf16[128,2048]{1,0:T(8,128)(2,1)}) custom-call(s32[1]{0:T(128)} %bitcast.here_ref, s32[2,16,128]{2,1,0:T(8,128)} %get-tuple-element.42.refs_3_.rank_ref, bf16[4,96,2048]{2,1,0:T(8,128)(2,1)} %forward_rows.4.own_ref, bf16[4,96,2048]{2,1,0:T(8,128)(2,1)} %copy-done.3), custom_call_target="tpu_custom_call" | custom-call | tf_op jit(solution)/shard_map/summed/pallas_call | solution.py:353
  184.9 1.1 collective-permute-done.16
  186.0 0.7 collective-permute-done.18
  186.7 0.8 copy-done.15
  187.5 1.3 add_convert_fusion.3
  188.8 5.7 %collective-permute-start.19 = (bf16[128,2048]{1,0:T(8,128)(2,1)S(1)}, bf16[128,2048]{1,0:T(8,128)(2,1)S(1)}, u32[]{:S(2)}, u32[]{:S(2)}) collective-permute-start(bf16[128,2048]{1,0:T(8,128)(2,1)S(1)} %add_convert_fusion.3), channel_id=1, source_target_pairs={{0,4},{1,5},{2,6},{3,7},{12,8},{13,9},{14,10},{15,11},{16,20},{17,... | collective-permute-start | bytes 1572872 | tf_op jit(solution)/shard_map/ppermute | solution.py:376
  195.2 2.8 %summed.4 = (bf16[128,2048]{1,0:T(8,128)(2,1)}, bf16[128,2048]{1,0:T(8,128)(2,1)}) custom-call(s32[1]{0:T(128)} %bitcast.here_ref, s32[2,16,128]{2,1,0:T(8,128)} %get-tuple-element.42.refs_3_.rank_ref, bf16[4,96,2048]{2,1,0:T(8,128)(2,1)} %forward_rows.4.own_ref, bf16[4,96,2048]{2,1,0:T(8,128)(2,1)} %copy-done.3), custom_call_target="tpu_custom_call" | custom-call | tf_op jit(solution)/shard_map/summed/pallas_call | solution.py:353
  198.6 6.3 %collective-permute-done.19 = bf16[128,2048]{1,0:T(8,128)(2,1)S(1)} collective-permute-done((bf16[128,2048]{1,0:T(8,128)(2,1)S(1)}, bf16[128,2048]{1,0:T(8,128)(2,1)S(1)}, u32[]{:S(2)}, u32[]{:S(2)}) %collective-permute-start.19) | collective-permute-done | bytes 524320 | tf_op jit(solution)/shard_map/ppermute | solution.py:376
  204.9 2.1 add_convert_fusion.2.refs_0_
  207.1 4.5 %collective-permute-start.20 = (bf16[128,2048]{1,0:T(8,128)(2,1)}, bf16[128,2048]{1,0:T(8,128)(2,1)S(1)}, u32[]{:S(2)}, u32[]{:S(2)}) collective-permute-start(bf16[128,2048]{1,0:T(8,128)(2,1)} %after.11), channel_id=1, source_target_pairs={{0,4},{1,5},{2,6},{3,7},{12,8},{13,9},{14,10},{15,11},{16,20},{17,... | collective-permute-start | bytes 1572872 | tf_op jit(solution)/shard_map/ppermute | solution.py:376
  212.3 2.1 add_convert_fusion.1
  214.4 1.3 collective-permute-start.23
  215.8 1.0 copy.39.place_ref
  216.9 1.0 reshape.94.gate_ref
  217.9 6.9 %unpack.1 = (bf16[1024,768]{1,0:T(8,128)(2,1)}, f32[1024,1]{1,0:T(8,128)}) custom-call(s32[1024,1]{1,0:T(8,128)} %copy.39.place_ref, f32[1024,1]{1,0:T(8,128)} %reshape.94.gate_ref, bf16[1024,768]{1,0:T(8,128)(2,1)} %bitcast.47, bf16[1536,768]{1,0:T(8,128)(2,1)} %bitcast.10.refs_1_.back_ref), custom_call_target="tpu_custom_call" | custom-call | tf_op jit(solution)/shard_map/unpack/pallas_call | solution.py:126
  224.8 1.2 reduce
  226.8 1.5 collective-permute-done.23
  228.3 1.2 add_convert_fusion
  (75 shorter events, 8.1 us)
Async XLA Ops:
  0.6 8.6 %copy-start = (s32[8]{0:T(128)S(1)}, s32[8]{0:T(128)}, u32[]{:S(2)}) copy-start(s32[8]{0:T(128)} %param.11) | copy-start | bytes 100
  0.6 16.4 %collective-permute-start = (bf16[128,2048]{1,0:T(8,128)(2,1)}, bf16[128,2048]{1,0:T(8,128)(2,1)S(1)}, u32[]{:S(2)}, u32[]{:S(2)}) collective-permute-start(bf16[128,2048]{1,0:T(8,128)(2,1)} %refs_0_.1), channel_id=1, source_target_pairs={{0,4},{1,5},{2,6},{3,7},{12,8},{13,9},{14,10},{15,11},{16,20},{17,... | collective-permute-start | bytes 1572872 | tf_op jit(solution)/shard_map/ppermute | solution.py:376
  5.6 12.2 %collective-permute-start.1 = (bf16[128,2048]{1,0:T(8,128)(2,1)}, bf16[128,2048]{1,0:T(8,128)(2,1)S(1)}, u32[]{:S(2)}, u32[]{:S(2)}) collective-permute-start(bf16[128,2048]{1,0:T(8,128)(2,1)} %refs_0_.1), channel_id=1, source_target_pairs={{4,8},{5,9},{6,10},{7,11},{8,4},{9,5},{10,6},{11,7},{20,24},{21,25... | collective-permute-start | bytes 1572872 | tf_op jit(solution)/shard_map/ppermute | solution.py:376
  6.3 15.5 %collective-permute-start.2 = (bf16[128,2048]{1,0:T(8,128)(2,1)}, bf16[128,2048]{1,0:T(8,128)(2,1)S(1)}, u32[]{:S(2)}, u32[]{:S(2)}) collective-permute-start(bf16[128,2048]{1,0:T(8,128)(2,1)} %refs_0_.1), channel_id=1, source_target_pairs={{4,0},{5,1},{6,2},{7,3},{8,12},{9,13},{10,14},{11,15},{20,16},{21,... | collective-permute-start | bytes 1572872 | tf_op jit(solution)/shard_map/ppermute | solution.py:376
  7.6 15.2 %collective-permute-start.3 = (bf16[128,2048]{1,0:T(8,128)(2,1)}, bf16[128,2048]{1,0:T(8,128)(2,1)S(1)}, u32[]{:S(2)}, u32[]{:S(2)}) collective-permute-start(bf16[128,2048]{1,0:T(8,128)(2,1)} %refs_0_.1), channel_id=1, source_target_pairs={{0,2},{1,3},{2,0},{3,1},{4,6},{5,7},{6,4},{7,5},{8,10},{9,11},{10,... | collective-permute-start | bytes 1572872 | tf_op jit(solution)/shard_map/ppermute | solution.py:381
  9.9 15.7 %copy-start.18 = (s32[128,8]{0,1:T(8,128)S(1)}, s32[128,8]{0,1:T(8,128)}, u32[]{:S(2)}) copy-start(s32[128,8]{0,1:T(8,128)} %param.8) | copy-start | bytes 12292
  9.9 17.4 %copy-start.16 = (f32[128,8]{0,1:T(8,128)S(1)}, f32[128,8]{0,1:T(8,128)}, u32[]{:S(2)}) copy-start(f32[128,8]{0,1:T(8,128)} %param.7) | copy-start | bytes 12292
  17.9 4.9 %copy-start.7 = (bf16[128,2048]{1,0:T(8,128)(2,1)}, bf16[128,2048]{1,0:T(8,128)(2,1)S(1)}, u32[]{:S(2)}) copy-start(bf16[128,2048]{1,0:T(8,128)(2,1)S(1)} %collective-permute-done.1.refs_1_) | copy-start | bytes 1572868
  22.8 0.8 copy-start.9
  23.6 10.1 %collective-permute-start.4 = (bf16[128,2048]{1,0:T(8,128)(2,1)}, bf16[128,2048]{1,0:T(8,128)(2,1)S(1)}, u32[]{:S(2)}, u32[]{:S(2)}) collective-permute-start(bf16[128,2048]{1,0:T(8,128)(2,1)} %get-tuple-element.37), channel_id=1, source_target_pairs={{4,8},{5,9},{6,10},{7,11},{8,4},{9,5},{10,6},{11,7},{20,24},{21,25... | collective-permute-start | bytes 1572872 | tf_op jit(solution)/shard_map/ppermute | solution.py:376
  24.3 15.3 %collective-permute-start.5 = (bf16[128,2048]{1,0:T(8,128)(2,1)}, bf16[128,2048]{1,0:T(8,128)(2,1)S(1)}, u32[]{:S(2)}, u32[]{:S(2)}) collective-permute-start(bf16[128,2048]{1,0:T(8,128)(2,1)} %get-tuple-element.38), channel_id=1, source_target_pairs={{4,0},{5,1},{6,2},{7,3},{8,12},{9,13},{10,14},{11,15},{20,16},{21,... | collective-permute-start | bytes 1572872 | tf_op jit(solution)/shard_map/ppermute | solution.py:376
  25.7 14.8 %collective-permute-start.6 = (bf16[128,2048]{1,0:T(8,128)(2,1)}, bf16[128,2048]{1,0:T(8,128)(2,1)S(1)}, u32[]{:S(2)}, u32[]{:S(2)}) collective-permute-start(bf16[128,2048]{1,0:T(8,128)(2,1)} %get-tuple-element.39.refs_2_), channel_id=1, source_target_pairs={{0,2},{1,3},{2,0},{3,1},{4,6},{5,7},{6,4},{7,5},{8,10},{9,11},{10,... | collective-permute-start | bytes 1572872 | tf_op jit(solution)/shard_map/ppermute | solution.py:381
  33.7 7.5 %copy-start.8 = (bf16[128,2048]{1,0:T(8,128)(2,1)}, bf16[128,2048]{1,0:T(8,128)(2,1)S(1)}, u32[]{:S(2)}) copy-start(bf16[128,2048]{1,0:T(8,128)(2,1)S(1)} %collective-permute-done.4.refs_0_) | copy-start | bytes 1572868
  40.5 0.8 copy-start.10
  41.4 18.6 %collective-permute-start.7 = (bf16[128,2048]{1,0:T(8,128)(2,1)}, bf16[128,2048]{1,0:T(8,128)(2,1)S(1)}, u32[]{:S(2)}, u32[]{:S(2)}) collective-permute-start(bf16[128,2048]{1,0:T(8,128)(2,1)} %get-tuple-element.44), channel_id=1, source_target_pairs={{4,0},{5,1},{6,2},{7,3},{8,12},{9,13},{10,14},{11,15},{20,16},{21,... | collective-permute-start | bytes 1572872 | tf_op jit(solution)/shard_map/ppermute | solution.py:376
  42.6 15.0 %all-to-all-start = ((f32[16,16,128]{2,1,0:T(8,128)}), f32[16,16,128]{2,1,0:T(8,128)S(1)}, u32[]{:S(2)}, u32[]{:S(2)}) async-start(f32[16,16,128]{2,1,0:T(8,128)} %get-tuple-element.41), calls=%async_computation | async-start | bytes 262144 | tf_op jit(solution)/shard_map/all_to_all | solution.py:431
  47.9 15.8 %collective-permute-start.8 = (bf16[128,2048]{1,0:T(8,128)(2,1)}, bf16[128,2048]{1,0:T(8,128)(2,1)S(1)}, u32[]{:S(2)}, u32[]{:S(2)}) collective-permute-start(bf16[128,2048]{1,0:T(8,128)(2,1)} %get-tuple-element.45.refs_0_), channel_id=1, source_target_pairs={{0,2},{1,3},{2,0},{3,1},{4,6},{5,7},{6,4},{7,5},{8,10},{9,11},{10,... | collective-permute-start | bytes 1572872 | tf_op jit(solution)/shard_map/ppermute | solution.py:381
  57.6 0.7 copy-start.12
  63.7 0.9 copy-start.6
  64.6 56.2 %all-to-all-start.1 = ((bf16[16,96,768]{2,1,0:T(8,128)(2,1)}), bf16[16,96,768]{2,1,0:T(8,128)(2,1)S(1)}, u32[]{:S(2)}, u32[]{:S(2)}) async-start(bf16[16,96,768]{2,1,0:T(8,128)(2,1)} %bitcast.45), calls=%async_computation.1 | async-start | bytes 4718592 | tf_op jit(solution)/shard_map/all_to_all | solution.py:434
  69.7 7.3 %copy-start.4 = (bf16[128,2048]{1,0:T(8,128)(2,1)S(1)}, bf16[128,2048]{1,0:T(8,128)(2,1)}, u32[]{:S(2)}) copy-start(bf16[128,2048]{1,0:T(8,128)(2,1)} %get-tuple-element.47.refs_2_) | copy-start | bytes 1572868
  76.5 3.9 %collective-permute-start.10 = (bf16[4,96,2048]{2,1,0:T(8,128)(2,1)}, bf16[4,96,2048]{2,1,0:T(8,128)(2,1)}, u32[]{:S(2)}, u32[]{:S(2)}) collective-permute-start(bf16[4,96,2048]{2,1,0:T(8,128)(2,1)} %get-tuple-element.48), channel_id=1, source_target_pairs={{0,1},{1,0},{2,3},{3,2},{4,5},{5,4},{6,7},{7,6},{8,9},{9,8},{10,11... | collective-permute-start | bytes 4718600 | tf_op jit(solution)/shard_map/ppermute | solution.py:381
  77.0 27.1 %collective-permute-start.9 = (bf16[128,2048]{1,0:T(8,128)(2,1)S(1)}, bf16[128,2048]{1,0:T(8,128)(2,1)S(1)}, u32[]{:S(2)}, u32[]{:S(2)}) collective-permute-start(bf16[128,2048]{1,0:T(8,128)(2,1)S(1)} %copy-done.4), channel_id=1, source_target_pairs={{0,2},{1,3},{2,0},{3,1},{4,6},{5,7},{6,4},{7,5},{8,10},{9,11},{10,... | collective-permute-start | bytes 1572872 | tf_op jit(solution)/shard_map/ppermute | solution.py:381
  104.1 0.8 copy-start.11
  111.7 3.8 %collective-permute-start.11 = (bf16[4,96,2048]{2,1,0:T(8,128)(2,1)}, bf16[4,96,2048]{2,1,0:T(8,128)(2,1)}, u32[]{:S(2)}, u32[]{:S(2)}) collective-permute-start(bf16[4,96,2048]{2,1,0:T(8,128)(2,1)} %get-tuple-element.53), channel_id=1, source_target_pairs={{0,1},{1,0},{2,3},{3,2},{4,5},{5,4},{6,7},{7,6},{8,9},{9,8},{10,11... | collective-permute-start | bytes 4718600 | tf_op jit(solution)/shard_map/ppermute | solution.py:381
  120.8 1.5 copy-start.1
  126.9 16.9 %collective-permute-start.15 = (bf16[4,96,2048]{2,1,0:T(8,128)(2,1)}, bf16[4,96,2048]{2,1,0:T(8,128)(2,1)}, u32[]{:S(2)}, u32[]{:S(2)}) collective-permute-start(bf16[4,96,2048]{2,1,0:T(8,128)(2,1)} %forward_rows.7), channel_id=1, source_target_pairs={{0,1},{1,0},{2,3},{3,2},{4,5},{5,4},{6,7},{7,6},{8,9},{9,8},{10,11... | collective-permute-start | bytes 4718600 | tf_op jit(solution)/shard_map/ppermute | solution.py:381
  127.0 80.1 %all-to-all-start.2 = ((bf16[16,96,768]{2,1,0:T(8,128)(2,1)}), bf16[16,96,768]{2,1,0:T(8,128)(2,1)}, u32[]{:S(2)}, u32[]{:S(2)}) async-start(bf16[16,96,768]{2,1,0:T(8,128)(2,1)} %get-tuple-element.66), calls=%async_computation.2 | async-start | bytes 4718592 | tf_op jit(solution)/shard_map/all_to_all | solution.py:447
  143.4 5.0 %copy-start.2 = (bf16[16,96,768]{2,1,0:T(8,128)(2,1)S(1)}, bf16[16,96,768]{2,1,0:T(8,128)(2,1)}, u32[]{:S(2)}) copy-start(bf16[16,96,768]{2,1,0:T(8,128)(2,1)} %after.9) | copy-start | bytes 7077892
  143.4 37.4 %collective-permute-start.12 = (bf16[4,96,2048]{2,1,0:T(8,128)(2,1)}, bf16[4,96,2048]{2,1,0:T(8,128)(2,1)S(1)}, u32[]{:S(2)}, u32[]{:S(2)}) collective-permute-start(bf16[4,96,2048]{2,1,0:T(8,128)(2,1)} %forward_rows.5), channel_id=1, source_target_pairs={{0,1},{1,0},{2,3},{3,2},{4,5},{5,4},{6,7},{7,6},{8,9},{9,8},{10,11... | collective-permute-start | bytes 4718600 | tf_op jit(solution)/shard_map/ppermute | solution.py:381
  146.8 24.0 %collective-permute-start.17 = (bf16[128,2048]{1,0:T(8,128)(2,1)}, bf16[128,2048]{1,0:T(8,128)(2,1)}, u32[]{:S(2)}, u32[]{:S(2)}) collective-permute-start(bf16[128,2048]{1,0:T(8,128)(2,1)} %get-tuple-element.65), channel_id=1, source_target_pairs={{0,2},{1,3},{2,0},{3,1},{4,6},{5,7},{6,4},{7,5},{8,10},{9,11},{10,... | collective-permute-start | bytes 1572872 | tf_op jit(solution)/shard_map/ppermute | solution.py:381
  157.7 28.3 %collective-permute-start.16 = (bf16[128,2048]{1,0:T(8,128)(2,1)}, bf16[128,2048]{1,0:T(8,128)(2,1)S(1)}, u32[]{:S(2)}, u32[]{:S(2)}) collective-permute-start(bf16[128,2048]{1,0:T(8,128)(2,1)} %get-tuple-element.62), channel_id=1, source_target_pairs={{0,2},{1,3},{2,0},{3,1},{4,6},{5,7},{6,4},{7,5},{8,10},{9,11},{10,... | collective-permute-start | bytes 1572872 | tf_op jit(solution)/shard_map/ppermute | solution.py:381
  172.2 14.5 %collective-permute-start.18 = (bf16[128,2048]{1,0:T(8,128)(2,1)S(1)}, bf16[128,2048]{1,0:T(8,128)(2,1)S(1)}, u32[]{:S(2)}, u32[]{:S(2)}) collective-permute-start(bf16[128,2048]{1,0:T(8,128)(2,1)S(1)} %fusion.1), channel_id=1, source_target_pairs={{0,4},{1,5},{2,6},{3,7},{12,8},{13,9},{14,10},{15,11},{16,20},{17,... | collective-permute-start | bytes 1572872 | tf_op jit(solution)/shard_map/ppermute | solution.py:376
  180.9 6.6 %copy-start.14 = (bf16[128,2048]{1,0:T(8,128)(2,1)S(1)}, bf16[128,2048]{1,0:T(8,128)(2,1)}, u32[]{:S(2)}) copy-start(bf16[128,2048]{1,0:T(8,128)(2,1)} %get-tuple-element.61) | copy-start | bytes 1572868
  180.9 1.2 copy-start.3
  184.9 13.7 %collective-permute-start.14 = (bf16[128,2048]{1,0:T(8,128)(2,1)}, bf16[128,2048]{1,0:T(8,128)(2,1)S(1)}, u32[]{:S(2)}, u32[]{:S(2)}) collective-permute-start(bf16[128,2048]{1,0:T(8,128)(2,1)} %get-tuple-element.60), channel_id=1, source_target_pairs={{0,2},{1,3},{2,0},{3,1},{4,6},{5,7},{6,4},{7,5},{8,10},{9,11},{10,... | collective-permute-start | bytes 1572872 | tf_op jit(solution)/shard_map/ppermute | solution.py:381
  186.7 0.8 copy-start.15
  188.8 16.1 %collective-permute-start.19 = (bf16[128,2048]{1,0:T(8,128)(2,1)S(1)}, bf16[128,2048]{1,0:T(8,128)(2,1)S(1)}, u32[]{:S(2)}, u32[]{:S(2)}) collective-permute-start(bf16[128,2048]{1,0:T(8,128)(2,1)S(1)} %add_convert_fusion.3), channel_id=1, source_target_pairs={{0,4},{1,5},{2,6},{3,7},{12,8},{13,9},{14,10},{15,11},{16,20},{17,... | collective-permute-start | bytes 1572872 | tf_op jit(solution)/shard_map/ppermute | solution.py:376
  194.5 17.9 %collective-permute-start.22 = (bf16[128,2048]{1,0:T(8,128)(2,1)S(1)}, bf16[128,2048]{1,0:T(8,128)(2,1)S(1)}, u32[]{:S(2)}, u32[]{:S(2)}) collective-permute-start(bf16[128,2048]{1,0:T(8,128)(2,1)S(1)} %add_convert_fusion.3), channel_id=1, source_target_pairs={{4,8},{5,9},{6,10},{7,11},{8,4},{9,5},{10,6},{11,7},{20,24},{21,25... | collective-permute-start | bytes 1572872 | tf_op jit(solution)/shard_map/ppermute | solution.py:376
  195.2 31.6 %collective-permute-start.13 = (bf16[128,2048]{1,0:T(8,128)(2,1)}, bf16[128,2048]{1,0:T(8,128)(2,1)S(1)}, u32[]{:S(2)}, u32[]{:S(2)}) collective-permute-start(bf16[128,2048]{1,0:T(8,128)(2,1)} %get-tuple-element.58), channel_id=1, source_target_pairs={{0,2},{1,3},{2,0},{3,1},{4,6},{5,7},{6,4},{7,5},{8,10},{9,11},{10,... | collective-permute-start | bytes 1572872 | tf_op jit(solution)/shard_map/ppermute | solution.py:381
  204.9 7.4 %copy-start.5 = (bf16[128,2048]{1,0:T(8,128)(2,1)S(1)}, bf16[128,2048]{1,0:T(8,128)(2,1)}, u32[]{:S(2)}) copy-start(bf16[128,2048]{1,0:T(8,128)(2,1)} %after.10) | copy-start | bytes 1572868
  207.1 8.8 %copy-start.17 = (s32[1,1024]{1,0:T(1,128)S(1)}, s32[1,1024]{1,0:T(1,128)}, u32[]{:S(2)}) copy-start(s32[1,1024]{1,0:T(1,128)} %get-tuple-element.67) | copy-start | bytes 12292
  207.1 19.7 %collective-permute-start.20 = (bf16[128,2048]{1,0:T(8,128)(2,1)}, bf16[128,2048]{1,0:T(8,128)(2,1)S(1)}, u32[]{:S(2)}, u32[]{:S(2)}) collective-permute-start(bf16[128,2048]{1,0:T(8,128)(2,1)} %after.11), channel_id=1, source_target_pairs={{0,4},{1,5},{2,6},{3,7},{12,8},{13,9},{14,10},{15,11},{16,20},{17,... | collective-permute-start | bytes 1572872 | tf_op jit(solution)/shard_map/ppermute | solution.py:376
  211.6 15.2 %collective-permute-start.21 = (bf16[128,2048]{1,0:T(8,128)(2,1)}, bf16[128,2048]{1,0:T(8,128)(2,1)S(1)}, u32[]{:S(2)}, u32[]{:S(2)}) collective-permute-start(bf16[128,2048]{1,0:T(8,128)(2,1)} %after.11), channel_id=1, source_target_pairs={{4,8},{5,9},{6,10},{7,11},{8,4},{9,5},{10,6},{11,7},{20,24},{21,25... | collective-permute-start | bytes 1572872 | tf_op jit(solution)/shard_map/ppermute | solution.py:376
  214.4 13.9 %collective-permute-start.23 = (bf16[128,2048]{1,0:T(8,128)(2,1)}, bf16[128,2048]{1,0:T(8,128)(2,1)S(1)}, u32[]{:S(2)}, u32[]{:S(2)}) collective-permute-start(bf16[128,2048]{1,0:T(8,128)(2,1)} %add_convert_fusion.1), channel_id=1, source_target_pairs={{4,0},{5,1},{6,2},{7,3},{8,12},{9,13},{10,14},{11,15},{20,16},{21,... | collective-permute-start | bytes 1572872 | tf_op jit(solution)/shard_map/ppermute | solution.py:376
  217.9 10.5 %copy-start.13 = (bf16[128,2048]{1,0:T(8,128)(2,1)S(1)}, bf16[128,2048]{1,0:T(8,128)(2,1)}, u32[]{:S(2)}) copy-start(bf16[128,2048]{1,0:T(8,128)(2,1)} %get-tuple-element.57) | copy-start | bytes 1572868

commit v11 on v10

--- a/solution.py
+++ b/solution.py
@@ -297,7 +297,7 @@
 
 
 def forward_kernel(capacity, slots, turn, here_ref, rank_ref, gate_ref, weight_ref, *refs):
-    blocks, out_ref = refs[:-1], refs[-1]
+    blocks, out_ref = refs[:2 * len(slots)], refs[-1]
     sources = lane_sources(here_ref[0], slots, (here_ref[0] % 2) ^ turn)
     flat = jnp.concatenate([block[0, 0] for block in blocks], axis=0)
     out = jnp.dot(flat, weight_ref[...], preferred_element_type=F32).astype(BF16).astype(F32)
@@ -306,7 +306,7 @@
         out_ref[j] = (out[j * capacity:(j + 1) * capacity, :] * gate).astype(BF16)
 
 
-def forward_rows(here, rank, gate, rows_h, weight, slots, turn):
+def forward_rows(here, rank, gate, rows_h, weight, slots, turn, waited):
     devices, capacity, hidden = rows_h.shape
     width = weight.shape[1]
     count = 2 * len(slots)
@@ -322,14 +322,15 @@
             num_scalar_prefetch=1,
             grid=(1,),
             in_specs=[whole, whole, pl.BlockSpec((hidden, width), lambda i, here: (0, 0))]
-            + [pl.BlockSpec((1, 1, capacity, hidden), block(j)) for j in range(count)],
+            + [pl.BlockSpec((1, 1, capacity, hidden), block(j)) for j in range(count)]
+            + [pl.BlockSpec(memory_space=pl.ANY)] * len(waited),
             out_specs=pl.BlockSpec((count, capacity, width), lambda i, here: (0, 0, 0)),
         ),
         out_shape=jax.ShapeDtypeStruct((count, capacity, width), BF16),
         compiler_params=pltpu.CompilerParams(vmem_limit_bytes=60 * MIB),
         cost_estimate=BRIEF,
         name="forward_rows",
-    )(here, rank, gate, weight, *[rows] * count)
+    )(here, rank, gate, weight, *[rows] * count, *waited)
 
 
 def sum_kernel(capacity, slots, turn, here_ref, rank_ref, own_ref, other_ref, *part_refs):
@@ -382,7 +383,7 @@
 
 
 OUTER, INNER = ((0, 1), (3, 2)), ((1, 2), (2, 1))
-ENDS = ((1, 0), (2, 3))
+ENDS, ENDS_SWAP = ((1, 0), (2, 3)), ((0, 3), (3, 0))
 
 
 def gate_kernel(*refs):
@@ -447,27 +448,28 @@
     back_rows = lax.all_to_all(back, "expert", split_axis=0, concat_axis=0, tiled=True).reshape(-1, hidden)
 
     rows_h, = after((rows_h,), ready)
-    beside, across = [], []
-    for slots in ((3, 2), (1, 0)):
-        other = swapped_with(forward_rows(here, rank, gate, rows_h, weight, slots, 1), 1)
-        mine = forward_rows(here, rank, gate, rows_h, weight, slots, 0)
-        across += [swapped_with(part, 2) for part in summed(here, rank, mine, other, slots, 1)]
+    beside, across, passing = [], [], []
+    for slots in ((2, 3), (1, 0)):
+        other = swapped_with(forward_rows(here, rank, gate, rows_h, weight, slots, 1, [*passing]), 1)
+        mine = forward_rows(here, rank, gate, rows_h, weight, slots, 0, [*passing, *across[:1]])
+        passing = summed(here, rank, mine, other, slots, 1)
         beside += summed(here, rank, mine, other, slots, 0)
+        across += [swapped_with(part, 2) for part in passing]
     grad_sum = lax.dot_general(
         rows_h.reshape(-1, hidden), z_rows.reshape(devices * capacity, -1), (((0,), (0,)), ((), ())),
         preferred_element_type=F32,
     )
     weight_grad = grad_sum.astype(BF16)[None]
-    far, mid, close, kept = zip(beside, across)
-    far = (*after((far[0],), weight_grad), far[1])
-    outer1 = passed(OUTER, added(*far))
-    mid = added(*mid, outer1)
-    outer2, inner2 = passed(OUTER, mid), passed(INNER, mid)
-    close, = after((added(*close, outer2),), back_rows)
-    outer3, inner3 = passed(OUTER, close), passed(INNER, close)
-    ends3 = passed(ENDS, added(*far, inner2))
-    mixed = added(*kept, outer3, inner3, ends3)
-
+    mid, far, close, kept = zip(beside, across)
+    mid, far, close = added(*mid), added(*far), added(*close)
+    mid_outer, mid_inner = passed(OUTER, mid), passed(INNER, mid)
+    far_far = passed(ENDS_SWAP, far)
+    close_outer = passed(OUTER, close)
+    mid_outer, = after((mid_outer,), weight_grad)
+    close_inner = passed(INNER, added(close, mid_outer))
+    mid_inner, = after((mid_inner,), back_rows)
+    far_ends = passed(ENDS, added(far, mid_inner))
+    mixed = added(*kept, far_far, close_outer, close_inner, far_ends)
     h_grad, gate_grad = unpack(place.reshape(-1, 1), gates.reshape(-1, 1), h_flat, back_rows)
     return (
         mixed,

time: 230 us -> 234 us (1.017)
  starting transfers between devices: 54.6 us -> 57 us
    ppermute x12, waiting for transfers between devices: 25.5 us -> 17 us  [passed(): lax.ppermute(value, 'expert', [(a * 4 + lane, b * 4 + lane) for a, b in p...]
    ppermute x12, waiting for transfers between devices: 38.3 us -> 45.3 us  [swapped_with(): return lax.ppermute(value, 'expert', [(i, i ^ bit) for i in range(devices)])]
    unnamed x41 -> x43, local copies, waits for them, and re-layouts: 8.27 us -> 9.55 us
    convert_element_type x8 -> x7, other arithmetic: 10.9 us -> 11.7 us  [added(): return total.astype(BF16)]
  transfers between devices with their start and end apart: 27 -> 27, of which waited for: 14 -> 9; matrix products, arithmetic and copies ran while one was open for 11% -> 11% of each run, Pallas kernels for 28% -> 27%
where the time goes in v11:
time: 234 us; the launch traced here: 233 us
  waiting for transfers between devices  70.1 us (30%)
  Pallas kernels  68.5 us (29%)
  starting transfers between devices  57 us (24%)
  local copies, waits for them, and re-layouts  13.8 us (6%)
  other arithmetic  13 us (6%)
  matrix products  9.32 us (4%)
    ppermute x12, waiting for transfers between devices, swapped_with(): return lax.ppermute(value, 'expert', [(i, i ^ bit) for i in range(devices)])  45.3 us
    ppermute x12, starting transfers between devices, passed(): lax.ppermute(value, 'expert', [(a * 4 + lane, b * 4 + lane) for a, b in p...  27.9 us
    pallas_call x4, Pallas kernels, forward_rows(): pl.pallas_call(functools.partial(forward_kernel, capacity, slots, turn),...  18.7 us
    ppermute x12, waiting for transfers between devices, passed(): lax.ppermute(value, 'expert', [(a * 4 + lane, b * 4 + lane) for a, b in p...  17 us
    pallas_call x2, Pallas kernels, scaled_rows(): pl.pallas_call(functools.partial(scale_kernel, capacity, slots, len(buffe...  13.7 us
    convert_element_type x7, other arithmetic, added(): return total.astype(BF16)  11.7 us
    ppermute x12, starting transfers between devices, swapped_with(): return lax.ppermute(value, 'expert', [(i, i ^ bit) for i in range(devices)])  11.6 us
    pallas_call x4, Pallas kernels, summed(): pl.pallas_call(functools.partial(sum_kernel, capacity, slots, turn), grid...  11.4 us
  transfers between devices with their start and end apart: 27, of which 9 were waited for; matrix products, arithmetic and copies ran while one was open for 11% of the time, Pallas kernels for 27%

profile of v11, /device:TPU:0, one launch (start us, length us, event | category | flops | bytes accessed | tf_op | source)
XLA Modules:
  0.0 232.8 jit_solution(621642961167798621)
XLA Ops:
  0.6 5.0 %collective-permute-start = (bf16[128,2048]{1,0:T(8,128)(2,1)}, bf16[128,2048]{1,0:T(8,128)(2,1)S(1)}, u32[]{:S(2)}, u32[]{:S(2)}) collective-permute-start(bf16[128,2048]{1,0:T(8,128)(2,1)} %refs_0_.1), channel_id=1, source_target_pairs={{0,4},{1,5},{2,6},{3,7},{12,8},{13,9},{14,10},{15,11},{16,20},{17,... | collective-permute-start | bytes 1572872 | tf_op jit(solution)/shard_map/ppermute | solution.py:377
  5.6 0.7 collective-permute-start.1
  6.3 1.3 collective-permute-start.2
  7.6 1.6 collective-permute-start.3
  9.9 7.2 %collective-permute-done = bf16[128,2048]{1,0:T(8,128)(2,1)S(1)} collective-permute-done((bf16[128,2048]{1,0:T(8,128)(2,1)}, bf16[128,2048]{1,0:T(8,128)(2,1)S(1)}, u32[]{:S(2)}, u32[]{:S(2)}) %collective-permute-start) | collective-permute-done | bytes 524320 | tf_op jit(solution)/shard_map/ppermute | solution.py:377
  17.1 0.8 copy.42.refs_0_
  17.9 3.9 %collective-permute-done.2 = bf16[128,2048]{1,0:T(8,128)(2,1)S(1)} collective-permute-done((bf16[128,2048]{1,0:T(8,128)(2,1)}, bf16[128,2048]{1,0:T(8,128)(2,1)S(1)}, u32[]{:S(2)}, u32[]{:S(2)}) %collective-permute-start.2) | collective-permute-done | bytes 524320 | tf_op jit(solution)/shard_map/ppermute | solution.py:377
  21.8 0.9 add_convert_fusion.8.refs_2_
  22.8 0.8 copy-done.11
  24.2 1.3 collective-permute-start.5
  25.7 1.6 collective-permute-start.6
  28.1 5.6 %pack.1 = (s32[1,1024]{1,0:T(1,128)}, bf16[1536,768]{1,0:T(8,128)(2,1)}) custom-call(s32[1,1024]{1,0:T(1,128)} %reshape.76.ids_ref, bf16[1024,768]{1,0:T(8,128)(2,1)} %bitcast.46), custom_call_target="tpu_custom_call" | custom-call | tf_op jit(solution)/shard_map/pack/pallas_call | solution.py:92
  33.7 5.9 %collective-permute-done.5 = bf16[128,2048]{1,0:T(8,128)(2,1)S(1)} collective-permute-done((bf16[128,2048]{1,0:T(8,128)(2,1)}, bf16[128,2048]{1,0:T(8,128)(2,1)S(1)}, u32[]{:S(2)}, u32[]{:S(2)}) %collective-permute-start.5) | collective-permute-done | bytes 524320 | tf_op jit(solution)/shard_map/ppermute | solution.py:377
  39.6 0.9 add_convert_fusion.7.refs_1_
  40.5 0.7 broadcast_in_dim.19.refs_2_
  41.4 1.3 collective-permute-start.7
  42.7 5.3 %all-to-all-start = ((f32[16,16,128]{2,1,0:T(8,128)}), f32[16,16,128]{2,1,0:T(8,128)S(1)}, u32[]{:S(2)}, u32[]{:S(2)}) async-start(f32[16,16,128]{2,1,0:T(8,128)} %get-tuple-element.41), calls=%async_computation | async-start | bytes 262144 | tf_op jit(solution)/shard_map/all_to_all | solution.py:432
  48.0 1.9 collective-permute-start.8
  49.9 7.8 %all-to-all-done.routing_ref = f32[16,16,128]{2,1,0:T(8,128)S(1)} async-done(((f32[16,16,128]{2,1,0:T(8,128)}), f32[16,16,128]{2,1,0:T(8,128)S(1)}, u32[]{:S(2)}, u32[]{:S(2)}) %all-to-all-start) | async-done | bytes 131104 | tf_op jit(solution)/shard_map/all_to_all | solution.py:432
  58.3 1.7 route.1
  60.0 0.9 add_convert_fusion.6.refs_1_
  60.9 2.8 %collective-permute-done.8.refs_2_.refs_1_ = bf16[128,2048]{1,0:T(8,128)(2,1)S(1)} collective-permute-done((bf16[128,2048]{1,0:T(8,128)(2,1)}, bf16[128,2048]{1,0:T(8,128)(2,1)S(1)}, u32[]{:S(2)}, u32[]{:S(2)}) %collective-permute-start.8) | collective-permute-done | bytes 524320 | tf_op jit(solution)/shard_map/ppermute | solution.py:382
  63.7 0.8 copy-done.8
  64.5 5.1 %all-to-all-start.1 = ((bf16[16,96,768]{2,1,0:T(8,128)(2,1)}), bf16[16,96,768]{2,1,0:T(8,128)(2,1)S(1)}, u32[]{:S(2)}, u32[]{:S(2)}) async-start(bf16[16,96,768]{2,1,0:T(8,128)(2,1)} %bitcast.45), calls=%async_computation.1 | async-start | bytes 4718592 | tf_op jit(solution)/shard_map/all_to_all | solution.py:435
  69.6 6.9 %scaled_rows.2 = (bf16[16,96,2048]{2,1,0:T(8,128)(2,1)}, bf16[16,96,768]{2,1,0:T(8,128)(2,1)}, bf16[4,96,2048]{2,1,0:T(8,128)(2,1)}) custom-call(s32[1]{0:T(128)} %bitcast.here_ref, s32[2,16,128]{2,1,0:T(8,128)} %get-tuple-element.42.refs_3_.rank_ref, f32[2,16,128]{2,1,0:T(8,128)} %get-tuple-element.43.gate_ref, bf16[768,2048]{1,0:T(8,128)(2,1)} %bitcast.37, ...), custom_call_target="tpu_custom_call" | custom-call | tf_op jit(solution)/shard_map/scaled_rows/pallas_call | solution.py:239
  77.0 1.7 collective-permute-start.9
  78.7 1.7 collective-permute-done.10.rows_ref
  80.4 5.2 %sibling_rows.2 = (bf16[16,96,2048]{2,1,0:T(8,128)(2,1)}, bf16[16,96,768]{2,1,0:T(8,128)(2,1)}, f32[8,128]{1,0:T(8,128)}) custom-call(s32[1]{0:T(128)} %bitcast.here_ref, bf16[768,2048]{1,0:T(8,128)(2,1)} %bitcast.38, bf16[4,96,2048]{2,1,0:T(8,128)(2,1)} %collective-permute-done.10.rows_ref, ...), custom_call_target="tpu_custom_call", output_to_operand_aliasing={{0}: (3, {}), {1}: (4, {})} | custom-call | tf_op jit(solution)/shard_map/sibling_rows/pallas_call | solution.py:278
  85.6 18.4 %collective-permute-done.9.refs_3_ = bf16[128,2048]{1,0:T(8,128)(2,1)S(1)} collective-permute-done((bf16[128,2048]{1,0:T(8,128)(2,1)S(1)}, bf16[128,2048]{1,0:T(8,128)(2,1)S(1)}, u32[]{:S(2)}, u32[]{:S(2)}) %collective-permute-start.9) | collective-permute-done | bytes 524320 | tf_op jit(solution)/shard_map/ppermute | solution.py:382
  104.0 0.8 copy-done.15
  104.8 6.8 %scaled_rows.3 = (bf16[16,96,2048]{2,1,0:T(8,128)(2,1)}, bf16[16,96,768]{2,1,0:T(8,128)(2,1)}, bf16[4,96,2048]{2,1,0:T(8,128)(2,1)}) custom-call(s32[1]{0:T(128)} %bitcast.here_ref, s32[2,16,128]{2,1,0:T(8,128)} %get-tuple-element.42.refs_3_.rank_ref, f32[2,16,128]{2,1,0:T(8,128)} %get-tuple-element.43.gate_ref, ...), custom_call_target="tpu_custom_call", output_to_operand_aliasing={{0}: (8, {}), {1}: (9, {})} | custom-call | tf_op jit(solution)/shard_map/scaled_rows/pallas_call | solution.py:239
  111.7 3.7 %collective-permute-done.11.rows_ref = bf16[4,96,2048]{2,1,0:T(8,128)(2,1)} collective-permute-done((bf16[4,96,2048]{2,1,0:T(8,128)(2,1)}, bf16[4,96,2048]{2,1,0:T(8,128)(2,1)}, u32[]{:S(2)}, u32[]{:S(2)}) %collective-permute-start.11) | collective-permute-done | bytes 1572896 | tf_op jit(solution)/shard_map/ppermute | solution.py:382
  115.4 5.3 %sibling_rows.3 = (bf16[16,96,2048]{2,1,0:T(8,128)(2,1)}, bf16[16,96,768]{2,1,0:T(8,128)(2,1)}, f32[8,128]{1,0:T(8,128)}) custom-call(s32[1]{0:T(128)} %bitcast.here_ref, bf16[768,2048]{1,0:T(8,128)(2,1)} %bitcast.40, bf16[4,96,2048]{2,1,0:T(8,128)(2,1)} %collective-permute-done.11.rows_ref, ...), custom_call_target="tpu_custom_call", output_to_operand_aliasing={{0}: (3, {}), {1}: (4, {})} | custom-call | tf_op jit(solution)/shard_map/sibling_rows/pallas_call | solution.py:278
  120.7 1.4 copy-done.1
  122.1 4.7 %forward_rows.5 = bf16[4,96,2048]{2,1,0:T(8,128)(2,1)} custom-call(s32[1]{0:T(128)} %bitcast.here_ref, s32[2,16,128]{2,1,0:T(8,128)} %get-tuple-element.42.refs_3_.rank_ref, f32[2,16,128]{2,1,0:T(8,128)} %get-tuple-element.43.gate_ref, bf16[768,2048]{1,0:T(8,128)(2,1)} %bitcast.41, bf16[8,2,96,768]{3,2,1,0:T(8,128)(2,1)} %bitcast.21, ...), custom_call_target="tpu_custom_call" | custom-call | tf_op jit(solution)/shard_map/forward_rows/pallas_call | solution.py:319
  127.0 7.2 %all-to-all-start.2 = ((bf16[16,96,768]{2,1,0:T(8,128)(2,1)}), bf16[16,96,768]{2,1,0:T(8,128)(2,1)}, u32[]{:S(2)}, u32[]{:S(2)}) async-start(bf16[16,96,768]{2,1,0:T(8,128)(2,1)} %get-tuple-element.66), calls=%async_computation.2 | async-start | bytes 4718592 | tf_op jit(solution)/shard_map/all_to_all | solution.py:448
  134.1 4.6 %forward_rows.4.own_ref = bf16[4,96,2048]{2,1,0:T(8,128)(2,1)} custom-call(s32[1]{0:T(128)} %bitcast.here_ref, s32[2,16,128]{2,1,0:T(8,128)} %get-tuple-element.42.refs_3_.rank_ref, f32[2,16,128]{2,1,0:T(8,128)} %get-tuple-element.43.gate_ref, bf16[768,2048]{1,0:T(8,128)(2,1)} %bitcast.42, bf16[8,2,96,768]{3,2,1,0:T(8,128)(2,1)} %bitcast.25, ...), custom_call_target="tpu_custom_call" | custom-call | tf_op jit(solution)/shard_map/forward_rows/pallas_call | solution.py:319
  138.8 1.2 copy-done.4
  139.9 2.9 %summed.4 = (bf16[128,2048]{1,0:T(8,128)(2,1)}, bf16[128,2048]{1,0:T(8,128)(2,1)}) custom-call(s32[1]{0:T(128)} %bitcast.here_ref, s32[2,16,128]{2,1,0:T(8,128)} %get-tuple-element.42.refs_3_.rank_ref, bf16[4,96,2048]{2,1,0:T(8,128)(2,1)} %forward_rows.4.own_ref, bf16[4,96,2048]{2,1,0:T(8,128)(2,1)} %copy-done.4), custom_call_target="tpu_custom_call" | custom-call | tf_op jit(solution)/shard_map/summed/pallas_call | solution.py:354
  142.8 4.7 %forward_rows.7 = bf16[4,96,2048]{2,1,0:T(8,128)(2,1)} custom-call(s32[1]{0:T(128)} %bitcast.here_ref, s32[2,16,128]{2,1,0:T(8,128)} %get-tuple-element.42.refs_3_.rank_ref, f32[2,16,128]{2,1,0:T(8,128)} %get-tuple-element.43.gate_ref, bf16[768,2048]{1,0:T(8,128)(2,1)} %bitcast.43, bf16[8,2,96,768]{3,2,1,0:T(8,128)(2,1)} %bitcast.29, ...), custom_call_target="tpu_custom_call" | custom-call | tf_op jit(solution)/shard_map/forward_rows/pallas_call | solution.py:319
  147.9 1.7 collective-permute-start.13
  149.9 2.8 %summed.7 = (bf16[128,2048]{1,0:T(8,128)(2,1)}, bf16[128,2048]{1,0:T(8,128)(2,1)}) custom-call(s32[1]{0:T(128)} %bitcast.here_ref, s32[2,16,128]{2,1,0:T(8,128)} %get-tuple-element.42.refs_3_.rank_ref, bf16[4,96,2048]{2,1,0:T(8,128)(2,1)} %forward_rows.4.own_ref, bf16[4,96,2048]{2,1,0:T(8,128)(2,1)} %copy-done.4), custom_call_target="tpu_custom_call" | custom-call | tf_op jit(solution)/shard_map/summed/pallas_call | solution.py:354
  152.7 18.6 %collective-permute-done.13.refs_6_ = bf16[128,2048]{1,0:T(8,128)(2,1)S(1)} collective-permute-done((bf16[128,2048]{1,0:T(8,128)(2,1)S(1)}, bf16[128,2048]{1,0:T(8,128)(2,1)S(1)}, u32[]{:S(2)}, u32[]{:S(2)}) %collective-permute-start.13) | collective-permute-done | bytes 524320 | tf_op jit(solution)/shard_map/ppermute | solution.py:382
  171.3 2.2 add_convert_fusion.3
  173.5 5.2 %collective-permute-start.20 = (bf16[128,2048]{1,0:T(8,128)(2,1)}, bf16[128,2048]{1,0:T(8,128)(2,1)}, u32[]{:S(2)}, u32[]{:S(2)}) collective-permute-start(bf16[128,2048]{1,0:T(8,128)(2,1)} %add_convert_fusion.3), channel_id=1, source_target_pairs={{0,4},{1,5},{2,6},{3,7},{12,8},{13,9},{14,10},{15,11},{16,20},{17,... | collective-permute-start | bytes 1572872 | tf_op jit(solution)/shard_map/ppermute | solution.py:377
  178.7 1.4 collective-permute-start.22
  180.2 4.6 %forward_rows.6.own_ref = bf16[4,96,2048]{2,1,0:T(8,128)(2,1)} custom-call(s32[1]{0:T(128)} %bitcast.here_ref, s32[2,16,128]{2,1,0:T(8,128)} %get-tuple-element.42.refs_3_.rank_ref, f32[2,16,128]{2,1,0:T(8,128)} %get-tuple-element.43.gate_ref, bf16[768,2048]{1,0:T(8,128)(2,1)} %bitcast.44, bf16[8,2,96,768]{3,2,1,0:T(8,128)(2,1)} %bitcast.33, ...), custom_call_target="tpu_custom_call" | custom-call | tf_op jit(solution)/shard_map/forward_rows/pallas_call | solution.py:319
  184.8 1.2 copy-done.3
  186.0 2.9 %summed.6 = (bf16[128,2048]{1,0:T(8,128)(2,1)}, bf16[128,2048]{1,0:T(8,128)(2,1)}) custom-call(s32[1]{0:T(128)} %bitcast.here_ref, s32[2,16,128]{2,1,0:T(8,128)} %get-tuple-element.42.refs_3_.rank_ref, bf16[4,96,2048]{2,1,0:T(8,128)(2,1)} %forward_rows.6.own_ref, bf16[4,96,2048]{2,1,0:T(8,128)(2,1)} %copy-done.3), custom_call_target="tpu_custom_call" | custom-call | tf_op jit(solution)/shard_map/summed/pallas_call | solution.py:354
  188.9 9.3 %fusion.refs_1_ = bf16[1,768,2048]{2,1,0:T(8,128)(2,1)} fusion(bf16[16,96,768]{2,1,0:T(8,128)(2,1)S(1)} %copy-done.2, bf16[16,96,2048]{2,1,0:T(8,128)(2,1)} %get-tuple-element.65), kind=kOutput, calls=%fused_computation.2 | convolution fusion | flops 4833411072 | bytes 11796480 | tf_op jit(solution)/shard_map/dot_general | solution.py:458
  198.3 1.0 copy-done.14
  199.3 1.5 add_convert_fusion.1
  200.8 2.8 %collective-permute-start.17 = (bf16[128,2048]{1,0:T(8,128)(2,1)S(1)}, bf16[128,2048]{1,0:T(8,128)(2,1)S(1)}, u32[]{:S(2)}, u32[]{:S(2)}) collective-permute-start(bf16[128,2048]{1,0:T(8,128)(2,1)S(1)} %get-tuple-element.85), channel_id=1, source_target_pairs={{0,12},{1,13},{2,14},{3,15},{12,0},{13,1},{14,2},{15,3},{16,28},{1... | collective-permute-start | bytes 1572872 | tf_op jit(solution)/shard_map/ppermute | solution.py:377
  203.6 1.3 collective-permute-start.23
  204.9 1.8 collective-permute-start.15
  206.8 2.8 %summed.5 = (bf16[128,2048]{1,0:T(8,128)(2,1)}, bf16[128,2048]{1,0:T(8,128)(2,1)}) custom-call(s32[1]{0:T(128)} %bitcast.here_ref, s32[2,16,128]{2,1,0:T(8,128)} %get-tuple-element.42.refs_3_.rank_ref, bf16[4,96,2048]{2,1,0:T(8,128)(2,1)} %forward_rows.6.own_ref, bf16[4,96,2048]{2,1,0:T(8,128)(2,1)} %copy-done.3), custom_call_target="tpu_custom_call" | custom-call | tf_op jit(solution)/shard_map/summed/pallas_call | solution.py:354
  209.6 2.6 %add_convert_fusion.2 = (bf16[128,2048]{1,0:T(8,128)(2,1)}, bf16[128,2048]{1,0:T(8,128)(2,1)}) fusion(bf16[128,2048]{1,0:T(8,128)(2,1)} %after.10, bf16[128,2048]{1,0:T(8,128)(2,1)} %collective-permute-done.18, bf16[128,2048]{1,0:T(8,128)(2,1)} %get-tuple-element.62), kind=kLoop, calls=%fused_computation.5 | loop fusion | flops 2097152 | bytes 2621440 | tf_op jit(solution)/shard_map/convert_element_type | solution.py:373
  212.3 5.4 %collective-permute-start.19 = (bf16[128,2048]{1,0:T(8,128)(2,1)}, bf16[128,2048]{1,0:T(8,128)(2,1)}, u32[]{:S(2)}, u32[]{:S(2)}) collective-permute-start(bf16[128,2048]{1,0:T(8,128)(2,1)} %get-tuple-element.83), channel_id=1, source_target_pairs={{0,4},{1,5},{2,6},{3,7},{12,8},{13,9},{14,10},{15,11},{16,20},{17,... | collective-permute-start | bytes 1572872 | tf_op jit(solution)/shard_map/ppermute | solution.py:377
  217.6 1.5 collective-permute-start.21
  219.2 1.0 copy.39.place_ref
  220.3 1.0 reshape.94.gate_ref
  221.3 6.9 %unpack.1 = (bf16[1024,768]{1,0:T(8,128)(2,1)}, f32[1024,1]{1,0:T(8,128)}) custom-call(s32[1024,1]{1,0:T(8,128)} %copy.39.place_ref, f32[1024,1]{1,0:T(8,128)} %reshape.94.gate_ref, bf16[1024,768]{1,0:T(8,128)(2,1)} %bitcast.47, bf16[1536,768]{1,0:T(8,128)(2,1)} %bitcast.10.refs_1_.back_ref), custom_call_target="tpu_custom_call" | custom-call | tf_op jit(solution)/shard_map/unpack/pallas_call | solution.py:126
  228.2 1.2 reduce
  230.2 2.5 %add_convert_fusion = bf16[128,2048]{1,0:T(8,128)(2,1)} fusion(bf16[128,2048]{1,0:T(8,128)(2,1)S(1)} %collective-permute-done.23, bf16[128,2048]{1,0:T(8,128)(2,1)} %collective-permute-done.21, bf16[128,2048]{1,0:T(8,128)(2,1)} %collective-permute-done.19, bf16[128,2048]{1,0:T(8,128)(2,1)S(1)} %collective-permute-done.17, ...), kind=kLoop, calls=%fused_computation.3 | loop fusion | flops 3145728 | bytes 3670016 | tf_op jit(solution)/shard_map/convert_element_type | solution.py:373
  (76 shorter events, 5.3 us)
Async XLA Ops:
  0.6 8.6 %copy-start = (s32[8]{0:T(128)S(1)}, s32[8]{0:T(128)}, u32[]{:S(2)}) copy-start(s32[8]{0:T(128)} %param.11) | copy-start | bytes 100
  0.6 16.4 %collective-permute-start = (bf16[128,2048]{1,0:T(8,128)(2,1)}, bf16[128,2048]{1,0:T(8,128)(2,1)S(1)}, u32[]{:S(2)}, u32[]{:S(2)}) collective-permute-start(bf16[128,2048]{1,0:T(8,128)(2,1)} %refs_0_.1), channel_id=1, source_target_pairs={{0,4},{1,5},{2,6},{3,7},{12,8},{13,9},{14,10},{15,11},{16,20},{17,... | collective-permute-start | bytes 1572872 | tf_op jit(solution)/shard_map/ppermute | solution.py:377
  5.6 12.2 %collective-permute-start.1 = (bf16[128,2048]{1,0:T(8,128)(2,1)}, bf16[128,2048]{1,0:T(8,128)(2,1)S(1)}, u32[]{:S(2)}, u32[]{:S(2)}) collective-permute-start(bf16[128,2048]{1,0:T(8,128)(2,1)} %refs_0_.1), channel_id=1, source_target_pairs={{4,8},{5,9},{6,10},{7,11},{8,4},{9,5},{10,6},{11,7},{20,24},{21,25... | collective-permute-start | bytes 1572872 | tf_op jit(solution)/shard_map/ppermute | solution.py:377
  6.3 15.5 %collective-permute-start.2 = (bf16[128,2048]{1,0:T(8,128)(2,1)}, bf16[128,2048]{1,0:T(8,128)(2,1)S(1)}, u32[]{:S(2)}, u32[]{:S(2)}) collective-permute-start(bf16[128,2048]{1,0:T(8,128)(2,1)} %refs_0_.1), channel_id=1, source_target_pairs={{4,0},{5,1},{6,2},{7,3},{8,12},{9,13},{10,14},{11,15},{20,16},{21,... | collective-permute-start | bytes 1572872 | tf_op jit(solution)/shard_map/ppermute | solution.py:377
  7.6 15.1 %collective-permute-start.3 = (bf16[128,2048]{1,0:T(8,128)(2,1)}, bf16[128,2048]{1,0:T(8,128)(2,1)S(1)}, u32[]{:S(2)}, u32[]{:S(2)}) collective-permute-start(bf16[128,2048]{1,0:T(8,128)(2,1)} %refs_0_.1), channel_id=1, source_target_pairs={{0,2},{1,3},{2,0},{3,1},{4,6},{5,7},{6,4},{7,5},{8,10},{9,11},{10,... | collective-permute-start | bytes 1572872 | tf_op jit(solution)/shard_map/ppermute | solution.py:382
  9.9 15.7 %copy-start.19 = (s32[128,8]{0,1:T(8,128)S(1)}, s32[128,8]{0,1:T(8,128)}, u32[]{:S(2)}) copy-start(s32[128,8]{0,1:T(8,128)} %param.8) | copy-start | bytes 12292
  9.9 17.4 %copy-start.17 = (f32[128,8]{0,1:T(8,128)S(1)}, f32[128,8]{0,1:T(8,128)}, u32[]{:S(2)}) copy-start(f32[128,8]{0,1:T(8,128)} %param.7) | copy-start | bytes 12292
  17.9 4.9 %copy-start.9 = (bf16[128,2048]{1,0:T(8,128)(2,1)}, bf16[128,2048]{1,0:T(8,128)(2,1)S(1)}, u32[]{:S(2)}) copy-start(bf16[128,2048]{1,0:T(8,128)(2,1)S(1)} %collective-permute-done.1.refs_1_) | copy-start | bytes 1572868
  22.8 0.8 copy-start.11
  23.6 10.1 %collective-permute-start.4 = (bf16[128,2048]{1,0:T(8,128)(2,1)}, bf16[128,2048]{1,0:T(8,128)(2,1)S(1)}, u32[]{:S(2)}, u32[]{:S(2)}) collective-permute-start(bf16[128,2048]{1,0:T(8,128)(2,1)} %get-tuple-element.37), channel_id=1, source_target_pairs={{4,8},{5,9},{6,10},{7,11},{8,4},{9,5},{10,6},{11,7},{20,24},{21,25... | collective-permute-start | bytes 1572872 | tf_op jit(solution)/shard_map/ppermute | solution.py:377
  24.2 15.3 %collective-permute-start.5 = (bf16[128,2048]{1,0:T(8,128)(2,1)}, bf16[128,2048]{1,0:T(8,128)(2,1)S(1)}, u32[]{:S(2)}, u32[]{:S(2)}) collective-permute-start(bf16[128,2048]{1,0:T(8,128)(2,1)} %get-tuple-element.38), channel_id=1, source_target_pairs={{4,0},{5,1},{6,2},{7,3},{8,12},{9,13},{10,14},{11,15},{20,16},{21,... | collective-permute-start | bytes 1572872 | tf_op jit(solution)/shard_map/ppermute | solution.py:377
  25.7 14.9 %collective-permute-start.6 = (bf16[128,2048]{1,0:T(8,128)(2,1)}, bf16[128,2048]{1,0:T(8,128)(2,1)S(1)}, u32[]{:S(2)}, u32[]{:S(2)}) collective-permute-start(bf16[128,2048]{1,0:T(8,128)(2,1)} %get-tuple-element.39.refs_2_), channel_id=1, source_target_pairs={{0,2},{1,3},{2,0},{3,1},{4,6},{5,7},{6,4},{7,5},{8,10},{9,11},{10,... | collective-permute-start | bytes 1572872 | tf_op jit(solution)/shard_map/ppermute | solution.py:382
  33.7 7.6 %copy-start.10 = (bf16[128,2048]{1,0:T(8,128)(2,1)}, bf16[128,2048]{1,0:T(8,128)(2,1)S(1)}, u32[]{:S(2)}) copy-start(bf16[128,2048]{1,0:T(8,128)(2,1)S(1)} %collective-permute-done.4.refs_0_) | copy-start | bytes 1572868
  40.5 0.9 copy-start.12
  41.4 18.6 %collective-permute-start.7 = (bf16[128,2048]{1,0:T(8,128)(2,1)}, bf16[128,2048]{1,0:T(8,128)(2,1)S(1)}, u32[]{:S(2)}, u32[]{:S(2)}) collective-permute-start(bf16[128,2048]{1,0:T(8,128)(2,1)} %get-tuple-element.44), channel_id=1, source_target_pairs={{4,0},{5,1},{6,2},{7,3},{8,12},{9,13},{10,14},{11,15},{20,16},{21,... | collective-permute-start | bytes 1572872 | tf_op jit(solution)/shard_map/ppermute | solution.py:377
  42.7 15.0 %all-to-all-start = ((f32[16,16,128]{2,1,0:T(8,128)}), f32[16,16,128]{2,1,0:T(8,128)S(1)}, u32[]{:S(2)}, u32[]{:S(2)}) async-start(f32[16,16,128]{2,1,0:T(8,128)} %get-tuple-element.41), calls=%async_computation | async-start | bytes 262144 | tf_op jit(solution)/shard_map/all_to_all | solution.py:432
  48.0 15.8 %collective-permute-start.8 = (bf16[128,2048]{1,0:T(8,128)(2,1)}, bf16[128,2048]{1,0:T(8,128)(2,1)S(1)}, u32[]{:S(2)}, u32[]{:S(2)}) collective-permute-start(bf16[128,2048]{1,0:T(8,128)(2,1)} %get-tuple-element.45.refs_0_), channel_id=1, source_target_pairs={{0,2},{1,3},{2,0},{3,1},{4,6},{5,7},{6,4},{7,5},{8,10},{9,11},{10,... | collective-permute-start | bytes 1572872 | tf_op jit(solution)/shard_map/ppermute | solution.py:382
  57.7 0.7 copy-start.16
  63.7 0.8 copy-start.8
  64.5 56.2 %all-to-all-start.1 = ((bf16[16,96,768]{2,1,0:T(8,128)(2,1)}), bf16[16,96,768]{2,1,0:T(8,128)(2,1)S(1)}, u32[]{:S(2)}, u32[]{:S(2)}) async-start(bf16[16,96,768]{2,1,0:T(8,128)(2,1)} %bitcast.45), calls=%async_computation.1 | async-start | bytes 4718592 | tf_op jit(solution)/shard_map/all_to_all | solution.py:435
  69.6 7.3 %copy-start.5 = (bf16[128,2048]{1,0:T(8,128)(2,1)S(1)}, bf16[128,2048]{1,0:T(8,128)(2,1)}, u32[]{:S(2)}) copy-start(bf16[128,2048]{1,0:T(8,128)(2,1)} %get-tuple-element.47.refs_2_) | copy-start | bytes 1572868
  76.5 3.8 %collective-permute-start.10 = (bf16[4,96,2048]{2,1,0:T(8,128)(2,1)}, bf16[4,96,2048]{2,1,0:T(8,128)(2,1)}, u32[]{:S(2)}, u32[]{:S(2)}) collective-permute-start(bf16[4,96,2048]{2,1,0:T(8,128)(2,1)} %get-tuple-element.48), channel_id=1, source_target_pairs={{0,1},{1,0},{2,3},{3,2},{4,5},{5,4},{6,7},{7,6},{8,9},{9,8},{10,11... | collective-permute-start | bytes 4718600 | tf_op jit(solution)/shard_map/ppermute | solution.py:382
  77.0 27.1 %collective-permute-start.9 = (bf16[128,2048]{1,0:T(8,128)(2,1)S(1)}, bf16[128,2048]{1,0:T(8,128)(2,1)S(1)}, u32[]{:S(2)}, u32[]{:S(2)}) collective-permute-start(bf16[128,2048]{1,0:T(8,128)(2,1)S(1)} %copy-done.5), channel_id=1, source_target_pairs={{0,2},{1,3},{2,0},{3,1},{4,6},{5,7},{6,4},{7,5},{8,10},{9,11},{10,... | collective-permute-start | bytes 1572872 | tf_op jit(solution)/shard_map/ppermute | solution.py:382
  104.0 0.8 copy-start.15
  111.6 3.8 %collective-permute-start.11 = (bf16[4,96,2048]{2,1,0:T(8,128)(2,1)}, bf16[4,96,2048]{2,1,0:T(8,128)(2,1)}, u32[]{:S(2)}, u32[]{:S(2)}) collective-permute-start(bf16[4,96,2048]{2,1,0:T(8,128)(2,1)} %get-tuple-element.53), channel_id=1, source_target_pairs={{0,1},{1,0},{2,3},{3,2},{4,5},{5,4},{6,7},{7,6},{8,9},{9,8},{10,11... | collective-permute-start | bytes 4718600 | tf_op jit(solution)/shard_map/ppermute | solution.py:382
  120.7 1.4 copy-start.1
  126.8 12.0 %collective-permute-start.12 = (bf16[4,96,2048]{2,1,0:T(8,128)(2,1)}, bf16[4,96,2048]{2,1,0:T(8,128)(2,1)S(1)}, u32[]{:S(2)}, u32[]{:S(2)}) collective-permute-start(bf16[4,96,2048]{2,1,0:T(8,128)(2,1)} %forward_rows.5), channel_id=1, source_target_pairs={{0,1},{1,0},{2,3},{3,2},{4,5},{5,4},{6,7},{7,6},{8,9},{9,8},{10,11... | collective-permute-start | bytes 4718600 | tf_op jit(solution)/shard_map/ppermute | solution.py:382
  127.0 71.3 %all-to-all-start.2 = ((bf16[16,96,768]{2,1,0:T(8,128)(2,1)}), bf16[16,96,768]{2,1,0:T(8,128)(2,1)}, u32[]{:S(2)}, u32[]{:S(2)}) async-start(bf16[16,96,768]{2,1,0:T(8,128)(2,1)} %get-tuple-element.66), calls=%async_computation.2 | async-start | bytes 4718592 | tf_op jit(solution)/shard_map/all_to_all | solution.py:448
  138.8 1.2 copy-start.4
  142.8 5.1 %copy-start.6 = (bf16[128,2048]{1,0:T(8,128)(2,1)S(1)}, bf16[128,2048]{1,0:T(8,128)(2,1)}, u32[]{:S(2)}) copy-start(bf16[128,2048]{1,0:T(8,128)(2,1)} %get-tuple-element.57.refs_4_) | copy-start | bytes 1572868
  147.5 37.3 %collective-permute-start.14 = (bf16[4,96,2048]{2,1,0:T(8,128)(2,1)}, bf16[4,96,2048]{2,1,0:T(8,128)(2,1)S(1)}, u32[]{:S(2)}, u32[]{:S(2)}) collective-permute-start(bf16[4,96,2048]{2,1,0:T(8,128)(2,1)} %forward_rows.7), channel_id=1, source_target_pairs={{0,1},{1,0},{2,3},{3,2},{4,5},{5,4},{6,7},{7,6},{8,9},{9,8},{10,11... | collective-permute-start | bytes 4718600 | tf_op jit(solution)/shard_map/ppermute | solution.py:382
  147.9 23.4 %collective-permute-start.13 = (bf16[128,2048]{1,0:T(8,128)(2,1)S(1)}, bf16[128,2048]{1,0:T(8,128)(2,1)S(1)}, u32[]{:S(2)}, u32[]{:S(2)}) collective-permute-start(bf16[128,2048]{1,0:T(8,128)(2,1)S(1)} %copy-done.6), channel_id=1, source_target_pairs={{0,2},{1,3},{2,0},{3,1},{4,6},{5,7},{6,4},{7,5},{8,10},{9,11},{10,... | collective-permute-start | bytes 1572872 | tf_op jit(solution)/shard_map/ppermute | solution.py:382
  149.6 48.7 %collective-permute-start.16 = (bf16[128,2048]{1,0:T(8,128)(2,1)}, bf16[128,2048]{1,0:T(8,128)(2,1)}, u32[]{:S(2)}, u32[]{:S(2)}) collective-permute-start(bf16[128,2048]{1,0:T(8,128)(2,1)} %get-tuple-element.58.refs_5_), channel_id=1, source_target_pairs={{0,2},{1,3},{2,0},{3,1},{4,6},{5,7},{6,4},{7,5},{8,10},{9,11},{10,... | collective-permute-start | bytes 1572872 | tf_op jit(solution)/shard_map/ppermute | solution.py:382
  171.3 8.9 %copy-start.7 = (bf16[128,2048]{1,0:T(8,128)(2,1)}, bf16[128,2048]{1,0:T(8,128)(2,1)S(1)}, u32[]{:S(2)}) copy-start(bf16[128,2048]{1,0:T(8,128)(2,1)S(1)} %collective-permute-done.13.refs_6_) | copy-start | bytes 1572868
  173.5 24.7 %collective-permute-start.20 = (bf16[128,2048]{1,0:T(8,128)(2,1)}, bf16[128,2048]{1,0:T(8,128)(2,1)}, u32[]{:S(2)}, u32[]{:S(2)}) collective-permute-start(bf16[128,2048]{1,0:T(8,128)(2,1)} %add_convert_fusion.3), channel_id=1, source_target_pairs={{0,4},{1,5},{2,6},{3,7},{12,8},{13,9},{14,10},{15,11},{16,20},{17,... | collective-permute-start | bytes 1572872 | tf_op jit(solution)/shard_map/ppermute | solution.py:377
  178.7 19.5 %collective-permute-start.22 = (bf16[128,2048]{1,0:T(8,128)(2,1)}, bf16[128,2048]{1,0:T(8,128)(2,1)}, u32[]{:S(2)}, u32[]{:S(2)}) collective-permute-start(bf16[128,2048]{1,0:T(8,128)(2,1)} %add_convert_fusion.3), channel_id=1, source_target_pairs={{4,8},{5,9},{6,10},{7,11},{8,4},{9,5},{10,6},{11,7},{20,24},{21,25... | collective-permute-start | bytes 1572872 | tf_op jit(solution)/shard_map/ppermute | solution.py:377
  184.8 4.1 %copy-start.2 = (bf16[16,96,768]{2,1,0:T(8,128)(2,1)S(1)}, bf16[16,96,768]{2,1,0:T(8,128)(2,1)}, u32[]{:S(2)}) copy-start(bf16[16,96,768]{2,1,0:T(8,128)(2,1)} %after.9) | copy-start | bytes 7077892
  184.8 1.2 copy-start.3
  188.9 20.7 %collective-permute-start.18 = (bf16[128,2048]{1,0:T(8,128)(2,1)}, bf16[128,2048]{1,0:T(8,128)(2,1)}, u32[]{:S(2)}, u32[]{:S(2)}) collective-permute-start(bf16[128,2048]{1,0:T(8,128)(2,1)} %get-tuple-element.63), channel_id=1, source_target_pairs={{0,2},{1,3},{2,0},{3,1},{4,6},{5,7},{6,4},{7,5},{8,10},{9,11},{10,... | collective-permute-start | bytes 1572872 | tf_op jit(solution)/shard_map/ppermute | solution.py:382
  198.2 1.0 copy-start.14
  200.8 29.4 %collective-permute-start.17 = (bf16[128,2048]{1,0:T(8,128)(2,1)S(1)}, bf16[128,2048]{1,0:T(8,128)(2,1)S(1)}, u32[]{:S(2)}, u32[]{:S(2)}) collective-permute-start(bf16[128,2048]{1,0:T(8,128)(2,1)S(1)} %get-tuple-element.85), channel_id=1, source_target_pairs={{0,12},{1,13},{2,14},{3,15},{12,0},{13,1},{14,2},{15,3},{16,28},{1... | collective-permute-start | bytes 1572872 | tf_op jit(solution)/shard_map/ppermute | solution.py:377
  203.6 26.6 %collective-permute-start.23 = (bf16[128,2048]{1,0:T(8,128)(2,1)S(1)}, bf16[128,2048]{1,0:T(8,128)(2,1)S(1)}, u32[]{:S(2)}, u32[]{:S(2)}) collective-permute-start(bf16[128,2048]{1,0:T(8,128)(2,1)S(1)} %get-tuple-element.84), channel_id=1, source_target_pairs={{4,0},{5,1},{6,2},{7,3},{8,12},{9,13},{10,14},{11,15},{20,16},{21,... | collective-permute-start | bytes 1572872 | tf_op jit(solution)/shard_map/ppermute | solution.py:377
  204.9 14.3 %copy-start.18 = (s32[1,1024]{1,0:T(1,128)S(1)}, s32[1,1024]{1,0:T(1,128)}, u32[]{:S(2)}) copy-start(s32[1,1024]{1,0:T(1,128)} %get-tuple-element.67) | copy-start | bytes 12292
  204.9 25.3 %collective-permute-start.15 = (bf16[128,2048]{1,0:T(8,128)(2,1)}, bf16[128,2048]{1,0:T(8,128)(2,1)S(1)}, u32[]{:S(2)}, u32[]{:S(2)}) collective-permute-start(bf16[128,2048]{1,0:T(8,128)(2,1)} %get-tuple-element.60), channel_id=1, source_target_pairs={{0,2},{1,3},{2,0},{3,1},{4,6},{5,7},{6,4},{7,5},{8,10},{9,11},{10,... | collective-permute-start | bytes 1572872 | tf_op jit(solution)/shard_map/ppermute | solution.py:382
  212.3 18.0 %collective-permute-start.19 = (bf16[128,2048]{1,0:T(8,128)(2,1)}, bf16[128,2048]{1,0:T(8,128)(2,1)}, u32[]{:S(2)}, u32[]{:S(2)}) collective-permute-start(bf16[128,2048]{1,0:T(8,128)(2,1)} %get-tuple-element.83), channel_id=1, source_target_pairs={{0,4},{1,5},{2,6},{3,7},{12,8},{13,9},{14,10},{15,11},{16,20},{17,... | collective-permute-start | bytes 1572872 | tf_op jit(solution)/shard_map/ppermute | solution.py:377
  217.6 12.6 %collective-permute-start.21 = (bf16[128,2048]{1,0:T(8,128)(2,1)}, bf16[128,2048]{1,0:T(8,128)(2,1)}, u32[]{:S(2)}, u32[]{:S(2)}) collective-permute-start(bf16[128,2048]{1,0:T(8,128)(2,1)} %get-tuple-element.82), channel_id=1, source_target_pairs={{4,8},{5,9},{6,10},{7,11},{8,4},{9,5},{10,6},{11,7},{20,24},{21,25... | collective-permute-start | bytes 1572872 | tf_op jit(solution)/shard_map/ppermute | solution.py:377
  221.3 9.0 %copy-start.13 = (bf16[128,2048]{1,0:T(8,128)(2,1)S(1)}, bf16[128,2048]{1,0:T(8,128)(2,1)}, u32[]{:S(2)}) copy-start(bf16[128,2048]{1,0:T(8,128)(2,1)} %get-tuple-element.59) | copy-start | bytes 1572868

commit v12 on v11

--- a/solution.py
+++ b/solution.py
@@ -451,7 +451,7 @@
     beside, across, passing = [], [], []
     for slots in ((2, 3), (1, 0)):
         other = swapped_with(forward_rows(here, rank, gate, rows_h, weight, slots, 1, [*passing]), 1)
-        mine = forward_rows(here, rank, gate, rows_h, weight, slots, 0, [*passing, *across[:1]])
+        mine = forward_rows(here, rank, gate, rows_h, weight, slots, 0, [*passing])
         passing = summed(here, rank, mine, other, slots, 1)
         beside += summed(here, rank, mine, other, slots, 0)
         across += [swapped_with(part, 2) for part in passing]
@@ -460,14 +460,14 @@
         preferred_element_type=F32,
     )
     weight_grad = grad_sum.astype(BF16)[None]
+    beside[0], = after((beside[0],), across[1], weight_grad, *passing)
     mid, far, close, kept = zip(beside, across)
-    mid, far, close = added(*mid), added(*far), added(*close)
+    mid, far = after((added(*mid), added(*far)))
     mid_outer, mid_inner = passed(OUTER, mid), passed(INNER, mid)
     far_far = passed(ENDS_SWAP, far)
+    close, = after((added(*close),), far_far, back_rows)
     close_outer = passed(OUTER, close)
-    mid_outer, = after((mid_outer,), weight_grad)
     close_inner = passed(INNER, added(close, mid_outer))
-    mid_inner, = after((mid_inner,), back_rows)
     far_ends = passed(ENDS, added(far, mid_inner))
     mixed = added(*kept, far_far, close_outer, close_inner, far_ends)
     h_grad, gate_grad = unpack(place.reshape(-1, 1), gates.reshape(-1, 1), h_flat, back_rows)

time: 234 us -> 236 us (level)
  waiting for transfers between devices: 70.1 us -> 78 us
  starting transfers between devices: 57 us -> 50.4 us
    ppermute x12, waiting for transfers between devices: 17 us -> 32.9 us  [passed(): lax.ppermute(value, 'expert', [(a * 4 + lane, b * 4 + lane) for a, b in p...]
    ppermute x12, waiting for transfers between devices: 45.3 us -> 37.4 us  [swapped_with(): return lax.ppermute(value, 'expert', [(i, i ^ bit) for i in range(devices)])]
    ppermute x12, starting transfers between devices: 27.9 us -> 20.8 us  [passed(): lax.ppermute(value, 'expert', [(a * 4 + lane, b * 4 + lane) for a, b in p...]
    convert_element_type x7 -> x9, other arithmetic: 11.7 us -> 13.4 us  [added(): return total.astype(BF16)]
  transfers between devices with their start and end apart: 27 -> 27, of which waited for: 9 -> 13; matrix products, arithmetic and copies ran while one was open for 11% -> 12% of each run, Pallas kernels for 27% -> 27%
where the time goes in v12:
time: 236 us; the launch traced here: 235 us
  waiting for transfers between devices  78 us (33%)
  Pallas kernels  68.4 us (29%)
  starting transfers between devices  50.4 us (21%)
  other arithmetic  14.7 us (6%)
  local copies, waits for them, and re-layouts  13.7 us (6%)
  matrix products  9.3 us (4%)
    ppermute x12, waiting for transfers between devices, swapped_with(): return lax.ppermute(value, 'expert', [(i, i ^ bit) for i in range(devices)])  37.4 us
    ppermute x12, waiting for transfers between devices, passed(): lax.ppermute(value, 'expert', [(a * 4 + lane, b * 4 + lane) for a, b in p...  32.9 us
    ppermute x12, starting transfers between devices, passed(): lax.ppermute(value, 'expert', [(a * 4 + lane, b * 4 + lane) for a, b in p...  20.8 us
    pallas_call x4, Pallas kernels, forward_rows(): pl.pallas_call(functools.partial(forward_kernel, capacity, slots, turn),...  18.7 us
    pallas_call x2, Pallas kernels, scaled_rows(): pl.pallas_call(functools.partial(scale_kernel, capacity, slots, len(buffe...  13.6 us
    convert_element_type x9, other arithmetic, added(): return total.astype(BF16)  13.4 us
    ppermute x12, starting transfers between devices, swapped_with(): return lax.ppermute(value, 'expert', [(i, i ^ bit) for i in range(devices)])  12 us
    pallas_call x4, Pallas kernels, summed(): pl.pallas_call(functools.partial(sum_kernel, capacity, slots, turn), grid...  11.3 us
  transfers between devices with their start and end apart: 27, of which 13 were waited for; matrix products, arithmetic and copies ran while one was open for 12% of the time, Pallas kernels for 27%

profile of v12, /device:TPU:0, one launch (start us, length us, event | category | flops | bytes accessed | tf_op | source)
XLA Modules:
  0.0 235.4 jit_solution(9682676974096486758)
XLA Ops:
  0.6 5.0 %collective-permute-start = (bf16[128,2048]{1,0:T(8,128)(2,1)}, bf16[128,2048]{1,0:T(8,128)(2,1)S(1)}, u32[]{:S(2)}, u32[]{:S(2)}) collective-permute-start(bf16[128,2048]{1,0:T(8,128)(2,1)} %refs_0_.1), channel_id=1, source_target_pairs={{0,4},{1,5},{2,6},{3,7},{12,8},{13,9},{14,10},{15,11},{16,20},{17,... | collective-permute-start | bytes 1572872 | tf_op jit(solution)/shard_map/ppermute | solution.py:377
  6.3 1.3 collective-permute-start.2
  7.6 1.6 collective-permute-start.3
  9.9 7.2 %collective-permute-done = bf16[128,2048]{1,0:T(8,128)(2,1)S(1)} collective-permute-done((bf16[128,2048]{1,0:T(8,128)(2,1)}, bf16[128,2048]{1,0:T(8,128)(2,1)S(1)}, u32[]{:S(2)}, u32[]{:S(2)}) %collective-permute-start) | collective-permute-done | bytes 524320 | tf_op jit(solution)/shard_map/ppermute | solution.py:377
  17.1 0.8 copy.44.refs_0_
  17.9 3.9 %collective-permute-done.2 = bf16[128,2048]{1,0:T(8,128)(2,1)S(1)} collective-permute-done((bf16[128,2048]{1,0:T(8,128)(2,1)}, bf16[128,2048]{1,0:T(8,128)(2,1)S(1)}, u32[]{:S(2)}, u32[]{:S(2)}) %collective-permute-start.2) | collective-permute-done | bytes 524320 | tf_op jit(solution)/shard_map/ppermute | solution.py:377
  21.8 1.0 add_convert_fusion.8.refs_2_
  24.3 1.3 collective-permute-start.5
  25.7 1.6 collective-permute-start.6
  28.1 5.6 %pack.1 = (s32[1,1024]{1,0:T(1,128)}, bf16[1536,768]{1,0:T(8,128)(2,1)}) custom-call(s32[1,1024]{1,0:T(1,128)} %reshape.76.ids_ref, bf16[1024,768]{1,0:T(8,128)(2,1)} %bitcast.46), custom_call_target="tpu_custom_call" | custom-call | tf_op jit(solution)/shard_map/pack/pallas_call | solution.py:92
  33.7 5.9 %collective-permute-done.5 = bf16[128,2048]{1,0:T(8,128)(2,1)S(1)} collective-permute-done((bf16[128,2048]{1,0:T(8,128)(2,1)}, bf16[128,2048]{1,0:T(8,128)(2,1)S(1)}, u32[]{:S(2)}, u32[]{:S(2)}) %collective-permute-start.5) | collective-permute-done | bytes 524320 | tf_op jit(solution)/shard_map/ppermute | solution.py:377
  39.6 0.9 add_convert_fusion.7.refs_1_
  41.4 1.3 collective-permute-start.7
  42.7 5.3 %all-to-all-start = ((f32[16,16,128]{2,1,0:T(8,128)}), f32[16,16,128]{2,1,0:T(8,128)S(1)}, u32[]{:S(2)}, u32[]{:S(2)}) async-start(f32[16,16,128]{2,1,0:T(8,128)} %get-tuple-element.43), calls=%async_computation | async-start | bytes 262144 | tf_op jit(solution)/shard_map/all_to_all | solution.py:432
  48.0 1.9 collective-permute-start.8
  49.9 7.7 %all-to-all-done.routing_ref = f32[16,16,128]{2,1,0:T(8,128)S(1)} async-done(((f32[16,16,128]{2,1,0:T(8,128)}), f32[16,16,128]{2,1,0:T(8,128)S(1)}, u32[]{:S(2)}, u32[]{:S(2)}) %all-to-all-start) | async-done | bytes 131104 | tf_op jit(solution)/shard_map/all_to_all | solution.py:432
  58.3 1.7 route.1
  59.9 0.9 add_convert_fusion.6.refs_1_
  60.9 2.9 %collective-permute-done.8.refs_2_.refs_1_ = bf16[128,2048]{1,0:T(8,128)(2,1)S(1)} collective-permute-done((bf16[128,2048]{1,0:T(8,128)(2,1)}, bf16[128,2048]{1,0:T(8,128)(2,1)S(1)}, u32[]{:S(2)}, u32[]{:S(2)}) %collective-permute-start.8) | collective-permute-done | bytes 524320 | tf_op jit(solution)/shard_map/ppermute | solution.py:382
  63.7 0.9 copy-done.9
  64.6 5.1 %all-to-all-start.1 = ((bf16[16,96,768]{2,1,0:T(8,128)(2,1)}), bf16[16,96,768]{2,1,0:T(8,128)(2,1)S(1)}, u32[]{:S(2)}, u32[]{:S(2)}) async-start(bf16[16,96,768]{2,1,0:T(8,128)(2,1)} %bitcast.45), calls=%async_computation.1 | async-start | bytes 4718592 | tf_op jit(solution)/shard_map/all_to_all | solution.py:435
  69.7 6.8 %scaled_rows.2 = (bf16[16,96,2048]{2,1,0:T(8,128)(2,1)}, bf16[16,96,768]{2,1,0:T(8,128)(2,1)}, bf16[4,96,2048]{2,1,0:T(8,128)(2,1)}) custom-call(s32[1]{0:T(128)} %bitcast.here_ref, s32[2,16,128]{2,1,0:T(8,128)} %get-tuple-element.44.refs_3_.rank_ref, f32[2,16,128]{2,1,0:T(8,128)} %get-tuple-element.45.gate_ref, bf16[768,2048]{1,0:T(8,128)(2,1)} %bitcast.37, ...), custom_call_target="tpu_custom_call" | custom-call | tf_op jit(solution)/shard_map/scaled_rows/pallas_call | solution.py:239
  77.0 1.7 collective-permute-start.9
  78.7 1.7 collective-permute-done.10.rows_ref
  80.4 5.3 %sibling_rows.2 = (bf16[16,96,2048]{2,1,0:T(8,128)(2,1)}, bf16[16,96,768]{2,1,0:T(8,128)(2,1)}, f32[8,128]{1,0:T(8,128)}) custom-call(s32[1]{0:T(128)} %bitcast.here_ref, bf16[768,2048]{1,0:T(8,128)(2,1)} %bitcast.38, bf16[4,96,2048]{2,1,0:T(8,128)(2,1)} %collective-permute-done.10.rows_ref, ...), custom_call_target="tpu_custom_call", output_to_operand_aliasing={{0}: (3, {}), {1}: (4, {})} | custom-call | tf_op jit(solution)/shard_map/sibling_rows/pallas_call | solution.py:278
  85.7 18.4 %collective-permute-done.9.refs_3_ = bf16[128,2048]{1,0:T(8,128)(2,1)S(1)} collective-permute-done((bf16[128,2048]{1,0:T(8,128)(2,1)S(1)}, bf16[128,2048]{1,0:T(8,128)(2,1)S(1)}, u32[]{:S(2)}, u32[]{:S(2)}) %collective-permute-start.9) | collective-permute-done | bytes 524320 | tf_op jit(solution)/shard_map/ppermute | solution.py:382
  104.9 6.8 %scaled_rows.3 = (bf16[16,96,2048]{2,1,0:T(8,128)(2,1)}, bf16[16,96,768]{2,1,0:T(8,128)(2,1)}, bf16[4,96,2048]{2,1,0:T(8,128)(2,1)}) custom-call(s32[1]{0:T(128)} %bitcast.here_ref, s32[2,16,128]{2,1,0:T(8,128)} %get-tuple-element.44.refs_3_.rank_ref, f32[2,16,128]{2,1,0:T(8,128)} %get-tuple-element.45.gate_ref, ...), custom_call_target="tpu_custom_call", output_to_operand_aliasing={{0}: (8, {}), {1}: (9, {})} | custom-call | tf_op jit(solution)/shard_map/scaled_rows/pallas_call | solution.py:239
  111.8 3.7 %collective-permute-done.11.rows_ref = bf16[4,96,2048]{2,1,0:T(8,128)(2,1)} collective-permute-done((bf16[4,96,2048]{2,1,0:T(8,128)(2,1)}, bf16[4,96,2048]{2,1,0:T(8,128)(2,1)}, u32[]{:S(2)}, u32[]{:S(2)}) %collective-permute-start.11) | collective-permute-done | bytes 1572896 | tf_op jit(solution)/shard_map/ppermute | solution.py:382
  115.5 5.3 %sibling_rows.3 = (bf16[16,96,2048]{2,1,0:T(8,128)(2,1)}, bf16[16,96,768]{2,1,0:T(8,128)(2,1)}, f32[8,128]{1,0:T(8,128)}) custom-call(s32[1]{0:T(128)} %bitcast.here_ref, bf16[768,2048]{1,0:T(8,128)(2,1)} %bitcast.40, bf16[4,96,2048]{2,1,0:T(8,128)(2,1)} %collective-permute-done.11.rows_ref, ...), custom_call_target="tpu_custom_call", output_to_operand_aliasing={{0}: (3, {}), {1}: (4, {})} | custom-call | tf_op jit(solution)/shard_map/sibling_rows/pallas_call | solution.py:278
  120.8 1.5 copy-done.1
  122.3 4.6 %forward_rows.5 = bf16[4,96,2048]{2,1,0:T(8,128)(2,1)} custom-call(s32[1]{0:T(128)} %bitcast.here_ref, s32[2,16,128]{2,1,0:T(8,128)} %get-tuple-element.44.refs_3_.rank_ref, f32[2,16,128]{2,1,0:T(8,128)} %get-tuple-element.45.gate_ref, bf16[768,2048]{1,0:T(8,128)(2,1)} %bitcast.41, bf16[8,2,96,768]{3,2,1,0:T(8,128)(2,1)} %bitcast.21, ...), custom_call_target="tpu_custom_call" | custom-call | tf_op jit(solution)/shard_map/forward_rows/pallas_call | solution.py:319
  127.0 7.2 %all-to-all-start.2 = ((bf16[16,96,768]{2,1,0:T(8,128)(2,1)}), bf16[16,96,768]{2,1,0:T(8,128)(2,1)}, u32[]{:S(2)}, u32[]{:S(2)}) async-start(bf16[16,96,768]{2,1,0:T(8,128)(2,1)} %get-tuple-element.69), calls=%async_computation.2 | async-start | bytes 4718592 | tf_op jit(solution)/shard_map/all_to_all | solution.py:448
  134.2 4.6 %forward_rows.4.own_ref = bf16[4,96,2048]{2,1,0:T(8,128)(2,1)} custom-call(s32[1]{0:T(128)} %bitcast.here_ref, s32[2,16,128]{2,1,0:T(8,128)} %get-tuple-element.44.refs_3_.rank_ref, f32[2,16,128]{2,1,0:T(8,128)} %get-tuple-element.45.gate_ref, bf16[768,2048]{1,0:T(8,128)(2,1)} %bitcast.42, bf16[8,2,96,768]{3,2,1,0:T(8,128)(2,1)} %bitcast.25, ...), custom_call_target="tpu_custom_call" | custom-call | tf_op jit(solution)/shard_map/forward_rows/pallas_call | solution.py:319
  138.8 1.1 copy-done.4
  140.0 2.8 %summed.4 = (bf16[128,2048]{1,0:T(8,128)(2,1)}, bf16[128,2048]{1,0:T(8,128)(2,1)}) custom-call(s32[1]{0:T(128)} %bitcast.here_ref, s32[2,16,128]{2,1,0:T(8,128)} %get-tuple-element.44.refs_3_.rank_ref, bf16[4,96,2048]{2,1,0:T(8,128)(2,1)} %forward_rows.4.own_ref, bf16[4,96,2048]{2,1,0:T(8,128)(2,1)} %copy-done.4), custom_call_target="tpu_custom_call" | custom-call | tf_op jit(solution)/shard_map/summed/pallas_call | solution.py:354
  142.8 1.9 collective-permute-start.15
  144.7 4.8 %forward_rows.7 = bf16[4,96,2048]{2,1,0:T(8,128)(2,1)} custom-call(s32[1]{0:T(128)} %bitcast.here_ref, s32[2,16,128]{2,1,0:T(8,128)} %get-tuple-element.44.refs_3_.rank_ref, f32[2,16,128]{2,1,0:T(8,128)} %get-tuple-element.45.gate_ref, bf16[768,2048]{1,0:T(8,128)(2,1)} %bitcast.43, bf16[8,2,96,768]{3,2,1,0:T(8,128)(2,1)} %bitcast.29, ...), custom_call_target="tpu_custom_call" | custom-call | tf_op jit(solution)/shard_map/forward_rows/pallas_call | solution.py:319
  149.6 9.3 %fusion.refs_2_ = bf16[1,768,2048]{2,1,0:T(8,128)(2,1)} fusion(bf16[16,96,768]{2,1,0:T(8,128)(2,1)S(1)} %copy-done.2, bf16[16,96,2048]{2,1,0:T(8,128)(2,1)} %get-tuple-element.64), kind=kOutput, calls=%fused_computation.2 | convolution fusion | flops 4833411072 | bytes 11796480 | tf_op jit(solution)/shard_map/dot_general | solution.py:458
  158.9 4.7 %forward_rows.6.own_ref = bf16[4,96,2048]{2,1,0:T(8,128)(2,1)} custom-call(s32[1]{0:T(128)} %bitcast.here_ref, s32[2,16,128]{2,1,0:T(8,128)} %get-tuple-element.44.refs_3_.rank_ref, f32[2,16,128]{2,1,0:T(8,128)} %get-tuple-element.45.gate_ref, bf16[768,2048]{1,0:T(8,128)(2,1)} %bitcast.44, bf16[8,2,96,768]{3,2,1,0:T(8,128)(2,1)} %bitcast.33, ...), custom_call_target="tpu_custom_call" | custom-call | tf_op jit(solution)/shard_map/forward_rows/pallas_call | solution.py:319
  163.5 2.8 %summed.7 = (bf16[128,2048]{1,0:T(8,128)(2,1)}, bf16[128,2048]{1,0:T(8,128)(2,1)}) custom-call(s32[1]{0:T(128)} %bitcast.here_ref, s32[2,16,128]{2,1,0:T(8,128)} %get-tuple-element.44.refs_3_.rank_ref, bf16[4,96,2048]{2,1,0:T(8,128)(2,1)} %forward_rows.4.own_ref, bf16[4,96,2048]{2,1,0:T(8,128)(2,1)} %copy-done.4), custom_call_target="tpu_custom_call" | custom-call | tf_op jit(solution)/shard_map/summed/pallas_call | solution.py:354
  166.3 3.5 %collective-permute-done.15.refs_1_ = bf16[128,2048]{1,0:T(8,128)(2,1)} collective-permute-done((bf16[128,2048]{1,0:T(8,128)(2,1)}, bf16[128,2048]{1,0:T(8,128)(2,1)}, u32[]{:S(2)}, u32[]{:S(2)}) %collective-permute-start.15) | collective-permute-done | bytes 524320 | tf_op jit(solution)/shard_map/ppermute | solution.py:382
  169.9 2.2 add_convert_fusion.4.refs_1_
  172.1 1.1 copy-done.3
  173.2 2.8 %summed.6 = (bf16[128,2048]{1,0:T(8,128)(2,1)}, bf16[128,2048]{1,0:T(8,128)(2,1)}) custom-call(s32[1]{0:T(128)} %bitcast.here_ref, s32[2,16,128]{2,1,0:T(8,128)} %get-tuple-element.44.refs_3_.rank_ref, bf16[4,96,2048]{2,1,0:T(8,128)(2,1)} %forward_rows.6.own_ref, bf16[4,96,2048]{2,1,0:T(8,128)(2,1)} %copy-done.3), custom_call_target="tpu_custom_call" | custom-call | tf_op jit(solution)/shard_map/summed/pallas_call | solution.py:354
  176.0 2.5 %collective-permute-start.18 = (bf16[128,2048]{1,0:T(8,128)(2,1)}, bf16[128,2048]{1,0:T(8,128)(2,1)S(1)}, u32[]{:S(2)}, u32[]{:S(2)}) collective-permute-start(bf16[128,2048]{1,0:T(8,128)(2,1)} %get-tuple-element.65.refs_3_), channel_id=1, source_target_pairs={{0,2},{1,3},{2,0},{3,1},{4,6},{5,7},{6,4},{7,5},{8,10},{9,11},{10,... | collective-permute-start | bytes 1572872 | tf_op jit(solution)/shard_map/ppermute | solution.py:382
  178.5 7.1 %collective-permute-done.16 = bf16[128,2048]{1,0:T(8,128)(2,1)} collective-permute-done((bf16[128,2048]{1,0:T(8,128)(2,1)}, bf16[128,2048]{1,0:T(8,128)(2,1)}, u32[]{:S(2)}, u32[]{:S(2)}) %collective-permute-start.16) | collective-permute-done | bytes 524320 | tf_op jit(solution)/shard_map/ppermute | solution.py:382
  185.6 2.1 add_convert_fusion.5.refs_0_
  187.7 5.2 %collective-permute-start.17 = (bf16[128,2048]{1,0:T(8,128)(2,1)}, bf16[128,2048]{1,0:T(8,128)(2,1)S(1)}, u32[]{:S(2)}, u32[]{:S(2)}) collective-permute-start(bf16[128,2048]{1,0:T(8,128)(2,1)} %get-tuple-element.67), channel_id=1, source_target_pairs={{0,12},{1,13},{2,14},{3,15},{12,0},{13,1},{14,2},{15,3},{16,28},{1... | collective-permute-start | bytes 1572872 | tf_op jit(solution)/shard_map/ppermute | solution.py:377
  192.9 1.3 collective-permute-start.20
  195.0 2.8 %summed.5 = (bf16[128,2048]{1,0:T(8,128)(2,1)}, bf16[128,2048]{1,0:T(8,128)(2,1)}) custom-call(s32[1]{0:T(128)} %bitcast.here_ref, s32[2,16,128]{2,1,0:T(8,128)} %get-tuple-element.44.refs_3_.rank_ref, bf16[4,96,2048]{2,1,0:T(8,128)(2,1)} %forward_rows.6.own_ref, bf16[4,96,2048]{2,1,0:T(8,128)(2,1)} %copy-done.3), custom_call_target="tpu_custom_call" | custom-call | tf_op jit(solution)/shard_map/summed/pallas_call | solution.py:354
  197.8 2.0 add_convert_fusion.3.refs_0_
  199.9 6.6 %collective-permute-done.17.refs_1_ = bf16[128,2048]{1,0:T(8,128)(2,1)S(1)} collective-permute-done((bf16[128,2048]{1,0:T(8,128)(2,1)}, bf16[128,2048]{1,0:T(8,128)(2,1)S(1)}, u32[]{:S(2)}, u32[]{:S(2)}) %collective-permute-start.17) | collective-permute-done | bytes 524320 | tf_op jit(solution)/shard_map/ppermute | solution.py:377
  206.5 0.8 copy-done.7
  207.3 1.4 collective-permute-start.19
  208.7 8.1 %collective-permute-done.20 = bf16[128,2048]{1,0:T(8,128)(2,1)S(1)} collective-permute-done((bf16[128,2048]{1,0:T(8,128)(2,1)}, bf16[128,2048]{1,0:T(8,128)(2,1)S(1)}, u32[]{:S(2)}, u32[]{:S(2)}) %collective-permute-start.20) | collective-permute-done | bytes 524320 | tf_op jit(solution)/shard_map/ppermute | solution.py:377
  216.8 2.0 add_convert_fusion.2
  219.5 0.9 add_convert_fusion.1
  220.5 1.3 collective-permute-start.23
  221.8 1.0 copy.41.place_ref
  222.9 1.0 reshape.94.gate_ref
  223.9 7.0 %unpack.1 = (bf16[1024,768]{1,0:T(8,128)(2,1)}, f32[1024,1]{1,0:T(8,128)}) custom-call(s32[1024,1]{1,0:T(8,128)} %copy.41.place_ref, f32[1024,1]{1,0:T(8,128)} %reshape.94.gate_ref, bf16[1024,768]{1,0:T(8,128)(2,1)} %bitcast.47, bf16[1536,768]{1,0:T(8,128)(2,1)} %bitcast.10.refs_2_.back_ref), custom_call_target="tpu_custom_call" | custom-call | tf_op jit(solution)/shard_map/unpack/pallas_call | solution.py:126
  230.8 1.2 reduce
  232.8 1.2 collective-permute-done.23
  234.1 1.3 add_convert_fusion
  (79 shorter events, 9.2 us)
Async XLA Ops:
  0.6 8.6 %copy-start = (s32[8]{0:T(128)S(1)}, s32[8]{0:T(128)}, u32[]{:S(2)}) copy-start(s32[8]{0:T(128)} %param.11) | copy-start | bytes 100
  0.6 16.4 %collective-permute-start = (bf16[128,2048]{1,0:T(8,128)(2,1)}, bf16[128,2048]{1,0:T(8,128)(2,1)S(1)}, u32[]{:S(2)}, u32[]{:S(2)}) collective-permute-start(bf16[128,2048]{1,0:T(8,128)(2,1)} %refs_0_.1), channel_id=1, source_target_pairs={{0,4},{1,5},{2,6},{3,7},{12,8},{13,9},{14,10},{15,11},{16,20},{17,... | collective-permute-start | bytes 1572872 | tf_op jit(solution)/shard_map/ppermute | solution.py:377
  5.6 12.2 %collective-permute-start.1 = (bf16[128,2048]{1,0:T(8,128)(2,1)}, bf16[128,2048]{1,0:T(8,128)(2,1)S(1)}, u32[]{:S(2)}, u32[]{:S(2)}) collective-permute-start(bf16[128,2048]{1,0:T(8,128)(2,1)} %refs_0_.1), channel_id=1, source_target_pairs={{4,8},{5,9},{6,10},{7,11},{8,4},{9,5},{10,6},{11,7},{20,24},{21,25... | collective-permute-start | bytes 1572872 | tf_op jit(solution)/shard_map/ppermute | solution.py:377
  6.3 15.5 %collective-permute-start.2 = (bf16[128,2048]{1,0:T(8,128)(2,1)}, bf16[128,2048]{1,0:T(8,128)(2,1)S(1)}, u32[]{:S(2)}, u32[]{:S(2)}) collective-permute-start(bf16[128,2048]{1,0:T(8,128)(2,1)} %refs_0_.1), channel_id=1, source_target_pairs={{4,0},{5,1},{6,2},{7,3},{8,12},{9,13},{10,14},{11,15},{20,16},{21,... | collective-permute-start | bytes 1572872 | tf_op jit(solution)/shard_map/ppermute | solution.py:377
  7.6 15.2 %collective-permute-start.3 = (bf16[128,2048]{1,0:T(8,128)(2,1)}, bf16[128,2048]{1,0:T(8,128)(2,1)S(1)}, u32[]{:S(2)}, u32[]{:S(2)}) collective-permute-start(bf16[128,2048]{1,0:T(8,128)(2,1)} %refs_0_.1), channel_id=1, source_target_pairs={{0,2},{1,3},{2,0},{3,1},{4,6},{5,7},{6,4},{7,5},{8,10},{9,11},{10,... | collective-permute-start | bytes 1572872 | tf_op jit(solution)/shard_map/ppermute | solution.py:382
  9.9 15.7 %copy-start.19 = (s32[128,8]{0,1:T(8,128)S(1)}, s32[128,8]{0,1:T(8,128)}, u32[]{:S(2)}) copy-start(s32[128,8]{0,1:T(8,128)} %param.8) | copy-start | bytes 12292
  9.9 17.4 %copy-start.17 = (f32[128,8]{0,1:T(8,128)S(1)}, f32[128,8]{0,1:T(8,128)}, u32[]{:S(2)}) copy-start(f32[128,8]{0,1:T(8,128)} %param.7) | copy-start | bytes 12292
  17.9 4.9 %copy-start.10 = (bf16[128,2048]{1,0:T(8,128)(2,1)}, bf16[128,2048]{1,0:T(8,128)(2,1)S(1)}, u32[]{:S(2)}) copy-start(bf16[128,2048]{1,0:T(8,128)(2,1)S(1)} %collective-permute-done.1.refs_1_) | copy-start | bytes 1572868
  22.8 0.8 copy-start.12
  23.6 10.1 %collective-permute-start.4 = (bf16[128,2048]{1,0:T(8,128)(2,1)}, bf16[128,2048]{1,0:T(8,128)(2,1)S(1)}, u32[]{:S(2)}, u32[]{:S(2)}) collective-permute-start(bf16[128,2048]{1,0:T(8,128)(2,1)} %get-tuple-element.39), channel_id=1, source_target_pairs={{4,8},{5,9},{6,10},{7,11},{8,4},{9,5},{10,6},{11,7},{20,24},{21,25... | collective-permute-start | bytes 1572872 | tf_op jit(solution)/shard_map/ppermute | solution.py:377
  24.3 15.3 %collective-permute-start.5 = (bf16[128,2048]{1,0:T(8,128)(2,1)}, bf16[128,2048]{1,0:T(8,128)(2,1)S(1)}, u32[]{:S(2)}, u32[]{:S(2)}) collective-permute-start(bf16[128,2048]{1,0:T(8,128)(2,1)} %get-tuple-element.40), channel_id=1, source_target_pairs={{4,0},{5,1},{6,2},{7,3},{8,12},{9,13},{10,14},{11,15},{20,16},{21,... | collective-permute-start | bytes 1572872 | tf_op jit(solution)/shard_map/ppermute | solution.py:377
  25.7 14.8 %collective-permute-start.6 = (bf16[128,2048]{1,0:T(8,128)(2,1)}, bf16[128,2048]{1,0:T(8,128)(2,1)S(1)}, u32[]{:S(2)}, u32[]{:S(2)}) collective-permute-start(bf16[128,2048]{1,0:T(8,128)(2,1)} %get-tuple-element.41.refs_2_), channel_id=1, source_target_pairs={{0,2},{1,3},{2,0},{3,1},{4,6},{5,7},{6,4},{7,5},{8,10},{9,11},{10,... | collective-permute-start | bytes 1572872 | tf_op jit(solution)/shard_map/ppermute | solution.py:382
  33.7 7.5 %copy-start.11 = (bf16[128,2048]{1,0:T(8,128)(2,1)}, bf16[128,2048]{1,0:T(8,128)(2,1)S(1)}, u32[]{:S(2)}) copy-start(bf16[128,2048]{1,0:T(8,128)(2,1)S(1)} %collective-permute-done.4.refs_0_) | copy-start | bytes 1572868
  40.5 0.9 copy-start.13
  41.4 18.6 %collective-permute-start.7 = (bf16[128,2048]{1,0:T(8,128)(2,1)}, bf16[128,2048]{1,0:T(8,128)(2,1)S(1)}, u32[]{:S(2)}, u32[]{:S(2)}) collective-permute-start(bf16[128,2048]{1,0:T(8,128)(2,1)} %get-tuple-element.46), channel_id=1, source_target_pairs={{4,0},{5,1},{6,2},{7,3},{8,12},{9,13},{10,14},{11,15},{20,16},{21,... | collective-permute-start | bytes 1572872 | tf_op jit(solution)/shard_map/ppermute | solution.py:377
  42.7 15.0 %all-to-all-start = ((f32[16,16,128]{2,1,0:T(8,128)}), f32[16,16,128]{2,1,0:T(8,128)S(1)}, u32[]{:S(2)}, u32[]{:S(2)}) async-start(f32[16,16,128]{2,1,0:T(8,128)} %get-tuple-element.43), calls=%async_computation | async-start | bytes 262144 | tf_op jit(solution)/shard_map/all_to_all | solution.py:432
  48.0 15.8 %collective-permute-start.8 = (bf16[128,2048]{1,0:T(8,128)(2,1)}, bf16[128,2048]{1,0:T(8,128)(2,1)S(1)}, u32[]{:S(2)}, u32[]{:S(2)}) collective-permute-start(bf16[128,2048]{1,0:T(8,128)(2,1)} %get-tuple-element.47.refs_0_), channel_id=1, source_target_pairs={{0,2},{1,3},{2,0},{3,1},{4,6},{5,7},{6,4},{7,5},{8,10},{9,11},{10,... | collective-permute-start | bytes 1572872 | tf_op jit(solution)/shard_map/ppermute | solution.py:382
  57.6 0.7 copy-start.16
  63.7 0.9 copy-start.9
  64.6 56.2 %all-to-all-start.1 = ((bf16[16,96,768]{2,1,0:T(8,128)(2,1)}), bf16[16,96,768]{2,1,0:T(8,128)(2,1)S(1)}, u32[]{:S(2)}, u32[]{:S(2)}) async-start(bf16[16,96,768]{2,1,0:T(8,128)(2,1)} %bitcast.45), calls=%async_computation.1 | async-start | bytes 4718592 | tf_op jit(solution)/shard_map/all_to_all | solution.py:435
  69.7 7.3 %copy-start.6 = (bf16[128,2048]{1,0:T(8,128)(2,1)S(1)}, bf16[128,2048]{1,0:T(8,128)(2,1)}, u32[]{:S(2)}) copy-start(bf16[128,2048]{1,0:T(8,128)(2,1)} %get-tuple-element.49.refs_2_) | copy-start | bytes 1572868
  76.6 3.9 %collective-permute-start.10 = (bf16[4,96,2048]{2,1,0:T(8,128)(2,1)}, bf16[4,96,2048]{2,1,0:T(8,128)(2,1)}, u32[]{:S(2)}, u32[]{:S(2)}) collective-permute-start(bf16[4,96,2048]{2,1,0:T(8,128)(2,1)} %get-tuple-element.50), channel_id=1, source_target_pairs={{0,1},{1,0},{2,3},{3,2},{4,5},{5,4},{6,7},{7,6},{8,9},{9,8},{10,11... | collective-permute-start | bytes 4718600 | tf_op jit(solution)/shard_map/ppermute | solution.py:382
  77.0 27.1 %collective-permute-start.9 = (bf16[128,2048]{1,0:T(8,128)(2,1)S(1)}, bf16[128,2048]{1,0:T(8,128)(2,1)S(1)}, u32[]{:S(2)}, u32[]{:S(2)}) collective-permute-start(bf16[128,2048]{1,0:T(8,128)(2,1)S(1)} %copy-done.6), channel_id=1, source_target_pairs={{0,2},{1,3},{2,0},{3,1},{4,6},{5,7},{6,4},{7,5},{8,10},{9,11},{10,... | collective-permute-start | bytes 1572872 | tf_op jit(solution)/shard_map/ppermute | solution.py:382
  104.1 0.8 copy-start.15
  111.7 3.8 %collective-permute-start.11 = (bf16[4,96,2048]{2,1,0:T(8,128)(2,1)}, bf16[4,96,2048]{2,1,0:T(8,128)(2,1)}, u32[]{:S(2)}, u32[]{:S(2)}) collective-permute-start(bf16[4,96,2048]{2,1,0:T(8,128)(2,1)} %get-tuple-element.55), channel_id=1, source_target_pairs={{0,1},{1,0},{2,3},{3,2},{4,5},{5,4},{6,7},{7,6},{8,9},{9,8},{10,11... | collective-permute-start | bytes 4718600 | tf_op jit(solution)/shard_map/ppermute | solution.py:382
  120.8 1.5 copy-start.1
  126.9 12.0 %collective-permute-start.12 = (bf16[4,96,2048]{2,1,0:T(8,128)(2,1)}, bf16[4,96,2048]{2,1,0:T(8,128)(2,1)S(1)}, u32[]{:S(2)}, u32[]{:S(2)}) collective-permute-start(bf16[4,96,2048]{2,1,0:T(8,128)(2,1)} %forward_rows.5), channel_id=1, source_target_pairs={{0,1},{1,0},{2,3},{3,2},{4,5},{5,4},{6,7},{7,6},{8,9},{9,8},{10,11... | collective-permute-start | bytes 4718600 | tf_op jit(solution)/shard_map/ppermute | solution.py:382
  127.0 72.9 %all-to-all-start.2 = ((bf16[16,96,768]{2,1,0:T(8,128)(2,1)}), bf16[16,96,768]{2,1,0:T(8,128)(2,1)}, u32[]{:S(2)}, u32[]{:S(2)}) async-start(bf16[16,96,768]{2,1,0:T(8,128)(2,1)} %get-tuple-element.69), calls=%async_computation.2 | async-start | bytes 4718592 | tf_op jit(solution)/shard_map/all_to_all | solution.py:448
  138.8 1.1 copy-start.4
  142.8 27.1 %collective-permute-start.15 = (bf16[128,2048]{1,0:T(8,128)(2,1)}, bf16[128,2048]{1,0:T(8,128)(2,1)}, u32[]{:S(2)}, u32[]{:S(2)}) collective-permute-start(bf16[128,2048]{1,0:T(8,128)(2,1)} %get-tuple-element.60.refs_5_), channel_id=1, source_target_pairs={{0,2},{1,3},{2,0},{3,1},{4,6},{5,7},{6,4},{7,5},{8,10},{9,11},{10,... | collective-permute-start | bytes 1572872 | tf_op jit(solution)/shard_map/ppermute | solution.py:382
  144.7 4.9 %copy-start.2 = (bf16[16,96,768]{2,1,0:T(8,128)(2,1)S(1)}, bf16[16,96,768]{2,1,0:T(8,128)(2,1)}, u32[]{:S(2)}) copy-start(bf16[16,96,768]{2,1,0:T(8,128)(2,1)} %after.10) | copy-start | bytes 7077892
  149.4 36.2 %collective-permute-start.16 = (bf16[128,2048]{1,0:T(8,128)(2,1)}, bf16[128,2048]{1,0:T(8,128)(2,1)}, u32[]{:S(2)}, u32[]{:S(2)}) collective-permute-start(bf16[128,2048]{1,0:T(8,128)(2,1)} %get-tuple-element.59.refs_4_), channel_id=1, source_target_pairs={{0,2},{1,3},{2,0},{3,1},{4,6},{5,7},{6,4},{7,5},{8,10},{9,11},{10,... | collective-permute-start | bytes 1572872 | tf_op jit(solution)/shard_map/ppermute | solution.py:382
  149.6 22.5 %collective-permute-start.13 = (bf16[4,96,2048]{2,1,0:T(8,128)(2,1)}, bf16[4,96,2048]{2,1,0:T(8,128)(2,1)S(1)}, u32[]{:S(2)}, u32[]{:S(2)}) collective-permute-start(bf16[4,96,2048]{2,1,0:T(8,128)(2,1)} %forward_rows.7), channel_id=1, source_target_pairs={{0,1},{1,0},{2,3},{3,2},{4,5},{5,4},{6,7},{7,6},{8,9},{9,8},{10,11... | collective-permute-start | bytes 4718600 | tf_op jit(solution)/shard_map/ppermute | solution.py:382
  172.1 1.1 copy-start.3
  176.0 21.8 %collective-permute-start.18 = (bf16[128,2048]{1,0:T(8,128)(2,1)}, bf16[128,2048]{1,0:T(8,128)(2,1)S(1)}, u32[]{:S(2)}, u32[]{:S(2)}) collective-permute-start(bf16[128,2048]{1,0:T(8,128)(2,1)} %get-tuple-element.65.refs_3_), channel_id=1, source_target_pairs={{0,2},{1,3},{2,0},{3,1},{4,6},{5,7},{6,4},{7,5},{8,10},{9,11},{10,... | collective-permute-start | bytes 1572872 | tf_op jit(solution)/shard_map/ppermute | solution.py:382
  187.7 18.8 %collective-permute-start.17 = (bf16[128,2048]{1,0:T(8,128)(2,1)}, bf16[128,2048]{1,0:T(8,128)(2,1)S(1)}, u32[]{:S(2)}, u32[]{:S(2)}) collective-permute-start(bf16[128,2048]{1,0:T(8,128)(2,1)} %get-tuple-element.67), channel_id=1, source_target_pairs={{0,12},{1,13},{2,14},{3,15},{12,0},{13,1},{14,2},{15,3},{16,28},{1... | collective-permute-start | bytes 1572872 | tf_op jit(solution)/shard_map/ppermute | solution.py:377
  192.9 23.9 %collective-permute-start.20 = (bf16[128,2048]{1,0:T(8,128)(2,1)}, bf16[128,2048]{1,0:T(8,128)(2,1)S(1)}, u32[]{:S(2)}, u32[]{:S(2)}) collective-permute-start(bf16[128,2048]{1,0:T(8,128)(2,1)} %get-tuple-element.70), channel_id=1, source_target_pairs={{0,4},{1,5},{2,6},{3,7},{12,8},{13,9},{14,10},{15,11},{16,20},{17,... | collective-permute-start | bytes 1572872 | tf_op jit(solution)/shard_map/ppermute | solution.py:377
  194.2 25.3 %collective-permute-start.22 = (bf16[128,2048]{1,0:T(8,128)(2,1)}, bf16[128,2048]{1,0:T(8,128)(2,1)S(1)}, u32[]{:S(2)}, u32[]{:S(2)}) collective-permute-start(bf16[128,2048]{1,0:T(8,128)(2,1)} %get-tuple-element.70), channel_id=1, source_target_pairs={{4,8},{5,9},{6,10},{7,11},{8,4},{9,5},{10,6},{11,7},{20,24},{21,25... | collective-permute-start | bytes 1572872 | tf_op jit(solution)/shard_map/ppermute | solution.py:377
  194.9 37.9 %collective-permute-start.14 = (bf16[128,2048]{1,0:T(8,128)(2,1)}, bf16[128,2048]{1,0:T(8,128)(2,1)S(1)}, u32[]{:S(2)}, u32[]{:S(2)}) collective-permute-start(bf16[128,2048]{1,0:T(8,128)(2,1)} %get-tuple-element.62.refs_4_), channel_id=1, source_target_pairs={{0,2},{1,3},{2,0},{3,1},{4,6},{5,7},{6,4},{7,5},{8,10},{9,11},{10,... | collective-permute-start | bytes 1572872 | tf_op jit(solution)/shard_map/ppermute | solution.py:382
  206.5 0.8 copy-start.7
  207.3 12.2 %copy-start.5 = (bf16[128,2048]{1,0:T(8,128)(2,1)S(1)}, bf16[128,2048]{1,0:T(8,128)(2,1)}, u32[]{:S(2)}) copy-start(bf16[128,2048]{1,0:T(8,128)(2,1)} %get-tuple-element.67) | copy-start | bytes 1572868
  207.3 14.6 %copy-start.18 = (s32[1,1024]{1,0:T(1,128)S(1)}, s32[1,1024]{1,0:T(1,128)}, u32[]{:S(2)}) copy-start(s32[1,1024]{1,0:T(1,128)} %get-tuple-element.71) | copy-start | bytes 12292
  207.3 25.6 %collective-permute-start.19 = (bf16[128,2048]{1,0:T(8,128)(2,1)}, bf16[128,2048]{1,0:T(8,128)(2,1)S(1)}, u32[]{:S(2)}, u32[]{:S(2)}) collective-permute-start(bf16[128,2048]{1,0:T(8,128)(2,1)} %after.13), channel_id=1, source_target_pairs={{0,4},{1,5},{2,6},{3,7},{12,8},{13,9},{14,10},{15,11},{16,20},{17,... | collective-permute-start | bytes 1572872 | tf_op jit(solution)/shard_map/ppermute | solution.py:377
  218.8 14.0 %collective-permute-start.21 = (bf16[128,2048]{1,0:T(8,128)(2,1)}, bf16[128,2048]{1,0:T(8,128)(2,1)S(1)}, u32[]{:S(2)}, u32[]{:S(2)}) collective-permute-start(bf16[128,2048]{1,0:T(8,128)(2,1)} %add_convert_fusion.2), channel_id=1, source_target_pairs={{4,8},{5,9},{6,10},{7,11},{8,4},{9,5},{10,6},{11,7},{20,24},{21,25... | collective-permute-start | bytes 1572872 | tf_op jit(solution)/shard_map/ppermute | solution.py:377
  220.5 13.6 %collective-permute-start.23 = (bf16[128,2048]{1,0:T(8,128)(2,1)}, bf16[128,2048]{1,0:T(8,128)(2,1)S(1)}, u32[]{:S(2)}, u32[]{:S(2)}) collective-permute-start(bf16[128,2048]{1,0:T(8,128)(2,1)} %add_convert_fusion.1), channel_id=1, source_target_pairs={{4,0},{5,1},{6,2},{7,3},{8,12},{9,13},{10,14},{11,15},{20,16},{21,... | collective-permute-start | bytes 1572872 | tf_op jit(solution)/shard_map/ppermute | solution.py:377
  223.8 10.2 %copy-start.8 = (bf16[128,2048]{1,0:T(8,128)(2,1)S(1)}, bf16[128,2048]{1,0:T(8,128)(2,1)}, u32[]{:S(2)}) copy-start(bf16[128,2048]{1,0:T(8,128)(2,1)} %copy-done.7) | copy-start | bytes 1572868
  223.9 10.2 %copy-start.14 = (bf16[128,2048]{1,0:T(8,128)(2,1)S(1)}, bf16[128,2048]{1,0:T(8,128)(2,1)}, u32[]{:S(2)}) copy-start(bf16[128,2048]{1,0:T(8,128)(2,1)} %get-tuple-element.61) | copy-start | bytes 1572868

commit v13 on v12

--- a/solution.py
+++ b/solution.py
@@ -448,24 +448,28 @@
     back_rows = lax.all_to_all(back, "expert", split_axis=0, concat_axis=0, tiled=True).reshape(-1, hidden)
 
     rows_h, = after((rows_h,), ready)
-    beside, across, passing = [], [], []
+    beside, leaving, waited = [], [], []
     for slots in ((2, 3), (1, 0)):
-        other = swapped_with(forward_rows(here, rank, gate, rows_h, weight, slots, 1, [*passing]), 1)
-        mine = forward_rows(here, rank, gate, rows_h, weight, slots, 0, [*passing])
-        passing = summed(here, rank, mine, other, slots, 1)
+        other = swapped_with(forward_rows(here, rank, gate, rows_h, weight, slots, 1, waited), 1)
+        mine = forward_rows(here, rank, gate, rows_h, weight, slots, 0, waited)
+        leaving += summed(here, rank, mine, other, slots, 1)
         beside += summed(here, rank, mine, other, slots, 0)
-        across += [swapped_with(part, 2) for part in passing]
+        waited = leaving[:1]
+    across = [swapped_with(leaving[0], 2)]
+    mid, = after((added(beside[0], across[0]),))
+    leaving[1], = after((leaving[1],), mid)
+    across += [swapped_with(part, 2) for part in leaving[1:]]
+    z_rows, = after((z_rows,), across[0])
     grad_sum = lax.dot_general(
         rows_h.reshape(-1, hidden), z_rows.reshape(devices * capacity, -1), (((0,), (0,)), ((), ())),
         preferred_element_type=F32,
     )
     weight_grad = grad_sum.astype(BF16)[None]
-    beside[0], = after((beside[0],), across[1], weight_grad, *passing)
-    mid, far, close, kept = zip(beside, across)
-    mid, far = after((added(*mid), added(*far)))
+    _, far, close, kept = zip(beside, across)
     mid_outer, mid_inner = passed(OUTER, mid), passed(INNER, mid)
+    far, = after((added(*far),))
     far_far = passed(ENDS_SWAP, far)
-    close, = after((added(*close),), far_far, back_rows)
+    close, = after((added(*close),), back_rows, weight_grad)
     close_outer = passed(OUTER, close)
     close_inner = passed(INNER, added(close, mid_outer))
     far_ends = passed(ENDS, added(far, mid_inner))

time: 236 us -> 242 us (1.025)
  starting transfers between devices: 50.4 us -> 68.3 us
  waiting for transfers between devices: 78 us -> 63.8 us
    ppermute x12, starting transfers between devices: 20.8 us -> 38.8 us  [passed(): lax.ppermute(value, 'expert', [(a * 4 + lane, b * 4 + lane) for a, b in p...]
    ppermute x12, waiting for transfers between devices: 32.9 us -> 17 us  [passed(): lax.ppermute(value, 'expert', [(a * 4 + lane, b * 4 + lane) for a, b in p...]
    unnamed x43 -> x41, local copies, waits for them, and re-layouts: 9.4 us -> 10.2 us
  transfers between devices with their start and end apart: 27 -> 27, of which waited for: 13 -> 9; matrix products, arithmetic and copies ran while one was open for 12% -> 12% of each run, Pallas kernels for 27% -> 26%
where the time goes in v13:
time: 242 us; the launch traced here: 241 us
  starting transfers between devices  68.3 us (28%)
  Pallas kernels  68.3 us (28%)
  waiting for transfers between devices  63.8 us (26%)
  other arithmetic  16.2 us (7%)
  local copies, waits for them, and re-layouts  14.5 us (6%)
  matrix products  9.3 us (4%)
    ppermute x12, waiting for transfers between devices, swapped_with(): return lax.ppermute(value, 'expert', [(i, i ^ bit) for i in range(devices)])  39 us
    ppermute x12, starting transfers between devices, passed(): lax.ppermute(value, 'expert', [(a * 4 + lane, b * 4 + lane) for a, b in p...  38.8 us
    pallas_call x4, Pallas kernels, forward_rows(): pl.pallas_call(functools.partial(forward_kernel, capacity, slots, turn),...  18.7 us
    ppermute x12, waiting for transfers between devices, passed(): lax.ppermute(value, 'expert', [(a * 4 + lane, b * 4 + lane) for a, b in p...  17 us
    convert_element_type x9, other arithmetic, added(): return total.astype(BF16)  14.9 us
    pallas_call x2, Pallas kernels, scaled_rows(): pl.pallas_call(functools.partial(scale_kernel, capacity, slots, len(buffe...  13.6 us
    ppermute x12, starting transfers between devices, swapped_with(): return lax.ppermute(value, 'expert', [(i, i ^ bit) for i in range(devices)])  12 us
    pallas_call x4, Pallas kernels, summed(): pl.pallas_call(functools.partial(sum_kernel, capacity, slots, turn), grid...  11.3 us
  transfers between devices with their start and end apart: 27, of which 9 were waited for; matrix products, arithmetic and copies ran while one was open for 12% of the time, Pallas kernels for 26%

profile of v13, /device:TPU:0, one launch (start us, length us, event | category | flops | bytes accessed | tf_op | source)
XLA Modules:
  0.0 241.4 jit_solution(11361760142289102739)
XLA Ops:
  0.6 5.0 %collective-permute-start = (bf16[128,2048]{1,0:T(8,128)(2,1)}, bf16[128,2048]{1,0:T(8,128)(2,1)S(1)}, u32[]{:S(2)}, u32[]{:S(2)}) collective-permute-start(bf16[128,2048]{1,0:T(8,128)(2,1)} %refs_0_.1), channel_id=1, source_target_pairs={{0,4},{1,5},{2,6},{3,7},{12,8},{13,9},{14,10},{15,11},{16,20},{17,... | collective-permute-start | bytes 1572872 | tf_op jit(solution)/shard_map/ppermute | solution.py:377
  6.3 1.3 collective-permute-start.2
  7.6 1.6 collective-permute-start.3
  9.9 7.2 %collective-permute-done = bf16[128,2048]{1,0:T(8,128)(2,1)S(1)} collective-permute-done((bf16[128,2048]{1,0:T(8,128)(2,1)}, bf16[128,2048]{1,0:T(8,128)(2,1)S(1)}, u32[]{:S(2)}, u32[]{:S(2)}) %collective-permute-start) | collective-permute-done | bytes 524320 | tf_op jit(solution)/shard_map/ppermute | solution.py:377
  17.1 0.8 copy.45.refs_0_
  17.9 3.9 %collective-permute-done.2 = bf16[128,2048]{1,0:T(8,128)(2,1)S(1)} collective-permute-done((bf16[128,2048]{1,0:T(8,128)(2,1)}, bf16[128,2048]{1,0:T(8,128)(2,1)S(1)}, u32[]{:S(2)}, u32[]{:S(2)}) %collective-permute-start.2) | collective-permute-done | bytes 524320 | tf_op jit(solution)/shard_map/ppermute | solution.py:377
  21.8 1.0 add_convert_fusion.8.refs_2_
  22.8 0.8 copy-done.10
  24.3 1.3 collective-permute-start.5
  25.7 1.6 collective-permute-start.6
  28.1 5.6 %pack.1 = (s32[1,1024]{1,0:T(1,128)}, bf16[1536,768]{1,0:T(8,128)(2,1)}) custom-call(s32[1,1024]{1,0:T(1,128)} %reshape.76.ids_ref, bf16[1024,768]{1,0:T(8,128)(2,1)} %bitcast.46), custom_call_target="tpu_custom_call" | custom-call | tf_op jit(solution)/shard_map/pack/pallas_call | solution.py:92
  33.7 5.9 %collective-permute-done.5 = bf16[128,2048]{1,0:T(8,128)(2,1)S(1)} collective-permute-done((bf16[128,2048]{1,0:T(8,128)(2,1)}, bf16[128,2048]{1,0:T(8,128)(2,1)S(1)}, u32[]{:S(2)}, u32[]{:S(2)}) %collective-permute-start.5) | collective-permute-done | bytes 524320 | tf_op jit(solution)/shard_map/ppermute | solution.py:377
  39.6 0.9 add_convert_fusion.7.refs_1_
  40.5 0.7 broadcast_in_dim.19.refs_2_
  41.4 1.3 collective-permute-start.7
  42.6 5.3 %all-to-all-start = ((f32[16,16,128]{2,1,0:T(8,128)}), f32[16,16,128]{2,1,0:T(8,128)S(1)}, u32[]{:S(2)}, u32[]{:S(2)}) async-start(f32[16,16,128]{2,1,0:T(8,128)} %get-tuple-element.41), calls=%async_computation | async-start | bytes 262144 | tf_op jit(solution)/shard_map/all_to_all | solution.py:432
  47.9 1.9 collective-permute-start.8
  49.9 7.7 %all-to-all-done.routing_ref = f32[16,16,128]{2,1,0:T(8,128)S(1)} async-done(((f32[16,16,128]{2,1,0:T(8,128)}), f32[16,16,128]{2,1,0:T(8,128)S(1)}, u32[]{:S(2)}, u32[]{:S(2)}) %all-to-all-start) | async-done | bytes 131104 | tf_op jit(solution)/shard_map/all_to_all | solution.py:432
  58.3 1.7 route.1
  59.9 0.9 add_convert_fusion.6.refs_1_
  60.9 2.9 %collective-permute-done.8.refs_2_.refs_1_ = bf16[128,2048]{1,0:T(8,128)(2,1)S(1)} collective-permute-done((bf16[128,2048]{1,0:T(8,128)(2,1)}, bf16[128,2048]{1,0:T(8,128)(2,1)S(1)}, u32[]{:S(2)}, u32[]{:S(2)}) %collective-permute-start.8) | collective-permute-done | bytes 524320 | tf_op jit(solution)/shard_map/ppermute | solution.py:382
  63.7 0.9 copy-done.7
  64.6 5.1 %all-to-all-start.1 = ((bf16[16,96,768]{2,1,0:T(8,128)(2,1)}), bf16[16,96,768]{2,1,0:T(8,128)(2,1)S(1)}, u32[]{:S(2)}, u32[]{:S(2)}) async-start(bf16[16,96,768]{2,1,0:T(8,128)(2,1)} %bitcast.45), calls=%async_computation.1 | async-start | bytes 4718592 | tf_op jit(solution)/shard_map/all_to_all | solution.py:435
  69.7 6.8 %scaled_rows.2 = (bf16[16,96,2048]{2,1,0:T(8,128)(2,1)}, bf16[16,96,768]{2,1,0:T(8,128)(2,1)}, bf16[4,96,2048]{2,1,0:T(8,128)(2,1)}) custom-call(s32[1]{0:T(128)} %bitcast.here_ref, s32[2,16,128]{2,1,0:T(8,128)} %get-tuple-element.42.refs_3_.rank_ref, f32[2,16,128]{2,1,0:T(8,128)} %get-tuple-element.43.gate_ref, bf16[768,2048]{1,0:T(8,128)(2,1)} %bitcast.37, ...), custom_call_target="tpu_custom_call" | custom-call | tf_op jit(solution)/shard_map/scaled_rows/pallas_call | solution.py:239
  77.0 1.7 collective-permute-start.9
  78.7 1.7 collective-permute-done.10.rows_ref
  80.4 5.3 %sibling_rows.2 = (bf16[16,96,2048]{2,1,0:T(8,128)(2,1)}, bf16[16,96,768]{2,1,0:T(8,128)(2,1)}, f32[8,128]{1,0:T(8,128)}) custom-call(s32[1]{0:T(128)} %bitcast.here_ref, bf16[768,2048]{1,0:T(8,128)(2,1)} %bitcast.38, bf16[4,96,2048]{2,1,0:T(8,128)(2,1)} %collective-permute-done.10.rows_ref, ...), custom_call_target="tpu_custom_call", output_to_operand_aliasing={{0}: (3, {}), {1}: (4, {})} | custom-call | tf_op jit(solution)/shard_map/sibling_rows/pallas_call | solution.py:278
  85.6 18.4 %collective-permute-done.9.refs_3_ = bf16[128,2048]{1,0:T(8,128)(2,1)S(1)} collective-permute-done((bf16[128,2048]{1,0:T(8,128)(2,1)S(1)}, bf16[128,2048]{1,0:T(8,128)(2,1)S(1)}, u32[]{:S(2)}, u32[]{:S(2)}) %collective-permute-start.9) | collective-permute-done | bytes 524320 | tf_op jit(solution)/shard_map/ppermute | solution.py:382
  104.1 0.8 copy-done.14
  104.9 6.8 %scaled_rows.3 = (bf16[16,96,2048]{2,1,0:T(8,128)(2,1)}, bf16[16,96,768]{2,1,0:T(8,128)(2,1)}, bf16[4,96,2048]{2,1,0:T(8,128)(2,1)}) custom-call(s32[1]{0:T(128)} %bitcast.here_ref, s32[2,16,128]{2,1,0:T(8,128)} %get-tuple-element.42.refs_3_.rank_ref, f32[2,16,128]{2,1,0:T(8,128)} %get-tuple-element.43.gate_ref, ...), custom_call_target="tpu_custom_call", output_to_operand_aliasing={{0}: (8, {}), {1}: (9, {})} | custom-call | tf_op jit(solution)/shard_map/scaled_rows/pallas_call | solution.py:239
  111.7 3.7 %collective-permute-done.11.rows_ref = bf16[4,96,2048]{2,1,0:T(8,128)(2,1)} collective-permute-done((bf16[4,96,2048]{2,1,0:T(8,128)(2,1)}, bf16[4,96,2048]{2,1,0:T(8,128)(2,1)}, u32[]{:S(2)}, u32[]{:S(2)}) %collective-permute-start.11) | collective-permute-done | bytes 1572896 | tf_op jit(solution)/shard_map/ppermute | solution.py:382
  115.5 5.3 %sibling_rows.3 = (bf16[16,96,2048]{2,1,0:T(8,128)(2,1)}, bf16[16,96,768]{2,1,0:T(8,128)(2,1)}, f32[8,128]{1,0:T(8,128)}) custom-call(s32[1]{0:T(128)} %bitcast.here_ref, bf16[768,2048]{1,0:T(8,128)(2,1)} %bitcast.40, bf16[4,96,2048]{2,1,0:T(8,128)(2,1)} %collective-permute-done.11.rows_ref, ...), custom_call_target="tpu_custom_call", output_to_operand_aliasing={{0}: (3, {}), {1}: (4, {})} | custom-call | tf_op jit(solution)/shard_map/sibling_rows/pallas_call | solution.py:278
  120.8 1.4 copy-done.1
  122.2 4.7 %forward_rows.5 = bf16[4,96,2048]{2,1,0:T(8,128)(2,1)} custom-call(s32[1]{0:T(128)} %bitcast.here_ref, s32[2,16,128]{2,1,0:T(8,128)} %get-tuple-element.42.refs_3_.rank_ref, f32[2,16,128]{2,1,0:T(8,128)} %get-tuple-element.43.gate_ref, bf16[768,2048]{1,0:T(8,128)(2,1)} %bitcast.41, bf16[8,2,96,768]{3,2,1,0:T(8,128)(2,1)} %bitcast.21, ...), custom_call_target="tpu_custom_call" | custom-call | tf_op jit(solution)/shard_map/forward_rows/pallas_call | solution.py:319
  127.0 7.2 %all-to-all-start.2 = ((bf16[16,96,768]{2,1,0:T(8,128)(2,1)}), bf16[16,96,768]{2,1,0:T(8,128)(2,1)}, u32[]{:S(2)}, u32[]{:S(2)}) async-start(bf16[16,96,768]{2,1,0:T(8,128)(2,1)} %get-tuple-element.65), calls=%async_computation.2 | async-start | bytes 4718592 | tf_op jit(solution)/shard_map/all_to_all | solution.py:448
  134.2 4.6 %forward_rows.4.own_ref = bf16[4,96,2048]{2,1,0:T(8,128)(2,1)} custom-call(s32[1]{0:T(128)} %bitcast.here_ref, s32[2,16,128]{2,1,0:T(8,128)} %get-tuple-element.42.refs_3_.rank_ref, f32[2,16,128]{2,1,0:T(8,128)} %get-tuple-element.43.gate_ref, bf16[768,2048]{1,0:T(8,128)(2,1)} %bitcast.42, bf16[8,2,96,768]{3,2,1,0:T(8,128)(2,1)} %bitcast.25, ...), custom_call_target="tpu_custom_call" | custom-call | tf_op jit(solution)/shard_map/forward_rows/pallas_call | solution.py:319
  138.9 1.2 copy-done.4
  140.0 2.8 %summed.4 = (bf16[128,2048]{1,0:T(8,128)(2,1)}, bf16[128,2048]{1,0:T(8,128)(2,1)}) custom-call(s32[1]{0:T(128)} %bitcast.here_ref, s32[2,16,128]{2,1,0:T(8,128)} %get-tuple-element.42.refs_3_.rank_ref, bf16[4,96,2048]{2,1,0:T(8,128)(2,1)} %forward_rows.4.own_ref, bf16[4,96,2048]{2,1,0:T(8,128)(2,1)} %copy-done.4), custom_call_target="tpu_custom_call" | custom-call | tf_op jit(solution)/shard_map/summed/pallas_call | solution.py:354
  142.8 1.9 collective-permute-start.15
  144.7 4.6 %forward_rows.7 = bf16[4,96,2048]{2,1,0:T(8,128)(2,1)} custom-call(s32[1]{0:T(128)} %bitcast.here_ref, s32[2,16,128]{2,1,0:T(8,128)} %get-tuple-element.42.refs_3_.rank_ref, f32[2,16,128]{2,1,0:T(8,128)} %get-tuple-element.43.gate_ref, bf16[768,2048]{1,0:T(8,128)(2,1)} %bitcast.43, bf16[8,2,96,768]{3,2,1,0:T(8,128)(2,1)} %bitcast.29, ...), custom_call_target="tpu_custom_call" | custom-call | tf_op jit(solution)/shard_map/forward_rows/pallas_call | solution.py:319
  149.3 4.7 %forward_rows.6.own_ref = bf16[4,96,2048]{2,1,0:T(8,128)(2,1)} custom-call(s32[1]{0:T(128)} %bitcast.here_ref, s32[2,16,128]{2,1,0:T(8,128)} %get-tuple-element.42.refs_3_.rank_ref, f32[2,16,128]{2,1,0:T(8,128)} %get-tuple-element.43.gate_ref, bf16[768,2048]{1,0:T(8,128)(2,1)} %bitcast.44, bf16[8,2,96,768]{3,2,1,0:T(8,128)(2,1)} %bitcast.33, ...), custom_call_target="tpu_custom_call" | custom-call | tf_op jit(solution)/shard_map/forward_rows/pallas_call | solution.py:319
  154.1 2.8 %summed.7 = (bf16[128,2048]{1,0:T(8,128)(2,1)}, bf16[128,2048]{1,0:T(8,128)(2,1)}) custom-call(s32[1]{0:T(128)} %bitcast.here_ref, s32[2,16,128]{2,1,0:T(8,128)} %get-tuple-element.42.refs_3_.rank_ref, bf16[4,96,2048]{2,1,0:T(8,128)(2,1)} %forward_rows.4.own_ref, bf16[4,96,2048]{2,1,0:T(8,128)(2,1)} %copy-done.4), custom_call_target="tpu_custom_call" | custom-call | tf_op jit(solution)/shard_map/summed/pallas_call | solution.py:354
  156.9 12.3 %collective-permute-done.15.refs_1_ = bf16[128,2048]{1,0:T(8,128)(2,1)S(1)} collective-permute-done((bf16[128,2048]{1,0:T(8,128)(2,1)}, bf16[128,2048]{1,0:T(8,128)(2,1)S(1)}, u32[]{:S(2)}, u32[]{:S(2)}) %collective-permute-start.15) | collective-permute-done | bytes 524320 | tf_op jit(solution)/shard_map/ppermute | solution.py:382
  169.2 2.2 add_convert_fusion.5.refs_0_
  171.4 2.1 collective-permute-start.20
  173.5 1.5 collective-permute-start.22
  174.9 2.4 collective-permute-start.16
  177.3 1.7 copy-done.2
  179.0 9.3 %fusion.refs_2_ = bf16[1,768,2048]{2,1,0:T(8,128)(2,1)} fusion(bf16[16,96,768]{2,1,0:T(8,128)(2,1)S(1)} %copy-done.2, bf16[16,96,2048]{2,1,0:T(8,128)(2,1)} %after.16), kind=kOutput, calls=%fused_computation.2 | convolution fusion | flops 4833411072 | bytes 11796480 | tf_op jit(solution)/shard_map/dot_general | solution.py:463
  188.3 1.1 copy-done.3
  189.4 2.8 %summed.6 = (bf16[128,2048]{1,0:T(8,128)(2,1)}, bf16[128,2048]{1,0:T(8,128)(2,1)}) custom-call(s32[1]{0:T(128)} %bitcast.here_ref, s32[2,16,128]{2,1,0:T(8,128)} %get-tuple-element.42.refs_3_.rank_ref, bf16[4,96,2048]{2,1,0:T(8,128)(2,1)} %forward_rows.6.own_ref, bf16[4,96,2048]{2,1,0:T(8,128)(2,1)} %copy-done.3), custom_call_target="tpu_custom_call" | custom-call | tf_op jit(solution)/shard_map/summed/pallas_call | solution.py:354
  192.3 2.0 add_convert_fusion.4.refs_0_
  194.3 6.2 %collective-permute-start.17 = (bf16[128,2048]{1,0:T(8,128)(2,1)}, bf16[128,2048]{1,0:T(8,128)(2,1)S(1)}, u32[]{:S(2)}, u32[]{:S(2)}) collective-permute-start(bf16[128,2048]{1,0:T(8,128)(2,1)} %after.15), channel_id=1, source_target_pairs={{0,12},{1,13},{2,14},{3,15},{12,0},{13,1},{14,2},{15,3},{16,28},{1... | collective-permute-start | bytes 1572872 | tf_op jit(solution)/shard_map/ppermute | solution.py:377
  200.6 1.3 add_convert_fusion.1
  201.9 1.3 collective-permute-start.23
  203.5 2.8 %summed.5 = (bf16[128,2048]{1,0:T(8,128)(2,1)}, bf16[128,2048]{1,0:T(8,128)(2,1)}) custom-call(s32[1]{0:T(128)} %bitcast.here_ref, s32[2,16,128]{2,1,0:T(8,128)} %get-tuple-element.42.refs_3_.rank_ref, bf16[4,96,2048]{2,1,0:T(8,128)(2,1)} %forward_rows.6.own_ref, bf16[4,96,2048]{2,1,0:T(8,128)(2,1)} %copy-done.3), custom_call_target="tpu_custom_call" | custom-call | tf_op jit(solution)/shard_map/summed/pallas_call | solution.py:354
  206.3 2.0 add_convert_fusion.3.refs_0_
  208.3 2.1 add_convert_fusion.2
  211.1 16.8 %collective-permute-start.19 = (bf16[128,2048]{1,0:T(8,128)(2,1)}, bf16[128,2048]{1,0:T(8,128)(2,1)}, u32[]{:S(2)}, u32[]{:S(2)}) collective-permute-start(bf16[128,2048]{1,0:T(8,128)(2,1)} %after.17), channel_id=1, source_target_pairs={{0,4},{1,5},{2,6},{3,7},{12,8},{13,9},{14,10},{15,11},{16,20},{17,... | collective-permute-start | bytes 1572872 | tf_op jit(solution)/shard_map/ppermute | solution.py:377
  228.0 1.0 copy.42.place_ref
  229.1 1.0 reshape.94.gate_ref
  230.1 6.9 %unpack.1 = (bf16[1024,768]{1,0:T(8,128)(2,1)}, f32[1024,1]{1,0:T(8,128)}) custom-call(s32[1024,1]{1,0:T(8,128)} %copy.42.place_ref, f32[1024,1]{1,0:T(8,128)} %reshape.94.gate_ref, bf16[1024,768]{1,0:T(8,128)(2,1)} %bitcast.47, bf16[1536,768]{1,0:T(8,128)(2,1)} %bitcast.8.refs_1_.back_ref), custom_call_target="tpu_custom_call" | custom-call | tf_op jit(solution)/shard_map/unpack/pallas_call | solution.py:126
  237.0 1.2 reduce
  239.1 2.3 add_convert_fusion
  (79 shorter events, 6.3 us)
Async XLA Ops:
  0.6 8.6 %copy-start = (s32[8]{0:T(128)S(1)}, s32[8]{0:T(128)}, u32[]{:S(2)}) copy-start(s32[8]{0:T(128)} %param.11) | copy-start | bytes 100
  0.6 16.4 %collective-permute-start = (bf16[128,2048]{1,0:T(8,128)(2,1)}, bf16[128,2048]{1,0:T(8,128)(2,1)S(1)}, u32[]{:S(2)}, u32[]{:S(2)}) collective-permute-start(bf16[128,2048]{1,0:T(8,128)(2,1)} %refs_0_.1), channel_id=1, source_target_pairs={{0,4},{1,5},{2,6},{3,7},{12,8},{13,9},{14,10},{15,11},{16,20},{17,... | collective-permute-start | bytes 1572872 | tf_op jit(solution)/shard_map/ppermute | solution.py:377
  5.6 12.2 %collective-permute-start.1 = (bf16[128,2048]{1,0:T(8,128)(2,1)}, bf16[128,2048]{1,0:T(8,128)(2,1)S(1)}, u32[]{:S(2)}, u32[]{:S(2)}) collective-permute-start(bf16[128,2048]{1,0:T(8,128)(2,1)} %refs_0_.1), channel_id=1, source_target_pairs={{4,8},{5,9},{6,10},{7,11},{8,4},{9,5},{10,6},{11,7},{20,24},{21,25... | collective-permute-start | bytes 1572872 | tf_op jit(solution)/shard_map/ppermute | solution.py:377
  6.3 15.5 %collective-permute-start.2 = (bf16[128,2048]{1,0:T(8,128)(2,1)}, bf16[128,2048]{1,0:T(8,128)(2,1)S(1)}, u32[]{:S(2)}, u32[]{:S(2)}) collective-permute-start(bf16[128,2048]{1,0:T(8,128)(2,1)} %refs_0_.1), channel_id=1, source_target_pairs={{4,0},{5,1},{6,2},{7,3},{8,12},{9,13},{10,14},{11,15},{20,16},{21,... | collective-permute-start | bytes 1572872 | tf_op jit(solution)/shard_map/ppermute | solution.py:377
  7.6 15.2 %collective-permute-start.3 = (bf16[128,2048]{1,0:T(8,128)(2,1)}, bf16[128,2048]{1,0:T(8,128)(2,1)S(1)}, u32[]{:S(2)}, u32[]{:S(2)}) collective-permute-start(bf16[128,2048]{1,0:T(8,128)(2,1)} %refs_0_.1), channel_id=1, source_target_pairs={{0,2},{1,3},{2,0},{3,1},{4,6},{5,7},{6,4},{7,5},{8,10},{9,11},{10,... | collective-permute-start | bytes 1572872 | tf_op jit(solution)/shard_map/ppermute | solution.py:382
  9.9 15.7 %copy-start.18 = (s32[128,8]{0,1:T(8,128)S(1)}, s32[128,8]{0,1:T(8,128)}, u32[]{:S(2)}) copy-start(s32[128,8]{0,1:T(8,128)} %param.8) | copy-start | bytes 12292
  9.9 17.4 %copy-start.16 = (f32[128,8]{0,1:T(8,128)S(1)}, f32[128,8]{0,1:T(8,128)}, u32[]{:S(2)}) copy-start(f32[128,8]{0,1:T(8,128)} %param.7) | copy-start | bytes 12292
  17.9 4.9 %copy-start.8 = (bf16[128,2048]{1,0:T(8,128)(2,1)}, bf16[128,2048]{1,0:T(8,128)(2,1)S(1)}, u32[]{:S(2)}) copy-start(bf16[128,2048]{1,0:T(8,128)(2,1)S(1)} %collective-permute-done.1.refs_1_) | copy-start | bytes 1572868
  22.8 0.8 copy-start.10
  23.6 10.1 %collective-permute-start.4 = (bf16[128,2048]{1,0:T(8,128)(2,1)}, bf16[128,2048]{1,0:T(8,128)(2,1)S(1)}, u32[]{:S(2)}, u32[]{:S(2)}) collective-permute-start(bf16[128,2048]{1,0:T(8,128)(2,1)} %get-tuple-element.37), channel_id=1, source_target_pairs={{4,8},{5,9},{6,10},{7,11},{8,4},{9,5},{10,6},{11,7},{20,24},{21,25... | collective-permute-start | bytes 1572872 | tf_op jit(solution)/shard_map/ppermute | solution.py:377
  24.3 15.3 %collective-permute-start.5 = (bf16[128,2048]{1,0:T(8,128)(2,1)}, bf16[128,2048]{1,0:T(8,128)(2,1)S(1)}, u32[]{:S(2)}, u32[]{:S(2)}) collective-permute-start(bf16[128,2048]{1,0:T(8,128)(2,1)} %get-tuple-element.38), channel_id=1, source_target_pairs={{4,0},{5,1},{6,2},{7,3},{8,12},{9,13},{10,14},{11,15},{20,16},{21,... | collective-permute-start | bytes 1572872 | tf_op jit(solution)/shard_map/ppermute | solution.py:377
  25.7 14.8 %collective-permute-start.6 = (bf16[128,2048]{1,0:T(8,128)(2,1)}, bf16[128,2048]{1,0:T(8,128)(2,1)S(1)}, u32[]{:S(2)}, u32[]{:S(2)}) collective-permute-start(bf16[128,2048]{1,0:T(8,128)(2,1)} %get-tuple-element.39.refs_2_), channel_id=1, source_target_pairs={{0,2},{1,3},{2,0},{3,1},{4,6},{5,7},{6,4},{7,5},{8,10},{9,11},{10,... | collective-permute-start | bytes 1572872 | tf_op jit(solution)/shard_map/ppermute | solution.py:382
  33.7 7.5 %copy-start.9 = (bf16[128,2048]{1,0:T(8,128)(2,1)}, bf16[128,2048]{1,0:T(8,128)(2,1)S(1)}, u32[]{:S(2)}) copy-start(bf16[128,2048]{1,0:T(8,128)(2,1)S(1)} %collective-permute-done.4.refs_0_) | copy-start | bytes 1572868
  40.5 0.8 copy-start.11
  41.4 18.6 %collective-permute-start.7 = (bf16[128,2048]{1,0:T(8,128)(2,1)}, bf16[128,2048]{1,0:T(8,128)(2,1)S(1)}, u32[]{:S(2)}, u32[]{:S(2)}) collective-permute-start(bf16[128,2048]{1,0:T(8,128)(2,1)} %get-tuple-element.44), channel_id=1, source_target_pairs={{4,0},{5,1},{6,2},{7,3},{8,12},{9,13},{10,14},{11,15},{20,16},{21,... | collective-permute-start | bytes 1572872 | tf_op jit(solution)/shard_map/ppermute | solution.py:377
  42.6 15.0 %all-to-all-start = ((f32[16,16,128]{2,1,0:T(8,128)}), f32[16,16,128]{2,1,0:T(8,128)S(1)}, u32[]{:S(2)}, u32[]{:S(2)}) async-start(f32[16,16,128]{2,1,0:T(8,128)} %get-tuple-element.41), calls=%async_computation | async-start | bytes 262144 | tf_op jit(solution)/shard_map/all_to_all | solution.py:432
  47.9 15.8 %collective-permute-start.8 = (bf16[128,2048]{1,0:T(8,128)(2,1)}, bf16[128,2048]{1,0:T(8,128)(2,1)S(1)}, u32[]{:S(2)}, u32[]{:S(2)}) collective-permute-start(bf16[128,2048]{1,0:T(8,128)(2,1)} %get-tuple-element.45.refs_0_), channel_id=1, source_target_pairs={{0,2},{1,3},{2,0},{3,1},{4,6},{5,7},{6,4},{7,5},{8,10},{9,11},{10,... | collective-permute-start | bytes 1572872 | tf_op jit(solution)/shard_map/ppermute | solution.py:382
  57.6 0.7 copy-start.15
  63.7 0.9 copy-start.7
  64.6 56.2 %all-to-all-start.1 = ((bf16[16,96,768]{2,1,0:T(8,128)(2,1)}), bf16[16,96,768]{2,1,0:T(8,128)(2,1)S(1)}, u32[]{:S(2)}, u32[]{:S(2)}) async-start(bf16[16,96,768]{2,1,0:T(8,128)(2,1)} %bitcast.45), calls=%async_computation.1 | async-start | bytes 4718592 | tf_op jit(solution)/shard_map/all_to_all | solution.py:435
  69.7 7.3 %copy-start.5 = (bf16[128,2048]{1,0:T(8,128)(2,1)S(1)}, bf16[128,2048]{1,0:T(8,128)(2,1)}, u32[]{:S(2)}) copy-start(bf16[128,2048]{1,0:T(8,128)(2,1)} %get-tuple-element.47.refs_2_) | copy-start | bytes 1572868
  76.5 3.9 %collective-permute-start.10 = (bf16[4,96,2048]{2,1,0:T(8,128)(2,1)}, bf16[4,96,2048]{2,1,0:T(8,128)(2,1)}, u32[]{:S(2)}, u32[]{:S(2)}) collective-permute-start(bf16[4,96,2048]{2,1,0:T(8,128)(2,1)} %get-tuple-element.48), channel_id=1, source_target_pairs={{0,1},{1,0},{2,3},{3,2},{4,5},{5,4},{6,7},{7,6},{8,9},{9,8},{10,11... | collective-permute-start | bytes 4718600 | tf_op jit(solution)/shard_map/ppermute | solution.py:382
  77.0 27.1 %collective-permute-start.9 = (bf16[128,2048]{1,0:T(8,128)(2,1)S(1)}, bf16[128,2048]{1,0:T(8,128)(2,1)S(1)}, u32[]{:S(2)}, u32[]{:S(2)}) collective-permute-start(bf16[128,2048]{1,0:T(8,128)(2,1)S(1)} %copy-done.5), channel_id=1, source_target_pairs={{0,2},{1,3},{2,0},{3,1},{4,6},{5,7},{6,4},{7,5},{8,10},{9,11},{10,... | collective-permute-start | bytes 1572872 | tf_op jit(solution)/shard_map/ppermute | solution.py:382
  104.1 0.8 copy-start.14
  111.7 3.8 %collective-permute-start.11 = (bf16[4,96,2048]{2,1,0:T(8,128)(2,1)}, bf16[4,96,2048]{2,1,0:T(8,128)(2,1)}, u32[]{:S(2)}, u32[]{:S(2)}) collective-permute-start(bf16[4,96,2048]{2,1,0:T(8,128)(2,1)} %get-tuple-element.53), channel_id=1, source_target_pairs={{0,1},{1,0},{2,3},{3,2},{4,5},{5,4},{6,7},{7,6},{8,9},{9,8},{10,11... | collective-permute-start | bytes 4718600 | tf_op jit(solution)/shard_map/ppermute | solution.py:382
  120.8 1.4 copy-start.1
  126.9 12.0 %collective-permute-start.12 = (bf16[4,96,2048]{2,1,0:T(8,128)(2,1)}, bf16[4,96,2048]{2,1,0:T(8,128)(2,1)S(1)}, u32[]{:S(2)}, u32[]{:S(2)}) collective-permute-start(bf16[4,96,2048]{2,1,0:T(8,128)(2,1)} %forward_rows.5), channel_id=1, source_target_pairs={{0,1},{1,0},{2,3},{3,2},{4,5},{5,4},{6,7},{7,6},{8,9},{9,8},{10,11... | collective-permute-start | bytes 4718600 | tf_op jit(solution)/shard_map/ppermute | solution.py:382
  127.0 81.3 %all-to-all-start.2 = ((bf16[16,96,768]{2,1,0:T(8,128)(2,1)}), bf16[16,96,768]{2,1,0:T(8,128)(2,1)}, u32[]{:S(2)}, u32[]{:S(2)}) async-start(bf16[16,96,768]{2,1,0:T(8,128)(2,1)} %get-tuple-element.65), calls=%async_computation.2 | async-start | bytes 4718592 | tf_op jit(solution)/shard_map/all_to_all | solution.py:448
  138.9 1.2 copy-start.4
  142.8 26.3 %collective-permute-start.15 = (bf16[128,2048]{1,0:T(8,128)(2,1)}, bf16[128,2048]{1,0:T(8,128)(2,1)S(1)}, u32[]{:S(2)}, u32[]{:S(2)}) collective-permute-start(bf16[128,2048]{1,0:T(8,128)(2,1)} %get-tuple-element.57.refs_4_), channel_id=1, source_target_pairs={{0,2},{1,3},{2,0},{3,1},{4,6},{5,7},{6,4},{7,5},{8,10},{9,11},{10,... | collective-permute-start | bytes 1572872 | tf_op jit(solution)/shard_map/ppermute | solution.py:382
  154.1 34.2 %collective-permute-start.13 = (bf16[4,96,2048]{2,1,0:T(8,128)(2,1)}, bf16[4,96,2048]{2,1,0:T(8,128)(2,1)S(1)}, u32[]{:S(2)}, u32[]{:S(2)}) collective-permute-start(bf16[4,96,2048]{2,1,0:T(8,128)(2,1)} %forward_rows.7), channel_id=1, source_target_pairs={{0,1},{1,0},{2,3},{3,2},{4,5},{5,4},{6,7},{7,6},{8,9},{9,8},{10,11... | collective-permute-start | bytes 4718600 | tf_op jit(solution)/shard_map/ppermute | solution.py:382
  169.2 8.1 %copy-start.6 = (bf16[128,2048]{1,0:T(8,128)(2,1)}, bf16[128,2048]{1,0:T(8,128)(2,1)S(1)}, u32[]{:S(2)}) copy-start(bf16[128,2048]{1,0:T(8,128)(2,1)S(1)} %collective-permute-done.15.refs_1_) | copy-start | bytes 1572868
  171.4 36.9 %collective-permute-start.20 = (bf16[128,2048]{1,0:T(8,128)(2,1)}, bf16[128,2048]{1,0:T(8,128)(2,1)}, u32[]{:S(2)}, u32[]{:S(2)}) collective-permute-start(bf16[128,2048]{1,0:T(8,128)(2,1)} %after.13.refs_1_), channel_id=1, source_target_pairs={{0,4},{1,5},{2,6},{3,7},{12,8},{13,9},{14,10},{15,11},{16,20},{17,... | collective-permute-start | bytes 1572872 | tf_op jit(solution)/shard_map/ppermute | solution.py:377
  173.5 27.1 %collective-permute-start.22 = (bf16[128,2048]{1,0:T(8,128)(2,1)}, bf16[128,2048]{1,0:T(8,128)(2,1)}, u32[]{:S(2)}, u32[]{:S(2)}) collective-permute-start(bf16[128,2048]{1,0:T(8,128)(2,1)} %after.13.refs_1_), channel_id=1, source_target_pairs={{4,8},{5,9},{6,10},{7,11},{8,4},{9,5},{10,6},{11,7},{20,24},{21,25... | collective-permute-start | bytes 1572872 | tf_op jit(solution)/shard_map/ppermute | solution.py:377
  174.9 17.3 %collective-permute-start.16 = (bf16[128,2048]{1,0:T(8,128)(2,1)}, bf16[128,2048]{1,0:T(8,128)(2,1)}, u32[]{:S(2)}, u32[]{:S(2)}) collective-permute-start(bf16[128,2048]{1,0:T(8,128)(2,1)} %after.14), channel_id=1, source_target_pairs={{0,2},{1,3},{2,0},{3,1},{4,6},{5,7},{6,4},{7,5},{8,10},{9,11},{10,... | collective-permute-start | bytes 1572872 | tf_op jit(solution)/shard_map/ppermute | solution.py:382
  177.3 1.7 copy-start.2
  188.3 4.0 %copy-start.13 = (bf16[128,2048]{1,0:T(8,128)(2,1)S(1)}, bf16[128,2048]{1,0:T(8,128)(2,1)}, u32[]{:S(2)}) copy-start(bf16[128,2048]{1,0:T(8,128)(2,1)} %get-tuple-element.60) | copy-start | bytes 1572868
  188.3 1.1 copy-start.3
  192.2 14.1 %collective-permute-start.18 = (bf16[128,2048]{1,0:T(8,128)(2,1)}, bf16[128,2048]{1,0:T(8,128)(2,1)S(1)}, u32[]{:S(2)}, u32[]{:S(2)}) collective-permute-start(bf16[128,2048]{1,0:T(8,128)(2,1)} %get-tuple-element.64), channel_id=1, source_target_pairs={{0,2},{1,3},{2,0},{3,1},{4,6},{5,7},{6,4},{7,5},{8,10},{9,11},{10,... | collective-permute-start | bytes 1572872 | tf_op jit(solution)/shard_map/ppermute | solution.py:382
  194.3 44.7 %collective-permute-start.17 = (bf16[128,2048]{1,0:T(8,128)(2,1)}, bf16[128,2048]{1,0:T(8,128)(2,1)S(1)}, u32[]{:S(2)}, u32[]{:S(2)}) collective-permute-start(bf16[128,2048]{1,0:T(8,128)(2,1)} %after.15), channel_id=1, source_target_pairs={{0,12},{1,13},{2,14},{3,15},{12,0},{13,1},{14,2},{15,3},{16,28},{1... | collective-permute-start | bytes 1572872 | tf_op jit(solution)/shard_map/ppermute | solution.py:377
  201.9 37.1 %collective-permute-start.23 = (bf16[128,2048]{1,0:T(8,128)(2,1)S(1)}, bf16[128,2048]{1,0:T(8,128)(2,1)S(1)}, u32[]{:S(2)}, u32[]{:S(2)}) collective-permute-start(bf16[128,2048]{1,0:T(8,128)(2,1)S(1)} %add_convert_fusion.1), channel_id=1, source_target_pairs={{4,0},{5,1},{6,2},{7,3},{8,12},{9,13},{10,14},{11,15},{20,16},{21,... | collective-permute-start | bytes 1572872 | tf_op jit(solution)/shard_map/ppermute | solution.py:377
  203.2 35.8 %collective-permute-start.14 = (bf16[128,2048]{1,0:T(8,128)(2,1)}, bf16[128,2048]{1,0:T(8,128)(2,1)S(1)}, u32[]{:S(2)}, u32[]{:S(2)}) collective-permute-start(bf16[128,2048]{1,0:T(8,128)(2,1)} %get-tuple-element.59), channel_id=1, source_target_pairs={{0,2},{1,3},{2,0},{3,1},{4,6},{5,7},{6,4},{7,5},{8,10},{9,11},{10,... | collective-permute-start | bytes 1572872 | tf_op jit(solution)/shard_map/ppermute | solution.py:382
  208.3 19.7 %copy-start.17 = (s32[1,1024]{1,0:T(1,128)S(1)}, s32[1,1024]{1,0:T(1,128)}, u32[]{:S(2)}) copy-start(s32[1,1024]{1,0:T(1,128)} %get-tuple-element.67) | copy-start | bytes 12292
  210.4 28.6 %collective-permute-start.21 = (bf16[128,2048]{1,0:T(8,128)(2,1)}, bf16[128,2048]{1,0:T(8,128)(2,1)S(1)}, u32[]{:S(2)}, u32[]{:S(2)}) collective-permute-start(bf16[128,2048]{1,0:T(8,128)(2,1)} %add_convert_fusion.2), channel_id=1, source_target_pairs={{4,8},{5,9},{6,10},{7,11},{8,4},{9,5},{10,6},{11,7},{20,24},{21,25... | collective-permute-start | bytes 1572872 | tf_op jit(solution)/shard_map/ppermute | solution.py:377
  211.1 27.9 %collective-permute-start.19 = (bf16[128,2048]{1,0:T(8,128)(2,1)}, bf16[128,2048]{1,0:T(8,128)(2,1)}, u32[]{:S(2)}, u32[]{:S(2)}) collective-permute-start(bf16[128,2048]{1,0:T(8,128)(2,1)} %after.17), channel_id=1, source_target_pairs={{0,4},{1,5},{2,6},{3,7},{12,8},{13,9},{14,10},{15,11},{16,20},{17,... | collective-permute-start | bytes 1572872 | tf_op jit(solution)/shard_map/ppermute | solution.py:377
  230.1 9.0 %copy-start.12 = (bf16[128,2048]{1,0:T(8,128)(2,1)S(1)}, bf16[128,2048]{1,0:T(8,128)(2,1)}, u32[]{:S(2)}) copy-start(bf16[128,2048]{1,0:T(8,128)(2,1)} %get-tuple-element.58) | copy-start | bytes 1572868

commit v14 on v10

--- a/solution.py
+++ b/solution.py
@@ -326,7 +326,7 @@
             out_specs=pl.BlockSpec((count, capacity, width), lambda i, here: (0, 0, 0)),
         ),
         out_shape=jax.ShapeDtypeStruct((count, capacity, width), BF16),
-        compiler_params=pltpu.CompilerParams(vmem_limit_bytes=60 * MIB),
+        compiler_params=pltpu.CompilerParams(vmem_limit_bytes=24 * MIB),
         cost_estimate=BRIEF,
         name="forward_rows",
     )(here, rank, gate, weight, *[rows] * count)

time: 230 us -> 230 us (level)
  Pallas kernels: 68.3 us -> 57.7 us
  local copies, waits for them, and re-layouts: 12.6 us -> 21.6 us
    pallas_call x4, Pallas kernels: 18.5 us -> 7.93 us  [forward_rows(): pl.pallas_call(functools.partial(forward_kernel, capacity, slots, turn),...]
    unnamed x41 -> x57, local copies, waits for them, and re-layouts: 8.27 us -> 17.3 us
    ppermute x12, starting transfers between devices: 9.89 us -> 12.8 us  [swapped_with(): return lax.ppermute(value, 'expert', [(i, i ^ bit) for i in range(devices)])]
  transfers between devices with their start and end apart: 27 -> 27, of which waited for: 14 -> 12; matrix products, arithmetic and copies ran while one was open for 11% -> 11% of each run, Pallas kernels for 28% -> 24%
where the time goes in v14:
time: 230 us; the launch traced here: 228 us
  waiting for transfers between devices  71.7 us (31%)
  Pallas kernels  57.7 us (25%)
  starting transfers between devices  55.5 us (24%)
  local copies, waits for them, and re-layouts  21.6 us (9%)
  other arithmetic  11.6 us (5%)
  matrix products  9.3 us (4%)
    ppermute x12, waiting for transfers between devices, swapped_with(): return lax.ppermute(value, 'expert', [(i, i ^ bit) for i in range(devices)])  40.4 us
    ppermute x12, starting transfers between devices, passed(): lax.ppermute(value, 'expert', [(a * 4 + lane, b * 4 + lane) for a, b in p...  24.9 us
    ppermute x12, waiting for transfers between devices, passed(): lax.ppermute(value, 'expert', [(a * 4 + lane, b * 4 + lane) for a, b in p...  23.6 us
    unnamed x57, local copies, waits for them, and re-layouts  17.3 us
    pallas_call x2, Pallas kernels, scaled_rows(): pl.pallas_call(functools.partial(scale_kernel, capacity, slots, len(buffe...  13.6 us
    ppermute x12, starting transfers between devices, swapped_with(): return lax.ppermute(value, 'expert', [(i, i ^ bit) for i in range(devices)])  12.8 us
    pallas_call x4, Pallas kernels, summed(): pl.pallas_call(functools.partial(sum_kernel, capacity, slots, turn), grid...  11.4 us
    pallas_call x2, Pallas kernels, sibling_rows(): pl.pallas_call(functools.partial(sibling_kernel, capacity, slots), in_spe...  10.5 us
  transfers between devices with their start and end apart: 27, of which 12 were waited for; matrix products, arithmetic and copies ran while one was open for 11% of the time, Pallas kernels for 24%

profile of v14, /device:TPU:0, one launch (start us, length us, event | category | flops | bytes accessed | tf_op | source)
XLA Modules:
  0.0 228.4 jit_solution(2677562223881274561)
XLA Ops:
  0.6 5.0 %collective-permute-start = (bf16[128,2048]{1,0:T(8,128)(2,1)}, bf16[128,2048]{1,0:T(8,128)(2,1)S(1)}, u32[]{:S(2)}, u32[]{:S(2)}) collective-permute-start(bf16[128,2048]{1,0:T(8,128)(2,1)} %refs_0_.1), channel_id=1, source_target_pairs={{0,4},{1,5},{2,6},{3,7},{12,8},{13,9},{14,10},{15,11},{16,20},{17,... | collective-permute-start | bytes 1572872 | tf_op jit(solution)/shard_map/ppermute | solution.py:376
  6.3 1.3 collective-permute-start.2
  7.6 1.6 collective-permute-start.3
  9.9 7.2 %collective-permute-done = bf16[128,2048]{1,0:T(8,128)(2,1)S(1)} collective-permute-done((bf16[128,2048]{1,0:T(8,128)(2,1)}, bf16[128,2048]{1,0:T(8,128)(2,1)S(1)}, u32[]{:S(2)}, u32[]{:S(2)}) %collective-permute-start) | collective-permute-done | bytes 524320 | tf_op jit(solution)/shard_map/ppermute | solution.py:376
  17.9 3.9 %collective-permute-done.2 = bf16[128,2048]{1,0:T(8,128)(2,1)S(1)} collective-permute-done((bf16[128,2048]{1,0:T(8,128)(2,1)}, bf16[128,2048]{1,0:T(8,128)(2,1)S(1)}, u32[]{:S(2)}, u32[]{:S(2)}) %collective-permute-start.2) | collective-permute-done | bytes 524320 | tf_op jit(solution)/shard_map/ppermute | solution.py:376
  21.8 1.0 add_convert_fusion.6.refs_2_
  24.3 1.3 collective-permute-start.5
  25.7 1.6 collective-permute-start.6
  28.1 5.6 %pack.1 = (s32[1,1024]{1,0:T(1,128)}, bf16[1536,768]{1,0:T(8,128)(2,1)}) custom-call(s32[1,1024]{1,0:T(1,128)} %reshape.76.ids_ref, bf16[1024,768]{1,0:T(8,128)(2,1)} %bitcast.46), custom_call_target="tpu_custom_call" | custom-call | tf_op jit(solution)/shard_map/pack/pallas_call | solution.py:92
  33.7 5.9 %collective-permute-done.5 = bf16[128,2048]{1,0:T(8,128)(2,1)S(1)} collective-permute-done((bf16[128,2048]{1,0:T(8,128)(2,1)}, bf16[128,2048]{1,0:T(8,128)(2,1)S(1)}, u32[]{:S(2)}, u32[]{:S(2)}) %collective-permute-start.5) | collective-permute-done | bytes 524320 | tf_op jit(solution)/shard_map/ppermute | solution.py:376
  39.6 0.9 add_convert_fusion.5.refs_1_
  41.4 1.3 collective-permute-start.7
  42.7 5.3 %all-to-all-start = ((f32[16,16,128]{2,1,0:T(8,128)}), f32[16,16,128]{2,1,0:T(8,128)S(1)}, u32[]{:S(2)}, u32[]{:S(2)}) async-start(f32[16,16,128]{2,1,0:T(8,128)} %get-tuple-element.41), calls=%async_computation | async-start | bytes 262144 | tf_op jit(solution)/shard_map/all_to_all | solution.py:431
  48.0 1.9 collective-permute-start.8
  49.9 7.7 %all-to-all-done.routing_ref = f32[16,16,128]{2,1,0:T(8,128)S(1)} async-done(((f32[16,16,128]{2,1,0:T(8,128)}), f32[16,16,128]{2,1,0:T(8,128)S(1)}, u32[]{:S(2)}, u32[]{:S(2)}) %all-to-all-start) | async-done | bytes 131104 | tf_op jit(solution)/shard_map/all_to_all | solution.py:431
  58.3 1.7 route.1
  60.0 0.9 add_convert_fusion.4.refs_1_
  60.9 2.9 %collective-permute-done.8.refs_2_.refs_1_ = bf16[128,2048]{1,0:T(8,128)(2,1)S(1)} collective-permute-done((bf16[128,2048]{1,0:T(8,128)(2,1)}, bf16[128,2048]{1,0:T(8,128)(2,1)S(1)}, u32[]{:S(2)}, u32[]{:S(2)}) %collective-permute-start.8) | collective-permute-done | bytes 524320 | tf_op jit(solution)/shard_map/ppermute | solution.py:381
  64.6 5.1 %all-to-all-start.1 = ((bf16[16,96,768]{2,1,0:T(8,128)(2,1)}), bf16[16,96,768]{2,1,0:T(8,128)(2,1)S(1)}, u32[]{:S(2)}, u32[]{:S(2)}) async-start(bf16[16,96,768]{2,1,0:T(8,128)(2,1)} %bitcast.45), calls=%async_computation.1 | async-start | bytes 4718592 | tf_op jit(solution)/shard_map/all_to_all | solution.py:434
  69.7 6.9 %scaled_rows.2 = (bf16[16,96,2048]{2,1,0:T(8,128)(2,1)}, bf16[16,96,768]{2,1,0:T(8,128)(2,1)}, bf16[4,96,2048]{2,1,0:T(8,128)(2,1)}) custom-call(s32[1]{0:T(128)} %bitcast.here_ref, s32[2,16,128]{2,1,0:T(8,128)} %get-tuple-element.42.refs_3_.rank_ref, f32[2,16,128]{2,1,0:T(8,128)} %get-tuple-element.43.gate_ref, bf16[768,2048]{1,0:T(8,128)(2,1)} %bitcast.37, ...), custom_call_target="tpu_custom_call" | custom-call | tf_op jit(solution)/shard_map/scaled_rows/pallas_call | solution.py:239
  77.0 1.7 collective-permute-start.9
  78.7 1.7 collective-permute-done.10.rows_ref
  80.4 5.3 %sibling_rows.2 = (bf16[16,96,2048]{2,1,0:T(8,128)(2,1)}, bf16[16,96,768]{2,1,0:T(8,128)(2,1)}, f32[8,128]{1,0:T(8,128)}) custom-call(s32[1]{0:T(128)} %bitcast.here_ref, bf16[768,2048]{1,0:T(8,128)(2,1)} %bitcast.38, bf16[4,96,2048]{2,1,0:T(8,128)(2,1)} %collective-permute-done.10.rows_ref, ...), custom_call_target="tpu_custom_call", output_to_operand_aliasing={{0}: (3, {}), {1}: (4, {})} | custom-call | tf_op jit(solution)/shard_map/sibling_rows/pallas_call | solution.py:278
  85.7 18.4 %collective-permute-done.9.refs_3_ = bf16[128,2048]{1,0:T(8,128)(2,1)S(1)} collective-permute-done((bf16[128,2048]{1,0:T(8,128)(2,1)S(1)}, bf16[128,2048]{1,0:T(8,128)(2,1)S(1)}, u32[]{:S(2)}, u32[]{:S(2)}) %collective-permute-start.9) | collective-permute-done | bytes 524320 | tf_op jit(solution)/shard_map/ppermute | solution.py:381
  104.9 6.8 %scaled_rows.3 = (bf16[16,96,2048]{2,1,0:T(8,128)(2,1)}, bf16[16,96,768]{2,1,0:T(8,128)(2,1)}, bf16[4,96,2048]{2,1,0:T(8,128)(2,1)}) custom-call(s32[1]{0:T(128)} %bitcast.here_ref, s32[2,16,128]{2,1,0:T(8,128)} %get-tuple-element.42.refs_3_.rank_ref, f32[2,16,128]{2,1,0:T(8,128)} %get-tuple-element.43.gate_ref, ...), custom_call_target="tpu_custom_call", output_to_operand_aliasing={{0}: (8, {}), {1}: (9, {})} | custom-call | tf_op jit(solution)/shard_map/scaled_rows/pallas_call | solution.py:239
  111.7 3.7 %collective-permute-done.11.rows_ref = bf16[4,96,2048]{2,1,0:T(8,128)(2,1)} collective-permute-done((bf16[4,96,2048]{2,1,0:T(8,128)(2,1)}, bf16[4,96,2048]{2,1,0:T(8,128)(2,1)}, u32[]{:S(2)}, u32[]{:S(2)}) %collective-permute-start.11) | collective-permute-done | bytes 1572896 | tf_op jit(solution)/shard_map/ppermute | solution.py:381
  115.5 5.3 %sibling_rows.3 = (bf16[16,96,2048]{2,1,0:T(8,128)(2,1)}, bf16[16,96,768]{2,1,0:T(8,128)(2,1)}, f32[8,128]{1,0:T(8,128)}) custom-call(s32[1]{0:T(128)} %bitcast.here_ref, bf16[768,2048]{1,0:T(8,128)(2,1)} %bitcast.40, bf16[4,96,2048]{2,1,0:T(8,128)(2,1)} %collective-permute-done.11.rows_ref, ...), custom_call_target="tpu_custom_call", output_to_operand_aliasing={{0}: (3, {}), {1}: (4, {})} | custom-call | tf_op jit(solution)/shard_map/sibling_rows/pallas_call | solution.py:278
  120.8 1.4 copy-done.1
  122.9 1.7 copy-done.2
  124.6 1.9 copy-done.4
  126.5 2.6 %forward_rows.7 = bf16[4,96,2048]{2,1,0:T(8,128)(2,1)} custom-call(s32[1]{0:T(128)} %bitcast.here_ref, s32[2,16,128]{2,1,0:T(8,128)S(1)} %copy-done.9, f32[2,16,128]{2,1,0:T(8,128)S(1)} %copy-done.11, bf16[768,2048]{1,0:T(8,128)(2,1)S(1)} %bitcast.41, bf16[8,2,96,768]{3,2,1,0:T(8,128)(2,1)S(1)} %bitcast.21, bf16[8,2,96,768]{3,2,1,0:T(8,128)(2,1)S(1)} %bitcast.22, ...), custom_call_target="tpu_custom_call" | custom-call | tf_op jit(solution)/shard_map/forward_rows/pallas_call | solution.py:319
  129.2 7.3 %all-to-all-start.2 = ((bf16[16,96,768]{2,1,0:T(8,128)(2,1)}), bf16[16,96,768]{2,1,0:T(8,128)(2,1)}, u32[]{:S(2)}, u32[]{:S(2)}) async-start(bf16[16,96,768]{2,1,0:T(8,128)(2,1)} %get-tuple-element.66), calls=%async_computation.2 | async-start | bytes 4718592 | tf_op jit(solution)/shard_map/all_to_all | solution.py:447
  136.5 1.9 copy-done.5
  138.4 2.6 %forward_rows.5 = bf16[4,96,2048]{2,1,0:T(8,128)(2,1)} custom-call(s32[1]{0:T(128)} %bitcast.here_ref, s32[2,16,128]{2,1,0:T(8,128)S(1)} %copy-done.9, f32[2,16,128]{2,1,0:T(8,128)S(1)} %copy-done.11, bf16[768,2048]{1,0:T(8,128)(2,1)S(1)} %bitcast.42, bf16[8,2,96,768]{3,2,1,0:T(8,128)(2,1)S(1)} %bitcast.25, bf16[8,2,96,768]{3,2,1,0:T(8,128)(2,1)S(1)} %bitcast.26, ...), custom_call_target="tpu_custom_call" | custom-call | tf_op jit(solution)/shard_map/forward_rows/pallas_call | solution.py:319
  140.9 1.4 forward_rows.6.own_ref
  142.4 1.1 copy-done.8
  143.9 2.8 %summed.7 = (bf16[128,2048]{1,0:T(8,128)(2,1)}, bf16[128,2048]{1,0:T(8,128)(2,1)}) custom-call(s32[1]{0:T(128)} %bitcast.here_ref, s32[2,16,128]{2,1,0:T(8,128)} %get-tuple-element.42.refs_3_.rank_ref, bf16[4,96,2048]{2,1,0:T(8,128)(2,1)} %copy-done.8, bf16[4,96,2048]{2,1,0:T(8,128)(2,1)} %collective-permute-done.15.other_ref), custom_call_target="tpu_custom_call" | custom-call | tf_op jit(solution)/shard_map/summed/pallas_call | solution.py:353
  146.7 1.7 collective-permute-start.17
  148.3 9.3 %fusion.refs_1_ = bf16[1,768,2048]{2,1,0:T(8,128)(2,1)} fusion(bf16[16,96,768]{2,1,0:T(8,128)(2,1)S(1)} %copy-done.3, bf16[16,96,2048]{2,1,0:T(8,128)(2,1)} %get-tuple-element.64), kind=kOutput, calls=%fused_computation.2 | convolution fusion | flops 4833411072 | bytes 11796480 | tf_op jit(solution)/shard_map/dot_general | solution.py:456
  158.0 2.8 %summed.6 = (bf16[128,2048]{1,0:T(8,128)(2,1)}, bf16[128,2048]{1,0:T(8,128)(2,1)}) custom-call(s32[1]{0:T(128)} %bitcast.here_ref, s32[2,16,128]{2,1,0:T(8,128)} %get-tuple-element.42.refs_3_.rank_ref, bf16[4,96,2048]{2,1,0:T(8,128)(2,1)} %copy-done.8, bf16[4,96,2048]{2,1,0:T(8,128)(2,1)} %collective-permute-done.15.other_ref), custom_call_target="tpu_custom_call" | custom-call | tf_op jit(solution)/shard_map/summed/pallas_call | solution.py:353
  160.8 12.3 %collective-permute-done.17 = bf16[128,2048]{1,0:T(8,128)(2,1)S(1)} collective-permute-done((bf16[128,2048]{1,0:T(8,128)(2,1)}, bf16[128,2048]{1,0:T(8,128)(2,1)S(1)}, u32[]{:S(2)}, u32[]{:S(2)}) %collective-permute-start.17) | collective-permute-done | bytes 524320 | tf_op jit(solution)/shard_map/ppermute | solution.py:381
  173.1 1.2 fusion.1
  174.3 2.1 collective-permute-start.18
  176.4 1.9 copy-done.6
  178.3 1.4 forward_rows.4.own_ref
  179.8 1.1 copy-done.7
  180.9 2.9 %summed.5 = (bf16[128,2048]{1,0:T(8,128)(2,1)}, bf16[128,2048]{1,0:T(8,128)(2,1)}) custom-call(s32[1]{0:T(128)} %bitcast.here_ref, s32[2,16,128]{2,1,0:T(8,128)} %get-tuple-element.42.refs_3_.rank_ref, bf16[4,96,2048]{2,1,0:T(8,128)(2,1)} %copy-done.7, bf16[4,96,2048]{2,1,0:T(8,128)(2,1)} %collective-permute-done.12.other_ref), custom_call_target="tpu_custom_call" | custom-call | tf_op jit(solution)/shard_map/summed/pallas_call | solution.py:353
  183.8 2.4 %collective-permute-start.14 = (bf16[128,2048]{1,0:T(8,128)(2,1)}, bf16[128,2048]{1,0:T(8,128)(2,1)S(1)}, u32[]{:S(2)}, u32[]{:S(2)}) collective-permute-start(bf16[128,2048]{1,0:T(8,128)(2,1)} %get-tuple-element.60), channel_id=1, source_target_pairs={{0,2},{1,3},{2,0},{3,1},{4,6},{5,7},{6,4},{7,5},{8,10},{9,11},{10,... | collective-permute-start | bytes 1572872 | tf_op jit(solution)/shard_map/ppermute | solution.py:381
  186.2 1.4 collective-permute-done.16
  188.4 1.5 add_convert_fusion.3
  189.9 4.6 %collective-permute-start.19 = (bf16[128,2048]{1,0:T(8,128)(2,1)S(1)}, bf16[128,2048]{1,0:T(8,128)(2,1)S(1)}, u32[]{:S(2)}, u32[]{:S(2)}) collective-permute-start(bf16[128,2048]{1,0:T(8,128)(2,1)S(1)} %add_convert_fusion.3), channel_id=1, source_target_pairs={{0,4},{1,5},{2,6},{3,7},{12,8},{13,9},{14,10},{15,11},{16,20},{17,... | collective-permute-start | bytes 1572872 | tf_op jit(solution)/shard_map/ppermute | solution.py:376
  194.5 1.5 collective-permute-start.22
  196.6 2.8 %summed.4 = (bf16[128,2048]{1,0:T(8,128)(2,1)}, bf16[128,2048]{1,0:T(8,128)(2,1)}) custom-call(s32[1]{0:T(128)} %bitcast.here_ref, s32[2,16,128]{2,1,0:T(8,128)} %get-tuple-element.42.refs_3_.rank_ref, bf16[4,96,2048]{2,1,0:T(8,128)(2,1)} %copy-done.7, bf16[4,96,2048]{2,1,0:T(8,128)(2,1)} %collective-permute-done.12.other_ref), custom_call_target="tpu_custom_call" | custom-call | tf_op jit(solution)/shard_map/summed/pallas_call | solution.py:353
  199.5 3.7 %collective-permute-done.19 = bf16[128,2048]{1,0:T(8,128)(2,1)S(1)} collective-permute-done((bf16[128,2048]{1,0:T(8,128)(2,1)S(1)}, bf16[128,2048]{1,0:T(8,128)(2,1)S(1)}, u32[]{:S(2)}, u32[]{:S(2)}) %collective-permute-start.19) | collective-permute-done | bytes 524320 | tf_op jit(solution)/shard_map/ppermute | solution.py:376
  203.2 2.2 add_convert_fusion.2.refs_0_
  205.3 4.5 %collective-permute-start.20 = (bf16[128,2048]{1,0:T(8,128)(2,1)}, bf16[128,2048]{1,0:T(8,128)(2,1)S(1)}, u32[]{:S(2)}, u32[]{:S(2)}) collective-permute-start(bf16[128,2048]{1,0:T(8,128)(2,1)} %after.11), channel_id=1, source_target_pairs={{0,4},{1,5},{2,6},{3,7},{12,8},{13,9},{14,10},{15,11},{16,20},{17,... | collective-permute-start | bytes 1572872 | tf_op jit(solution)/shard_map/ppermute | solution.py:376
  210.6 1.3 add_convert_fusion.1
  211.9 1.3 collective-permute-start.23
  213.3 1.0 copy.39.place_ref
  214.3 1.0 reshape.94.gate_ref
  215.3 6.9 %unpack.1 = (bf16[1024,768]{1,0:T(8,128)(2,1)}, f32[1024,1]{1,0:T(8,128)}) custom-call(s32[1024,1]{1,0:T(8,128)} %copy.39.place_ref, f32[1024,1]{1,0:T(8,128)} %reshape.94.gate_ref, bf16[1024,768]{1,0:T(8,128)(2,1)} %bitcast.47, bf16[1536,768]{1,0:T(8,128)(2,1)} %bitcast.10.refs_1_.back_ref), custom_call_target="tpu_custom_call" | custom-call | tf_op jit(solution)/shard_map/unpack/pallas_call | solution.py:126
  222.2 1.2 reduce
  224.3 2.9 %collective-permute-done.23 = bf16[128,2048]{1,0:T(8,128)(2,1)S(1)} collective-permute-done((bf16[128,2048]{1,0:T(8,128)(2,1)S(1)}, bf16[128,2048]{1,0:T(8,128)(2,1)S(1)}, u32[]{:S(2)}, u32[]{:S(2)}) %collective-permute-start.23) | collective-permute-done | bytes 524320 | tf_op jit(solution)/shard_map/ppermute | solution.py:376
  227.2 1.2 add_convert_fusion
  (91 shorter events, 12.9 us)
Async XLA Ops:
  0.6 8.6 %copy-start = (s32[8]{0:T(128)S(1)}, s32[8]{0:T(128)}, u32[]{:S(2)}) copy-start(s32[8]{0:T(128)} %param.11) | copy-start | bytes 100
  0.6 16.4 %collective-permute-start = (bf16[128,2048]{1,0:T(8,128)(2,1)}, bf16[128,2048]{1,0:T(8,128)(2,1)S(1)}, u32[]{:S(2)}, u32[]{:S(2)}) collective-permute-start(bf16[128,2048]{1,0:T(8,128)(2,1)} %refs_0_.1), channel_id=1, source_target_pairs={{0,4},{1,5},{2,6},{3,7},{12,8},{13,9},{14,10},{15,11},{16,20},{17,... | collective-permute-start | bytes 1572872 | tf_op jit(solution)/shard_map/ppermute | solution.py:376
  5.6 12.2 %collective-permute-start.1 = (bf16[128,2048]{1,0:T(8,128)(2,1)}, bf16[128,2048]{1,0:T(8,128)(2,1)S(1)}, u32[]{:S(2)}, u32[]{:S(2)}) collective-permute-start(bf16[128,2048]{1,0:T(8,128)(2,1)} %refs_0_.1), channel_id=1, source_target_pairs={{4,8},{5,9},{6,10},{7,11},{8,4},{9,5},{10,6},{11,7},{20,24},{21,25... | collective-permute-start | bytes 1572872 | tf_op jit(solution)/shard_map/ppermute | solution.py:376
  6.3 15.5 %collective-permute-start.2 = (bf16[128,2048]{1,0:T(8,128)(2,1)}, bf16[128,2048]{1,0:T(8,128)(2,1)S(1)}, u32[]{:S(2)}, u32[]{:S(2)}) collective-permute-start(bf16[128,2048]{1,0:T(8,128)(2,1)} %refs_0_.1), channel_id=1, source_target_pairs={{4,0},{5,1},{6,2},{7,3},{8,12},{9,13},{10,14},{11,15},{20,16},{21,... | collective-permute-start | bytes 1572872 | tf_op jit(solution)/shard_map/ppermute | solution.py:376
  7.6 15.2 %collective-permute-start.3 = (bf16[128,2048]{1,0:T(8,128)(2,1)}, bf16[128,2048]{1,0:T(8,128)(2,1)S(1)}, u32[]{:S(2)}, u32[]{:S(2)}) collective-permute-start(bf16[128,2048]{1,0:T(8,128)(2,1)} %refs_0_.1), channel_id=1, source_target_pairs={{0,2},{1,3},{2,0},{3,1},{4,6},{5,7},{6,4},{7,5},{8,10},{9,11},{10,... | collective-permute-start | bytes 1572872 | tf_op jit(solution)/shard_map/ppermute | solution.py:381
  9.9 15.7 %copy-start.26 = (s32[128,8]{0,1:T(8,128)S(1)}, s32[128,8]{0,1:T(8,128)}, u32[]{:S(2)}) copy-start(s32[128,8]{0,1:T(8,128)} %param.8) | copy-start | bytes 12292
  9.9 17.4 %copy-start.24 = (f32[128,8]{0,1:T(8,128)S(1)}, f32[128,8]{0,1:T(8,128)}, u32[]{:S(2)}) copy-start(f32[128,8]{0,1:T(8,128)} %param.7) | copy-start | bytes 12292
  17.9 4.9 %copy-start.15 = (bf16[128,2048]{1,0:T(8,128)(2,1)}, bf16[128,2048]{1,0:T(8,128)(2,1)S(1)}, u32[]{:S(2)}) copy-start(bf16[128,2048]{1,0:T(8,128)(2,1)S(1)} %collective-permute-done.1.refs_1_) | copy-start | bytes 1572868
  22.8 0.8 copy-start.17
  23.6 10.1 %collective-permute-start.4 = (bf16[128,2048]{1,0:T(8,128)(2,1)}, bf16[128,2048]{1,0:T(8,128)(2,1)S(1)}, u32[]{:S(2)}, u32[]{:S(2)}) collective-permute-start(bf16[128,2048]{1,0:T(8,128)(2,1)} %get-tuple-element.37), channel_id=1, source_target_pairs={{4,8},{5,9},{6,10},{7,11},{8,4},{9,5},{10,6},{11,7},{20,24},{21,25... | collective-permute-start | bytes 1572872 | tf_op jit(solution)/shard_map/ppermute | solution.py:376
  24.3 15.3 %collective-permute-start.5 = (bf16[128,2048]{1,0:T(8,128)(2,1)}, bf16[128,2048]{1,0:T(8,128)(2,1)S(1)}, u32[]{:S(2)}, u32[]{:S(2)}) collective-permute-start(bf16[128,2048]{1,0:T(8,128)(2,1)} %get-tuple-element.38), channel_id=1, source_target_pairs={{4,0},{5,1},{6,2},{7,3},{8,12},{9,13},{10,14},{11,15},{20,16},{21,... | collective-permute-start | bytes 1572872 | tf_op jit(solution)/shard_map/ppermute | solution.py:376
  25.7 14.8 %collective-permute-start.6 = (bf16[128,2048]{1,0:T(8,128)(2,1)}, bf16[128,2048]{1,0:T(8,128)(2,1)S(1)}, u32[]{:S(2)}, u32[]{:S(2)}) collective-permute-start(bf16[128,2048]{1,0:T(8,128)(2,1)} %get-tuple-element.39.refs_2_), channel_id=1, source_target_pairs={{0,2},{1,3},{2,0},{3,1},{4,6},{5,7},{6,4},{7,5},{8,10},{9,11},{10,... | collective-permute-start | bytes 1572872 | tf_op jit(solution)/shard_map/ppermute | solution.py:381
  33.7 7.5 %copy-start.16 = (bf16[128,2048]{1,0:T(8,128)(2,1)}, bf16[128,2048]{1,0:T(8,128)(2,1)S(1)}, u32[]{:S(2)}) copy-start(bf16[128,2048]{1,0:T(8,128)(2,1)S(1)} %collective-permute-done.4.refs_0_) | copy-start | bytes 1572868
  40.5 0.9 copy-start.18
  41.4 18.6 %collective-permute-start.7 = (bf16[128,2048]{1,0:T(8,128)(2,1)}, bf16[128,2048]{1,0:T(8,128)(2,1)S(1)}, u32[]{:S(2)}, u32[]{:S(2)}) collective-permute-start(bf16[128,2048]{1,0:T(8,128)(2,1)} %get-tuple-element.44), channel_id=1, source_target_pairs={{4,0},{5,1},{6,2},{7,3},{8,12},{9,13},{10,14},{11,15},{20,16},{21,... | collective-permute-start | bytes 1572872 | tf_op jit(solution)/shard_map/ppermute | solution.py:376
  42.7 15.0 %all-to-all-start = ((f32[16,16,128]{2,1,0:T(8,128)}), f32[16,16,128]{2,1,0:T(8,128)S(1)}, u32[]{:S(2)}, u32[]{:S(2)}) async-start(f32[16,16,128]{2,1,0:T(8,128)} %get-tuple-element.41), calls=%async_computation | async-start | bytes 262144 | tf_op jit(solution)/shard_map/all_to_all | solution.py:431
  48.0 15.8 %collective-permute-start.8 = (bf16[128,2048]{1,0:T(8,128)(2,1)}, bf16[128,2048]{1,0:T(8,128)(2,1)S(1)}, u32[]{:S(2)}, u32[]{:S(2)}) collective-permute-start(bf16[128,2048]{1,0:T(8,128)(2,1)} %get-tuple-element.45.refs_0_), channel_id=1, source_target_pairs={{0,2},{1,3},{2,0},{3,1},{4,6},{5,7},{6,4},{7,5},{8,10},{9,11},{10,... | collective-permute-start | bytes 1572872 | tf_op jit(solution)/shard_map/ppermute | solution.py:381
  57.6 0.7 copy-start.20
  63.7 0.8 copy-start.14
  64.6 56.2 %all-to-all-start.1 = ((bf16[16,96,768]{2,1,0:T(8,128)(2,1)}), bf16[16,96,768]{2,1,0:T(8,128)(2,1)S(1)}, u32[]{:S(2)}, u32[]{:S(2)}) async-start(bf16[16,96,768]{2,1,0:T(8,128)(2,1)} %bitcast.45), calls=%async_computation.1 | async-start | bytes 4718592 | tf_op jit(solution)/shard_map/all_to_all | solution.py:434
  69.7 7.3 %copy-start.12 = (bf16[128,2048]{1,0:T(8,128)(2,1)S(1)}, bf16[128,2048]{1,0:T(8,128)(2,1)}, u32[]{:S(2)}) copy-start(bf16[128,2048]{1,0:T(8,128)(2,1)} %get-tuple-element.47.refs_2_) | copy-start | bytes 1572868
  76.6 3.8 %collective-permute-start.10 = (bf16[4,96,2048]{2,1,0:T(8,128)(2,1)}, bf16[4,96,2048]{2,1,0:T(8,128)(2,1)}, u32[]{:S(2)}, u32[]{:S(2)}) collective-permute-start(bf16[4,96,2048]{2,1,0:T(8,128)(2,1)} %get-tuple-element.48), channel_id=1, source_target_pairs={{0,1},{1,0},{2,3},{3,2},{4,5},{5,4},{6,7},{7,6},{8,9},{9,8},{10,11... | collective-permute-start | bytes 4718600 | tf_op jit(solution)/shard_map/ppermute | solution.py:381
  77.0 27.1 %collective-permute-start.9 = (bf16[128,2048]{1,0:T(8,128)(2,1)S(1)}, bf16[128,2048]{1,0:T(8,128)(2,1)S(1)}, u32[]{:S(2)}, u32[]{:S(2)}) collective-permute-start(bf16[128,2048]{1,0:T(8,128)(2,1)S(1)} %copy-done.12), channel_id=1, source_target_pairs={{0,2},{1,3},{2,0},{3,1},{4,6},{5,7},{6,4},{7,5},{8,10},{9,11},{10,... | collective-permute-start | bytes 1572872 | tf_op jit(solution)/shard_map/ppermute | solution.py:381
  104.1 0.8 copy-start.19
  111.7 3.8 %collective-permute-start.11 = (bf16[4,96,2048]{2,1,0:T(8,128)(2,1)}, bf16[4,96,2048]{2,1,0:T(8,128)(2,1)}, u32[]{:S(2)}, u32[]{:S(2)}) collective-permute-start(bf16[4,96,2048]{2,1,0:T(8,128)(2,1)} %get-tuple-element.53), channel_id=1, source_target_pairs={{0,1},{1,0},{2,3},{3,2},{4,5},{5,4},{6,7},{7,6},{8,9},{9,8},{10,11... | collective-permute-start | bytes 4718600 | tf_op jit(solution)/shard_map/ppermute | solution.py:381
  120.8 1.4 copy-start.1
  122.2 0.7 copy-start.9
  122.2 0.7 copy-start.11
  122.9 1.7 copy-start.2
  124.6 1.9 copy-start.4
  129.0 14.8 %collective-permute-start.15 = (bf16[4,96,2048]{2,1,0:T(8,128)(2,1)}, bf16[4,96,2048]{2,1,0:T(8,128)(2,1)}, u32[]{:S(2)}, u32[]{:S(2)}) collective-permute-start(bf16[4,96,2048]{2,1,0:T(8,128)(2,1)} %forward_rows.7), channel_id=1, source_target_pairs={{0,1},{1,0},{2,3},{3,2},{4,5},{5,4},{6,7},{7,6},{8,9},{9,8},{10,11... | collective-permute-start | bytes 4718600 | tf_op jit(solution)/shard_map/ppermute | solution.py:381
  129.2 7.3 %copy-start.3 = (bf16[16,96,768]{2,1,0:T(8,128)(2,1)S(1)}, bf16[16,96,768]{2,1,0:T(8,128)(2,1)}, u32[]{:S(2)}) copy-start(bf16[16,96,768]{2,1,0:T(8,128)(2,1)} %after.9) | copy-start | bytes 7077892
  129.2 76.2 %all-to-all-start.2 = ((bf16[16,96,768]{2,1,0:T(8,128)(2,1)}), bf16[16,96,768]{2,1,0:T(8,128)(2,1)}, u32[]{:S(2)}, u32[]{:S(2)}) async-start(bf16[16,96,768]{2,1,0:T(8,128)(2,1)} %get-tuple-element.66), calls=%async_computation.2 | async-start | bytes 4718592 | tf_op jit(solution)/shard_map/all_to_all | solution.py:447
  136.5 1.9 copy-start.5
  142.4 1.1 copy-start.8
  143.5 37.4 %collective-permute-start.12 = (bf16[4,96,2048]{2,1,0:T(8,128)(2,1)}, bf16[4,96,2048]{2,1,0:T(8,128)(2,1)}, u32[]{:S(2)}, u32[]{:S(2)}) collective-permute-start(bf16[4,96,2048]{2,1,0:T(8,128)(2,1)} %forward_rows.5), channel_id=1, source_target_pairs={{0,1},{1,0},{2,3},{3,2},{4,5},{5,4},{6,7},{7,6},{8,9},{9,8},{10,11... | collective-permute-start | bytes 4718600 | tf_op jit(solution)/shard_map/ppermute | solution.py:381
  146.7 26.4 %collective-permute-start.17 = (bf16[128,2048]{1,0:T(8,128)(2,1)}, bf16[128,2048]{1,0:T(8,128)(2,1)S(1)}, u32[]{:S(2)}, u32[]{:S(2)}) collective-permute-start(bf16[128,2048]{1,0:T(8,128)(2,1)} %get-tuple-element.65), channel_id=1, source_target_pairs={{0,2},{1,3},{2,0},{3,1},{4,6},{5,7},{6,4},{7,5},{8,10},{9,11},{10,... | collective-permute-start | bytes 1572872 | tf_op jit(solution)/shard_map/ppermute | solution.py:381
  157.6 30.0 %collective-permute-start.16 = (bf16[128,2048]{1,0:T(8,128)(2,1)}, bf16[128,2048]{1,0:T(8,128)(2,1)S(1)}, u32[]{:S(2)}, u32[]{:S(2)}) collective-permute-start(bf16[128,2048]{1,0:T(8,128)(2,1)} %get-tuple-element.62), channel_id=1, source_target_pairs={{0,2},{1,3},{2,0},{3,1},{4,6},{5,7},{6,4},{7,5},{8,10},{9,11},{10,... | collective-permute-start | bytes 1572872 | tf_op jit(solution)/shard_map/ppermute | solution.py:381
  160.8 15.6 %copy-start.10 = (s32[2,16,128]{2,1,0:T(8,128)S(1)}, s32[2,16,128]{2,1,0:T(8,128)}, u32[]{:S(2)}) copy-start(s32[2,16,128]{2,1,0:T(8,128)} %get-tuple-element.42.refs_3_.rank_ref) | copy-start | bytes 49156
  174.3 13.3 %collective-permute-start.18 = (bf16[128,2048]{1,0:T(8,128)(2,1)S(1)}, bf16[128,2048]{1,0:T(8,128)(2,1)}, u32[]{:S(2)}, u32[]{:S(2)}) collective-permute-start(bf16[128,2048]{1,0:T(8,128)(2,1)S(1)} %fusion.1), channel_id=1, source_target_pairs={{0,4},{1,5},{2,6},{3,7},{12,8},{13,9},{14,10},{15,11},{16,20},{17,... | collective-permute-start | bytes 1572872 | tf_op jit(solution)/shard_map/ppermute | solution.py:376
  176.4 1.9 copy-start.6
  179.7 1.1 copy-start.7
  180.9 7.5 %copy-start.23 = (bf16[128,2048]{1,0:T(8,128)(2,1)S(1)}, bf16[128,2048]{1,0:T(8,128)(2,1)}, u32[]{:S(2)}) copy-start(bf16[128,2048]{1,0:T(8,128)(2,1)} %get-tuple-element.61) | copy-start | bytes 1572868
  183.8 15.7 %collective-permute-start.14 = (bf16[128,2048]{1,0:T(8,128)(2,1)}, bf16[128,2048]{1,0:T(8,128)(2,1)S(1)}, u32[]{:S(2)}, u32[]{:S(2)}) collective-permute-start(bf16[128,2048]{1,0:T(8,128)(2,1)} %get-tuple-element.60), channel_id=1, source_target_pairs={{0,2},{1,3},{2,0},{3,1},{4,6},{5,7},{6,4},{7,5},{8,10},{9,11},{10,... | collective-permute-start | bytes 1572872 | tf_op jit(solution)/shard_map/ppermute | solution.py:381
  187.6 0.8 copy-start.22
  189.9 13.3 %collective-permute-start.19 = (bf16[128,2048]{1,0:T(8,128)(2,1)S(1)}, bf16[128,2048]{1,0:T(8,128)(2,1)S(1)}, u32[]{:S(2)}, u32[]{:S(2)}) collective-permute-start(bf16[128,2048]{1,0:T(8,128)(2,1)S(1)} %add_convert_fusion.3), channel_id=1, source_target_pairs={{0,4},{1,5},{2,6},{3,7},{12,8},{13,9},{14,10},{15,11},{16,20},{17,... | collective-permute-start | bytes 1572872 | tf_op jit(solution)/shard_map/ppermute | solution.py:376
  194.5 16.1 %collective-permute-start.22 = (bf16[128,2048]{1,0:T(8,128)(2,1)S(1)}, bf16[128,2048]{1,0:T(8,128)(2,1)}, u32[]{:S(2)}, u32[]{:S(2)}) collective-permute-start(bf16[128,2048]{1,0:T(8,128)(2,1)S(1)} %add_convert_fusion.3), channel_id=1, source_target_pairs={{4,8},{5,9},{6,10},{7,11},{8,4},{9,5},{10,6},{11,7},{20,24},{21,25... | collective-permute-start | bytes 1572872 | tf_op jit(solution)/shard_map/ppermute | solution.py:376
  196.0 28.3 %collective-permute-start.13 = (bf16[128,2048]{1,0:T(8,128)(2,1)}, bf16[128,2048]{1,0:T(8,128)(2,1)S(1)}, u32[]{:S(2)}, u32[]{:S(2)}) collective-permute-start(bf16[128,2048]{1,0:T(8,128)(2,1)} %get-tuple-element.58), channel_id=1, source_target_pairs={{0,2},{1,3},{2,0},{3,1},{4,6},{5,7},{6,4},{7,5},{8,10},{9,11},{10,... | collective-permute-start | bytes 1572872 | tf_op jit(solution)/shard_map/ppermute | solution.py:381
  203.2 7.4 %copy-start.13 = (bf16[128,2048]{1,0:T(8,128)(2,1)S(1)}, bf16[128,2048]{1,0:T(8,128)(2,1)}, u32[]{:S(2)}) copy-start(bf16[128,2048]{1,0:T(8,128)(2,1)} %after.10) | copy-start | bytes 1572868
  205.3 8.0 %copy-start.25 = (s32[1,1024]{1,0:T(1,128)S(1)}, s32[1,1024]{1,0:T(1,128)}, u32[]{:S(2)}) copy-start(s32[1,1024]{1,0:T(1,128)} %get-tuple-element.67) | copy-start | bytes 12292
  205.3 18.9 %collective-permute-start.20 = (bf16[128,2048]{1,0:T(8,128)(2,1)}, bf16[128,2048]{1,0:T(8,128)(2,1)S(1)}, u32[]{:S(2)}, u32[]{:S(2)}) collective-permute-start(bf16[128,2048]{1,0:T(8,128)(2,1)} %after.11), channel_id=1, source_target_pairs={{0,4},{1,5},{2,6},{3,7},{12,8},{13,9},{14,10},{15,11},{16,20},{17,... | collective-permute-start | bytes 1572872 | tf_op jit(solution)/shard_map/ppermute | solution.py:376
  209.9 14.4 %collective-permute-start.21 = (bf16[128,2048]{1,0:T(8,128)(2,1)}, bf16[128,2048]{1,0:T(8,128)(2,1)S(1)}, u32[]{:S(2)}, u32[]{:S(2)}) collective-permute-start(bf16[128,2048]{1,0:T(8,128)(2,1)} %after.11), channel_id=1, source_target_pairs={{4,8},{5,9},{6,10},{7,11},{8,4},{9,5},{10,6},{11,7},{20,24},{21,25... | collective-permute-start | bytes 1572872 | tf_op jit(solution)/shard_map/ppermute | solution.py:376
  211.9 15.3 %collective-permute-start.23 = (bf16[128,2048]{1,0:T(8,128)(2,1)S(1)}, bf16[128,2048]{1,0:T(8,128)(2,1)S(1)}, u32[]{:S(2)}, u32[]{:S(2)}) collective-permute-start(bf16[128,2048]{1,0:T(8,128)(2,1)S(1)} %add_convert_fusion.1), channel_id=1, source_target_pairs={{4,0},{5,1},{6,2},{7,3},{8,12},{9,13},{10,14},{11,15},{20,16},{21,... | collective-permute-start | bytes 1572872 | tf_op jit(solution)/shard_map/ppermute | solution.py:376
  215.3 11.8 %copy-start.21 = (bf16[128,2048]{1,0:T(8,128)(2,1)S(1)}, bf16[128,2048]{1,0:T(8,128)(2,1)}, u32[]{:S(2)}) copy-start(bf16[128,2048]{1,0:T(8,128)(2,1)} %get-tuple-element.57) | copy-start | bytes 1572868

commit v15 on v14

--- a/solution.py
+++ b/solution.py
@@ -359,7 +359,7 @@
             out_specs=[pl.BlockSpec((tokens, width), lambda i, here: (0, 0))] * len(slots),
         ),
         out_shape=[jax.ShapeDtypeStruct((tokens, width), BF16)] * len(slots),
-        compiler_params=pltpu.CompilerParams(vmem_limit_bytes=60 * MIB),
+        compiler_params=pltpu.CompilerParams(vmem_limit_bytes=24 * MIB),
         cost_estimate=BRIEF,
         name="summed",
     )(here, rank, own, other)
@@ -398,7 +398,7 @@
         out_specs=[anywhere] * count,
         out_shape=[jax.ShapeDtypeStruct(value.shape, value.dtype) for value in values],
         input_output_aliases={i: i for i in range(count)},
-        compiler_params=pltpu.CompilerParams(vmem_limit_bytes=60 * MIB),
+        compiler_params=pltpu.CompilerParams(vmem_limit_bytes=1 * MIB),
         cost_estimate=BRIEF,
         name="after",
     )(*values, *waited)

time: 230 us -> 230 us (level)
  waiting for transfers between devices: 71.7 us -> 90.1 us
  Pallas kernels: 57.7 us -> 50.3 us
  local copies, waits for them, and re-layouts: 21.6 us -> 15.5 us
  matrix products: 9.3 us -> 5.41 us
    ppermute x12, waiting for transfers between devices: 40.4 us -> 57.9 us  [swapped_with(): return lax.ppermute(value, 'expert', [(i, i ^ bit) for i in range(devices)])]
    pallas_call x4, Pallas kernels: 11.4 us -> 5.26 us  [summed(): pl.pallas_call(functools.partial(sum_kernel, capacity, slots, turn), grid...]
    unnamed x57 -> x51, local copies, waits for them, and re-layouts: 17.3 us -> 11.3 us
    dot_general x1, matrix products: 9.3 us -> 5.41 us  [dense_shards(): lax.dot_general(rows_h.reshape(-1, hidden), z_rows.reshape(devices * capa...]
  transfers between devices with their start and end apart: 27 -> 27, of which waited for: 12 -> 13; matrix products, arithmetic and copies ran while one was open for 11% -> 8% of each run, Pallas kernels for 24% -> 21%
where the time goes in v15:
time: 230 us; the launch traced here: 229 us
  waiting for transfers between devices  90.1 us (39%)
  starting transfers between devices  56.6 us (25%)
  Pallas kernels  50.3 us (22%)
  local copies, waits for them, and re-layouts  15.5 us (7%)
  other arithmetic  9.97 us (4%)
  matrix products  5.41 us (2%)
    ppermute x12, waiting for transfers between devices, swapped_with(): return lax.ppermute(value, 'expert', [(i, i ^ bit) for i in range(devices)])  57.9 us
    ppermute x12, waiting for transfers between devices, passed(): lax.ppermute(value, 'expert', [(a * 4 + lane, b * 4 + lane) for a, b in p...  25.2 us
    ppermute x12, starting transfers between devices, passed(): lax.ppermute(value, 'expert', [(a * 4 + lane, b * 4 + lane) for a, b in p...  23.9 us
    ppermute x12, starting transfers between devices, swapped_with(): return lax.ppermute(value, 'expert', [(i, i ^ bit) for i in range(devices)])  14.8 us
    pallas_call x2, Pallas kernels, scaled_rows(): pl.pallas_call(functools.partial(scale_kernel, capacity, slots, len(buffe...  13.6 us
    unnamed x51, local copies, waits for them, and re-layouts  11.3 us
    pallas_call x2, Pallas kernels, sibling_rows(): pl.pallas_call(functools.partial(sibling_kernel, capacity, slots), in_spe...  10.6 us
    convert_element_type x8, other arithmetic, added(): return total.astype(BF16)  8.62 us
  transfers between devices with their start and end apart: 27, of which 13 were waited for; matrix products, arithmetic and copies ran while one was open for 8% of the time, Pallas kernels for 21%

profile of v15, /device:TPU:0, one launch (start us, length us, event | category | flops | bytes accessed | tf_op | source)
XLA Modules:
  0.0 229.1 jit_solution(5785895253482031518)
XLA Ops:
  0.6 5.0 %collective-permute-start = (bf16[128,2048]{1,0:T(8,128)(2,1)}, bf16[128,2048]{1,0:T(8,128)(2,1)S(1)}, u32[]{:S(2)}, u32[]{:S(2)}) collective-permute-start(bf16[128,2048]{1,0:T(8,128)(2,1)} %refs_0_.1), channel_id=1, source_target_pairs={{0,4},{1,5},{2,6},{3,7},{12,8},{13,9},{14,10},{15,11},{16,20},{17,... | collective-permute-start | bytes 1572872 | tf_op jit(solution)/shard_map/ppermute | solution.py:376
  6.3 1.3 collective-permute-start.2
  7.6 1.6 collective-permute-start.3
  9.9 7.2 %collective-permute-done = bf16[128,2048]{1,0:T(8,128)(2,1)S(1)} collective-permute-done((bf16[128,2048]{1,0:T(8,128)(2,1)}, bf16[128,2048]{1,0:T(8,128)(2,1)S(1)}, u32[]{:S(2)}, u32[]{:S(2)}) %collective-permute-start) | collective-permute-done | bytes 524320 | tf_op jit(solution)/shard_map/ppermute | solution.py:376
  17.1 0.7 copy-done.16
  17.9 4.0 %collective-permute-done.2 = bf16[128,2048]{1,0:T(8,128)(2,1)S(1)} collective-permute-done((bf16[128,2048]{1,0:T(8,128)(2,1)}, bf16[128,2048]{1,0:T(8,128)(2,1)S(1)}, u32[]{:S(2)}, u32[]{:S(2)}) %collective-permute-start.2) | collective-permute-done | bytes 524320 | tf_op jit(solution)/shard_map/ppermute | solution.py:376
  22.7 1.3 collective-permute-start.5
  24.1 1.6 collective-permute-start.6
  26.5 5.6 %pack.1 = (s32[1,1024]{1,0:T(1,128)}, bf16[1536,768]{1,0:T(8,128)(2,1)}) custom-call(s32[1,1024]{1,0:T(1,128)} %reshape.76.ids_ref, bf16[1024,768]{1,0:T(8,128)(2,1)} %bitcast.48), custom_call_target="tpu_custom_call" | custom-call | tf_op jit(solution)/shard_map/pack/pallas_call | solution.py:92
  32.1 6.6 %collective-permute-done.5 = bf16[128,2048]{1,0:T(8,128)(2,1)} collective-permute-done((bf16[128,2048]{1,0:T(8,128)(2,1)S(1)}, bf16[128,2048]{1,0:T(8,128)(2,1)}, u32[]{:S(2)}, u32[]{:S(2)}) %collective-permute-start.5) | collective-permute-done | bytes 524320 | tf_op jit(solution)/shard_map/ppermute | solution.py:376
  38.7 1.2 add_convert_fusion.5.refs_1_
  40.6 1.7 copy-done.4
  42.3 1.5 collective-permute-start.7
  43.8 5.8 %all-to-all-start = ((f32[16,16,128]{2,1,0:T(8,128)}), f32[16,16,128]{2,1,0:T(8,128)S(1)}, u32[]{:S(2)}, u32[]{:S(2)}) async-start(f32[16,16,128]{2,1,0:T(8,128)} %get-tuple-element.41), calls=%async_computation | async-start | bytes 262144 | tf_op jit(solution)/shard_map/all_to_all | solution.py:431
  49.6 1.9 collective-permute-start.8
  51.6 7.0 %all-to-all-done.routing_ref = f32[16,16,128]{2,1,0:T(8,128)S(1)} async-done(((f32[16,16,128]{2,1,0:T(8,128)}), f32[16,16,128]{2,1,0:T(8,128)S(1)}, u32[]{:S(2)}, u32[]{:S(2)}) %all-to-all-start) | async-done | bytes 131104 | tf_op jit(solution)/shard_map/all_to_all | solution.py:431
  59.3 1.7 route.1
  60.9 1.3 add_convert_fusion.4.refs_1_
  62.3 3.2 %collective-permute-done.8.refs_2_.refs_1_ = bf16[128,2048]{1,0:T(8,128)(2,1)} collective-permute-done((bf16[128,2048]{1,0:T(8,128)(2,1)S(1)}, bf16[128,2048]{1,0:T(8,128)(2,1)}, u32[]{:S(2)}, u32[]{:S(2)}) %collective-permute-start.8) | collective-permute-done | bytes 524320 | tf_op jit(solution)/shard_map/ppermute | solution.py:381
  65.5 0.7 copy-done.12
  66.2 1.4 copy-done.6
  67.6 5.0 %all-to-all-start.1 = ((bf16[16,96,768]{2,1,0:T(8,128)(2,1)}), bf16[16,96,768]{2,1,0:T(8,128)(2,1)S(1)}, u32[]{:S(2)}, u32[]{:S(2)}) async-start(bf16[16,96,768]{2,1,0:T(8,128)(2,1)} %bitcast.45), calls=%async_computation.1 | async-start | bytes 4718592 | tf_op jit(solution)/shard_map/all_to_all | solution.py:434
  72.6 6.8 %scaled_rows.2 = (bf16[16,96,2048]{2,1,0:T(8,128)(2,1)}, bf16[16,96,768]{2,1,0:T(8,128)(2,1)}, bf16[4,96,2048]{2,1,0:T(8,128)(2,1)}) custom-call(s32[1]{0:T(128)} %bitcast.here_ref, s32[2,16,128]{2,1,0:T(8,128)} %get-tuple-element.42.refs_3_.rank_ref, f32[2,16,128]{2,1,0:T(8,128)} %get-tuple-element.43.gate_ref, bf16[768,2048]{1,0:T(8,128)(2,1)} %bitcast.37, ...), custom_call_target="tpu_custom_call" | custom-call | tf_op jit(solution)/shard_map/scaled_rows/pallas_call | solution.py:239
  79.9 1.7 collective-permute-start.9
  81.6 1.7 collective-permute-done.10.rows_ref
  83.3 5.3 %sibling_rows.2 = (bf16[16,96,2048]{2,1,0:T(8,128)(2,1)}, bf16[16,96,768]{2,1,0:T(8,128)(2,1)}, f32[8,128]{1,0:T(8,128)}) custom-call(s32[1]{0:T(128)} %bitcast.here_ref, bf16[768,2048]{1,0:T(8,128)(2,1)} %bitcast.38, bf16[4,96,2048]{2,1,0:T(8,128)(2,1)} %collective-permute-done.10.rows_ref, ...), custom_call_target="tpu_custom_call", output_to_operand_aliasing={{0}: (3, {}), {1}: (4, {})} | custom-call | tf_op jit(solution)/shard_map/sibling_rows/pallas_call | solution.py:278
  88.6 18.5 %collective-permute-done.9.refs_3_ = bf16[128,2048]{1,0:T(8,128)(2,1)S(1)} collective-permute-done((bf16[128,2048]{1,0:T(8,128)(2,1)S(1)}, bf16[128,2048]{1,0:T(8,128)(2,1)S(1)}, u32[]{:S(2)}, u32[]{:S(2)}) %collective-permute-start.9) | collective-permute-done | bytes 524320 | tf_op jit(solution)/shard_map/ppermute | solution.py:381
  107.0 0.8 copy-done.17
  107.8 6.8 %scaled_rows.3 = (bf16[16,96,2048]{2,1,0:T(8,128)(2,1)}, bf16[16,96,768]{2,1,0:T(8,128)(2,1)}, bf16[4,96,2048]{2,1,0:T(8,128)(2,1)}) custom-call(s32[1]{0:T(128)} %bitcast.here_ref, s32[2,16,128]{2,1,0:T(8,128)} %get-tuple-element.42.refs_3_.rank_ref, f32[2,16,128]{2,1,0:T(8,128)} %get-tuple-element.43.gate_ref, ...), custom_call_target="tpu_custom_call", output_to_operand_aliasing={{0}: (8, {}), {1}: (9, {})} | custom-call | tf_op jit(solution)/shard_map/scaled_rows/pallas_call | solution.py:239
  114.7 3.7 %collective-permute-done.11.rows_ref = bf16[4,96,2048]{2,1,0:T(8,128)(2,1)} collective-permute-done((bf16[4,96,2048]{2,1,0:T(8,128)(2,1)}, bf16[4,96,2048]{2,1,0:T(8,128)(2,1)}, u32[]{:S(2)}, u32[]{:S(2)}) %collective-permute-start.11) | collective-permute-done | bytes 1572896 | tf_op jit(solution)/shard_map/ppermute | solution.py:381
  118.5 5.3 %sibling_rows.3 = (bf16[16,96,2048]{2,1,0:T(8,128)(2,1)}, bf16[16,96,768]{2,1,0:T(8,128)(2,1)}, f32[8,128]{1,0:T(8,128)}) custom-call(s32[1]{0:T(128)} %bitcast.here_ref, bf16[768,2048]{1,0:T(8,128)(2,1)} %bitcast.40, bf16[4,96,2048]{2,1,0:T(8,128)(2,1)} %collective-permute-done.11.rows_ref, ...), custom_call_target="tpu_custom_call", output_to_operand_aliasing={{0}: (3, {}), {1}: (4, {})} | custom-call | tf_op jit(solution)/shard_map/sibling_rows/pallas_call | solution.py:278
  124.5 1.9 copy-done.1
  126.4 2.5 %forward_rows.7 = bf16[4,96,2048]{2,1,0:T(8,128)(2,1)} custom-call(s32[1]{0:T(128)} %bitcast.here_ref, s32[2,16,128]{2,1,0:T(8,128)S(1)} %copy-done.13, f32[2,16,128]{2,1,0:T(8,128)S(1)} %copy-done.14, bf16[768,2048]{1,0:T(8,128)(2,1)S(1)} %bitcast.41, bf16[8,2,96,768]{3,2,1,0:T(8,128)(2,1)S(1)} %bitcast.21, bf16[8,2,96,768]{3,2,1,0:T(8,128)(2,1)S(1)} %bitcast.22, ...), custom_call_target="tpu_custom_call" | custom-call | tf_op jit(solution)/shard_map/forward_rows/pallas_call | solution.py:319
  129.0 7.1 %all-to-all-start.2 = ((bf16[16,96,768]{2,1,0:T(8,128)(2,1)}), bf16[16,96,768]{2,1,0:T(8,128)(2,1)}, u32[]{:S(2)}, u32[]{:S(2)}) async-start(bf16[16,96,768]{2,1,0:T(8,128)(2,1)} %get-tuple-element.66), calls=%async_computation.2 | async-start | bytes 4718592 | tf_op jit(solution)/shard_map/all_to_all | solution.py:447
  136.2 1.9 copy-done.2
  138.1 1.4 forward_rows.5
  139.5 1.4 forward_rows.6.own_ref
  141.3 1.7 summed.7
  143.1 1.7 collective-permute-start.17
  144.8 5.4 %fusion.refs_1_ = bf16[1,768,2048]{2,1,0:T(8,128)(2,1)S(1)} fusion(bf16[16,96,768]{2,1,0:T(8,128)(2,1)S(1)} %after.9, bf16[16,96,2048]{2,1,0:T(8,128)(2,1)S(1)} %bitcast.47), kind=kOutput, calls=%fused_computation.2 | convolution fusion | flops 4833411072 | bytes 11796480 | tf_op jit(solution)/shard_map/dot_general | solution.py:456
  150.7 2.1 summed.6
  152.8 17.7 %collective-permute-done.17 = bf16[128,2048]{1,0:T(8,128)(2,1)S(1)} collective-permute-done((bf16[128,2048]{1,0:T(8,128)(2,1)S(1)}, bf16[128,2048]{1,0:T(8,128)(2,1)S(1)}, u32[]{:S(2)}, u32[]{:S(2)}) %collective-permute-start.17) | collective-permute-done | bytes 524320 | tf_op jit(solution)/shard_map/ppermute | solution.py:381
  170.6 1.3 collective-permute-start.18
  172.0 1.4 forward_rows.4.own_ref
  173.4 0.7 summed.5
  174.1 2.6 %collective-permute-start.14 = (bf16[128,2048]{1,0:T(8,128)(2,1)S(1)}, bf16[128,2048]{1,0:T(8,128)(2,1)S(1)}, u32[]{:S(2)}, u32[]{:S(2)}) collective-permute-start(bf16[128,2048]{1,0:T(8,128)(2,1)S(1)} %get-tuple-element.60), channel_id=1, source_target_pairs={{0,2},{1,3},{2,0},{3,1},{4,6},{5,7},{6,4},{7,5},{8,10},{9,11},{10,... | collective-permute-start | bytes 1572872 | tf_op jit(solution)/shard_map/ppermute | solution.py:381
  176.7 10.8 %collective-permute-done.16 = bf16[128,2048]{1,0:T(8,128)(2,1)S(1)} collective-permute-done((bf16[128,2048]{1,0:T(8,128)(2,1)S(1)}, bf16[128,2048]{1,0:T(8,128)(2,1)S(1)}, u32[]{:S(2)}, u32[]{:S(2)}) %collective-permute-start.16) | collective-permute-done | bytes 524320 | tf_op jit(solution)/shard_map/ppermute | solution.py:381
  187.5 1.0 add_convert_fusion.3
  188.5 3.5 %collective-permute-start.19 = (bf16[128,2048]{1,0:T(8,128)(2,1)}, bf16[128,2048]{1,0:T(8,128)(2,1)S(1)}, u32[]{:S(2)}, u32[]{:S(2)}) collective-permute-start(bf16[128,2048]{1,0:T(8,128)(2,1)} %add_convert_fusion.3), channel_id=1, source_target_pairs={{0,4},{1,5},{2,6},{3,7},{12,8},{13,9},{14,10},{15,11},{16,20},{17,... | collective-permute-start | bytes 1572872 | tf_op jit(solution)/shard_map/ppermute | solution.py:376
  192.0 1.5 collective-permute-start.22
  193.5 2.3 collective-permute-start.13
  195.8 0.7 summed.4
  196.5 2.2 collective-permute-done.14
  198.7 4.9 %collective-permute-done.19 = bf16[128,2048]{1,0:T(8,128)(2,1)S(1)} collective-permute-done((bf16[128,2048]{1,0:T(8,128)(2,1)}, bf16[128,2048]{1,0:T(8,128)(2,1)S(1)}, u32[]{:S(2)}, u32[]{:S(2)}) %collective-permute-start.19) | collective-permute-done | bytes 524320 | tf_op jit(solution)/shard_map/ppermute | solution.py:376
  203.9 4.3 %collective-permute-start.20 = (bf16[128,2048]{1,0:T(8,128)(2,1)S(1)}, bf16[128,2048]{1,0:T(8,128)(2,1)S(1)}, u32[]{:S(2)}, u32[]{:S(2)}) collective-permute-start(bf16[128,2048]{1,0:T(8,128)(2,1)S(1)} %after.11), channel_id=1, source_target_pairs={{0,4},{1,5},{2,6},{3,7},{12,8},{13,9},{14,10},{15,11},{16,20},{17,... | collective-permute-start | bytes 1572872 | tf_op jit(solution)/shard_map/ppermute | solution.py:376
  208.2 1.5 collective-permute-start.21
  209.7 2.1 add_convert_fusion.1
  211.8 1.3 collective-permute-start.23
  213.2 1.0 copy.39.place_ref
  214.2 1.0 reshape.94.gate_ref
  215.2 6.9 %unpack.1 = (bf16[1024,768]{1,0:T(8,128)(2,1)}, f32[1024,1]{1,0:T(8,128)}) custom-call(s32[1024,1]{1,0:T(8,128)} %copy.39.place_ref, f32[1024,1]{1,0:T(8,128)} %reshape.94.gate_ref, bf16[1024,768]{1,0:T(8,128)(2,1)} %bitcast.49, bf16[1536,768]{1,0:T(8,128)(2,1)} %bitcast.10.refs_1_.back_ref), custom_call_target="tpu_custom_call" | custom-call | tf_op jit(solution)/shard_map/unpack/pallas_call | solution.py:126
  222.1 1.2 reduce
  224.1 2.6 %collective-permute-done.23 = bf16[128,2048]{1,0:T(8,128)(2,1)S(1)} collective-permute-done((bf16[128,2048]{1,0:T(8,128)(2,1)}, bf16[128,2048]{1,0:T(8,128)(2,1)S(1)}, u32[]{:S(2)}, u32[]{:S(2)}) %collective-permute-start.23) | collective-permute-done | bytes 524320 | tf_op jit(solution)/shard_map/ppermute | solution.py:376
  226.7 2.4 %add_convert_fusion = bf16[128,2048]{1,0:T(8,128)(2,1)} fusion(bf16[128,2048]{1,0:T(8,128)(2,1)S(1)} %collective-permute-done.23, bf16[128,2048]{1,0:T(8,128)(2,1)} %collective-permute-done.21, bf16[128,2048]{1,0:T(8,128)(2,1)S(1)} %collective-permute-done.20, bf16[128,2048]{1,0:T(8,128)(2,1)} %collective-permute-done.13, ...), kind=kLoop, calls=%fused_computation.3 | loop fusion | flops 2621440 | bytes 3145728 | tf_op jit(solution)/shard_map/convert_element_type | solution.py:372
  (86 shorter events, 8.0 us)
Async XLA Ops:
  0.6 8.6 %copy-start = (s32[8]{0:T(128)S(1)}, s32[8]{0:T(128)}, u32[]{:S(2)}) copy-start(s32[8]{0:T(128)} %param.11) | copy-start | bytes 100
  0.6 16.4 %collective-permute-start = (bf16[128,2048]{1,0:T(8,128)(2,1)}, bf16[128,2048]{1,0:T(8,128)(2,1)S(1)}, u32[]{:S(2)}, u32[]{:S(2)}) collective-permute-start(bf16[128,2048]{1,0:T(8,128)(2,1)} %refs_0_.1), channel_id=1, source_target_pairs={{0,4},{1,5},{2,6},{3,7},{12,8},{13,9},{14,10},{15,11},{16,20},{17,... | collective-permute-start | bytes 1572872 | tf_op jit(solution)/shard_map/ppermute | solution.py:376
  5.6 11.5 %collective-permute-start.1 = (bf16[128,2048]{1,0:T(8,128)(2,1)}, bf16[128,2048]{1,0:T(8,128)(2,1)S(1)}, u32[]{:S(2)}, u32[]{:S(2)}) collective-permute-start(bf16[128,2048]{1,0:T(8,128)(2,1)} %refs_0_.1), channel_id=1, source_target_pairs={{4,8},{5,9},{6,10},{7,11},{8,4},{9,5},{10,6},{11,7},{20,24},{21,25... | collective-permute-start | bytes 1572872 | tf_op jit(solution)/shard_map/ppermute | solution.py:376
  6.3 15.5 %collective-permute-start.2 = (bf16[128,2048]{1,0:T(8,128)(2,1)}, bf16[128,2048]{1,0:T(8,128)(2,1)S(1)}, u32[]{:S(2)}, u32[]{:S(2)}) collective-permute-start(bf16[128,2048]{1,0:T(8,128)(2,1)} %refs_0_.1), channel_id=1, source_target_pairs={{4,0},{5,1},{6,2},{7,3},{8,12},{9,13},{10,14},{11,15},{20,16},{21,... | collective-permute-start | bytes 1572872 | tf_op jit(solution)/shard_map/ppermute | solution.py:376
  7.6 14.3 %collective-permute-start.3 = (bf16[128,2048]{1,0:T(8,128)(2,1)}, bf16[128,2048]{1,0:T(8,128)(2,1)S(1)}, u32[]{:S(2)}, u32[]{:S(2)}) collective-permute-start(bf16[128,2048]{1,0:T(8,128)(2,1)} %refs_0_.1), channel_id=1, source_target_pairs={{0,2},{1,3},{2,0},{3,1},{4,6},{5,7},{6,4},{7,5},{8,10},{9,11},{10,... | collective-permute-start | bytes 1572872 | tf_op jit(solution)/shard_map/ppermute | solution.py:381
  9.9 14.1 %copy-start.21 = (s32[128,8]{0,1:T(8,128)S(1)}, s32[128,8]{0,1:T(8,128)}, u32[]{:S(2)}) copy-start(s32[128,8]{0,1:T(8,128)} %param.8) | copy-start | bytes 12292
  9.9 15.8 %copy-start.19 = (f32[128,8]{0,1:T(8,128)S(1)}, f32[128,8]{0,1:T(8,128)}, u32[]{:S(2)}) copy-start(f32[128,8]{0,1:T(8,128)} %param.7) | copy-start | bytes 12292
  17.1 0.8 copy-start.16
  22.0 18.0 %copy-start.11 = (bf16[128,2048]{1,0:T(8,128)(2,1)}, bf16[128,2048]{1,0:T(8,128)(2,1)S(1)}, u32[]{:S(2)}) copy-start(bf16[128,2048]{1,0:T(8,128)(2,1)S(1)} %collective-permute-done.3.refs_3_.refs_1_) | copy-start | bytes 1572868
  22.0 18.0 %copy-start.9 = (bf16[128,2048]{1,0:T(8,128)(2,1)}, bf16[128,2048]{1,0:T(8,128)(2,1)S(1)}, u32[]{:S(2)}) copy-start(bf16[128,2048]{1,0:T(8,128)(2,1)S(1)} %get-tuple-element.39.refs_2_) | copy-start | bytes 1572868
  22.0 10.1 %collective-permute-start.4 = (bf16[128,2048]{1,0:T(8,128)(2,1)S(1)}, bf16[128,2048]{1,0:T(8,128)(2,1)S(1)}, u32[]{:S(2)}, u32[]{:S(2)}) collective-permute-start(bf16[128,2048]{1,0:T(8,128)(2,1)S(1)} %get-tuple-element.37), channel_id=1, source_target_pairs={{4,8},{5,9},{6,10},{7,11},{8,4},{9,5},{10,6},{11,7},{20,24},{21,25... | collective-permute-start | bytes 1572872 | tf_op jit(solution)/shard_map/ppermute | solution.py:376
  22.7 16.0 %collective-permute-start.5 = (bf16[128,2048]{1,0:T(8,128)(2,1)S(1)}, bf16[128,2048]{1,0:T(8,128)(2,1)}, u32[]{:S(2)}, u32[]{:S(2)}) collective-permute-start(bf16[128,2048]{1,0:T(8,128)(2,1)S(1)} %get-tuple-element.38), channel_id=1, source_target_pairs={{4,0},{5,1},{6,2},{7,3},{8,12},{9,13},{10,14},{11,15},{20,16},{21,... | collective-permute-start | bytes 1572872 | tf_op jit(solution)/shard_map/ppermute | solution.py:376
  24.1 15.8 %collective-permute-start.6 = (bf16[128,2048]{1,0:T(8,128)(2,1)S(1)}, bf16[128,2048]{1,0:T(8,128)(2,1)}, u32[]{:S(2)}, u32[]{:S(2)}) collective-permute-start(bf16[128,2048]{1,0:T(8,128)(2,1)S(1)} %get-tuple-element.39.refs_2_), channel_id=1, source_target_pairs={{0,2},{1,3},{2,0},{3,1},{4,6},{5,7},{6,4},{7,5},{8,10},{9,11},{10,... | collective-permute-start | bytes 1572872 | tf_op jit(solution)/shard_map/ppermute | solution.py:381
  40.6 1.7 copy-start.4
  42.3 23.2 %copy-start.5 = (bf16[1536,768]{1,0:T(8,128)(2,1)S(1)}, bf16[1536,768]{1,0:T(8,128)(2,1)}, u32[]{:S(2)}) copy-start(bf16[1536,768]{1,0:T(8,128)(2,1)} %get-tuple-element.40.refs_4_.refs_0_) | copy-start | bytes 7077892
  42.3 23.9 %copy-start.8 = (bf16[128,2048]{1,0:T(8,128)(2,1)}, bf16[128,2048]{1,0:T(8,128)(2,1)S(1)}, u32[]{:S(2)}) copy-start(bf16[128,2048]{1,0:T(8,128)(2,1)S(1)} %get-tuple-element.45.refs_0_) | copy-start | bytes 1572868
  42.3 18.6 %collective-permute-start.7 = (bf16[128,2048]{1,0:T(8,128)(2,1)S(1)}, bf16[128,2048]{1,0:T(8,128)(2,1)}, u32[]{:S(2)}, u32[]{:S(2)}) collective-permute-start(bf16[128,2048]{1,0:T(8,128)(2,1)S(1)} %get-tuple-element.44), channel_id=1, source_target_pairs={{4,0},{5,1},{6,2},{7,3},{8,12},{9,13},{10,14},{11,15},{20,16},{21,... | collective-permute-start | bytes 1572872 | tf_op jit(solution)/shard_map/ppermute | solution.py:376
  43.8 14.8 %all-to-all-start = ((f32[16,16,128]{2,1,0:T(8,128)}), f32[16,16,128]{2,1,0:T(8,128)S(1)}, u32[]{:S(2)}, u32[]{:S(2)}) async-start(f32[16,16,128]{2,1,0:T(8,128)} %get-tuple-element.41), calls=%async_computation | async-start | bytes 262144 | tf_op jit(solution)/shard_map/all_to_all | solution.py:431
  49.6 15.9 %collective-permute-start.8 = (bf16[128,2048]{1,0:T(8,128)(2,1)S(1)}, bf16[128,2048]{1,0:T(8,128)(2,1)}, u32[]{:S(2)}, u32[]{:S(2)}) collective-permute-start(bf16[128,2048]{1,0:T(8,128)(2,1)S(1)} %get-tuple-element.45.refs_0_), channel_id=1, source_target_pairs={{0,2},{1,3},{2,0},{3,1},{4,6},{5,7},{6,4},{7,5},{8,10},{9,11},{10,... | collective-permute-start | bytes 1572872 | tf_op jit(solution)/shard_map/ppermute | solution.py:381
  58.6 0.7 copy-start.18
  65.5 0.7 copy-start.12
  66.2 1.4 copy-start.6
  67.6 12.3 %copy-start.7 = (bf16[128,2048]{1,0:T(8,128)(2,1)}, bf16[128,2048]{1,0:T(8,128)(2,1)S(1)}, u32[]{:S(2)}) copy-start(bf16[128,2048]{1,0:T(8,128)(2,1)S(1)} %get-tuple-element.47.refs_2_) | copy-start | bytes 1572868
  67.6 56.1 %all-to-all-start.1 = ((bf16[16,96,768]{2,1,0:T(8,128)(2,1)}), bf16[16,96,768]{2,1,0:T(8,128)(2,1)S(1)}, u32[]{:S(2)}, u32[]{:S(2)}) async-start(bf16[16,96,768]{2,1,0:T(8,128)(2,1)} %bitcast.45), calls=%async_computation.1 | async-start | bytes 4718592 | tf_op jit(solution)/shard_map/all_to_all | solution.py:434
  79.4 3.9 %collective-permute-start.10 = (bf16[4,96,2048]{2,1,0:T(8,128)(2,1)}, bf16[4,96,2048]{2,1,0:T(8,128)(2,1)}, u32[]{:S(2)}, u32[]{:S(2)}) collective-permute-start(bf16[4,96,2048]{2,1,0:T(8,128)(2,1)} %get-tuple-element.48), channel_id=1, source_target_pairs={{0,1},{1,0},{2,3},{3,2},{4,5},{5,4},{6,7},{7,6},{8,9},{9,8},{10,11... | collective-permute-start | bytes 4718600 | tf_op jit(solution)/shard_map/ppermute | solution.py:381
  79.9 27.1 %collective-permute-start.9 = (bf16[128,2048]{1,0:T(8,128)(2,1)S(1)}, bf16[128,2048]{1,0:T(8,128)(2,1)S(1)}, u32[]{:S(2)}, u32[]{:S(2)}) collective-permute-start(bf16[128,2048]{1,0:T(8,128)(2,1)S(1)} %get-tuple-element.47.refs_2_), channel_id=1, source_target_pairs={{0,2},{1,3},{2,0},{3,1},{4,6},{5,7},{6,4},{7,5},{8,10},{9,11},{10,... | collective-permute-start | bytes 1572872 | tf_op jit(solution)/shard_map/ppermute | solution.py:381
  107.0 0.8 copy-start.17
  114.6 3.8 %collective-permute-start.11 = (bf16[4,96,2048]{2,1,0:T(8,128)(2,1)}, bf16[4,96,2048]{2,1,0:T(8,128)(2,1)}, u32[]{:S(2)}, u32[]{:S(2)}) collective-permute-start(bf16[4,96,2048]{2,1,0:T(8,128)(2,1)} %get-tuple-element.53), channel_id=1, source_target_pairs={{0,1},{1,0},{2,3},{3,2},{4,5},{5,4},{6,7},{7,6},{8,9},{9,8},{10,11... | collective-permute-start | bytes 4718600 | tf_op jit(solution)/shard_map/ppermute | solution.py:381
  123.8 0.7 copy-start.15
  124.5 1.9 copy-start.1
  124.5 1.9 copy-start.13
  124.5 1.9 copy-start.14
  128.9 12.4 %collective-permute-start.15 = (bf16[4,96,2048]{2,1,0:T(8,128)(2,1)}, bf16[4,96,2048]{2,1,0:T(8,128)(2,1)}, u32[]{:S(2)}, u32[]{:S(2)}) collective-permute-start(bf16[4,96,2048]{2,1,0:T(8,128)(2,1)} %forward_rows.7), channel_id=1, source_target_pairs={{0,1},{1,0},{2,3},{3,2},{4,5},{5,4},{6,7},{7,6},{8,9},{9,8},{10,11... | collective-permute-start | bytes 4718600 | tf_op jit(solution)/shard_map/ppermute | solution.py:381
  129.0 74.9 %all-to-all-start.2 = ((bf16[16,96,768]{2,1,0:T(8,128)(2,1)}), bf16[16,96,768]{2,1,0:T(8,128)(2,1)}, u32[]{:S(2)}, u32[]{:S(2)}) async-start(bf16[16,96,768]{2,1,0:T(8,128)(2,1)} %get-tuple-element.66), calls=%async_computation.2 | async-start | bytes 4718592 | tf_op jit(solution)/shard_map/all_to_all | solution.py:447
  136.2 1.9 copy-start.2
  138.1 6.7 %slice-start = ((s8[6291456]{0:T(1024)(128)(4,1)}), s8[4194304]{0:T(1024)(128)(4,1)S(1)}, s32[]{:S(2)}) async-start(s8[6291456]{0:T(1024)(128)(4,1)} %bitcast.46), calls=%async_computation.3 | async-start | bytes 8388608
  139.5 5.3 %slice-start.1 = ((s8[6291456]{0:T(1024)(128)(4,1)}), s8[2097152]{0:T(1024)(128)(4,1)S(1)}, s32[]{:S(2)}) async-start(s8[6291456]{0:T(1024)(128)(4,1)} %bitcast.46), calls=%async_computation.4 | async-start | bytes 4194304
  140.9 32.5 %collective-permute-start.12 = (bf16[4,96,2048]{2,1,0:T(8,128)(2,1)S(1)}, bf16[4,96,2048]{2,1,0:T(8,128)(2,1)S(1)}, u32[]{:S(2)}, u32[]{:S(2)}) collective-permute-start(bf16[4,96,2048]{2,1,0:T(8,128)(2,1)S(1)} %forward_rows.5), channel_id=1, source_target_pairs={{0,1},{1,0},{2,3},{3,2},{4,5},{5,4},{6,7},{7,6},{8,9},{9,8},{10,11... | collective-permute-start | bytes 4718600 | tf_op jit(solution)/shard_map/ppermute | solution.py:381
  143.1 27.4 %collective-permute-start.17 = (bf16[128,2048]{1,0:T(8,128)(2,1)S(1)}, bf16[128,2048]{1,0:T(8,128)(2,1)S(1)}, u32[]{:S(2)}, u32[]{:S(2)}) collective-permute-start(bf16[128,2048]{1,0:T(8,128)(2,1)S(1)} %get-tuple-element.65), channel_id=1, source_target_pairs={{0,2},{1,3},{2,0},{3,1},{4,6},{5,7},{6,4},{7,5},{8,10},{9,11},{10,... | collective-permute-start | bytes 1572872 | tf_op jit(solution)/shard_map/ppermute | solution.py:381
  150.2 2.5 %copy-start.10 = (bf16[1,768,2048]{2,1,0:T(8,128)(2,1)}, bf16[1,768,2048]{2,1,0:T(8,128)(2,1)S(1)}, u32[]{:S(2)}) copy-start(bf16[1,768,2048]{2,1,0:T(8,128)(2,1)S(1)} %fusion.refs_1_) | copy-start | bytes 9437188
  150.2 37.2 %collective-permute-start.16 = (bf16[128,2048]{1,0:T(8,128)(2,1)S(1)}, bf16[128,2048]{1,0:T(8,128)(2,1)S(1)}, u32[]{:S(2)}, u32[]{:S(2)}) collective-permute-start(bf16[128,2048]{1,0:T(8,128)(2,1)S(1)} %get-tuple-element.62), channel_id=1, source_target_pairs={{0,2},{1,3},{2,0},{3,1},{4,6},{5,7},{6,4},{7,5},{8,10},{9,11},{10,... | collective-permute-start | bytes 1572872 | tf_op jit(solution)/shard_map/ppermute | solution.py:381
  152.7 19.2 %copy-start.3 = (bf16[1,768,2048]{2,1,0:T(8,128)(2,1)S(1)}, bf16[1,768,2048]{2,1,0:T(8,128)(2,1)}, u32[]{:S(2)}) copy-start(bf16[1,768,2048]{2,1,0:T(8,128)(2,1)} %param.10) | copy-start | bytes 9437188
  170.6 16.8 %collective-permute-start.18 = (bf16[128,2048]{1,0:T(8,128)(2,1)S(1)}, bf16[128,2048]{1,0:T(8,128)(2,1)S(1)}, u32[]{:S(2)}, u32[]{:S(2)}) collective-permute-start(bf16[128,2048]{1,0:T(8,128)(2,1)S(1)} %fusion.1), channel_id=1, source_target_pairs={{0,4},{1,5},{2,6},{3,7},{12,8},{13,9},{14,10},{15,11},{16,20},{17,... | collective-permute-start | bytes 1572872 | tf_op jit(solution)/shard_map/ppermute | solution.py:376
  174.1 24.6 %collective-permute-start.14 = (bf16[128,2048]{1,0:T(8,128)(2,1)S(1)}, bf16[128,2048]{1,0:T(8,128)(2,1)S(1)}, u32[]{:S(2)}, u32[]{:S(2)}) collective-permute-start(bf16[128,2048]{1,0:T(8,128)(2,1)S(1)} %get-tuple-element.60), channel_id=1, source_target_pairs={{0,2},{1,3},{2,0},{3,1},{4,6},{5,7},{6,4},{7,5},{8,10},{9,11},{10,... | collective-permute-start | bytes 1572872 | tf_op jit(solution)/shard_map/ppermute | solution.py:381
  188.5 15.1 %collective-permute-start.19 = (bf16[128,2048]{1,0:T(8,128)(2,1)}, bf16[128,2048]{1,0:T(8,128)(2,1)S(1)}, u32[]{:S(2)}, u32[]{:S(2)}) collective-permute-start(bf16[128,2048]{1,0:T(8,128)(2,1)} %add_convert_fusion.3), channel_id=1, source_target_pairs={{0,4},{1,5},{2,6},{3,7},{12,8},{13,9},{14,10},{15,11},{16,20},{17,... | collective-permute-start | bytes 1572872 | tf_op jit(solution)/shard_map/ppermute | solution.py:376
  192.0 17.7 %collective-permute-start.22 = (bf16[128,2048]{1,0:T(8,128)(2,1)}, bf16[128,2048]{1,0:T(8,128)(2,1)}, u32[]{:S(2)}, u32[]{:S(2)}) collective-permute-start(bf16[128,2048]{1,0:T(8,128)(2,1)} %add_convert_fusion.3), channel_id=1, source_target_pairs={{4,8},{5,9},{6,10},{7,11},{8,4},{9,5},{10,6},{11,7},{20,24},{21,25... | collective-permute-start | bytes 1572872 | tf_op jit(solution)/shard_map/ppermute | solution.py:376
  193.5 30.6 %collective-permute-start.13 = (bf16[128,2048]{1,0:T(8,128)(2,1)S(1)}, bf16[128,2048]{1,0:T(8,128)(2,1)}, u32[]{:S(2)}, u32[]{:S(2)}) collective-permute-start(bf16[128,2048]{1,0:T(8,128)(2,1)S(1)} %get-tuple-element.58), channel_id=1, source_target_pairs={{0,2},{1,3},{2,0},{3,1},{4,6},{5,7},{6,4},{7,5},{8,10},{9,11},{10,... | collective-permute-start | bytes 1572872 | tf_op jit(solution)/shard_map/ppermute | solution.py:381
  203.9 9.3 %copy-start.20 = (s32[1,1024]{1,0:T(1,128)S(1)}, s32[1,1024]{1,0:T(1,128)}, u32[]{:S(2)}) copy-start(s32[1,1024]{1,0:T(1,128)} %get-tuple-element.67) | copy-start | bytes 12292
  203.9 20.2 %collective-permute-start.20 = (bf16[128,2048]{1,0:T(8,128)(2,1)S(1)}, bf16[128,2048]{1,0:T(8,128)(2,1)S(1)}, u32[]{:S(2)}, u32[]{:S(2)}) collective-permute-start(bf16[128,2048]{1,0:T(8,128)(2,1)S(1)} %after.11), channel_id=1, source_target_pairs={{0,4},{1,5},{2,6},{3,7},{12,8},{13,9},{14,10},{15,11},{16,20},{17,... | collective-permute-start | bytes 1572872 | tf_op jit(solution)/shard_map/ppermute | solution.py:376
  208.2 15.9 %collective-permute-start.21 = (bf16[128,2048]{1,0:T(8,128)(2,1)S(1)}, bf16[128,2048]{1,0:T(8,128)(2,1)}, u32[]{:S(2)}, u32[]{:S(2)}) collective-permute-start(bf16[128,2048]{1,0:T(8,128)(2,1)S(1)} %after.11), channel_id=1, source_target_pairs={{4,8},{5,9},{6,10},{7,11},{8,4},{9,5},{10,6},{11,7},{20,24},{21,25... | collective-permute-start | bytes 1572872 | tf_op jit(solution)/shard_map/ppermute | solution.py:376
  211.8 14.9 %collective-permute-start.23 = (bf16[128,2048]{1,0:T(8,128)(2,1)}, bf16[128,2048]{1,0:T(8,128)(2,1)S(1)}, u32[]{:S(2)}, u32[]{:S(2)}) collective-permute-start(bf16[128,2048]{1,0:T(8,128)(2,1)} %add_convert_fusion.1), channel_id=1, source_target_pairs={{4,0},{5,1},{6,2},{7,3},{8,12},{9,13},{10,14},{11,15},{20,16},{21,... | collective-permute-start | bytes 1572872 | tf_op jit(solution)/shard_map/ppermute | solution.py:376
